TPU v7x, 128 devices: a whole 4x4x4 slice. The times are simulated.
128 devices in a mesh: row: 32 (over x, z, core), col: 4 (over y).
Axes of the slice: x: 4, y: 4, z: 4, core: 2. Of those that a mesh axis runs over, the one named last changes fastest.
Arguments:
- strips: bfloat16 [160, 32, 4, 64, 512], P('col', 'row'), may hold values from -6 to 6
- pair_counts: int32 [160, 32, 2], P('col', 'row'), may hold values from 0 to 5, as said below
- pair_offsets: int32 [160, 32, 2], P('col', 'row'), may hold values from 0 to 63
- tile_stiffness: float32 [160, 32], P('col', 'row'), may hold values from 0.1 to 1
- anchor: float32 [160, 32, 896], P('col', 'row'), may hold values from 0.02 to 0.2
Outputs:
- match_terms: float32 [160, 32, 2, 3, 8], P('col', 'row')
- positions: float32 [160, 32, 2, 896], P('col', 'row')
- residual: float32 [160, 32, 2, 896], P('col', 'row')
Inputs may be any that keep to these rules, and one draw needn't show every extreme that they name: `pair_counts`: entry [r, c, 0] belongs to the pair of tiles (r, c) and (r, c + 1), entry [r, c, 1] to tiles (r, c) and (r + 1, c); it is 0 where the second tile does not exist. The 40 tiles of one device (40 consecutive tile rows of one tile column) hold at most 400 valid blocks in all, and some device holds exactly 400.
All inputs are finite; a program needn't handle non-finite values.
Results may differ from a plain program's by a relative error of at most 0.0082.
Values may be sent and summed in bfloat16 or wider, within the bound.
No kernel may reach another device: no remote copies, remote signals or barrier semaphores. Data moves between devices by JAX's collectives and lax.ppermute only.
A program may use at most 128 MiB of HBM per device.

v0:
```python
import math

import jax
import jax.numpy as jnp
from jax import lax
from jax.sharding import PartitionSpec as P

MESH_Y = 28
MESH_X = 32
ITERS = 3


SMALL_WEIGHT = 1e-06
NODE_GAP = 16.0
HIGHEST_PREC = lax.Precision.HIGHEST


def passed_along(x, axis, by):
    peers = lax.axis_size(axis)
    pairs = [(i, i + by) for i in range(peers) if 0 <= i + by < peers]
    return lax.ppermute(x, axis, pairs)


def padded_2(block, sides, width):
    for axis, dim in sides:
        count = lax.axis_size(axis)
        forward = [(i, i + 1) for i in range(count - 1)]
        backward = [(target, source) for source, target in forward]
        low = lax.ppermute(
            lax.slice_in_dim(block, block.shape[dim] - width, None, axis=dim), axis, forward
        )
        high = lax.ppermute(lax.slice_in_dim(block, 0, width, axis=dim), axis, backward)
        block = jnp.concatenate([low, block, high], axis=dim)
    return block


def dft_tables(patch_len):
    index_line = jnp.arange(patch_len, dtype=jnp.int32)
    product = index_line[:, None] * index_line[None, :] % patch_len
    angles = product.astype(jnp.float32) * (2.0 * math.pi / patch_len)
    return (jnp.cos(angles).astype(jnp.bfloat16), jnp.sin(angles).astype(jnp.bfloat16))


def spectrum(patches, cosine, sine_table):
    patch_len = cosine.shape[0]
    depth_table = jnp.concatenate([cosine, -sine_table], axis=0)
    length_table = jnp.concatenate([cosine, sine_table], axis=1)
    half_spec = jnp.einsum(
        "fd,ndbk->nfbk", depth_table, patches, preferred_element_type=jnp.float32
    )
    half_spec = half_spec.astype(jnp.bfloat16)
    full_spec = jnp.einsum(
        "nfbk,kg->nfbg", half_spec, length_table, preferred_element_type=jnp.float32
    )
    real_part = full_spec[:, :patch_len, :, :patch_len] + full_spec[:, patch_len:, :, patch_len:]
    imag_part = full_spec[:, patch_len:, :, :patch_len] - full_spec[:, :patch_len, :, patch_len:]
    return (real_part, imag_part)


def correlate(first_blocks, second_blocks, cosine, sine_table):
    patch_len = cosine.shape[0]
    first_real, first_imag = spectrum(first_blocks, cosine, sine_table)
    second_real, second_imag = spectrum(second_blocks, cosine, sine_table)
    denominator = (
        0.5
        * (
            first_real * first_real
            + first_imag * first_imag
            + second_real * second_real
            + second_imag * second_imag
        )
        + 1.0
    )
    cross_real = ((first_real * second_real + first_imag * second_imag) / denominator).astype(
        jnp.bfloat16
    )
    cross_imag = ((first_imag * second_real - first_real * second_imag) / denominator).astype(
        jnp.bfloat16
    )
    cross_stack = jnp.concatenate([cross_real, cross_imag], axis=1)
    length_table = jnp.concatenate([cosine, sine_table], axis=1)
    back_spec = jnp.einsum(
        "nubv,vg->nubg", cross_stack, length_table, preferred_element_type=jnp.float32
    )
    inverse_real = back_spec[:, :patch_len, :, :patch_len] - back_spec[:, patch_len:, :, patch_len:]
    inverse_imag = back_spec[:, patch_len:, :, :patch_len] + back_spec[:, :patch_len, :, patch_len:]
    half_back = jnp.concatenate([inverse_real, inverse_imag], axis=1).astype(jnp.bfloat16)
    back_table = jnp.concatenate([cosine, -sine_table], axis=1)
    surface = jnp.einsum("xu,nubv->nxbv", back_table, half_back, preferred_element_type=jnp.float32)
    surface = surface / float(patch_len * patch_len)
    power_map = surface * surface
    offsets = (
        (jnp.arange(patch_len, dtype=jnp.int32) + patch_len // 2) % patch_len - patch_len // 2
    ).astype(jnp.float32)
    weight = jnp.sum(power_map, axis=(1, 3))
    weight_total = weight + SMALL_WEIGHT
    shift_depth = jnp.sum(power_map * offsets[None, :, None, None], axis=(1, 3)) / weight_total
    shift_along = jnp.sum(power_map * offsets[None, None, None, :], axis=(1, 3)) / weight_total
    return (weight, shift_depth, shift_along)


def edge_tents(offsets, node_count, blocks, patch_len):
    centres = offsets[..., None] + (
        patch_len * jnp.arange(blocks, dtype=jnp.int32) + patch_len // 2
    ).astype(offsets.dtype)
    node_pos = (
        NODE_GAP * jnp.arange(node_count, dtype=jnp.int32).astype(offsets.dtype) + NODE_GAP / 2
    )
    return jnp.maximum(0.0, 1.0 - jnp.abs(centres[..., None] - node_pos) / NODE_GAP)


def spread(tent_table, weight, vectors):
    return jnp.einsum(
        "...kn,...ck->...cn", tent_table * weight[..., None], vectors, precision=HIGHEST_PREC
    )


def edge_force(tent_table, weight, difference):
    projected = jnp.einsum("...kn,...cn->...ck", tent_table, difference, precision=HIGHEST_PREC)
    return spread(tent_table, weight, projected)


def intra_term(mesh_grid, stiffness, anchor_grid):
    count_y, count_x = (mesh_grid.shape[-2], mesh_grid.shape[-1])
    widths = [(0, 0)] * (mesh_grid.ndim - 2) + [(1, 1), (1, 1)]
    padded = jnp.pad(mesh_grid, widths)
    beside = (
        padded[..., :-2, 1:-1]
        + padded[..., 2:, 1:-1]
        + padded[..., 1:-1, :-2]
        + padded[..., 1:-1, 2:]
    )
    row_ids = jnp.arange(count_y, dtype=jnp.int32)[:, None]
    col_ids = jnp.arange(count_x, dtype=jnp.int32)[None, :]
    degree = (
        (row_ids > 0).astype(mesh_grid.dtype)
        + (row_ids < count_y - 1).astype(mesh_grid.dtype)
        + (col_ids > 0).astype(mesh_grid.dtype)
        + (col_ids < count_x - 1).astype(mesh_grid.dtype)
    )
    return stiffness * (degree * mesh_grid - beside) + anchor_grid * mesh_grid


def place_edges(result, east_force, west_force, south_force, north_force):
    result = result.at[..., :, MESH_X - 1].add(east_force)
    result = result.at[..., :, 0].add(-west_force)
    result = result.at[..., MESH_Y - 1, :].add(south_force)
    result = result.at[..., 0, :].add(-north_force)
    return result


def per_device(strips, pair_counts, pair_offsets, tile_stiffness, anchor):
    tile_count = strips.shape[0]
    patch_len = strips.shape[3]
    full_len = strips.shape[4]
    blocks = full_len // patch_len
    pair_count = 2 * tile_count
    cosine, sine_table = dft_tables(patch_len)
    own_strips = strips[:, 0]
    east_tiles = passed_along(own_strips, "row", -1)
    east_left = east_tiles[:, 0]
    next_tile = passed_along(own_strips[0:1], "col", -1)
    south_top = jnp.concatenate([own_strips[1:, 1], next_tile[:, 1]], axis=0)
    first_blocks = jnp.concatenate([own_strips[:, 3], own_strips[:, 2]], axis=0)
    second_blocks = jnp.concatenate([east_left, south_top], axis=0)
    first_blocks = first_blocks.reshape(pair_count, patch_len, blocks, patch_len)
    second_blocks = second_blocks.reshape(pair_count, patch_len, blocks, patch_len)
    counts = jnp.concatenate([pair_counts[:, 0, 0], pair_counts[:, 0, 1]], axis=0)
    is_valid = jnp.arange(blocks, dtype=jnp.int32)[None, :] < counts[:, None]

    def correlate_group(group_pair):
        return correlate(group_pair[0], group_pair[1], cosine, sine_table)

    group_size = 8
    grouped = (
        first_blocks.reshape(pair_count // group_size, group_size, patch_len, blocks, patch_len),
        second_blocks.reshape(pair_count // group_size, group_size, patch_len, blocks, patch_len),
    )
    results = lax.map(correlate_group, grouped)
    weight, shift_depth, shift_along = [
        stat_block.reshape(pair_count, blocks) for stat_block in results
    ]
    weight = jnp.where(is_valid, weight, 0.0)
    shift_depth = jnp.where(is_valid, shift_depth, 0.0)
    shift_along = jnp.where(is_valid, shift_along, 0.0)
    east_weight = weight[:tile_count]
    south_weight = weight[tile_count:]
    east_shift = jnp.stack([shift_depth[:tile_count], shift_along[:tile_count]], axis=1)
    south_shift = jnp.stack([shift_along[tile_count:], shift_depth[tile_count:]], axis=1)
    east_terms = jnp.concatenate([east_weight[:, None], east_shift], axis=1)
    south_terms = jnp.concatenate([south_weight[:, None], south_shift], axis=1)
    match_terms = jnp.stack([east_terms, south_terms], axis=1)
    east_offset = pair_offsets[:, 0, 0].astype(jnp.float32)
    south_offset = pair_offsets[:, 0, 1].astype(jnp.float32)
    south_pack = jnp.concatenate(
        [south_terms, jnp.broadcast_to(south_offset[:, None, None], (tile_count, 1, blocks))],
        axis=1,
    )
    east_pack = jnp.concatenate(
        [east_terms, jnp.broadcast_to(east_offset[:, None, None], (tile_count, 1, blocks))], axis=1
    )
    west_pack = passed_along(east_pack, "row", 1)
    above_last = passed_along(south_pack[tile_count - 1 : tile_count], "col", 1)
    north_pack = jnp.concatenate([above_last, south_pack[: tile_count - 1]], axis=0)
    east_tent = edge_tents(east_offset, MESH_Y, blocks, patch_len)
    west_tent = edge_tents(west_pack[:, 3, 0], MESH_Y, blocks, patch_len)
    south_tent = edge_tents(south_offset, MESH_X, blocks, patch_len)
    north_tent = edge_tents(north_pack[:, 3, 0], MESH_X, blocks, patch_len)
    west_weight = west_pack[:, 0]
    north_weight = north_pack[:, 0]
    zero_grid = jnp.zeros((tile_count, 2, MESH_Y, MESH_X), jnp.float32)
    rhs_grid = place_edges(
        zero_grid,
        spread(east_tent, east_weight, east_shift),
        spread(west_tent, west_weight, west_pack[:, 1:3]),
        spread(south_tent, south_weight, south_shift),
        spread(north_tent, north_weight, north_pack[:, 1:3]),
    )
    right_side = rhs_grid.reshape(tile_count, 2, MESH_Y * MESH_X)
    stiffness = tile_stiffness[:, 0][:, None, None, None]
    anchor_grid = anchor[:, 0].reshape(tile_count, 1, MESH_Y, MESH_X)
    widen = ((0, 0), (0, 0), (0, MESH_X - MESH_Y))

    def squared_norm(vector_now):
        return lax.psum(jnp.sum(vector_now * vector_now), ("row", "col"))

    positions = jnp.zeros_like(right_side)
    residual = right_side
    direction = right_side
    norm_now = squared_norm(residual)
    for iteration in range(ITERS):
        mesh_grid = direction.reshape(tile_count, 2, MESH_Y, MESH_X)
        result = intra_term(mesh_grid, stiffness, anchor_grid)
        left_col = mesh_grid[..., :, 0]
        right_col = mesh_grid[..., :, MESH_X - 1]
        top_row = mesh_grid[..., 0, :]
        bottom_row = mesh_grid[..., MESH_Y - 1, :]
        side_stack = jnp.stack(
            [jnp.pad(left_col, widen), top_row, bottom_row, jnp.pad(right_col, widen)], axis=0
        )
        with_edges = padded_2(side_stack.astype(jnp.bfloat16), (("row", 0), ("col", 1)), 1).astype(
            side_stack.dtype
        )
        east_left_col = with_edges[5, 1 : tile_count + 1, :, :MESH_Y]
        west_right_col = with_edges[0, 1 : tile_count + 1, :, :MESH_Y]
        south_top_row = with_edges[2, 2 : tile_count + 2]
        north_bottom_row = with_edges[3, 0:tile_count]
        result = place_edges(
            result,
            edge_force(east_tent, east_weight, right_col - east_left_col),
            edge_force(west_tent, west_weight, west_right_col - left_col),
            edge_force(south_tent, south_weight, bottom_row - south_top_row),
            edge_force(north_tent, north_weight, north_bottom_row - top_row),
        )
        applied = result.reshape(tile_count, 2, MESH_Y * MESH_X)
        step_size = norm_now / lax.psum(jnp.sum(direction * applied), ("row", "col"))
        positions = positions + step_size * direction
        residual = residual - step_size * applied
        norm_next = squared_norm(residual)
        direction = residual + norm_next / norm_now * direction
        norm_now = norm_next
    return (match_terms[:, None], positions[:, None], residual[:, None])


def solution(mesh):
    return jax.shard_map(
        per_device,
        mesh=mesh,
        in_specs=(
            P("col", "row", None, None, None),
            P("col", "row", None),
            P("col", "row", None),
            P("col", "row"),
            P("col", "row", None),
        ),
        out_specs=(
            P("col", "row", None, None, None),
            P("col", "row", None, None),
            P("col", "row", None, None),
        ),
        check_vma=False,
    )
```

profile of v0, /device:TPU:0, one launch (start us, length us, event | category | flops | bytes accessed | tf_op | source)
XLA Modules:
  0.0 807.9 jit_solution(1781763101096415105)
XLA Ops:
  17.9 10.2 %copy.543 = bf16[80,64,512]{1,2,0:T(8,128)(2,1)} copy(bf16[80,64,512]{2,1,0:T(8,128)(2,1)} %pad_maximum_fusion) | data formatting | bytes 10485760 | tf_op jit(solution)/shard_map/concatenate | solution.py:164
  34.9 10.1 %copy.544 = bf16[80,64,512]{1,2,0:T(8,128)(2,1)} copy(bf16[80,64,512]{2,1,0:T(8,128)(2,1)} %pad_maximum_fusion.1) | data formatting | bytes 10485760 | tf_op jit(solution)/shard_map/concatenate | solution.py:165
  45.0 195.8 %while.32 = (s32[]{:T(128)}, f32[10,8,8]{2,1,0:T(8,128)S(1)}, f32[10,8,8]{2,1,0:T(8,128)S(1)}, f32[10,8,8]{2,1,0:T(8,128)S(1)}, bf16[10,8,64,8,64]{2,4,3,1,0:T(8...) while((s32[]{:T(128)}, f32[10,8,8]{2,1,0:T(8,128)S(1)}, ...), condition=%wide.region_4.5_spmd, body=%wide.region_0.4_spmd.sunk | while | flops 618136448 | bytes 31582568 | solution.py:179
  49.3 4.4 fusion.436
  53.7 7.3 divide_convert_fusion.3
  68.9 4.4 fusion.436
  73.3 7.3 divide_convert_fusion.3
  88.5 4.4 fusion.436
  92.9 7.3 divide_convert_fusion.3
  108.1 4.4 fusion.436
  112.5 7.3 divide_convert_fusion.3
  127.7 4.4 fusion.436
  132.0 7.3 divide_convert_fusion.3
  147.2 4.4 fusion.436
  151.6 7.3 divide_convert_fusion.3
  166.8 4.4 fusion.436
  171.2 7.3 divide_convert_fusion.3
  186.4 4.4 fusion.436
  190.8 7.3 divide_convert_fusion.3
  206.0 4.4 fusion.436
  210.3 7.3 divide_convert_fusion.3
  225.5 4.4 fusion.436
  229.9 7.3 divide_convert_fusion.3
  241.9 4.5 collective-permute-start.3
  246.6 89.8 %collective-permute-start.2 = (f32[40,4,8]{2,1,0:T(4,128)S(1)}, f32[40,4,8]{2,1,0:T(4,128)S(1)}, u32[]{:S(2)}, u32[]{:S(2)}) collective-permute-start(f32[40,4,8]{2,1,0:T(4,128)S(1)} %copy.553), channel_id=1, source_target_pairs={{0,4},{4,8},{8,12},{12,16},{16,20},{20,24},{24,28},{28,32},{32,36}... | collective-permute-start | bytes 15368 | tf_op jit(solution)/shard_map/ppermute | solution.py:21
  373.5 73.3 %all-reduce.10 = (f32[]{:T(128)}, f32[]{:T(128)}) all-reduce(f32[]{:T(128)} %get-tuple-element.431, f32[]{:T(128)} %get-tuple-element.430), channel_id=1, replica_groups=mesh['row'=32,'col'=4] {'row','col'}, use_global_device_ids=true, to_apply=%region_6.7 | all-reduce | flops 2 | bytes 16 | tf_op jit(solution)/shard_map/psum | solution.py:225
  449.6 62.4 %psum.44 = f32[]{:T(128)} all-reduce(f32[]{:T(128)} %multiply_reduce_fusion.3), channel_id=1, replica_groups=mesh['row'=32,'col'=4] {'row','col'}, use_global_device_ids=true, to_apply=%region_10.11 | all-reduce | flops 1 | bytes 8 | tf_op jit(solution)/shard_map/psum | solution.py:225
  525.5 4.3 collective-permute-done.11
  561.2 67.7 %psum.45 = f32[]{:T(128)} all-reduce(f32[]{:T(128)} %multiply_reduce_fusion.2), channel_id=1, replica_groups=mesh['row'=32,'col'=4] {'row','col'}, use_global_device_ids=true, to_apply=%region_12.13 | all-reduce | flops 1 | bytes 8 | tf_op jit(solution)/shard_map/psum | solution.py:256
  633.2 62.8 %psum.46 = f32[]{:T(128)} all-reduce(f32[]{:T(128)} %get-tuple-element.452), channel_id=1, replica_groups=mesh['row'=32,'col'=4] {'row','col'}, use_global_device_ids=true, to_apply=%region_14.15 | all-reduce | flops 1 | bytes 8 | tf_op jit(solution)/shard_map/psum | solution.py:225
  710.4 4.3 collective-permute-done.15
  730.6 67.6 %psum.47 = f32[]{:T(128)} all-reduce(f32[]{:T(128)} %multiply_reduce_fusion), channel_id=1, replica_groups=mesh['row'=32,'col'=4] {'row','col'}, use_global_device_ids=true, to_apply=%region_16.17 | all-reduce | flops 1 | bytes 8 | tf_op jit(solution)/shard_map/psum | solution.py:256
  (382 shorter events, 224.8 us)
Async XLA Ops:
  0.6 28.7 %collective-permute-start = (bf16[40,4,64,512]{3,2,1,0:T(8,128)(2,1)}, bf16[40,4,64,512]{3,2,1,0:T(8,128)(2,1)}, u32[]{:S(2)}, u32[]{:S(2)}) collective-permute-start(bf16[40,4,64,512]{3,2,1,0:T(8,128)(2,1)} %bitcast.338), channel_id=1, source_target_pairs={{4,0},{8,4},{12,8},{16,12},{20,16},{24,20},{28,24},{32,28},{36,32}... | collective-permute-start | bytes 31457288 | tf_op jit(solution)/shard_map/ppermute | solution.py:21
  2.9 25.6 %collective-permute-start.1 = (bf16[1,4,64,512]{3,2,1,0:T(8,128)(2,1)S(1)}, bf16[1,4,64,512]{3,2,1,0:T(8,128)(2,1)}, u32[]{:S(2)}, u32[]{:S(2)}) collective-permute-start(bf16[1,4,64,512]{3,2,1,0:T(8,128)(2,1)S(1)} %slice_bitcast_fusion.4), channel_id=1, source_target_pairs={{1,0},{2,1},{3,2},{5,4},{6,5},{7,6},{9,8},{10,9},{11,10},{13,12},{... | collective-permute-start | bytes 786440 | tf_op jit(solution)/shard_map/ppermute | solution.py:21
  8.3 232.9 %copy-start.41 = (f32[40]{0:T(128)}, f32[40]{0:T(128)S(1)}, u32[]{:S(2)}) copy-start(f32[40]{0:T(128)S(1)} %get-tuple-element.505) | copy-start | bytes 484
  45.0 201.5 %copy-start.42 = (f32[40]{0:T(128)S(1)}, f32[40]{0:T(128)}, u32[]{:S(2)}) copy-start(f32[40]{0:T(128)} %get-tuple-element.506) | copy-start | bytes 484
  45.0 292.6 %copy-start.43 = (f32[8]{0:T(128)S(1)}, f32[8]{0:T(128)}, u32[]{:S(2)}) copy-start(f32[8]{0:T(128)} %add_convert_fusion) | copy-start | bytes 100
  45.0 293.3 %copy-start.47 = (f32[32]{0:T(128)S(1)}, f32[32]{0:T(128)}, u32[]{:S(2)}) copy-start(f32[32]{0:T(128)} %multiply_add_fusion.4) | copy-start | bytes 388
  240.8 99.3 %copy-start.44 = (f32[28]{0:T(128)S(1)}, f32[28]{0:T(128)}, u32[]{:S(2)}) copy-start(f32[28]{0:T(128)} %multiply_add_fusion.5) | copy-start | bytes 340
  241.9 94.9 %collective-permute-start.3 = (f32[1,4,8]{0,2,1:T(8,128)S(1)}, f32[1,4,8]{0,2,1:T(8,128)S(1)}, u32[]{:S(2)}, u32[]{:S(2)}) collective-permute-start(f32[1,4,8]{0,2,1:T(8,128)S(1)} %slice.806), channel_id=1, source_target_pairs={{0,1},{1,2},{2,3},{4,5},{5,6},{6,7},{8,9},{9,10},{10,11},{12,13},{... | collective-permute-start | bytes 392 | tf_op jit(solution)/shard_map/ppermute | solution.py:21
  246.6 90.6 %collective-permute-start.2 = (f32[40,4,8]{2,1,0:T(4,128)S(1)}, f32[40,4,8]{2,1,0:T(4,128)S(1)}, u32[]{:S(2)}, u32[]{:S(2)}) collective-permute-start(f32[40,4,8]{2,1,0:T(4,128)S(1)} %copy.553), channel_id=1, source_target_pairs={{0,4},{4,8},{8,12},{12,16},{16,20},{20,24},{24,28},{28,32},{32,36}... | collective-permute-start | bytes 15368 | tf_op jit(solution)/shard_map/ppermute | solution.py:21
  341.8 3.6 collective-permute-start.4
  344.2 5.0 collective-permute-start.5
  349.2 5.9 collective-permute-start.6
  352.7 6.5 collective-permute-start.7
  372.1 76.9 %copy-start.12 = (f32[40,1,8]{0,2,1:T(8,128)S(1)}, f32[40,1,8]{0,2,1:T(8,128)}, u32[]{:S(2)}) copy-start(f32[40,1,8]{0,2,1:T(8,128)} %copy-done.11) | copy-start | bytes 3844
  372.1 76.9 %copy-start.14 = (f32[40,1,8]{0,2,1:T(8,128)S(1)}, f32[40,1,8]{0,2,1:T(8,128)}, u32[]{:S(2)}) copy-start(f32[40,1,8]{0,2,1:T(8,128)} %copy-done.13) | copy-start | bytes 3844
  372.1 76.9 %copy-start.21 = (f32[40,1,8]{0,2,1:T(8,128)S(1)}, f32[40,1,8]{0,2,1:T(8,128)}, u32[]{:S(2)}) copy-start(f32[40,1,8]{0,2,1:T(8,128)} %copy-done.20) | copy-start | bytes 3844
  448.1 65.6 %copy-start.40 = (f32[40,1]{0,1:T(1,128)S(1)}, f32[40,1]{0,1:T(1,128)}, u32[]{:S(2)}) copy-start(f32[40,1]{0,1:T(1,128)} %param.42) | copy-start | bytes 484
  515.2 3.1 collective-permute-start.8
  517.0 3.9 collective-permute-start.9
  521.2 4.3 collective-permute-start.10
  523.3 6.5 collective-permute-start.11
  698.7 16.3 %copy-start.39 = (f32[40,8]{1,0:T(8,128)S(1)}, f32[40,8]{1,0:T(8,128)}, u32[]{:S(2)}) copy-start(f32[40,8]{1,0:T(8,128)} %copy-done.38) | copy-start | bytes 3844
  698.7 16.8 %copy-start.30 = (f32[40,8]{1,0:T(8,128)S(1)}, f32[40,8]{1,0:T(8,128)}, u32[]{:S(2)}) copy-start(f32[40,8]{1,0:T(8,128)} %copy-done.29) | copy-start | bytes 3844
  698.8 17.4 %copy-start.37 = (f32[40,8]{1,0:T(8,128)S(1)}, f32[40,8]{1,0:T(8,128)}, u32[]{:S(2)}) copy-start(f32[40,8]{1,0:T(8,128)} %copy-done.36) | copy-start | bytes 3844
  698.8 17.8 %copy-start.26 = (f32[40,8]{1,0:T(8,128)S(1)}, f32[40,8]{1,0:T(8,128)}, u32[]{:S(2)}) copy-start(f32[40,8]{1,0:T(8,128)} %copy-done.25) | copy-start | bytes 3844
  700.2 17.3 %copy-start.35 = (f32[40,8]{1,0:T(8,128)S(1)}, f32[40,8]{1,0:T(8,128)}, u32[]{:S(2)}) copy-start(f32[40,8]{1,0:T(8,128)} %copy-done.34) | copy-start | bytes 3844
  700.2 17.3 %copy-start.46 = (f32[28]{0:T(128)S(1)}, f32[28]{0:T(128)}, u32[]{:S(2)}) copy-start(f32[28]{0:T(128)} %multiply_add_fusion.5) | copy-start | bytes 340
  700.2 17.7 %copy-start.28 = (f32[40,1,8]{2,1,0:T(1,128)S(1)}, f32[40,1,8]{2,1,0:T(1,128)}, u32[]{:S(2)}) copy-start(f32[40,1,8]{2,1,0:T(1,128)} %copy-done.27) | copy-start | bytes 3844
  700.2 3.1 collective-permute-start.12
  702.1 3.7 collective-permute-start.13
  706.0 4.4 collective-permute-start.14
  708.2 6.5 collective-permute-start.15
  (33 other events, 226.2 us)
where the time goes:
time: 821 us; the launch traced here: 808 us
  blocking collectives  334 us (41%)
  matrix products  136 us (17%)
  other arithmetic  128 us (16%)
  starting transfers between devices  119 us (14%)
  local copies, waits for them, and re-layouts  59.4 us (7%)
  waiting for transfers between devices  22.5 us (3%)
  between operations  8.79 us (1%)
    psum x3, blocking collectives, squared_norm(): return lax.psum(jnp.sum(vector_now * vector_now), ('row', 'col'))  199 us
    psum x2, blocking collectives, per_device(): lax.psum(jnp.sum(direction * applied), ('row', 'col'))  135 us
    ppermute x4, starting transfers between devices, passed_along(): return lax.ppermute(x, axis, pairs)  96.9 us
    dot_general x20, matrix products, spectrum(): jnp.einsum('nfbk,kg->nfbg', half_spec, length_table, preferred_element_ty...  86.8 us
    convert_element_type x10, other arithmetic, correlate(): ((first_real * second_real + first_imag * second_imag) / denominator).ast...  73.1 us
    ppermute x6, waiting for transfers between devices, padded_2(): lax.ppermute(lax.slice_in_dim(block, 0, width, axis=dim), axis, backward)  21 us
  transfers between devices with their start and end apart: 16, of which 8 were waited for; matrix products, arithmetic and copies ran while one was open for 4% of the time, Pallas kernels for 0%

commit v1 on v0

v1 whole, which is shorter than its diff:
```python
import functools
import math

import jax
import jax.numpy as jnp
import numpy as np
from jax import lax
from jax.experimental import pallas as pl
from jax.experimental.pallas import tpu as pltpu
from jax.sharding import PartitionSpec as P

MESH_Y = 28
MESH_X = 32
NODES = MESH_Y * MESH_X
PATCH = 64
MOST = 5
WIDE = MOST * PATCH
HALF_ROWS = 40
LANES = 128
COMP = 64
GROUP = 4
SMALL_WEIGHT = 1e-06
GAP = 16.0
F32 = jnp.float32
BF16 = jnp.bfloat16
HIGHEST = lax.Precision.HIGHEST


def tables():
    index = np.arange(PATCH)
    angle = (index[:, None] * index[None, :] % PATCH) * (2.0 * math.pi / PATCH)
    bf = jnp.bfloat16
    cos = np.cos(angle).astype(bf).astype(np.float32)
    sin = np.sin(angle).astype(bf).astype(np.float32)
    half = PATCH // 2 + 1
    depth = np.zeros((2 * HALF_ROWS, PATCH), np.float32)
    depth[:half] = cos[:half]
    depth[HALF_ROWS : HALF_ROWS + half] = -sin[:half]
    pair = np.zeros((2, 2), np.float32)
    np.fill_diagonal(pair, 1.0)
    cos2, sin2 = np.kron(pair, cos), np.kron(pair, sin)
    forward = np.block([[cos2, -sin2], [sin2, cos2]])
    back = np.block([[cos2, sin2], [-sin2, cos2]])
    back_swapped = np.block([[cos2, sin2], [sin2, -cos2]])
    twice = np.full((half,), 2.0, np.float32)
    twice[0] = twice[-1] = 1.0
    final = np.zeros((PATCH, 2 * HALF_ROWS), np.float32)
    final[:, :half] = cos[:, :half] * twice
    final[:, HALF_ROWS : HALF_ROWS + half] = -sin[:, :half] * twice
    offset = ((index + PATCH // 2) % PATCH - PATCH // 2).astype(np.float32)
    pick = np.zeros((8, LANES), np.float32)
    pick[0, :PATCH] = 1.0
    pick[1, PATCH:] = 1.0
    pick[2, :PATCH] = offset
    pick[3, PATCH:] = offset
    rows = np.repeat(offset[:, None], LANES, axis=1)
    as_bf = lambda a: jnp.asarray(a, BF16)
    backs = np.stack([back, back_swapped])
    return as_bf(depth), as_bf(forward), as_bf(backs), as_bf(final), jnp.asarray(pick), jnp.asarray(rows)


def block_pairs(strips):
    one, two = strips
    return [
        one[:, 0:128],
        one[:, 128:256],
        two[:, 0:128],
        two[:, 128:256],
        jnp.concatenate([one[:, 256:320], two[:, 256:320]], axis=1),
    ]


def correlate_group(firsts, seconds, depth, forward, back, final, rows, r0, r1, at):
    cols = block_pairs(firsts) + block_pairs(seconds)
    count = len(cols)
    half = count // 2
    spec = jnp.dot(depth, jnp.concatenate(cols, axis=1), preferred_element_type=F32)
    stacked = jnp.concatenate(
        [
            jnp.concatenate(
                [
                    spec[0:HALF_ROWS, LANES * i : LANES * (i + 1)],
                    spec[HALF_ROWS:, LANES * i : LANES * (i + 1)],
                ],
                axis=1,
            )
            for i in range(count)
        ],
        axis=0,
    ).astype(BF16)
    full = jnp.dot(stacked, forward, preferred_element_type=F32)
    split = half * HALF_ROWS
    first_real, first_imag = full[:split, :LANES], full[:split, LANES:]
    second_real, second_imag = full[split:, :LANES], full[split:, LANES:]
    denominator = (
        0.5
        * (
            first_real * first_real
            + first_imag * first_imag
            + second_real * second_real
            + second_imag * second_imag
        )
        + 1.0
    )
    inverse = 1.0 / denominator
    cross_real = (first_real * second_real + first_imag * second_imag) * inverse
    cross_imag = (first_imag * second_real - first_real * second_imag) * inverse
    cross = jnp.concatenate([cross_real, cross_imag], axis=1).astype(BF16)
    back_half = jnp.dot(cross, back, preferred_element_type=F32)
    sides = jnp.concatenate(
        [
            jnp.concatenate(
                [
                    back_half[HALF_ROWS * i : HALF_ROWS * (i + 1), :LANES],
                    back_half[HALF_ROWS * i : HALF_ROWS * (i + 1), LANES:],
                ],
                axis=0,
            )
            for i in range(half)
        ],
        axis=1,
    ).astype(BF16)
    surface = jnp.dot(final, sides, preferred_element_type=F32)
    for i in range(half):
        part = surface[:, LANES * i : LANES * (i + 1)]
        power = part * part
        total = jnp.sum(power, axis=0, keepdims=True)
        moment = jnp.sum(power * rows, axis=0, keepdims=True)
        if i < 4:
            row = at + i // 2
            r0[i % 2, pl.ds(row, 1), :] = total
            r1[i % 2, pl.ds(row, 1), :] = moment
        else:
            for row in (at, at + 1):
                r0[2, pl.ds(row, 1), :] = total
                r1[2, pl.ds(row, 1), :] = moment


def lane_sums(pick, table):
    return lax.dot_general(
        pick, table, (((1,), (1,)), ((), ())), precision=HIGHEST, preferred_element_type=F32
    )


def finish_terms(pick, r0, r1, counts, offsets, out):
    scale = 1.0 / float(PATCH * PATCH) ** 2
    even = lax.broadcasted_iota(jnp.int32, (1, LANES), 1) % 2 == 0
    plain = [lane_sums(pick, r0[s]) for s in range(3)]
    tilted = [lane_sums(pick, r1[s]) for s in range(3)]
    out[...] = jnp.zeros_like(out)
    for k in range(MOST):
        slot, side = k // 2, k % 2
        if k < 4:
            weight = plain[slot][side : side + 1]
            along = plain[slot][2 + side : 3 + side]
            deep = tilted[slot][side : side + 1]
        else:
            weight = jnp.where(even, plain[2][0:1], plain[2][1:2])
            along = jnp.where(even, plain[2][2:3], plain[2][3:4])
            deep = jnp.where(even, tilted[2][0:1], tilted[2][1:2])
        valid = counts > float(k) + 0.5
        weight = weight * scale
        inverse = scale / (weight + SMALL_WEIGHT)
        out[k : k + 1, :] = jnp.where(valid, weight, 0.0)
        out[8 + k : 9 + k, :] = jnp.where(valid, deep * inverse, 0.0)
        out[16 + k : 17 + k, :] = jnp.where(valid, along * inverse, 0.0)
    out[24:25, :] = offsets


def south_kernel(first, sec0, sec1, sec2, sec3, nxt, info, depth, forward, back, final, pick, rows, out, r0, r1):
    step = pl.program_id(0)
    last = pl.num_programs(0) - 1

    @pl.when(step == 0)
    def _():
        r0[...] = jnp.zeros_like(r0)
        r1[...] = jnp.zeros_like(r1)

    seconds = [ref[0, 0, :, :WIDE] for ref in (sec0, sec1, sec2, sec3)]
    seconds[3] = jnp.where(step == last, nxt[0], seconds[3])
    for g in range(GROUP // 2):
        correlate_group(
            [first[2 * g + j, 0, :, :WIDE] for j in range(2)],
            seconds[2 * g : 2 * g + 2],
            depth[...], forward[...], back[0], final[...], rows[...], r0, r1, GROUP * step + 2 * g,
        )

    @pl.when(step == last)
    def _():
        finish_terms(pick[...], r0, r1, info[2:3, :], info[3:4, :], out)


def side_kernel(own, from_east, from_west, info, info_west, depth, forward, back, final, pick, rows, out, r0, r1):
    step = pl.program_id(0)
    steps = pl.num_programs(0)

    @pl.when(step == 0)
    def _():
        r0[...] = jnp.zeros_like(r0)
        r1[...] = jnp.zeros_like(r1)

    east_part = step < steps // 2
    for g in range(GROUP // 2):
        others = [jnp.where(east_part, from_east[2 * g + j], from_west[2 * g + j]) for j in range(2)]
        correlate_group(
            [own[2 * g + j, 0, :, :WIDE] for j in range(2)],
            others,
            depth[...], forward[...], back[0], final[...], rows[...], r0, r1, GROUP * step + 2 * g,
        )

    @pl.when(step == steps - 1)
    def _():
        lane = lax.broadcasted_iota(jnp.int32, (1, LANES), 1)
        east = lane < GROUP * (steps // 2)
        counts = jnp.where(east, info[0:1, :], info_west[0:1, :])
        offsets = jnp.where(east, info[1:2, :], info_west[1:2, :])
        finish_terms(pick[...], r0, r1, counts, offsets, out)


def const_spec(shape):
    return pl.BlockSpec(shape, lambda i: (0,) * len(shape))


SUMS = [pltpu.VMEM((3, LANES, LANES), F32), pltpu.VMEM((3, LANES, LANES), F32)]
VMEM_BYTES = 48 * 1024 * 1024


def table_specs(tabs, back_map):
    depth, forward, backs, final, pick, rows = tabs
    return [
        const_spec(depth.shape),
        const_spec(forward.shape),
        pl.BlockSpec((1, 2 * LANES, 2 * LANES), back_map),
        const_spec(final.shape),
        const_spec(pick.shape),
        const_spec(rows.shape),
    ]


def correlation_cost(pairs):
    return pl.CostEstimate(
        flops=pairs * MOST * 12_000_000, bytes_accessed=pairs * 2 * 64 * 384 * 2, transcendentals=0
    )


def south_terms(strips, nxt, info, tabs):
    tiles = strips.shape[0]
    steps = tiles // GROUP
    side = 384

    def second_spec(j):
        return pl.BlockSpec(
            (1, 1, PATCH, side), lambda i: (jnp.minimum(GROUP * i + 1 + j, tiles - 1), 1, 0, 0)
        )

    return pl.pallas_call(
        south_kernel,
        name="south_pairs",
        grid=(steps,),
        in_specs=[pl.BlockSpec((GROUP, 1, PATCH, side), lambda i: (i, 2, 0, 0))]
        + [second_spec(j) for j in range(GROUP)]
        + [const_spec(nxt.shape), const_spec(info.shape)]
        + table_specs(tabs, lambda i: (0, 0, 0)),
        out_specs=const_spec((32, LANES)),
        out_shape=jax.ShapeDtypeStruct((32, LANES), F32),
        scratch_shapes=SUMS,
        compiler_params=pltpu.CompilerParams(vmem_limit_bytes=VMEM_BYTES),
        cost_estimate=correlation_cost(tiles),
    )(strips, strips, strips, strips, strips, nxt, info, *tabs)


def side_terms(strips, from_east, from_west, info, info_west, tabs):
    tiles = strips.shape[0]
    steps = tiles // GROUP
    mid = steps // 2
    return pl.pallas_call(
        side_kernel,
        name="side_pairs",
        grid=(steps,),
        in_specs=[
            pl.BlockSpec((GROUP, 1, PATCH, 384), lambda i: (i, jnp.where(i < mid, 3, 0), 0, 0)),
            pl.BlockSpec((GROUP, PATCH, WIDE), lambda i: (jnp.minimum(i, mid - 1), 0, 0)),
            pl.BlockSpec((GROUP, PATCH, WIDE), lambda i: (jnp.maximum(i - mid, 0), 0, 0)),
            const_spec(info.shape),
            const_spec(info.shape),
        ]
        + table_specs(tabs, lambda i: (jnp.where(i < mid, 0, 1), 0, 0)),
        out_specs=const_spec((32, LANES)),
        out_shape=jax.ShapeDtypeStruct((32, LANES), F32),
        scratch_shapes=SUMS,
        compiler_params=pltpu.CompilerParams(vmem_limit_bytes=VMEM_BYTES),
        cost_estimate=correlation_cost(tiles),
    )(strips, from_east, from_west, info, info_west, *tabs)


def prepare_kernel(counts, offsets, stiffness, anchor, info, anchor_t, small, wide):
    tiles = anchor.shape[0]
    small[...] = jnp.zeros_like(small)
    small[0:tiles, 0:1] = counts[:, 0:1].astype(F32)
    small[0:tiles, 1:2] = offsets[:, 0:1].astype(F32)
    small[0:tiles, 2:3] = counts[:, 1:2].astype(F32)
    small[0:tiles, 3:4] = offsets[:, 1:2].astype(F32)
    small[0:tiles, 4:5] = stiffness[...]
    info[...] = small[...].T[0:8, :]
    wide[...] = jnp.zeros_like(wide)
    wide[0:tiles, :] = anchor[...]
    wide[COMP : COMP + tiles, :] = anchor[...]
    for i in range(NODES // LANES):
        anchor_t[LANES * i : LANES * (i + 1), :] = wide[:, LANES * i : LANES * (i + 1)].T


def whole(kernel, outs, name, scratch=()):
    vmem = pl.BlockSpec(memory_space=pltpu.VMEM)
    shapes = [jax.ShapeDtypeStruct(s, F32) for s in outs]

    def call(*args):
        return pl.pallas_call(
            kernel,
            name=name,
            in_specs=[vmem] * len(args),
            out_specs=[vmem] * len(outs),
            out_shape=shapes,
            scratch_shapes=list(scratch),
            compiler_params=pltpu.CompilerParams(vmem_limit_bytes=VMEM_BYTES),
            cost_estimate=pl.CostEstimate(
                flops=4_000_000, bytes_accessed=2_000_000, transcendentals=0
            ),
        )(*args)

    return call


def both(x):
    return x + pltpu.roll(x, COMP, axis=1)


def pair_tables(tiles, terms_south, terms_side, from_east, from_west, from_north, info, info_west):
    lane = lax.broadcasted_iota(jnp.int32, (1, LANES), 1)
    low = lane < tiles // 2
    inside = lane < tiles
    east = jnp.where(low, terms_side[...], from_east[...])
    west = jnp.where(low, from_west[...], terms_side[...])
    south = terms_south[...]
    north = jnp.where(
        lane == 0, pltpu.roll(from_north[...], LANES - (tiles - 1), axis=1), pltpu.roll(south, 1, axis=1)
    )
    east, west, south, north = [jnp.where(inside, a, 0.0) for a in (east, west, south, north)]

    def unpack(terms, offset, swapped):
        deep, along = terms[8:16], terms[16:24]
        x, y = (along, deep) if swapped else (deep, along)
        return terms[0:8], x, y, offset

    return (
        unpack(east, info[1:2, :], False),
        unpack(west, info_west[1:2, :], False),
        unpack(south, south[24:25], True),
        unpack(north, north[24:25], True),
    )


def tents(offset, count):
    offset = both(offset)
    node = lax.broadcasted_iota(jnp.int32, (count, LANES), 0).astype(F32) * GAP + GAP / 2
    out = []
    for k in range(MOST):
        centre = offset + float(PATCH * k + PATCH // 2)
        out.append(jnp.maximum(0.0, 1.0 - jnp.abs(centre - node) / GAP))
    return out


def load_force(table, count):
    weight, x, y, offset = table
    loads = weight * x + pltpu.roll(weight * y, COMP, axis=1)
    return sum(t * loads[k : k + 1] for k, t in enumerate(tents(offset, count)))


def edge_force(table, difference):
    weight, _, _, offset = table
    weight = both(weight)
    out = 0.0
    for k, t in enumerate(tents(offset, difference.shape[0])):
        projected = jnp.sum(t * difference, axis=0, keepdims=True)
        out = out + t * (projected * weight[k : k + 1])
    return out


LEFT = pl.ds(0, MESH_Y, stride=MESH_X)
RIGHT = pl.ds(MESH_X - 1, MESH_Y, stride=MESH_X)
TOP = pl.ds(0, MESH_X)
BOTTOM = pl.ds(NODES - MESH_X, MESH_X)


def apply_inside(v, out, stiffness, anchor_t):
    column = lax.broadcasted_iota(jnp.int32, (MESH_X, LANES), 0)
    inner = jnp.where((column == 0) | (column == MESH_X - 1), 1.0, 2.0)
    for i in range(MESH_Y):
        here = v[MESH_X * i : MESH_X * (i + 1), :]
        beside = jnp.where(column == 0, 0.0, pltpu.roll(here, 1, axis=0))
        beside += jnp.where(column == MESH_X - 1, 0.0, pltpu.roll(here, MESH_X - 1, axis=0))
        degree = inner
        if i > 0:
            beside += v[MESH_X * (i - 1) : MESH_X * i, :]
            degree = degree + 1.0
        if i < MESH_Y - 1:
            beside += v[MESH_X * (i + 1) : MESH_X * (i + 2), :]
            degree = degree + 1.0
        out[MESH_X * i : MESH_X * (i + 1), :] = (
            stiffness * (degree * here - beside) + anchor_t[MESH_X * i : MESH_X * (i + 1), :] * here
        )


def add_forces(out, east, west, south, north):
    out[RIGHT, :] += east
    out[LEFT, :] -= west
    out[BOTTOM, :] += south
    out[TOP, :] -= north


def inner_product(a, b):
    return jnp.sum(a[...] * b[...], axis=0, keepdims=True)


def apply_exchanged(v, out, tables_here, beyond, stiffness, anchor_t, tiles):
    from_east, from_west, from_south, from_north = beyond
    lane = lax.broadcasted_iota(jnp.int32, (1, LANES), 1) % COMP
    apply_inside(v, out, stiffness, anchor_t)
    top, bottom = v[TOP, :], v[BOTTOM, :]
    below = jnp.where(
        lane == tiles - 1,
        pltpu.roll(from_south[...], tiles - 1, axis=1),
        pltpu.roll(top, LANES - 1, axis=1),
    )
    above = jnp.where(
        lane == 0,
        pltpu.roll(from_north[...], LANES - (tiles - 1), axis=1),
        pltpu.roll(bottom, 1, axis=1),
    )
    east, west, south, north = tables_here
    add_forces(
        out,
        edge_force(east, v[RIGHT, :] - from_east[...]),
        edge_force(west, from_west[...] - v[LEFT, :]),
        edge_force(south, bottom - below),
        edge_force(north, above - top),
    )


def start_kernel(tiles, *refs):
    ins, outs = refs[:8], refs[8:]
    info, anchor_t = ins[5], ins[7]
    v0, v1, left, right, top, bottom, match, gram, flip = outs
    tabs = pair_tables(tiles, *ins[:7])
    east, west, south, north = tabs
    stiffness = both(info[4:5, :])
    force_e = load_force(east, MESH_Y)
    force_w = load_force(west, MESH_Y)
    force_s = load_force(south, MESH_X)
    force_n = load_force(north, MESH_X)
    v0[...] = jnp.zeros_like(v0)
    add_forces(v0, force_e, force_w, force_s, force_n)
    apply_inside(v0, v1, stiffness, anchor_t)
    add_forces(
        v1,
        edge_force(east, v0[RIGHT, :] + force_e),
        edge_force(west, force_w - v0[LEFT, :]),
        edge_force(south, v0[BOTTOM, :] + force_s),
        edge_force(north, force_n - v0[TOP, :]),
    )
    left[...] = v1[LEFT, :]
    right[...] = v1[RIGHT, :]
    top[...] = v1[TOP, :]
    bottom[...] = v1[BOTTOM, :]
    gram[...] = jnp.zeros_like(gram)
    gram[0:1, :] = inner_product(v0, v0)
    gram[1:2, :] = inner_product(v0, v1)
    gram[2:3, :] = inner_product(v1, v1)
    flip[...] = jnp.zeros_like(flip)
    for q, (weight, x, y, _) in enumerate((east, south)):
        for s, rows in enumerate((weight, x, y)):
            flip[24 * q + 8 * s : 24 * q + 8 * s + 8, :] = rows
    match[...] = flip[...].T[0:tiles, 0:48]


def next_kernel(tiles, want_edges, *refs):
    ins, outs = refs[:14], refs[14:]
    info, anchor_t, previous, v, gram_in, = ins[5], ins[7], ins[8], ins[9], None
    beyond = ins[10:14]
    tabs = pair_tables(tiles, *ins[:7])
    stiffness = both(info[4:5, :])
    out, gram = outs[0], outs[1]
    apply_exchanged(v, out, tabs, beyond, stiffness, anchor_t, tiles)
    gram[...] = jnp.zeros_like(gram)
    if want_edges:
        left, right, top, bottom = outs[2:6]
        left[...] = out[LEFT, :]
        right[...] = out[RIGHT, :]
        top[...] = out[TOP, :]
        bottom[...] = out[BOTTOM, :]
        gram[3:4, :] = inner_product(v, out)
        gram[4:5, :] = inner_product(out, out)
    else:
        gram[5:6, :] = inner_product(v, out)


def final_kernel(tiles, gram, v0, v1, v2, v3, positions, residual):
    moments = jnp.sum(gram[...], axis=1, keepdims=True)
    mu = [moments[k : k + 1, :] for k in range(6)]
    zero, one = jnp.zeros_like(mu[0]), jnp.ones_like(mu[0])

    def form(a, b, shift):
        out = zero
        for i, x in enumerate(a):
            for j, y in enumerate(b):
                out = out + x * y * mu[i + j + shift]
        return out

    res, direction, pos = [one], [one], []
    norm_now = mu[0]
    for iteration in range(3):
        step = norm_now / form(direction, direction, 1)
        pos = [p + step * d for p, d in zip(pos + [zero] * (len(direction) - len(pos)), direction)]
        res = [
            r - step * d for r, d in zip(res + [zero], [zero] + direction)
        ]
        if iteration == 2:
            break
        norm_next = form(res, res, 0)
        ratio = norm_next / norm_now
        direction = [r + ratio * d for r, d in zip(res, direction + [zero])]
        norm_now = norm_next
    for out, coefficients in ((positions, pos), (residual, res)):
        for i in range(NODES // LANES):
            rows = slice(LANES * i, LANES * (i + 1))
            part = sum(c * v[rows, :] for c, v in zip(coefficients, (v0, v1, v2, v3)))
            part = part.T
            for c in range(2):
                out[:, c, rows] = part[COMP * c : COMP * c + tiles, :]


def shifted(x, axis, by):
    peers = lax.axis_size(axis)
    return lax.ppermute(x, axis, [(i, i + by) for i in range(peers) if 0 <= i + by < peers])


def add_over(x, axis, stride, radix):
    peers = lax.axis_size(axis)
    got = []
    for k in range(1, radix):
        pairs = []
        for i in range(peers):
            digit = i // stride % radix
            pairs.append((i, i + ((digit + k) % radix - digit) * stride))
        got.append(lax.ppermute(x, axis, pairs))
    for other in got:
        x = x + other
    return x


def sum_everywhere(x):
    for axis, order in (("row", (2, 4, 4)), ("col", (4,))):
        left, stride = lax.axis_size(axis), 1
        for radix in order:
            radix = math.gcd(radix, left)
            if radix > 1:
                x = add_over(x, axis, stride, radix)
                stride, left = stride * radix, left // radix
        if left > 1:
            x = add_over(x, axis, stride, left)
    return x


def per_device(strips, pair_counts, pair_offsets, tile_stiffness, anchor):
    tiles = strips.shape[0]
    half = tiles // 2
    own = strips[:, 0]
    field, column, line = (NODES, LANES), (MESH_Y, LANES), (MESH_X, LANES)
    from_east_strips = shifted(own[:half, 0, :, :WIDE], "row", -1)
    from_west_strips = shifted(own[half:, 3, :, :WIDE], "row", 1)
    next_top = shifted(own[0:1, 1, :, :WIDE], "col", -1)
    info, anchor_t = whole(
        prepare_kernel,
        [(8, LANES), field],
        "prepare",
        [pltpu.VMEM((LANES, LANES), F32), pltpu.VMEM((LANES, NODES), F32)],
    )(pair_counts[:, 0], pair_offsets[:, 0], tile_stiffness, anchor[:, 0])
    info_west = shifted(info, "row", 1)
    tabs = tables()
    terms_south = south_terms(own, next_top, info, tabs)
    from_north = shifted(terms_south, "col", 1)
    terms_side = side_terms(own, from_east_strips, from_west_strips, info, info_west, tabs)
    from_east = shifted(terms_side, "row", -1)
    from_west = shifted(terms_side, "row", 1)
    common = (terms_south, terms_side, from_east, from_west, from_north, info, info_west, anchor_t)

    def exchanged(left, right, top, bottom):
        return (
            shifted(left, "row", -1),
            shifted(right, "row", 1),
            shifted(top, "col", -1),
            shifted(bottom, "col", 1),
        )

    v0, v1, *edges, match, gram_a = whole(
        functools.partial(start_kernel, tiles),
        [field, field, column, column, line, line, (tiles, 48), (8, LANES)],
        "start",
        [pltpu.VMEM((LANES, LANES), F32)],
    )(*common)
    v2, gram_b, *edges = whole(
        functools.partial(next_kernel, tiles, True),
        [field, (8, LANES), column, column, line, line],
        "second",
    )(*common, v0, v1, *exchanged(*edges))
    v3, gram_c = whole(
        functools.partial(next_kernel, tiles, False), [field, (8, LANES)], "third"
    )(*common, v1, v2, *exchanged(*edges))
    gram = sum_everywhere(gram_a + gram_b + gram_c)
    positions, residual = whole(
        functools.partial(final_kernel, tiles),
        [(tiles, 2, NODES), (tiles, 2, NODES)],
        "combine",
    )(gram, v0, v1, v2, v3)
    return match.reshape(tiles, 1, 2, 3, 8), positions[:, None], residual[:, None]


def solution(mesh):
    return jax.shard_map(
        per_device,
        mesh=mesh,
        in_specs=(
            P("col", "row", None, None, None),
            P("col", "row", None),
            P("col", "row", None),
            P("col", "row"),
            P("col", "row", None),
        ),
        out_specs=(
            P("col", "row", None, None, None),
            P("col", "row", None, None),
            P("col", "row", None, None),
        ),
        check_vma=False,
    )
```

time: 821 us -> 130 us (0.16); the launches traced: 808 us -> 129 us
  blocking collectives: 334 us -> 0 us
  matrix products: 136 us -> 0 us
  other arithmetic: 128 us -> 0.03 us
  starting transfers between devices: 119 us -> 66 us
  local copies, waits for them, and re-layouts: 59.4 us -> 14.6 us
  Pallas kernels: 0 us -> 31.7 us
    psum x5 -> x0, blocking collectives: 334 us -> none  [the longest x3 199 us: squared_norm(): return lax.psum(jnp.sum(vector_now * vector_now), ('row', 'col'))]
    dot_general x68 -> x0, matrix products: 136 us -> none  [the longest x20 86.8 us: spectrum(): jnp.einsum('nfbk,kg->nfbg', half_spec, length_table, preferred_element_ty...]
    convert_element_type x24 -> x0, other arithmetic: 75.1 us -> none  [the longest x10 73.1 us: correlate(): ((first_real * second_real + first_imag * second_imag) / denominator).ast...]
    ppermute x16 -> x25, starting transfers between devices: 119 us -> 66 us  [the longest x15 40 us: shifted(): lax.ppermute(x, axis, [(i, i + by) for i in range(peers) if 0 <= i + by <...]
    pallas_call x0 -> x7, Pallas kernels: none -> 31.7 us  [the longest x1 14.4 us: south_terms(): pl.pallas_call(south_kernel, name='south_pairs', grid=(steps,), in_specs=...]
    concatenate x6 -> x0, local copies, waits for them, and re-layouts: 20.5 us -> none  [the longest x1 10.2 us: per_device(): first_blocks = jnp.concatenate([own_strips[:, 3], own_strips[:, 2]], axis=0)]
    add x18 -> x5, other arithmetic: 12.7 us -> 0.03 us  [the longest x4 0.02 us: add_over(): x = x + other]
    another operation x17 -> x0, other arithmetic: 12.3 us -> none
  transfers between devices with their start and end apart: 16 -> 25, of which waited for: 8 -> 11; matrix products, arithmetic and copies ran while one was open for 4% -> 1% of each run, Pallas kernels for 0% -> 22%
where the time goes in v1:
time: 130 us; the launch traced here: 129 us
  starting transfers between devices  66 us (51%)
  Pallas kernels  31.7 us (24%)
  waiting for transfers between devices  15.5 us (12%)
  local copies, waits for them, and re-layouts  14.6 us (11%)
    ppermute x15, starting transfers between devices, shifted(): lax.ppermute(x, axis, [(i, i + by) for i in range(peers) if 0 <= i + by <...  40 us
    ppermute x10, starting transfers between devices, add_over(): got.append(lax.ppermute(x, axis, pairs))  26 us
    pallas_call x1, Pallas kernels, south_terms(): pl.pallas_call(south_kernel, name='south_pairs', grid=(steps,), in_specs=...  14.4 us
    pallas_call x1, Pallas kernels, side_terms(): pl.pallas_call(side_kernel, name='side_pairs', grid=(steps,), in_specs=[p...  13.9 us
    ppermute x10, waiting for transfers between devices, add_over(): got.append(lax.ppermute(x, axis, pairs))  12.4 us
    unnamed x23, local copies, waits for them, and re-layouts  9.94 us
    pallas_call x5, Pallas kernels, call(): pl.pallas_call(kernel, name=name, in_specs=[vmem] * len(args), out_specs=...  3.46 us
    ppermute x15, waiting for transfers between devices, shifted(): lax.ppermute(x, axis, [(i, i + by) for i in range(peers) if 0 <= i + by <...  3.1 us
  transfers between devices with their start and end apart: 25, of which 11 were waited for; matrix products, arithmetic and copies ran while one was open for 1% of the time, Pallas kernels for 22%

profile of v1, /device:TPU:0, one launch (start us, length us, event | category | flops | bytes accessed | tf_op | source)
XLA Modules:
  0.0 128.9 jit_solution(6939261077266351485)
XLA Ops:
  0.7 9.8 %copy.44 = bf16[40,1,4,64,512]{4,3,0,2,1:T(8,128)(2,1)} copy(bf16[40,1,4,64,512]{4,3,2,1,0:T(8,128)(2,1)} %param.11) | data formatting | bytes 20971520 | tf_op args[0]
  10.5 3.0 %slice_bitcast_fusion = (bf16[20,64,320]{2,1,0:T(8,128)(2,1)}, bf16[20,64,320]{2,1,0:T(8,128)(2,1)}) fusion(bf16[40,4,64,512]{3,2,0,1:T(8,128)(2,1)} %bitcast.29), kind=kLoop, calls=%fused_computation.1 | loop fusion | bytes 3276800 | tf_op jit(solution)/shard_map/squeeze | solution.py:579
  13.6 1.3 collective-permute-start.1
  14.9 3.1 %collective-permute-start.2 = (bf16[20,64,320]{2,1,0:T(8,128)(2,1)}, bf16[20,64,320]{2,1,0:T(8,128)(2,1)S(1)}, u32[]{:S(2)}, u32[]{:S(2)}) collective-permute-start(bf16[20,64,320]{2,1,0:T(8,128)(2,1)} %get-tuple-element.49), channel_id=1, source_target_pairs={{0,4},{4,8},{8,12},{12,16},{16,20},{20,24},{24,28},{28,32},{32,36}... | collective-permute-start | bytes 2457608 | tf_op jit(solution)/shard_map/ppermute | solution.py:543
  18.8 1.3 collective-permute-start
  20.6 3.5 %collective-permute-start.3 = (f32[8,128]{1,0:T(8,128)S(1)}, f32[8,128]{1,0:T(8,128)S(1)}, u32[]{:S(2)}, u32[]{:S(2)}) collective-permute-start(f32[8,128]{1,0:T(8,128)S(1)} %get-tuple-element.23.info.refs_5_), channel_id=1, source_target_pairs={{0,4},{4,8},{8,12},{12,16},{16,20},{20,24},{24,28},{28,32},{32,36}... | collective-permute-start | bytes 12296 | tf_op jit(solution)/shard_map/ppermute | solution.py:543
  24.8 14.4 %south_pairs.1.refs_0_ = f32[32,128]{1,0:T(8,128)S(1)} custom-call(bf16[40,4,64,512]{3,2,1,0:T(8,128)(2,1)} %bitcast.23, bf16[40,4,64,512]{3,2,1,0:T(8,128)(2,1)} %bitcast.24, bf16[40,4,64,512]{3,2,1,0:T(8,128)(2,1)} %bitcast.25, bf16[40,4,64,512]{3,2,1,0:T(8,128)(2,1)} %bitcast.26, bf16[40,4,64,512]{3,2,1,0:T(8,128)(2,1)} %bitcast.27, ...), custom_call_target="tpu_custom_call" | custom-call | flops 2400000000 | bytes 3932160 | tf_op jit(solution)/shard_map/south_pairs/pallas_call | solution.py:256
  39.2 3.7 %collective-permute-start.6 = (f32[32,128]{1,0:T(8,128)S(1)}, f32[32,128]{1,0:T(8,128)S(1)}, u32[]{:S(2)}, u32[]{:S(2)}) collective-permute-start(f32[32,128]{1,0:T(8,128)S(1)} %south_pairs.1.refs_0_), channel_id=1, source_target_pairs={{0,1},{1,2},{2,3},{4,5},{5,6},{6,7},{8,9},{9,10},{10,11},{12,13},{... | collective-permute-start | bytes 49160 | tf_op jit(solution)/shard_map/ppermute | solution.py:543
  42.9 13.9 %side_pairs.1.refs_1_ = f32[32,128]{1,0:T(8,128)S(1)} custom-call(bf16[40,4,64,512]{3,2,1,0:T(8,128)(2,1)} %bitcast.28, bf16[20,64,320]{2,1,0:T(8,128)(2,1)S(1)} %collective-permute-done.1.from_east, bf16[20,64,320]{2,1,0:T(8,128)(2,1)S(1)} %collective-permute-done.2.from_west, f32[8,128]{1,0:T(8,128)S(1)} %get-tuple-element.23.info.refs_5_, ...), custom_call_target="tpu_custom_call" | custom-call | flops 2400000000 | bytes 3932160 | tf_op jit(solution)/shard_map/side_pairs/pallas_call | solution.py:276
  56.7 1.3 %collective-permute-start.4 = (f32[32,128]{1,0:T(8,128)S(1)}, f32[32,128]{1,0:T(8,128)S(1)}, u32[]{:S(2)}, u32[]{:S(2)}) collective-permute-start(f32[32,128]{1,0:T(8,128)S(1)} %side_pairs.1.refs_1_), channel_id=1, source_target_pairs={{4,0},{8,4},{12,8},{16,12},{20,16},{24,20},{28,24},{32,28},{36,32}... | collective-permute-start | bytes 49160 | tf_op jit(solution)/shard_map/ppermute | solution.py:543
  58.1 3.0 %collective-permute-start.5 = (f32[32,128]{1,0:T(8,128)S(1)}, f32[32,128]{1,0:T(8,128)S(1)}, u32[]{:S(2)}, u32[]{:S(2)}) collective-permute-start(f32[32,128]{1,0:T(8,128)S(1)} %side_pairs.1.refs_1_), channel_id=1, source_target_pairs={{0,4},{4,8},{8,12},{12,16},{16,20},{20,24},{24,28},{28,32},{32,36}... | collective-permute-start | bytes 49160 | tf_op jit(solution)/shard_map/ppermute | solution.py:543
  62.6 1.3 %collective-permute-start.9 = (f32[32,128]{1,0:T(8,128)S(1)}, f32[32,128]{1,0:T(8,128)S(1)}, u32[]{:S(2)}, u32[]{:S(2)}) collective-permute-start(f32[32,128]{1,0:T(8,128)S(1)} %get-tuple-element.31), channel_id=1, source_target_pairs={{1,0},{2,1},{3,2},{5,4},{6,5},{7,6},{9,8},{10,9},{11,10},{13,12},{... | collective-permute-start | bytes 49160 | tf_op jit(solution)/shard_map/ppermute | solution.py:543
  63.9 4.5 %collective-permute-start.10 = (f32[32,128]{1,0:T(8,128)S(1)}, f32[32,128]{1,0:T(8,128)S(1)}, u32[]{:S(2)}, u32[]{:S(2)}) collective-permute-start(f32[32,128]{1,0:T(8,128)S(1)} %get-tuple-element.32), channel_id=1, source_target_pairs={{0,1},{1,2},{2,3},{4,5},{5,6},{6,7},{8,9},{9,10},{10,11},{12,13},{... | collective-permute-start | bytes 49160 | tf_op jit(solution)/shard_map/ppermute | solution.py:543
  68.4 1.3 %collective-permute-start.7 = (f32[28,128]{1,0:T(8,128)S(1)}, f32[28,128]{1,0:T(8,128)S(1)}, u32[]{:S(2)}, u32[]{:S(2)}) collective-permute-start(f32[28,128]{1,0:T(8,128)S(1)} %get-tuple-element.29), channel_id=1, source_target_pairs={{4,0},{8,4},{12,8},{16,12},{20,16},{24,20},{28,24},{32,28},{36,32}... | collective-permute-start | bytes 43016 | tf_op jit(solution)/shard_map/ppermute | solution.py:543
  69.7 3.7 %collective-permute-start.8 = (f32[28,128]{1,0:T(8,128)S(1)}, f32[28,128]{1,0:T(8,128)S(1)}, u32[]{:S(2)}, u32[]{:S(2)}) collective-permute-start(f32[28,128]{1,0:T(8,128)S(1)} %get-tuple-element.30), channel_id=1, source_target_pairs={{0,4},{4,8},{8,12},{12,16},{16,20},{20,24},{24,28},{28,32},{32,36}... | collective-permute-start | bytes 43016 | tf_op jit(solution)/shard_map/ppermute | solution.py:543
  74.9 1.3 %collective-permute-start.13 = (f32[32,128]{1,0:T(8,128)S(1)}, f32[32,128]{1,0:T(8,128)S(1)}, u32[]{:S(2)}, u32[]{:S(2)}) collective-permute-start(f32[32,128]{1,0:T(8,128)S(1)} %get-tuple-element.37), channel_id=1, source_target_pairs={{1,0},{2,1},{3,2},{5,4},{6,5},{7,6},{9,8},{10,9},{11,10},{13,12},{... | collective-permute-start | bytes 49160 | tf_op jit(solution)/shard_map/ppermute | solution.py:543
  76.2 4.5 %collective-permute-start.14 = (f32[32,128]{1,0:T(8,128)S(1)}, f32[32,128]{1,0:T(8,128)S(1)}, u32[]{:S(2)}, u32[]{:S(2)}) collective-permute-start(f32[32,128]{1,0:T(8,128)S(1)} %get-tuple-element.38), channel_id=1, source_target_pairs={{0,1},{1,2},{2,3},{4,5},{5,6},{6,7},{8,9},{9,10},{10,11},{12,13},{... | collective-permute-start | bytes 49160 | tf_op jit(solution)/shard_map/ppermute | solution.py:543
  80.7 1.3 %collective-permute-start.11 = (f32[28,128]{1,0:T(8,128)S(1)}, f32[28,128]{1,0:T(8,128)S(1)}, u32[]{:S(2)}, u32[]{:S(2)}) collective-permute-start(f32[28,128]{1,0:T(8,128)S(1)} %get-tuple-element.35), channel_id=1, source_target_pairs={{4,0},{8,4},{12,8},{16,12},{20,16},{24,20},{28,24},{32,28},{36,32}... | collective-permute-start | bytes 43016 | tf_op jit(solution)/shard_map/ppermute | solution.py:543
  82.0 4.9 %collective-permute-start.12 = (f32[28,128]{1,0:T(8,128)S(1)}, f32[28,128]{1,0:T(8,128)S(1)}, u32[]{:S(2)}, u32[]{:S(2)}) collective-permute-start(f32[28,128]{1,0:T(8,128)S(1)} %get-tuple-element.36), channel_id=1, source_target_pairs={{0,4},{4,8},{8,12},{12,16},{16,20},{20,24},{24,28},{28,32},{32,36}... | collective-permute-start | bytes 43016 | tf_op jit(solution)/shard_map/ppermute | solution.py:543
  88.3 3.0 %collective-permute-start.15 = (f32[8,128]{1,0:T(8,128)S(1)}, f32[8,128]{1,0:T(8,128)S(1)}, u32[]{:S(2)}, u32[]{:S(2)}) collective-permute-start(f32[8,128]{1,0:T(8,128)S(1)} %add_add_fusion.3), channel_id=1, source_target_pairs={{0,4},{4,0},{8,12},{12,8},{16,20},{20,16},{24,28},{28,24},{32,36},... | collective-permute-start | bytes 12296 | tf_op jit(solution)/shard_map/ppermute | solution.py:554
  91.2 0.8 collective-permute-done.15
  92.1 11.8 %collective-permute-start.18 = (f32[8,128]{1,0:T(8,128)S(1)}, f32[8,128]{1,0:T(8,128)S(1)}, u32[]{:S(2)}, u32[]{:S(2)}) collective-permute-start(f32[8,128]{1,0:T(8,128)S(1)} %add.38), channel_id=1, source_target_pairs={{0,24},{4,28},{8,0},{12,4},{16,8},{20,12},{24,16},{28,20},{32,56},... | collective-permute-start | bytes 12296 | tf_op jit(solution)/shard_map/ppermute | solution.py:554
  103.8 0.9 collective-permute-start.16
  105.2 3.8 %collective-permute-done.17 = f32[8,128]{1,0:T(8,128)S(1)} collective-permute-done((f32[8,128]{1,0:T(8,128)S(1)}, f32[8,128]{1,0:T(8,128)S(1)}, u32[]{:S(2)}, u32[]{:S(2)}) %collective-permute-start.17) | collective-permute-done | bytes 4128 | tf_op jit(solution)/shard_map/ppermute | solution.py:554
  109.0 4.7 %collective-permute-start.21 = (f32[8,128]{1,0:T(8,128)S(1)}, f32[8,128]{1,0:T(8,128)S(1)}, u32[]{:S(2)}, u32[]{:S(2)}) collective-permute-start(f32[8,128]{1,0:T(8,128)S(1)} %add_add_fusion.2), channel_id=1, source_target_pairs={{0,96},{4,100},{8,104},{12,108},{16,112},{20,116},{24,120},{28,124... | collective-permute-start | bytes 12296 | tf_op jit(solution)/shard_map/ppermute | solution.py:554
  114.2 0.9 collective-permute-start.19
  115.0 3.7 %collective-permute-done.20 = f32[8,128]{1,0:T(8,128)S(1)} collective-permute-done((f32[8,128]{1,0:T(8,128)S(1)}, f32[8,128]{1,0:T(8,128)S(1)}, u32[]{:S(2)}, u32[]{:S(2)}) %collective-permute-start.20) | collective-permute-done | bytes 4128 | tf_op jit(solution)/shard_map/ppermute | solution.py:554
  119.0 0.9 collective-permute-start.24
  119.9 2.8 %collective-permute-start.23 = (f32[8,128]{1,0:T(8,128)S(1)}, f32[8,128]{1,0:T(8,128)S(1)}, u32[]{:S(2)}, u32[]{:S(2)}) collective-permute-start(f32[8,128]{1,0:T(8,128)S(1)} %add_add_fusion.1), channel_id=1, source_target_pairs={{0,2},{1,3},{2,0},{3,1},{4,6},{5,7},{6,4},{7,5},{8,10},{9,11},{10,... | collective-permute-start | bytes 12296 | tf_op jit(solution)/shard_map/ppermute | solution.py:554
  124.0 0.9 collective-permute-done.23
  125.0 2.5 %collective-permute-done.22 = f32[8,128]{1,0:T(8,128)S(1)} collective-permute-done((f32[8,128]{1,0:T(8,128)S(1)}, f32[8,128]{1,0:T(8,128)S(1)}, u32[]{:S(2)}, u32[]{:S(2)}) %collective-permute-start.22) | collective-permute-done | bytes 4128 | tf_op jit(solution)/shard_map/ppermute | solution.py:554
  127.5 1.4 %combine.1 = (f32[40,2,896]{2,1,0:T(2,128)}, f32[40,2,896]{2,1,0:T(2,128)}) custom-call(f32[8,128]{1,0:T(8,128)S(1)} %add_add_fusion.gram, f32[896,128]{1,0:T(8,128)S(1)} %get-tuple-element.27.refs_8_.v0, f32[896,128]{1,0:T(8,128)S(1)} %get-tuple-element.28.refs_9_.refs_8_.v1, f32[896,128]{1,0:T(8,128)S(1)} %get-tuple-element.34.refs_9_.v2, ...), custom_call_target="tpu_custom_call" | custom-call | flops 4000000 | bytes 2000000 | tf_op jit(solution)/shard_map/combine/pallas_call | solution.py:317
  (58 shorter events, 8.9 us)
Async XLA Ops:
  0.6 24.1 %copy-start = (bf16[2,256,256]{2,1,0:T(8,128)(2,1)S(1)}, bf16[2,256,256]{2,1,0:T(8,128)(2,1)}, u32[]{:S(2)}) copy-start(bf16[2,256,256]{2,1,0:T(8,128)(2,1)} %constant.14.clone.back) | copy-start | bytes 786436
  0.6 24.1 %copy-start.1 = (bf16[256,256]{1,0:T(8,128)(2,1)S(1)}, bf16[256,256]{1,0:T(8,128)(2,1)}, u32[]{:S(2)}) copy-start(bf16[256,256]{1,0:T(8,128)(2,1)} %constant.13.clone.forward) | copy-start | bytes 393220
  0.7 24.1 %copy-start.2 = (f32[64,128]{1,0:T(8,128)S(1)}, f32[64,128]{1,0:T(8,128)}, u32[]{:S(2)}) copy-start(f32[64,128]{1,0:T(8,128)} %constant.17.clone.rows) | copy-start | bytes 98308
  0.7 24.1 %copy-start.3 = (bf16[80,64]{1,0:T(8,128)(2,1)S(1)}, bf16[80,64]{1,0:T(8,128)(2,1)}, u32[]{:S(2)}) copy-start(bf16[80,64]{1,0:T(8,128)(2,1)} %constant.12.clone.depth) | copy-start | bytes 30724
  0.7 24.1 %copy-start.4 = (bf16[64,80]{1,0:T(8,128)(2,1)S(1)}, bf16[64,80]{1,0:T(8,128)(2,1)}, u32[]{:S(2)}) copy-start(bf16[64,80]{1,0:T(8,128)(2,1)} %constant.15.clone.final) | copy-start | bytes 30724
  0.7 24.1 %copy-start.5 = (f32[8,128]{1,0:T(8,128)S(1)}, f32[8,128]{1,0:T(8,128)}, u32[]{:S(2)}) copy-start(f32[8,128]{1,0:T(8,128)} %constant.16.clone.pick) | copy-start | bytes 12292
  0.7 19.6 %copy-start.6 = (f32[40,1,896]{2,1,0:T(1,128)S(1)}, f32[40,1,896]{2,1,0:T(1,128)}, u32[]{:S(2)}) copy-start(f32[40,1,896]{2,1,0:T(1,128)} %param.15) | copy-start | bytes 430084
  13.6 29.3 %collective-permute-start.1 = (bf16[20,64,320]{2,1,0:T(8,128)(2,1)}, bf16[20,64,320]{2,1,0:T(8,128)(2,1)S(1)}, u32[]{:S(2)}, u32[]{:S(2)}) collective-permute-start(bf16[20,64,320]{2,1,0:T(8,128)(2,1)} %get-tuple-element.50), channel_id=1, source_target_pairs={{4,0},{8,4},{12,8},{16,12},{20,16},{24,20},{28,24},{32,28},{36,32}... | collective-permute-start | bytes 2457608 | tf_op jit(solution)/shard_map/ppermute | solution.py:543
  14.9 28.0 %collective-permute-start.2 = (bf16[20,64,320]{2,1,0:T(8,128)(2,1)}, bf16[20,64,320]{2,1,0:T(8,128)(2,1)S(1)}, u32[]{:S(2)}, u32[]{:S(2)}) collective-permute-start(bf16[20,64,320]{2,1,0:T(8,128)(2,1)} %get-tuple-element.49), channel_id=1, source_target_pairs={{0,4},{4,8},{8,12},{12,16},{16,20},{20,24},{24,28},{28,32},{32,36}... | collective-permute-start | bytes 2457608 | tf_op jit(solution)/shard_map/ppermute | solution.py:543
  18.8 6.0 %collective-permute-start = (bf16[1,64,320]{2,1,0:T(8,128)(2,1)S(1)}, bf16[1,64,320]{2,1,0:T(8,128)(2,1)S(1)}, u32[]{:S(2)}, u32[]{:S(2)}) collective-permute-start(bf16[1,64,320]{2,1,0:T(8,128)(2,1)S(1)} %slice_bitcast_fusion.2), channel_id=1, source_target_pairs={{1,0},{2,1},{3,2},{5,4},{6,5},{7,6},{9,8},{10,9},{11,10},{13,12},{... | collective-permute-start | bytes 122888 | tf_op jit(solution)/shard_map/ppermute | solution.py:543
  20.6 22.3 %collective-permute-start.3 = (f32[8,128]{1,0:T(8,128)S(1)}, f32[8,128]{1,0:T(8,128)S(1)}, u32[]{:S(2)}, u32[]{:S(2)}) collective-permute-start(f32[8,128]{1,0:T(8,128)S(1)} %get-tuple-element.23.info.refs_5_), channel_id=1, source_target_pairs={{0,4},{4,8},{8,12},{12,16},{16,20},{20,24},{24,28},{28,32},{32,36}... | collective-permute-start | bytes 12296 | tf_op jit(solution)/shard_map/ppermute | solution.py:543
  39.2 21.9 %collective-permute-start.6 = (f32[32,128]{1,0:T(8,128)S(1)}, f32[32,128]{1,0:T(8,128)S(1)}, u32[]{:S(2)}, u32[]{:S(2)}) collective-permute-start(f32[32,128]{1,0:T(8,128)S(1)} %south_pairs.1.refs_0_), channel_id=1, source_target_pairs={{0,1},{1,2},{2,3},{4,5},{5,6},{6,7},{8,9},{9,10},{10,11},{12,13},{... | collective-permute-start | bytes 49160 | tf_op jit(solution)/shard_map/ppermute | solution.py:543
  56.7 4.4 %collective-permute-start.4 = (f32[32,128]{1,0:T(8,128)S(1)}, f32[32,128]{1,0:T(8,128)S(1)}, u32[]{:S(2)}, u32[]{:S(2)}) collective-permute-start(f32[32,128]{1,0:T(8,128)S(1)} %side_pairs.1.refs_1_), channel_id=1, source_target_pairs={{4,0},{8,4},{12,8},{16,12},{20,16},{24,20},{28,24},{32,28},{36,32}... | collective-permute-start | bytes 49160 | tf_op jit(solution)/shard_map/ppermute | solution.py:543
  58.1 3.9 %collective-permute-start.5 = (f32[32,128]{1,0:T(8,128)S(1)}, f32[32,128]{1,0:T(8,128)S(1)}, u32[]{:S(2)}, u32[]{:S(2)}) collective-permute-start(f32[32,128]{1,0:T(8,128)S(1)} %side_pairs.1.refs_1_), channel_id=1, source_target_pairs={{0,4},{4,8},{8,12},{12,16},{16,20},{20,24},{24,28},{28,32},{32,36}... | collective-permute-start | bytes 49160 | tf_op jit(solution)/shard_map/ppermute | solution.py:543
  62.6 11.7 %collective-permute-start.9 = (f32[32,128]{1,0:T(8,128)S(1)}, f32[32,128]{1,0:T(8,128)S(1)}, u32[]{:S(2)}, u32[]{:S(2)}) collective-permute-start(f32[32,128]{1,0:T(8,128)S(1)} %get-tuple-element.31), channel_id=1, source_target_pairs={{1,0},{2,1},{3,2},{5,4},{6,5},{7,6},{9,8},{10,9},{11,10},{13,12},{... | collective-permute-start | bytes 49160 | tf_op jit(solution)/shard_map/ppermute | solution.py:543
  63.9 10.4 %collective-permute-start.10 = (f32[32,128]{1,0:T(8,128)S(1)}, f32[32,128]{1,0:T(8,128)S(1)}, u32[]{:S(2)}, u32[]{:S(2)}) collective-permute-start(f32[32,128]{1,0:T(8,128)S(1)} %get-tuple-element.32), channel_id=1, source_target_pairs={{0,1},{1,2},{2,3},{4,5},{5,6},{6,7},{8,9},{9,10},{10,11},{12,13},{... | collective-permute-start | bytes 49160 | tf_op jit(solution)/shard_map/ppermute | solution.py:543
  68.4 5.0 %collective-permute-start.7 = (f32[28,128]{1,0:T(8,128)S(1)}, f32[28,128]{1,0:T(8,128)S(1)}, u32[]{:S(2)}, u32[]{:S(2)}) collective-permute-start(f32[28,128]{1,0:T(8,128)S(1)} %get-tuple-element.29), channel_id=1, source_target_pairs={{4,0},{8,4},{12,8},{16,12},{20,16},{24,20},{28,24},{32,28},{36,32}... | collective-permute-start | bytes 43016 | tf_op jit(solution)/shard_map/ppermute | solution.py:543
  69.7 4.6 %collective-permute-start.8 = (f32[28,128]{1,0:T(8,128)S(1)}, f32[28,128]{1,0:T(8,128)S(1)}, u32[]{:S(2)}, u32[]{:S(2)}) collective-permute-start(f32[28,128]{1,0:T(8,128)S(1)} %get-tuple-element.30), channel_id=1, source_target_pairs={{0,4},{4,8},{8,12},{12,16},{16,20},{20,24},{24,28},{28,32},{32,36}... | collective-permute-start | bytes 43016 | tf_op jit(solution)/shard_map/ppermute | solution.py:543
  74.9 12.8 %collective-permute-start.13 = (f32[32,128]{1,0:T(8,128)S(1)}, f32[32,128]{1,0:T(8,128)S(1)}, u32[]{:S(2)}, u32[]{:S(2)}) collective-permute-start(f32[32,128]{1,0:T(8,128)S(1)} %get-tuple-element.37), channel_id=1, source_target_pairs={{1,0},{2,1},{3,2},{5,4},{6,5},{7,6},{9,8},{10,9},{11,10},{13,12},{... | collective-permute-start | bytes 49160 | tf_op jit(solution)/shard_map/ppermute | solution.py:543
  76.2 11.5 %collective-permute-start.14 = (f32[32,128]{1,0:T(8,128)S(1)}, f32[32,128]{1,0:T(8,128)S(1)}, u32[]{:S(2)}, u32[]{:S(2)}) collective-permute-start(f32[32,128]{1,0:T(8,128)S(1)} %get-tuple-element.38), channel_id=1, source_target_pairs={{0,1},{1,2},{2,3},{4,5},{5,6},{6,7},{8,9},{9,10},{10,11},{12,13},{... | collective-permute-start | bytes 49160 | tf_op jit(solution)/shard_map/ppermute | solution.py:543
  80.7 6.2 %collective-permute-start.11 = (f32[28,128]{1,0:T(8,128)S(1)}, f32[28,128]{1,0:T(8,128)S(1)}, u32[]{:S(2)}, u32[]{:S(2)}) collective-permute-start(f32[28,128]{1,0:T(8,128)S(1)} %get-tuple-element.35), channel_id=1, source_target_pairs={{4,0},{8,4},{12,8},{16,12},{20,16},{24,20},{28,24},{32,28},{36,32}... | collective-permute-start | bytes 43016 | tf_op jit(solution)/shard_map/ppermute | solution.py:543
  82.0 5.7 %collective-permute-start.12 = (f32[28,128]{1,0:T(8,128)S(1)}, f32[28,128]{1,0:T(8,128)S(1)}, u32[]{:S(2)}, u32[]{:S(2)}) collective-permute-start(f32[28,128]{1,0:T(8,128)S(1)} %get-tuple-element.36), channel_id=1, source_target_pairs={{0,4},{4,8},{8,12},{12,16},{16,20},{20,24},{24,28},{28,32},{32,36}... | collective-permute-start | bytes 43016 | tf_op jit(solution)/shard_map/ppermute | solution.py:543
  88.3 3.8 %collective-permute-start.15 = (f32[8,128]{1,0:T(8,128)S(1)}, f32[8,128]{1,0:T(8,128)S(1)}, u32[]{:S(2)}, u32[]{:S(2)}) collective-permute-start(f32[8,128]{1,0:T(8,128)S(1)} %add_add_fusion.3), channel_id=1, source_target_pairs={{0,4},{4,0},{8,12},{12,8},{16,20},{20,16},{24,28},{28,24},{32,36},... | collective-permute-start | bytes 12296 | tf_op jit(solution)/shard_map/ppermute | solution.py:554
  92.1 13.1 %collective-permute-start.18 = (f32[8,128]{1,0:T(8,128)S(1)}, f32[8,128]{1,0:T(8,128)S(1)}, u32[]{:S(2)}, u32[]{:S(2)}) collective-permute-start(f32[8,128]{1,0:T(8,128)S(1)} %add.38), channel_id=1, source_target_pairs={{0,24},{4,28},{8,0},{12,4},{16,8},{20,12},{24,16},{28,20},{32,56},... | collective-permute-start | bytes 12296 | tf_op jit(solution)/shard_map/ppermute | solution.py:554
  103.8 5.1 %collective-permute-start.17 = (f32[8,128]{1,0:T(8,128)S(1)}, f32[8,128]{1,0:T(8,128)S(1)}, u32[]{:S(2)}, u32[]{:S(2)}) collective-permute-start(f32[8,128]{1,0:T(8,128)S(1)} %add.38), channel_id=1, source_target_pairs={{0,16},{4,20},{8,24},{12,28},{16,0},{20,4},{24,8},{28,12},{32,48},... | collective-permute-start | bytes 12296 | tf_op jit(solution)/shard_map/ppermute | solution.py:554
  103.8 5.1 %collective-permute-start.16 = (f32[8,128]{1,0:T(8,128)S(1)}, f32[8,128]{1,0:T(8,128)S(1)}, u32[]{:S(2)}, u32[]{:S(2)}) collective-permute-start(f32[8,128]{1,0:T(8,128)S(1)} %add.38), channel_id=1, source_target_pairs={{0,8},{4,12},{8,16},{12,20},{16,24},{20,28},{24,0},{28,4},{32,40},... | collective-permute-start | bytes 12296 | tf_op jit(solution)/shard_map/ppermute | solution.py:554
  109.0 6.1 %collective-permute-start.21 = (f32[8,128]{1,0:T(8,128)S(1)}, f32[8,128]{1,0:T(8,128)S(1)}, u32[]{:S(2)}, u32[]{:S(2)}) collective-permute-start(f32[8,128]{1,0:T(8,128)S(1)} %add_add_fusion.2), channel_id=1, source_target_pairs={{0,96},{4,100},{8,104},{12,108},{16,112},{20,116},{24,120},{28,124... | collective-permute-start | bytes 12296 | tf_op jit(solution)/shard_map/ppermute | solution.py:554
  113.6 5.1 %collective-permute-start.20 = (f32[8,128]{1,0:T(8,128)S(1)}, f32[8,128]{1,0:T(8,128)S(1)}, u32[]{:S(2)}, u32[]{:S(2)}) collective-permute-start(f32[8,128]{1,0:T(8,128)S(1)} %add_add_fusion.2), channel_id=1, source_target_pairs={{0,64},{4,68},{8,72},{12,76},{16,80},{20,84},{24,88},{28,92},{32,9... | collective-permute-start | bytes 12296 | tf_op jit(solution)/shard_map/ppermute | solution.py:554
  114.2 4.8 %collective-permute-start.19 = (f32[8,128]{1,0:T(8,128)S(1)}, f32[8,128]{1,0:T(8,128)S(1)}, u32[]{:S(2)}, u32[]{:S(2)}) collective-permute-start(f32[8,128]{1,0:T(8,128)S(1)} %add_add_fusion.2), channel_id=1, source_target_pairs={{0,32},{4,36},{8,40},{12,44},{16,48},{20,52},{24,56},{28,60},{32,6... | collective-permute-start | bytes 12296 | tf_op jit(solution)/shard_map/ppermute | solution.py:554
  119.0 5.1 %collective-permute-start.24 = (f32[8,128]{1,0:T(8,128)S(1)}, f32[8,128]{1,0:T(8,128)S(1)}, u32[]{:S(2)}, u32[]{:S(2)}) collective-permute-start(f32[8,128]{1,0:T(8,128)S(1)} %add_add_fusion.1), channel_id=1, source_target_pairs={{0,3},{1,0},{2,1},{3,2},{4,7},{5,4},{6,5},{7,6},{8,11},{9,8},{10,9... | collective-permute-start | bytes 12296 | tf_op jit(solution)/shard_map/ppermute | solution.py:554
  119.9 5.1 %collective-permute-start.23 = (f32[8,128]{1,0:T(8,128)S(1)}, f32[8,128]{1,0:T(8,128)S(1)}, u32[]{:S(2)}, u32[]{:S(2)}) collective-permute-start(f32[8,128]{1,0:T(8,128)S(1)} %add_add_fusion.1), channel_id=1, source_target_pairs={{0,2},{1,3},{2,0},{3,1},{4,6},{5,7},{6,4},{7,5},{8,10},{9,11},{10,... | collective-permute-start | bytes 12296 | tf_op jit(solution)/shard_map/ppermute | solution.py:554
  122.6 4.8 %collective-permute-start.22 = (f32[8,128]{1,0:T(8,128)S(1)}, f32[8,128]{1,0:T(8,128)S(1)}, u32[]{:S(2)}, u32[]{:S(2)}) collective-permute-start(f32[8,128]{1,0:T(8,128)S(1)} %add_add_fusion.1), channel_id=1, source_target_pairs={{0,1},{1,2},{2,3},{3,0},{4,5},{5,6},{6,7},{7,4},{8,9},{9,10},{10,1... | collective-permute-start | bytes 12296 | tf_op jit(solution)/shard_map/ppermute | solution.py:554
  (3 other events, 58.3 us)

commit v2 on v1

v2 whole, which is shorter than its diff:
```python
import functools
import math

import jax
import jax.numpy as jnp
import numpy as np
from jax import lax
from jax.experimental import pallas as pl
from jax.experimental.pallas import tpu as pltpu
from jax.sharding import PartitionSpec as P

MESH_Y = 28
MESH_X = 32
NODES = MESH_Y * MESH_X
PATCH = 64
MOST = 5
WIDE = MOST * PATCH
ROWS = 32
EXTRA = 40
LANES = 128
COMP = 64
GROUP = 10
TALL = MESH_X * MESH_X
SMALL_WEIGHT = 1e-06
GAP = 16.0
F32 = jnp.float32
BF16 = jnp.bfloat16
HIGHEST = lax.Precision.HIGHEST


def tables():
    index = np.arange(PATCH)
    angle = (index[:, None] * index[None, :] % PATCH) * (2.0 * math.pi / PATCH)
    bf = jnp.bfloat16
    cos = np.cos(angle).astype(bf).astype(np.float32)
    sin = np.sin(angle).astype(bf).astype(np.float32)
    half = PATCH // 2
    depth = np.concatenate([cos[: half + 1], -sin[1:half]])
    pair = np.eye(2, dtype=np.float32)
    cos2, sin2 = np.kron(pair, cos), np.kron(pair, sin)
    forward = np.block([[cos2, -sin2], [sin2, cos2]])
    ends = np.kron(pair, np.concatenate([cos2, -sin2], axis=1))
    back = np.block([[cos2, sin2], [-sin2, cos2]])
    back_swapped = np.block([[cos2, sin2], [sin2, -cos2]])
    twice = np.full((PATCH,), 2.0, np.float32)
    twice[0] = twice[half] = 1.0
    final = np.concatenate([cos[:, : half + 1], -sin[:, 1:half]], axis=1) * twice
    offset = ((index + PATCH // 2) % PATCH - PATCH // 2).astype(np.float32)
    pick = np.zeros((8, LANES), np.float32)
    pick[0, :PATCH] = 1.0
    pick[1, PATCH:] = 1.0
    pick[2, :PATCH] = offset
    pick[3, PATCH:] = offset
    rows = np.repeat(offset[:, None], LANES, axis=1)
    as_bf = lambda a: jnp.asarray(a, BF16)
    backs = np.stack([back, back_swapped])
    return as_bf(depth), as_bf(forward), as_bf(ends), as_bf(backs), as_bf(final), jnp.asarray(pick), jnp.asarray(rows)


def block_pairs(strips):
    out = []
    for one, two in zip(strips[0::2], strips[1::2]):
        out += [
            one[:, 0:128],
            one[:, 128:256],
            two[:, 0:128],
            two[:, 128:256],
            jnp.concatenate([one[:, 256:320], two[:, 256:320]], axis=1),
        ]
    return out


def cross_power(first_real, first_imag, second_real, second_imag):
    denominator = (
        0.5
        * (
            first_real * first_real
            + first_imag * first_imag
            + second_real * second_real
            + second_imag * second_imag
        )
        + 1.0
    )
    inverse = 1.0 / denominator
    real = (first_real * second_real + first_imag * second_imag) * inverse
    imag = (first_imag * second_real - first_real * second_imag) * inverse
    return real, imag


def correlate_group(cols, depth, forward, ends, back, final, rows, r0, r1, at):
    count = len(cols)
    half = count // 2
    lanes = [slice(LANES * i, LANES * (i + 1)) for i in range(count)]
    spec = jnp.dot(depth, jnp.concatenate(cols, axis=1), preferred_element_type=F32)
    stacked = jnp.concatenate(
        [jnp.concatenate([spec[:ROWS, s], spec[ROWS:, s]], axis=1) for s in lanes], axis=0
    ).astype(BF16)
    end_rows = jnp.concatenate(
        [
            jnp.concatenate([spec[0:1, s] for s in lanes], axis=0),
            jnp.concatenate([spec[ROWS : ROWS + 1, s] for s in lanes], axis=0),
        ],
        axis=1,
    ).astype(BF16)
    full = jnp.dot(stacked, forward, preferred_element_type=F32)
    end = jnp.dot(end_rows, ends, preferred_element_type=F32)
    split = half * ROWS
    cross_real, cross_imag = cross_power(
        full[:split, :LANES], full[:split, LANES:], full[split:, :LANES], full[split:, LANES:]
    )
    cross = jnp.concatenate([cross_real, cross_imag], axis=1).astype(BF16)
    end_cross = []
    for s in (0, 2 * LANES):
        end_cross.append(
            jnp.concatenate(
                cross_power(
                    end[:half, s : s + LANES],
                    end[:half, s + LANES : s + 2 * LANES],
                    end[half:, s : s + LANES],
                    end[half:, s + LANES : s + 2 * LANES],
                ),
                axis=1,
            )
        )
    end_back = [
        jnp.dot(c.astype(BF16), back[:, :LANES], preferred_element_type=F32) for c in end_cross
    ]
    back_half = jnp.dot(cross, back, preferred_element_type=F32)
    is_end = lax.broadcasted_iota(jnp.int32, (8, LANES), 0) == 0

    def side(i):
        parts = []
        for part in range(2):
            block = back_half[ROWS * i : ROWS * (i + 1), lanes[part]]
            parts.append(jnp.where(is_end, end_back[part][i : i + 1], block[:8]))
            parts.append(block[8:])
        return jnp.concatenate(parts, axis=0)

    sides = jnp.concatenate([side(i) for i in range(half)], axis=1).astype(BF16)
    surface = jnp.dot(final, sides, preferred_element_type=F32)
    for i in range(half):
        part = surface[:, lanes[i]]
        power = part * part
        total = jnp.sum(power, axis=0, keepdims=True)
        moment = jnp.sum(power * rows, axis=0, keepdims=True)
        place = i % 5
        if i == 5 * (half // 5):
            r0[0, EXTRA : EXTRA + 1, :] = total
            r1[0, EXTRA : EXTRA + 1, :] = moment
        elif place < 4:
            row = at + 2 * (i // 5) + place // 2
            r0[place % 2, pl.ds(row, 1), :] = total
            r1[place % 2, pl.ds(row, 1), :] = moment
        else:
            for row in (at + 2 * (i // 5), at + 2 * (i // 5) + 1):
                r0[2, pl.ds(row, 1), :] = total
                r1[2, pl.ds(row, 1), :] = moment


def lane_sums(pick, table):
    return lax.dot_general(
        pick, table, (((1,), (1,)), ((), ())), precision=HIGHEST, preferred_element_type=F32
    )


def finish_terms(pick, r0, r1, counts, offsets, out):
    scale = 1.0 / float(PATCH * PATCH) ** 2
    even = lax.broadcasted_iota(jnp.int32, (1, LANES), 1) % 2 == 0
    plain = [lane_sums(pick, r0[s]) for s in range(3)]
    tilted = [lane_sums(pick, r1[s]) for s in range(3)]
    out[...] = jnp.zeros_like(out)
    for k in range(MOST):
        slot, side = k // 2, k % 2
        if k < 4:
            weight = plain[slot][side : side + 1]
            along = plain[slot][2 + side : 3 + side]
            deep = tilted[slot][side : side + 1]
        else:
            weight = jnp.where(even, plain[2][0:1], plain[2][1:2])
            along = jnp.where(even, plain[2][2:3], plain[2][3:4])
            deep = jnp.where(even, tilted[2][0:1], tilted[2][1:2])
        valid = counts > float(k) + 0.5
        weight = weight * scale
        inverse = scale / (weight + SMALL_WEIGHT)
        out[k : k + 1, :] = jnp.where(valid, weight, 0.0)
        out[8 + k : 9 + k, :] = jnp.where(valid, deep * inverse, 0.0)
        out[16 + k : 17 + k, :] = jnp.where(valid, along * inverse, 0.0)
    out[24:25, :] = offsets


def south_kernel(*refs):
    first, seconds = refs[0], refs[1 : 1 + GROUP]
    nxt, info, anchor_t, depth, forward, ends, back, final, pick, rows, out, r0, r1 = refs[1 + GROUP :]
    step = pl.program_id(0)
    last = pl.num_programs(0) - 1

    @pl.when(step == 0)
    def _():
        r0[...] = jnp.zeros_like(r0)
        r1[...] = jnp.zeros_like(r1)

    seconds = [ref[0, 0, :, :WIDE] for ref in seconds]
    seconds[-1] = jnp.where(step == last, nxt[0, :, :WIDE], seconds[-1])
    firsts = [first[j, 0, :, :WIDE] for j in range(GROUP)]
    correlate_group(
        block_pairs(firsts) + block_pairs(seconds),
        depth[...], forward[...], ends[...], back[0], final[...], rows[...], r0, r1, GROUP * step,
    )

    @pl.when(step == last)
    def _():
        finish_terms(pick[...], r0, r1, info[2:3, :], info[3:4, :], out)
        out[25:26, :] = info[4:5, :]
        out[32:, :] = anchor_t[...]


def side_kernel(own, from_east, from_west, own_extra, extra, info, depth, forward, ends, back, final, pick, rows, out, r0, r1):
    step = pl.program_id(0)
    steps = pl.num_programs(0)

    @pl.when(step == 0)
    def _():
        r0[...] = jnp.zeros_like(r0)
        r1[...] = jnp.zeros_like(r1)

    east_part = step < steps // 2
    others = []
    for slot in range(GROUP // 2):
        packed = jnp.where(east_part, from_east[slot], from_west[slot])
        others += [packed[:, LANES * i : LANES * (i + 1)] for i in range(5)]
    owns = block_pairs([own[j, 0, :, :WIDE] for j in range(GROUP)])
    correlate_group(
        owns + [own_extra[0, 0]] + others + [extra[0, :, :LANES]],
        depth[...], forward[...], ends[...], back[0], final[...], rows[...], r0, r1, GROUP * step,
    )

    @pl.when(step == steps - 1)
    def _():
        lane = lax.broadcasted_iota(jnp.int32, (8, LANES), 1)
        info_west = extra[0, 0:16, 2 * LANES : 3 * LANES].astype(F32)[0:8]
        table = jnp.where(lane < GROUP * (steps // 2), info[...], info_west)
        table = jnp.where(lane == EXTRA, pltpu.roll(info_west, EXTRA, axis=1), table)
        finish_terms(pick[...], r0, r1, table[0:1], table[1:2], out)


def const_spec(shape):
    return pl.BlockSpec(shape, lambda i: (0,) * len(shape))


SUMS = [pltpu.VMEM((3, LANES, LANES), F32), pltpu.VMEM((3, LANES, LANES), F32)]
VMEM_BYTES = 48 * 1024 * 1024


def table_specs(tabs, back_map):
    depth, forward, ends, backs, final, pick, rows = tabs
    return [
        const_spec(depth.shape),
        const_spec(forward.shape),
        const_spec(ends.shape),
        pl.BlockSpec((1, 2 * LANES, 2 * LANES), back_map),
        const_spec(final.shape),
        const_spec(pick.shape),
        const_spec(rows.shape),
    ]


def correlation_cost(pairs):
    return pl.CostEstimate(
        flops=pairs * MOST * 12_000_000, bytes_accessed=pairs * 2 * 64 * 384 * 2, transcendentals=0
    )


def south_terms(strips, nxt, info, anchor_t, tabs):
    tiles = strips.shape[0]
    steps = tiles // GROUP
    side = 384

    def second_spec(j):
        return pl.BlockSpec(
            (1, 1, PATCH, side), lambda i: (jnp.minimum(GROUP * i + 1 + j, tiles - 1), 1, 0, 0)
        )

    return pl.pallas_call(
        south_kernel,
        name="south_pairs",
        grid=(steps,),
        in_specs=[pl.BlockSpec((GROUP, 1, PATCH, side), lambda i: (i, 2, 0, 0))]
        + [second_spec(j) for j in range(GROUP)]
        + [const_spec(nxt.shape), const_spec(info.shape)]
        + [pl.BlockSpec((MESH_X, LANES), lambda i: (MESH_Y - 1, 0))]
        + table_specs(tabs, lambda i: (0, 0, 0)),
        out_specs=const_spec((64, LANES)),
        out_shape=jax.ShapeDtypeStruct((64, LANES), F32),
        scratch_shapes=SUMS,
        compiler_params=pltpu.CompilerParams(vmem_limit_bytes=VMEM_BYTES),
        cost_estimate=correlation_cost(tiles),
    )(*[strips] * (1 + GROUP), nxt, info, anchor_t, *tabs)


def side_terms(strips, from_east, from_west, info, tabs):
    tiles = strips.shape[0]
    steps = tiles // GROUP
    mid = steps // 2
    packed = (GROUP // 2, PATCH, 2 * WIDE)
    return pl.pallas_call(
        side_kernel,
        name="side_pairs",
        grid=(steps,),
        in_specs=[
            pl.BlockSpec((GROUP, 1, PATCH, 384), lambda i: (i, jnp.where(i < mid, 3, 0), 0, 0)),
            pl.BlockSpec(packed, lambda i: (jnp.minimum(i, mid - 1), 0, 0)),
            pl.BlockSpec(packed, lambda i: (jnp.maximum(i - mid, 0), 0, 0)),
            pl.BlockSpec((1, 1, PATCH, LANES), lambda i: (0, 0, 0, 0)),
            pl.BlockSpec((1, PATCH, 2 * WIDE), lambda i: (tiles // 4, 0, 0)),
            const_spec(info.shape),
        ]
        + table_specs(tabs, lambda i: (jnp.where(i < mid, 0, 1), 0, 0)),
        out_specs=const_spec((32, LANES)),
        out_shape=jax.ShapeDtypeStruct((32, LANES), F32),
        scratch_shapes=SUMS,
        compiler_params=pltpu.CompilerParams(vmem_limit_bytes=VMEM_BYTES),
        cost_estimate=correlation_cost(tiles),
    )(strips, from_east, from_west, strips, from_west, info, *tabs)


def prepare_kernel(strips, counts, offsets, stiffness, anchor, west, east, north, info, anchor_t, left, right, small, wide, sems):
    tiles = anchor.shape[0]
    half = tiles // 2
    moves = [
        (strips.at[pl.ds(half, half), 3, :, pl.ds(0, 384)], right),
        (strips.at[pl.ds(0, half), 0, :, pl.ds(0, 384)], left),
        (strips.at[0, 3, :, pl.ds(0, LANES)], east.at[half // 2, :, pl.ds(0, LANES)]),
        (strips.at[0, 1, :, pl.ds(0, 384)], north.at[0]),
    ]
    moves = [pltpu.make_async_copy(a, b, sems.at[k]) for k, (a, b) in enumerate(moves)]
    for move in moves:
        move.start()
    small[...] = jnp.zeros_like(small)
    small[0:tiles, 0:1] = counts[:, 0:1].astype(F32)
    small[0:tiles, 1:2] = offsets[:, 0:1].astype(F32)
    small[0:tiles, 2:3] = counts[:, 1:2].astype(F32)
    small[0:tiles, 3:4] = offsets[:, 1:2].astype(F32)
    small[0:tiles, 4:5] = stiffness[...]
    flat = small[...].T
    info[...] = flat[0:8, :]
    wide[...] = jnp.zeros_like(wide)
    wide[0:tiles, :] = anchor[...]
    wide[COMP : COMP + tiles, :] = anchor[...]
    for i in range(NODES // LANES):
        anchor_t[LANES * i : LANES * (i + 1), :] = wide[:, LANES * i : LANES * (i + 1)].T
    east[half // 2, :, LANES:] = jnp.zeros((PATCH, 2 * WIDE - LANES), BF16)
    east[half // 2, 0:16, 2 * LANES : 3 * LANES] = flat[0:16, :].astype(BF16)
    for move, source, packed in ((moves[0], right, east), (moves[1], left, west)):
        move.wait()
        for slot in range(half // 2):
            columns = block_pairs([source[2 * slot + j, :, :WIDE] for j in range(2)])
            for i, x in enumerate(columns):
                packed[slot, :, LANES * i : LANES * (i + 1)] = x
    moves[2].wait()
    moves[3].wait()


def prepare(strips, counts, offsets, stiffness, anchor):
    tiles = anchor.shape[0]
    vmem = pl.BlockSpec(memory_space=pltpu.VMEM)
    slots = tiles // 4
    return pl.pallas_call(
        prepare_kernel,
        name="prepare",
        in_specs=[pl.BlockSpec(memory_space=pl.ANY)] + [vmem] * 4,
        out_specs=[vmem] * 5,
        out_shape=[
            jax.ShapeDtypeStruct((slots, PATCH, 2 * WIDE), BF16),
            jax.ShapeDtypeStruct((slots + 1, PATCH, 2 * WIDE), BF16),
            jax.ShapeDtypeStruct((1, PATCH, 384), BF16),
            jax.ShapeDtypeStruct((8, LANES), F32),
            jax.ShapeDtypeStruct((NODES, LANES), F32),
        ],
        scratch_shapes=[
            pltpu.VMEM((tiles // 2, PATCH, 384), BF16),
            pltpu.VMEM((tiles // 2, PATCH, 384), BF16),
            pltpu.VMEM((LANES, LANES), F32),
            pltpu.VMEM((LANES, NODES), F32),
            pltpu.SemaphoreType.DMA((4,)),
        ],
        compiler_params=pltpu.CompilerParams(vmem_limit_bytes=VMEM_BYTES),
    )(strips, counts, offsets, stiffness, anchor)


def whole(kernel, outs, name, scratch=()):
    vmem = pl.BlockSpec(memory_space=pltpu.VMEM)
    shapes = [jax.ShapeDtypeStruct(s, F32) for s in outs]

    def call(*args):
        return pl.pallas_call(
            kernel,
            name=name,
            in_specs=[vmem] * len(args),
            out_specs=[vmem] * len(outs),
            out_shape=shapes,
            scratch_shapes=list(scratch),
            compiler_params=pltpu.CompilerParams(vmem_limit_bytes=VMEM_BYTES),
            cost_estimate=pl.CostEstimate(
                flops=4_000_000, bytes_accessed=2_000_000, transcendentals=0
            ),
        )(*args)

    return call


def both(x):
    return x + pltpu.roll(x, COMP, axis=1)


def tents(offset, count):
    offset = both(offset)
    node = lax.broadcasted_iota(jnp.int32, (count, LANES), 0).astype(F32) * GAP + GAP / 2
    out = []
    for k in range(MOST):
        centre = offset + float(PATCH * k + PATCH // 2)
        out.append(jnp.maximum(0.0, 1.0 - jnp.abs(centre - node) / GAP))
    return out


def load_force(table):
    weight, x, y, shapes = table
    lane = lax.broadcasted_iota(jnp.int32, (1, LANES), 1)
    loads = weight * jnp.where(lane < COMP, x, pltpu.roll(y, COMP, axis=1))
    return sum(t * loads[k : k + 1] for k, t in enumerate(shapes))


def edge_force(table, difference):
    weight, _, _, shapes = table
    out = 0.0
    for k, t in enumerate(shapes):
        projected = jnp.sum(t * difference, axis=0, keepdims=True)
        out = out + t * (projected * weight[k : k + 1])
    return out


LEFT = pl.ds(0, MESH_X, stride=MESH_X)
RIGHT = pl.ds(MESH_X - 1, MESH_X, stride=MESH_X)
TOP = pl.ds(0, MESH_X)
BOTTOM = pl.ds(NODES - MESH_X, MESH_X)


def apply_inside(v, out, stiffness, anchor_t):
    column = lax.broadcasted_iota(jnp.int32, (MESH_X, LANES), 0)
    inner = jnp.where((column == 0) | (column == MESH_X - 1), 1.0, 2.0)
    for i in range(MESH_Y):
        here = v[MESH_X * i : MESH_X * (i + 1), :]
        beside = along_row(here, column)
        degree = inner
        if i > 0:
            beside += v[MESH_X * (i - 1) : MESH_X * i, :]
            degree = degree + 1.0
        if i < MESH_Y - 1:
            beside += v[MESH_X * (i + 1) : MESH_X * (i + 2), :]
            degree = degree + 1.0
        out[MESH_X * i : MESH_X * (i + 1), :] = (
            stiffness * (degree * here - beside) + anchor_t[MESH_X * i : MESH_X * (i + 1), :] * here
        )
    out[NODES:, :] = jnp.zeros((TALL - NODES, LANES), F32)


def along_row(x, node):
    before = jnp.where(node == 0, 0.0, pltpu.roll(x, 1, axis=0))
    return before + jnp.where(node == MESH_X - 1, 0.0, pltpu.roll(x, MESH_X - 1, axis=0))


def along_column(x, node):
    after = jnp.where(node >= MESH_Y - 1, 0.0, pltpu.roll(x, MESH_X - 1, axis=0))
    return after + jnp.where(node >= MESH_Y, 0.0, pltpu.roll(x, 1, axis=0))


def add_forces(out, east, west, south, north):
    out[RIGHT, :] += east
    out[LEFT, :] -= west
    out[BOTTOM, :] += south
    out[TOP, :] -= north


def inner_product(a, b):
    return jnp.sum(a[0:NODES, :] * b[0:NODES, :], axis=0, keepdims=True)


def message_kernel(tiles, terms_south, terms_side, from_north, info, anchor_t, to_west, to_east, to_north):
    lane = lax.broadcasted_iota(jnp.int32, (1, LANES), 1)
    side = terms_side[...]
    for out in (to_west, to_east, to_north):
        out[0:32, :] = side
        out[25:26, :] = info[4:5, :]
    south = terms_south[0:32, :]
    north = roll_tiles(south, 1, from_north[0:32, :], tiles)
    for q, terms in enumerate((south, north)):
        for k, row in enumerate((0, 8, 16, 24)):
            to_west[32 + 4 * q + k : 33 + 4 * q + k, :] = terms[row : row + 1]
    first = anchor_t[pl.ds(0, MESH_Y, stride=MESH_X), :]
    second = anchor_t[pl.ds(1, MESH_Y, stride=MESH_X), :]
    to_west[40 : 40 + MESH_Y, :] = jnp.where(lane < COMP, first, second)
    to_west[40 + MESH_Y :, :] = jnp.zeros((4, LANES), F32)
    to_east[32 : 32 + MESH_Y, :] = anchor_t[pl.ds(MESH_X - 1, MESH_Y, stride=MESH_X), :]
    to_east[32 + MESH_Y :, :] = jnp.zeros((4, LANES), F32)
    to_north[32:, :] = jnp.where(
        lane == 0, anchor_t[0:MESH_X, :], pltpu.roll(anchor_t[MESH_X : 2 * MESH_X, :], 1, axis=1)
    )


def roll_tiles(x, by, outside, tiles):
    lane = lax.broadcasted_iota(jnp.int32, (1, LANES), 1) % COMP
    if by == 1:
        edge, beyond = lane == 0, pltpu.roll(outside, LANES - (tiles - 1), axis=1)
    else:
        edge, beyond = lane == tiles - 1, pltpu.roll(outside, tiles - 1, axis=1)
    return jnp.where(edge, beyond, pltpu.roll(x, by % LANES, axis=1))


def pick_lane(x, source, target):
    lane = lax.broadcasted_iota(jnp.int32, (1, LANES), 1)
    return both(jnp.where(lane == target, pltpu.roll(x, (target - source) % LANES, axis=1), 0.0))


def near_tents(offset):
    return [
        jnp.maximum(0.0, 1.0 - jnp.abs(offset + (PATCH // 2 - GAP * n - GAP / 2)) / GAP) for n in (1, 2)
    ]


def near_pair(weight, x, y, offset):
    one, two = near_tents(offset)
    lane = lax.broadcasted_iota(jnp.int32, (1, LANES), 1)
    load = weight * jnp.where(lane < COMP, x, y)
    force = weight * one * (one * (2.0 * one * load) + two * (2.0 * two * load))
    return one * load, two * load, force


def mesh_kernel(tiles, *refs):
    terms_south, terms_side, from_east, from_west, from_south, from_north, info, anchor_t = refs[:8]
    v0, v1, v2, v3, match, gram, flip = refs[8:]
    lane = lax.broadcasted_iota(jnp.int32, (1, LANES), 1)
    node = lax.broadcasted_iota(jnp.int32, (MESH_X, LANES), 0)
    low, inside = lane < tiles // 2, lane < tiles
    side = terms_side[...]
    south_terms = terms_south[0:32, :]
    terms = [
        jnp.where(low, side, from_east[0:32, :]),
        jnp.where(low, from_west[0:32, :], side),
        south_terms,
        roll_tiles(south_terms, 1, from_north[0:32, :], tiles),
    ]
    tables_here = []
    for q, table in enumerate(terms):
        table = jnp.where(inside, table, 0.0)
        deep, along = table[8:16], table[16:24]
        x, y = (deep, along) if q < 2 else (along, deep)
        tables_here.append((both(table[0:8]), x, y, tents(table[24:25], MESH_X)))
    east, west, south, north = tables_here
    stiffness = both(info[4:5, :])

    flip[...] = jnp.zeros_like(flip)
    for q, (weight, x, y, _) in enumerate((east, south)):
        for s, rows in enumerate((jnp.where(lane < COMP, weight, 0.0), x, y)):
            flip[24 * q + 8 * s : 24 * q + 8 * s + 8, :] = rows
    match[...] = flip[...].T[0:tiles, 0:48]

    force_e, force_w, force_s, force_n = [load_force(t) for t in tables_here]
    v0[...] = jnp.zeros_like(v0)
    add_forces(v0, force_e, force_w, force_s, force_n)

    outside_east, outside_west = both(from_east[25:26, :]), both(from_west[25:26, :])
    packed = from_east[40:72, :]
    turned = pltpu.roll(packed, COMP, axis=1)
    anchor_e0 = jnp.where(lane < COMP, packed, turned)
    anchor_e1 = jnp.where(lane < COMP, turned, packed)
    anchor_w0 = from_west[32:64, :]
    last = tiles - 1
    outside_south = pick_lane(from_south[25:26, :], 0, last)
    anchor_s0 = pick_lane(from_south[32:64, :], 0, last)
    anchor_s1 = pick_lane(from_south[32:64, :], 1, last)
    outside_north = pick_lane(from_north[25:26, :], last, 0)
    anchor_n0 = pick_lane(from_north[32:64, :], last, 0)

    degree_c = jnp.where((node == 0) | (node == MESH_Y - 1), 2.0, 3.0)
    degree_r = jnp.where((node == 0) | (node == MESH_X - 1), 2.0, 3.0)

    near_s = near_pair(*[both(from_east[32 + k : 33 + k, :]) for k in (0, 2, 1, 3)])
    near_n = near_pair(*[both(from_east[36 + k : 37 + k, :]) for k in (0, 2, 1, 3)])
    at_ends = lambda a, b, x, y: jnp.where(node == a, x, 0.0) - jnp.where(node == b, y, 0.0)
    e0 = -force_e
    e1 = at_ends(MESH_Y - 1, 0, near_s[0], near_n[0])
    e2 = at_ends(MESH_Y - 1, 0, near_s[1], near_n[1])
    e1_pairs = at_ends(MESH_Y - 1, 0, near_s[2], near_n[2])
    w0 = force_w
    near_e = near_pair(*[pick_lane(from_south[k : k + 1, :], 0, last) for k in (0, 8, 16, 24)])
    near_w = near_pair(*[pick_lane(from_south[k : k + 1, :], EXTRA, last) for k in (0, 8, 16, 24)])
    s0 = -force_s
    s1 = at_ends(MESH_X - 1, 0, near_e[0], near_w[0])
    s2 = at_ends(MESH_X - 1, 0, near_e[1], near_w[1])
    s1_pairs = at_ends(MESH_X - 1, 0, near_e[2], near_w[2])
    n0 = force_n

    apply_inside(v0, v1, stiffness, anchor_t)
    pull_e = edge_force(east, v0[RIGHT, :] - e0)
    pull_w = edge_force(west, w0 - v0[LEFT, :])
    pull_s = edge_force(south, v0[BOTTOM, :] - s0)
    pull_n = edge_force(north, n0 - v0[TOP, :])
    add_forces(v1, pull_e, pull_w, pull_s, pull_n)
    e0, e1 = (
        outside_east * (degree_c * e0 - along_column(e0, node) - e1) + anchor_e0 * e0 - pull_e,
        outside_east * ((degree_c + 1.0) * e1 - along_column(e1, node) - e0 - e2) + anchor_e1 * e1 + e1_pairs,
    )
    w0, w1 = (
        outside_west * (degree_c * w0 - along_column(w0, node)) + anchor_w0 * w0 + pull_w,
        -outside_west * w0,
    )
    s0, s1 = (
        outside_south * (degree_r * s0 - along_row(s0, node) - s1) + anchor_s0 * s0 - pull_s,
        outside_south * ((degree_r + 1.0) * s1 - along_row(s1, node) - s0 - s2) + anchor_s1 * s1 + s1_pairs,
    )
    n0, n1 = (
        outside_north * (degree_r * n0 - along_row(n0, node)) + anchor_n0 * n0 + pull_n,
        -outside_north * n0,
    )

    def pulls(v, e0, w0, s0, n0):
        top, bottom = v[TOP, :], v[BOTTOM, :]
        spot = lane % COMP
        below = jnp.where(spot == last, s0, pltpu.roll(top, LANES - 1, axis=1))
        above = jnp.where(spot == 0, n0, pltpu.roll(bottom, 1, axis=1))
        return (
            edge_force(east, v[RIGHT, :] - e0),
            edge_force(west, w0 - v[LEFT, :]),
            edge_force(south, bottom - below),
            edge_force(north, above - top),
        )

    apply_inside(v1, v2, stiffness, anchor_t)
    pull_e, pull_w, pull_s, pull_n = pulls(v1, e0, w0, s0, n0)
    add_forces(v2, pull_e, pull_w, pull_s, pull_n)
    e0 = outside_east * (degree_c * e0 - along_column(e0, node) - e1) + anchor_e0 * e0 - pull_e
    w0 = outside_west * (degree_c * w0 - along_column(w0, node) - w1) + anchor_w0 * w0 + pull_w
    s0 = outside_south * (degree_r * s0 - along_row(s0, node) - s1) + anchor_s0 * s0 - pull_s
    n0 = outside_north * (degree_r * n0 - along_row(n0, node) - n1) + anchor_n0 * n0 + pull_n

    apply_inside(v2, v3, stiffness, anchor_t)
    add_forces(v3, *pulls(v2, e0, w0, s0, n0))

    gram[...] = jnp.zeros_like(gram)
    for k, (a, b) in enumerate(((v0, v0), (v0, v1), (v1, v1), (v1, v2), (v2, v2), (v2, v3))):
        gram[k : k + 1, :] = inner_product(a, b)


def final_kernel(tiles, gram, v0, v1, v2, v3, positions, residual):
    moments = jnp.sum(gram[...], axis=1, keepdims=True)
    mu = [moments[k : k + 1, :] for k in range(6)]
    zero, one = jnp.zeros_like(mu[0]), jnp.ones_like(mu[0])

    def form(a, b, shift):
        out = zero
        for i, x in enumerate(a):
            for j, y in enumerate(b):
                out = out + x * y * mu[i + j + shift]
        return out

    res, direction, pos = [one], [one], []
    norm_now = mu[0]
    for iteration in range(3):
        step = norm_now / form(direction, direction, 1)
        pos = [p + step * d for p, d in zip(pos + [zero] * (len(direction) - len(pos)), direction)]
        res = [
            r - step * d for r, d in zip(res + [zero], [zero] + direction)
        ]
        if iteration == 2:
            break
        norm_next = form(res, res, 0)
        ratio = norm_next / norm_now
        direction = [r + ratio * d for r, d in zip(res, direction + [zero])]
        norm_now = norm_next
    for out, coefficients in ((positions, pos), (residual, res)):
        for i in range(NODES // LANES):
            rows = slice(LANES * i, LANES * (i + 1))
            part = sum(c * v[rows, :] for c, v in zip(coefficients, (v0, v1, v2, v3)))
            part = part.T
            for c in range(2):
                out[:, c, rows] = part[COMP * c : COMP * c + tiles, :]


def shifted(x, axis, by):
    peers = lax.axis_size(axis)
    return lax.ppermute(x, axis, [(i, i + by) for i in range(peers) if 0 <= i + by < peers])


def add_over(x, axis, stride, radix):
    peers = lax.axis_size(axis)
    got = []
    for k in range(1, radix):
        pairs = []
        for i in range(peers):
            digit = i // stride % radix
            pairs.append((i, i + ((digit + k) % radix - digit) * stride))
        got.append(lax.ppermute(x, axis, pairs))
    for other in got:
        x = x + other
    return x


def sum_everywhere(x):
    for axis, order in (("row", (2, 4, 4)), ("col", (4,))):
        left, stride = lax.axis_size(axis), 1
        for radix in order:
            radix = math.gcd(radix, left)
            if radix > 1:
                x = add_over(x, axis, stride, radix)
                stride, left = stride * radix, left // radix
        if left > 1:
            x = add_over(x, axis, stride, left)
    return x


def per_device(strips, pair_counts, pair_offsets, tile_stiffness, anchor):
    tiles = strips.shape[0]
    own = strips[:, 0]
    field = (TALL, LANES)
    to_west, to_east, to_north, info, anchor_t = prepare(
        own, pair_counts[:, 0], pair_offsets[:, 0], tile_stiffness, anchor[:, 0]
    )
    strips_west = shifted(to_east, "row", 1)
    strips_east = shifted(to_west, "row", -1)
    next_top = shifted(to_north, "col", -1)
    tabs = tables()
    terms_south = south_terms(own, next_top, info, anchor_t, tabs)
    from_north = shifted(terms_south, "col", 1)
    terms_side = side_terms(own, strips_east, strips_west, info, tabs)
    to_west, to_east, to_north = whole(
        functools.partial(message_kernel, tiles),
        [(72, LANES), (64, LANES), (64, LANES)],
        "messages",
    )(terms_south, terms_side, from_north, info, anchor_t)
    from_east = shifted(to_west, "row", -1)
    from_west = shifted(to_east, "row", 1)
    from_south = shifted(to_north, "col", -1)
    v0, v1, v2, v3, match, gram = whole(
        functools.partial(mesh_kernel, tiles),
        [field, field, field, field, (tiles, 48), (8, LANES)],
        "powers",
        [pltpu.VMEM((LANES, LANES), F32)],
    )(terms_south, terms_side, from_east, from_west, from_south, from_north, info, anchor_t)
    gram = sum_everywhere(gram)
    positions, residual = whole(
        functools.partial(final_kernel, tiles),
        [(tiles, 2, NODES), (tiles, 2, NODES)],
        "combine",
    )(gram, v0, v1, v2, v3)
    return match.reshape(tiles, 1, 2, 3, 8), positions[:, None], residual[:, None]


def solution(mesh):
    return jax.shard_map(
        per_device,
        mesh=mesh,
        in_specs=(
            P("col", "row", None, None, None),
            P("col", "row", None),
            P("col", "row", None),
            P("col", "row"),
            P("col", "row", None),
        ),
        out_specs=(
            P("col", "row", None, None, None),
            P("col", "row", None, None),
            P("col", "row", None, None),
        ),
        check_vma=False,
    )
```

time: 130 us -> 76.2 us (0.59)
  starting transfers between devices: 66 us -> 29.5 us
  Pallas kernels: 31.7 us -> 18.7 us
  local copies, waits for them, and re-layouts: 14.6 us -> 3.98 us
  waiting for transfers between devices: 15.5 us -> 22.7 us
    ppermute x15 -> x7, starting transfers between devices: 40 us -> 14.4 us  [shifted(): lax.ppermute(x, axis, [(i, i + by) for i in range(peers) if 0 <= i + by <...]
    ppermute x10, starting transfers between devices: 26 us -> 15.2 us  [add_over(): got.append(lax.ppermute(x, axis, pairs))]
    unnamed x23 -> x16, local copies, waits for them, and re-layouts: 9.94 us -> 1.7 us
    pallas_call x1, Pallas kernels: 14.4 us -> 7.13 us  [south_terms(): pl.pallas_call(south_kernel, name='south_pairs', grid=(steps,), in_specs=...]
    pallas_call x1, Pallas kernels: 13.9 us -> 6.83 us  [side_terms(): pl.pallas_call(side_kernel, name='side_pairs', grid=(steps,), in_specs=[p...]
    ppermute x15 -> x7, waiting for transfers between devices: 3.1 us -> 9.29 us  [shifted(): lax.ppermute(x, axis, [(i, i + by) for i in range(peers) if 0 <= i + by <...]
    squeeze x2 -> x0, local copies, waits for them, and re-layouts: 3.84 us -> none  [the longest x1 3.03 us: per_device(): from_west_strips = shifted(own[half:, 3, :, :WIDE], 'row', 1)]
    pallas_call x0 -> x1, Pallas kernels: none -> 1.77 us  [prepare(): pl.pallas_call(prepare_kernel, name='prepare', in_specs=[pl.BlockSpec(mem...]
  transfers between devices with their start and end apart: 25 -> 17, of which waited for: 11 -> 9; matrix products, arithmetic and copies ran while one was open for 1% -> 1% of each run, Pallas kernels for 22% -> 18%
where the time goes in v2:
time: 76.2 us; the launch traced here: 75.8 us
  starting transfers between devices  29.5 us (39%)
  waiting for transfers between devices  22.7 us (30%)
  Pallas kernels  18.7 us (25%)
  local copies, waits for them, and re-layouts  3.98 us (5%)
  between operations  0.85 us (1%)
    ppermute x10, starting transfers between devices, add_over(): got.append(lax.ppermute(x, axis, pairs))  15.2 us
    ppermute x7, starting transfers between devices, shifted(): lax.ppermute(x, axis, [(i, i + by) for i in range(peers) if 0 <= i + by <...  14.4 us
    ppermute x10, waiting for transfers between devices, add_over(): got.append(lax.ppermute(x, axis, pairs))  13.4 us
    ppermute x7, waiting for transfers between devices, shifted(): lax.ppermute(x, axis, [(i, i + by) for i in range(peers) if 0 <= i + by <...  9.29 us
    pallas_call x1, Pallas kernels, south_terms(): pl.pallas_call(south_kernel, name='south_pairs', grid=(steps,), in_specs=...  7.13 us
    pallas_call x1, Pallas kernels, side_terms(): pl.pallas_call(side_kernel, name='side_pairs', grid=(steps,), in_specs=[p...  6.83 us
    pallas_call x3, Pallas kernels, call(): pl.pallas_call(kernel, name=name, in_specs=[vmem] * len(args), out_specs=...  3 us
    pallas_call x1, Pallas kernels, prepare(): pl.pallas_call(prepare_kernel, name='prepare', in_specs=[pl.BlockSpec(mem...  1.77 us
  transfers between devices with their start and end apart: 17, of which 9 were waited for; matrix products, arithmetic and copies ran while one was open for 1% of the time, Pallas kernels for 18%

profile of v2, /device:TPU:0, one launch (start us, length us, event | category | flops | bytes accessed | tf_op | source)
XLA Modules:
  0.0 75.8 jit_solution(8507384803277576996)
XLA Ops:
  0.7 0.8 %copy.21.counts = s32[40,2]{1,0:T(8,128)S(1)} copy(s32[40,2]{0,1:T(2,128)} %bitcast.29) | data formatting | bytes 640 | tf_op jit(solution)/shard_map/squeeze | solution.py:725
  1.5 0.8 %copy.22.offsets = s32[40,2]{1,0:T(8,128)S(1)} copy(s32[40,2]{0,1:T(2,128)} %bitcast.30) | data formatting | bytes 640 | tf_op jit(solution)/shard_map/squeeze | solution.py:725
  2.3 0.7 copy.23.stiffness
  3.0 0.9 %copy.29 = f32[40,1,896]{2,0,1:T(8,128)S(1)} copy(f32[40,1,896]{2,1,0:T(1,128)} %param.16) | data formatting | bytes 286720
  4.0 1.8 %prepare.1 = (bf16[10,64,640]{2,1,0:T(8,128)(2,1)S(1)}, bf16[11,64,640]{2,1,0:T(8,128)(2,1)S(1)}, bf16[1,64,384]{2,1,0:T(8,128)(2,1)S(1)}, f32[8,128]{1,0:T(8,128)S(1)}, f32[896,128]{1,0:T(8,128)S(1)}) custom-call(bf16[40,4,64,512]{3,2,1,0:T(8,128)(2,1)} %bitcast.14, s32[40,2]{1,0:T(8,128)S(1)} %copy.21.counts, s32[40,2]{1,0:T(8,128)S(1)} %copy.22.offsets, ...), custom_call_target="tpu_custom_call" | custom-call | tf_op jit(solution)/shard_map/prepare/pallas_call | solution.py:367
  5.7 1.3 %collective-permute-start.2 = (bf16[11,64,640]{2,1,0:T(8,128)(2,1)S(1)}, bf16[11,64,640]{2,1,0:T(8,128)(2,1)S(1)}, u32[]{:S(2)}, u32[]{:S(2)}) collective-permute-start(bf16[11,64,640]{2,1,0:T(8,128)(2,1)S(1)} %get-tuple-element.23), channel_id=1, source_target_pairs={{0,4},{4,8},{8,12},{12,16},{16,20},{20,24},{24,28},{28,32},{32,36}... | collective-permute-start | bytes 2703368 | tf_op jit(solution)/shard_map/ppermute | solution.py:690
  7.1 1.3 %collective-permute-start.1 = (bf16[10,64,640]{2,1,0:T(8,128)(2,1)S(1)}, bf16[10,64,640]{2,1,0:T(8,128)(2,1)S(1)}, u32[]{:S(2)}, u32[]{:S(2)}) collective-permute-start(bf16[10,64,640]{2,1,0:T(8,128)(2,1)S(1)} %get-tuple-element.22), channel_id=1, source_target_pairs={{4,0},{8,4},{12,8},{16,12},{20,16},{24,20},{28,24},{32,28},{36,32}... | collective-permute-start | bytes 2457608 | tf_op jit(solution)/shard_map/ppermute | solution.py:690
  8.4 1.3 %collective-permute-start = (bf16[1,64,384]{2,1,0:T(8,128)(2,1)S(1)}, bf16[1,64,384]{2,1,0:T(8,128)(2,1)S(1)}, u32[]{:S(2)}, u32[]{:S(2)}) collective-permute-start(bf16[1,64,384]{2,1,0:T(8,128)(2,1)S(1)} %get-tuple-element.19), channel_id=1, source_target_pairs={{1,0},{2,1},{3,2},{5,4},{6,5},{7,6},{9,8},{10,9},{11,10},{13,12},{... | collective-permute-start | bytes 147464 | tf_op jit(solution)/shard_map/ppermute | solution.py:690
  9.7 4.8 %collective-permute-done.refs_11_ = bf16[1,64,384]{2,1,0:T(8,128)(2,1)S(1)} collective-permute-done((bf16[1,64,384]{2,1,0:T(8,128)(2,1)S(1)}, bf16[1,64,384]{2,1,0:T(8,128)(2,1)S(1)}, u32[]{:S(2)}, u32[]{:S(2)}) %collective-permute-start) | collective-permute-done | bytes 49184 | tf_op jit(solution)/shard_map/ppermute | solution.py:690
  14.5 7.1 %south_pairs.1.terms_south.refs_0_ = f32[64,128]{1,0:T(8,128)S(1)} custom-call(bf16[40,4,64,512]{3,2,1,0:T(8,128)(2,1)} %bitcast.15, bf16[40,4,64,512]{3,2,1,0:T(8,128)(2,1)} %bitcast.16, bf16[40,4,64,512]{3,2,1,0:T(8,128)(2,1)} %bitcast.17, bf16[40,4,64,512]{3,2,1,0:T(8,128)(2,1)} %bitcast.18, bf16[40,4,64,512]{3,2,1,0:T(8,128)(2,1)} %bitcast.19, ...), custom_call_target="tpu_custom_call" | custom-call | flops 2400000000 | bytes 3932160 | tf_op jit(solution)/shard_map/south_pairs/pallas_call | solution.py:283
  21.7 3.9 %collective-permute-start.3 = (f32[64,128]{1,0:T(8,128)S(1)}, f32[64,128]{1,0:T(8,128)S(1)}, u32[]{:S(2)}, u32[]{:S(2)}) collective-permute-start(f32[64,128]{1,0:T(8,128)S(1)} %south_pairs.1.terms_south.refs_0_), channel_id=1, source_target_pairs={{0,1},{1,2},{2,3},{4,5},{5,6},{6,7},{8,9},{9,10},{10,11},{12,13},{... | collective-permute-start | bytes 98312 | tf_op jit(solution)/shard_map/ppermute | solution.py:690
  25.6 6.8 %side_pairs.1.terms_side.refs_1_ = f32[32,128]{1,0:T(8,128)S(1)} custom-call(bf16[40,4,64,512]{3,2,1,0:T(8,128)(2,1)} %bitcast.26, bf16[10,64,640]{2,1,0:T(8,128)(2,1)S(1)} %collective-permute-done.1.from_east, bf16[11,64,640]{2,1,0:T(8,128)(2,1)S(1)} %collective-permute-done.2.from_west.extra, bf16[40,4,64,512]{3,2,1,0:T(8,128)(2,1)} %bitcast.27, ...), custom_call_target="tpu_custom_call" | custom-call | flops 2400000000 | bytes 3932160 | tf_op jit(solution)/shard_map/side_pairs/pallas_call | solution.py:305
  32.5 1.3 %collective-permute-start.4 = (f32[72,128]{1,0:T(8,128)S(1)}, f32[72,128]{1,0:T(8,128)S(1)}, u32[]{:S(2)}, u32[]{:S(2)}) collective-permute-start(f32[72,128]{1,0:T(8,128)S(1)} %get-tuple-element.24), channel_id=1, source_target_pairs={{4,0},{8,4},{12,8},{16,12},{20,16},{24,20},{28,24},{32,28},{36,32}... | collective-permute-start | bytes 110600 | tf_op jit(solution)/shard_map/ppermute | solution.py:690
  33.8 3.9 %collective-permute-start.5 = (f32[64,128]{1,0:T(8,128)S(1)}, f32[64,128]{1,0:T(8,128)S(1)}, u32[]{:S(2)}, u32[]{:S(2)}) collective-permute-start(f32[64,128]{1,0:T(8,128)S(1)} %get-tuple-element.25), channel_id=1, source_target_pairs={{0,4},{4,8},{8,12},{12,16},{16,20},{20,24},{24,28},{28,32},{32,36}... | collective-permute-start | bytes 98312 | tf_op jit(solution)/shard_map/ppermute | solution.py:690
  37.8 1.3 %collective-permute-start.6 = (f32[64,128]{1,0:T(8,128)S(1)}, f32[64,128]{1,0:T(8,128)S(1)}, u32[]{:S(2)}, u32[]{:S(2)}) collective-permute-start(f32[64,128]{1,0:T(8,128)S(1)} %get-tuple-element.26), channel_id=1, source_target_pairs={{1,0},{2,1},{3,2},{5,4},{6,5},{7,6},{9,8},{10,9},{11,10},{13,12},{... | collective-permute-start | bytes 98312 | tf_op jit(solution)/shard_map/ppermute | solution.py:690
  39.1 4.5 %collective-permute-done.6.refs_4_ = f32[64,128]{1,0:T(8,128)S(1)} collective-permute-done((f32[64,128]{1,0:T(8,128)S(1)}, f32[64,128]{1,0:T(8,128)S(1)}, u32[]{:S(2)}, u32[]{:S(2)}) %collective-permute-start.6) | collective-permute-done | bytes 32800 | tf_op jit(solution)/shard_map/ppermute | solution.py:690
  43.6 1.5 %powers.1 = (f32[1024,128]{1,0:T(8,128)S(1)}, f32[1024,128]{1,0:T(8,128)S(1)}, f32[1024,128]{1,0:T(8,128)S(1)}, f32[1024,128]{1,0:T(8,128)S(1)}, f32[40,48]{1,0:T(8,128)S(1)}, /*index=5*/f32[8,128]{1,0:T(8,128)S(1)}) custom-call(f32[64,128]{1,0:T(8,128)S(1)} %south_pairs.1.terms_south.refs_0_, f32[32,128]{1,0:T(8,128)S(1)} %side_pairs.1.terms_side.refs_1_, ...), custom_call_target="tpu_custom_call" | custom-call | flops 4000000 | bytes 2000000 | tf_op jit(solution)/shard_map/powers/pallas_call | solution.py:395
  45.1 2.0 %collective-permute-start.7 = (f32[8,128]{1,0:T(8,128)S(1)}, f32[8,128]{1,0:T(8,128)S(1)}, u32[]{:S(2)}, u32[]{:S(2)}) collective-permute-start(f32[8,128]{1,0:T(8,128)S(1)} %get-tuple-element.28), channel_id=1, source_target_pairs={{0,4},{4,0},{8,12},{12,8},{16,20},{20,16},{24,28},{28,24},{32,36},... | collective-permute-start | bytes 12296 | tf_op jit(solution)/shard_map/ppermute | solution.py:701
  47.2 0.8 %collective-permute-done.7 = f32[8,128]{1,0:T(8,128)S(1)} collective-permute-done((f32[8,128]{1,0:T(8,128)S(1)}, f32[8,128]{1,0:T(8,128)S(1)}, u32[]{:S(2)}, u32[]{:S(2)}) %collective-permute-start.7) | collective-permute-done | bytes 4128 | tf_op jit(solution)/shard_map/ppermute | solution.py:701
  48.0 4.4 %collective-permute-start.10 = (f32[8,128]{1,0:T(8,128)S(1)}, f32[8,128]{1,0:T(8,128)S(1)}, u32[]{:S(2)}, u32[]{:S(2)}) collective-permute-start(f32[8,128]{1,0:T(8,128)S(1)} %add.30), channel_id=1, source_target_pairs={{0,24},{4,28},{8,0},{12,4},{16,8},{20,12},{24,16},{28,20},{32,56},... | collective-permute-start | bytes 12296 | tf_op jit(solution)/shard_map/ppermute | solution.py:701
  52.4 0.9 %collective-permute-start.8 = (f32[8,128]{1,0:T(8,128)S(1)}, f32[8,128]{1,0:T(8,128)S(1)}, u32[]{:S(2)}, u32[]{:S(2)}) collective-permute-start(f32[8,128]{1,0:T(8,128)S(1)} %add.30), channel_id=1, source_target_pairs={{0,8},{4,12},{8,16},{12,20},{16,24},{20,28},{24,0},{28,4},{32,40},... | collective-permute-start | bytes 12296 | tf_op jit(solution)/shard_map/ppermute | solution.py:701
  53.7 3.8 %collective-permute-done.9 = f32[8,128]{1,0:T(8,128)S(1)} collective-permute-done((f32[8,128]{1,0:T(8,128)S(1)}, f32[8,128]{1,0:T(8,128)S(1)}, u32[]{:S(2)}, u32[]{:S(2)}) %collective-permute-start.9) | collective-permute-done | bytes 4128 | tf_op jit(solution)/shard_map/ppermute | solution.py:701
  57.5 2.5 %collective-permute-start.13 = (f32[8,128]{1,0:T(8,128)S(1)}, f32[8,128]{1,0:T(8,128)S(1)}, u32[]{:S(2)}, u32[]{:S(2)}) collective-permute-start(f32[8,128]{1,0:T(8,128)S(1)} %add_add_fusion.2), channel_id=1, source_target_pairs={{0,96},{4,100},{8,104},{12,108},{16,112},{20,116},{24,120},{28,124... | collective-permute-start | bytes 12296 | tf_op jit(solution)/shard_map/ppermute | solution.py:701
  59.9 1.2 %collective-permute-start.12 = (f32[8,128]{1,0:T(8,128)S(1)}, f32[8,128]{1,0:T(8,128)S(1)}, u32[]{:S(2)}, u32[]{:S(2)}) collective-permute-start(f32[8,128]{1,0:T(8,128)S(1)} %add_add_fusion.2), channel_id=1, source_target_pairs={{0,64},{4,68},{8,72},{12,76},{16,80},{20,84},{24,88},{28,92},{32,9... | collective-permute-start | bytes 12296 | tf_op jit(solution)/shard_map/ppermute | solution.py:701
  61.1 0.5 collective-permute-start.11
  61.7 3.3 %collective-permute-done.12 = f32[8,128]{1,0:T(8,128)S(1)} collective-permute-done((f32[8,128]{1,0:T(8,128)S(1)}, f32[8,128]{1,0:T(8,128)S(1)}, u32[]{:S(2)}, u32[]{:S(2)}) %collective-permute-start.12) | collective-permute-done | bytes 4128 | tf_op jit(solution)/shard_map/ppermute | solution.py:701
  65.0 0.9 %collective-permute-done.11 = f32[8,128]{1,0:T(8,128)S(1)} collective-permute-done((f32[8,128]{1,0:T(8,128)S(1)}, f32[8,128]{1,0:T(8,128)S(1)}, u32[]{:S(2)}, u32[]{:S(2)}) %collective-permute-start.11) | collective-permute-done | bytes 4128 | tf_op jit(solution)/shard_map/ppermute | solution.py:701
  66.1 3.5 %collective-permute-start.15 = (f32[8,128]{1,0:T(8,128)S(1)}, f32[8,128]{1,0:T(8,128)S(1)}, u32[]{:S(2)}, u32[]{:S(2)}) collective-permute-start(f32[8,128]{1,0:T(8,128)S(1)} %add_add_fusion.1), channel_id=1, source_target_pairs={{0,2},{1,3},{2,0},{3,1},{4,6},{5,7},{6,4},{7,5},{8,10},{9,11},{10,... | collective-permute-start | bytes 12296 | tf_op jit(solution)/shard_map/ppermute | solution.py:701
  69.6 0.7 copy.24
  70.3 1.0 %collective-permute-done.15 = f32[8,128]{1,0:T(8,128)S(1)} collective-permute-done((f32[8,128]{1,0:T(8,128)S(1)}, f32[8,128]{1,0:T(8,128)S(1)}, u32[]{:S(2)}, u32[]{:S(2)}) %collective-permute-start.15) | collective-permute-done | bytes 4128 | tf_op jit(solution)/shard_map/ppermute | solution.py:701
  71.2 3.2 %collective-permute-done.14 = f32[8,128]{1,0:T(8,128)S(1)} collective-permute-done((f32[8,128]{1,0:T(8,128)S(1)}, f32[8,128]{1,0:T(8,128)S(1)}, u32[]{:S(2)}, u32[]{:S(2)}) %collective-permute-start.14) | collective-permute-done | bytes 4128 | tf_op jit(solution)/shard_map/ppermute | solution.py:701
  74.4 1.4 %combine.1 = (f32[40,2,896]{2,1,0:T(2,128)}, f32[40,2,896]{2,1,0:T(2,128)}) custom-call(f32[8,128]{1,0:T(8,128)S(1)} %add_add_fusion.gram, f32[1024,128]{1,0:T(8,128)S(1)} %get-tuple-element.29.v0, f32[1024,128]{1,0:T(8,128)S(1)} %get-tuple-element.30.v1, f32[1024,128]{1,0:T(8,128)S(1)} %get-tuple-element.31.v2, f32[1024,128]{1,0:T(8,128)S(1)} %get-tuple-element.32.v3), custom_call_target="tpu_custom_call" | custom-call | flops 4000000 | bytes 2000000 | tf_op jit(solution)/shard_map/combine/pallas_call | solution.py:395
  (31 shorter events, 0.7 us)
Async XLA Ops:
  0.6 13.8 %copy-start.4 = (bf16[64,64]{1,0:T(8,128)(2,1)S(1)}, bf16[64,64]{1,0:T(8,128)(2,1)}, u32[]{:S(2)}) copy-start(bf16[64,64]{1,0:T(8,128)(2,1)} %constant.14.clone.refs_14_.depth) | copy-start | bytes 24580
  0.6 13.8 %copy-start.2 = (bf16[256,256]{1,0:T(8,128)(2,1)S(1)}, bf16[256,256]{1,0:T(8,128)(2,1)}, u32[]{:S(2)}) copy-start(bf16[256,256]{1,0:T(8,128)(2,1)} %constant.15.clone.refs_15_.forward) | copy-start | bytes 393220
  0.7 13.8 %copy-start = (bf16[256,512]{1,0:T(8,128)(2,1)S(1)}, bf16[256,512]{1,0:T(8,128)(2,1)}, u32[]{:S(2)}) copy-start(bf16[256,512]{1,0:T(8,128)(2,1)} %constant.16.clone.refs_16_.ends) | copy-start | bytes 786436
  0.7 13.8 %copy-start.1 = (bf16[2,256,256]{2,1,0:T(8,128)(2,1)S(1)}, bf16[2,256,256]{2,1,0:T(8,128)(2,1)}, u32[]{:S(2)}) copy-start(bf16[2,256,256]{2,1,0:T(8,128)(2,1)} %constant.17.clone.refs_17_.back) | copy-start | bytes 786436
  0.7 13.8 %copy-start.5 = (bf16[64,64]{1,0:T(8,128)(2,1)S(1)}, bf16[64,64]{1,0:T(8,128)(2,1)}, u32[]{:S(2)}) copy-start(bf16[64,64]{1,0:T(8,128)(2,1)} %constant.18.clone.refs_18_.final) | copy-start | bytes 24580
  0.7 13.8 %copy-start.6 = (f32[8,128]{1,0:T(8,128)S(1)}, f32[8,128]{1,0:T(8,128)}, u32[]{:S(2)}) copy-start(f32[8,128]{1,0:T(8,128)} %constant.19.clone.refs_19_.pick) | copy-start | bytes 12292
  0.7 13.8 %copy-start.3 = (f32[64,128]{1,0:T(8,128)S(1)}, f32[64,128]{1,0:T(8,128)}, u32[]{:S(2)}) copy-start(f32[64,128]{1,0:T(8,128)} %constant.20.clone.refs_20_.rows) | copy-start | bytes 98308
  5.7 19.9 %collective-permute-start.2 = (bf16[11,64,640]{2,1,0:T(8,128)(2,1)S(1)}, bf16[11,64,640]{2,1,0:T(8,128)(2,1)S(1)}, u32[]{:S(2)}, u32[]{:S(2)}) collective-permute-start(bf16[11,64,640]{2,1,0:T(8,128)(2,1)S(1)} %get-tuple-element.23), channel_id=1, source_target_pairs={{0,4},{4,8},{8,12},{12,16},{16,20},{20,24},{24,28},{28,32},{32,36}... | collective-permute-start | bytes 2703368 | tf_op jit(solution)/shard_map/ppermute | solution.py:690
  7.1 18.5 %collective-permute-start.1 = (bf16[10,64,640]{2,1,0:T(8,128)(2,1)S(1)}, bf16[10,64,640]{2,1,0:T(8,128)(2,1)S(1)}, u32[]{:S(2)}, u32[]{:S(2)}) collective-permute-start(bf16[10,64,640]{2,1,0:T(8,128)(2,1)S(1)} %get-tuple-element.22), channel_id=1, source_target_pairs={{4,0},{8,4},{12,8},{16,12},{20,16},{24,20},{28,24},{32,28},{36,32}... | collective-permute-start | bytes 2457608 | tf_op jit(solution)/shard_map/ppermute | solution.py:690
  8.4 6.1 %collective-permute-start = (bf16[1,64,384]{2,1,0:T(8,128)(2,1)S(1)}, bf16[1,64,384]{2,1,0:T(8,128)(2,1)S(1)}, u32[]{:S(2)}, u32[]{:S(2)}) collective-permute-start(bf16[1,64,384]{2,1,0:T(8,128)(2,1)S(1)} %get-tuple-element.19), channel_id=1, source_target_pairs={{1,0},{2,1},{3,2},{5,4},{6,5},{7,6},{9,8},{10,9},{11,10},{13,12},{... | collective-permute-start | bytes 147464 | tf_op jit(solution)/shard_map/ppermute | solution.py:690
  21.7 10.8 %collective-permute-start.3 = (f32[64,128]{1,0:T(8,128)S(1)}, f32[64,128]{1,0:T(8,128)S(1)}, u32[]{:S(2)}, u32[]{:S(2)}) collective-permute-start(f32[64,128]{1,0:T(8,128)S(1)} %south_pairs.1.terms_south.refs_0_), channel_id=1, source_target_pairs={{0,1},{1,2},{2,3},{4,5},{5,6},{6,7},{8,9},{9,10},{10,11},{12,13},{... | collective-permute-start | bytes 98312 | tf_op jit(solution)/shard_map/ppermute | solution.py:690
  32.5 11.1 %collective-permute-start.4 = (f32[72,128]{1,0:T(8,128)S(1)}, f32[72,128]{1,0:T(8,128)S(1)}, u32[]{:S(2)}, u32[]{:S(2)}) collective-permute-start(f32[72,128]{1,0:T(8,128)S(1)} %get-tuple-element.24), channel_id=1, source_target_pairs={{4,0},{8,4},{12,8},{16,12},{20,16},{24,20},{28,24},{32,28},{36,32}... | collective-permute-start | bytes 110600 | tf_op jit(solution)/shard_map/ppermute | solution.py:690
  33.8 5.3 %collective-permute-start.5 = (f32[64,128]{1,0:T(8,128)S(1)}, f32[64,128]{1,0:T(8,128)S(1)}, u32[]{:S(2)}, u32[]{:S(2)}) collective-permute-start(f32[64,128]{1,0:T(8,128)S(1)} %get-tuple-element.25), channel_id=1, source_target_pairs={{0,4},{4,8},{8,12},{12,16},{16,20},{20,24},{24,28},{28,32},{32,36}... | collective-permute-start | bytes 98312 | tf_op jit(solution)/shard_map/ppermute | solution.py:690
  37.8 5.8 %collective-permute-start.6 = (f32[64,128]{1,0:T(8,128)S(1)}, f32[64,128]{1,0:T(8,128)S(1)}, u32[]{:S(2)}, u32[]{:S(2)}) collective-permute-start(f32[64,128]{1,0:T(8,128)S(1)} %get-tuple-element.26), channel_id=1, source_target_pairs={{1,0},{2,1},{3,2},{5,4},{6,5},{7,6},{9,8},{10,9},{11,10},{13,12},{... | collective-permute-start | bytes 98312 | tf_op jit(solution)/shard_map/ppermute | solution.py:690
  45.1 2.9 %collective-permute-start.7 = (f32[8,128]{1,0:T(8,128)S(1)}, f32[8,128]{1,0:T(8,128)S(1)}, u32[]{:S(2)}, u32[]{:S(2)}) collective-permute-start(f32[8,128]{1,0:T(8,128)S(1)} %get-tuple-element.28), channel_id=1, source_target_pairs={{0,4},{4,0},{8,12},{12,8},{16,20},{20,16},{24,28},{28,24},{32,36},... | collective-permute-start | bytes 12296 | tf_op jit(solution)/shard_map/ppermute | solution.py:701
  48.0 5.7 %collective-permute-start.10 = (f32[8,128]{1,0:T(8,128)S(1)}, f32[8,128]{1,0:T(8,128)S(1)}, u32[]{:S(2)}, u32[]{:S(2)}) collective-permute-start(f32[8,128]{1,0:T(8,128)S(1)} %add.30), channel_id=1, source_target_pairs={{0,24},{4,28},{8,0},{12,4},{16,8},{20,12},{24,16},{28,20},{32,56},... | collective-permute-start | bytes 12296 | tf_op jit(solution)/shard_map/ppermute | solution.py:701
  52.3 5.1 %collective-permute-start.9 = (f32[8,128]{1,0:T(8,128)S(1)}, f32[8,128]{1,0:T(8,128)S(1)}, u32[]{:S(2)}, u32[]{:S(2)}) collective-permute-start(f32[8,128]{1,0:T(8,128)S(1)} %add.30), channel_id=1, source_target_pairs={{0,16},{4,20},{8,24},{12,28},{16,0},{20,4},{24,8},{28,12},{32,48},... | collective-permute-start | bytes 12296 | tf_op jit(solution)/shard_map/ppermute | solution.py:701
  52.4 5.1 %collective-permute-start.8 = (f32[8,128]{1,0:T(8,128)S(1)}, f32[8,128]{1,0:T(8,128)S(1)}, u32[]{:S(2)}, u32[]{:S(2)}) collective-permute-start(f32[8,128]{1,0:T(8,128)S(1)} %add.30), channel_id=1, source_target_pairs={{0,8},{4,12},{8,16},{12,20},{16,24},{20,28},{24,0},{28,4},{32,40},... | collective-permute-start | bytes 12296 | tf_op jit(solution)/shard_map/ppermute | solution.py:701
  57.5 4.2 %collective-permute-start.13 = (f32[8,128]{1,0:T(8,128)S(1)}, f32[8,128]{1,0:T(8,128)S(1)}, u32[]{:S(2)}, u32[]{:S(2)}) collective-permute-start(f32[8,128]{1,0:T(8,128)S(1)} %add_add_fusion.2), channel_id=1, source_target_pairs={{0,96},{4,100},{8,104},{12,108},{16,112},{20,116},{24,120},{28,124... | collective-permute-start | bytes 12296 | tf_op jit(solution)/shard_map/ppermute | solution.py:701
  59.9 5.1 %collective-permute-start.12 = (f32[8,128]{1,0:T(8,128)S(1)}, f32[8,128]{1,0:T(8,128)S(1)}, u32[]{:S(2)}, u32[]{:S(2)}) collective-permute-start(f32[8,128]{1,0:T(8,128)S(1)} %add_add_fusion.2), channel_id=1, source_target_pairs={{0,64},{4,68},{8,72},{12,76},{16,80},{20,84},{24,88},{28,92},{32,9... | collective-permute-start | bytes 12296 | tf_op jit(solution)/shard_map/ppermute | solution.py:701
  61.1 4.8 %collective-permute-start.11 = (f32[8,128]{1,0:T(8,128)S(1)}, f32[8,128]{1,0:T(8,128)S(1)}, u32[]{:S(2)}, u32[]{:S(2)}) collective-permute-start(f32[8,128]{1,0:T(8,128)S(1)} %add_add_fusion.2), channel_id=1, source_target_pairs={{0,32},{4,36},{8,40},{12,44},{16,48},{20,52},{24,56},{28,60},{32,6... | collective-permute-start | bytes 12296 | tf_op jit(solution)/shard_map/ppermute | solution.py:701
  66.0 4.3 %collective-permute-start.16 = (f32[8,128]{1,0:T(8,128)S(1)}, f32[8,128]{1,0:T(8,128)S(1)}, u32[]{:S(2)}, u32[]{:S(2)}) collective-permute-start(f32[8,128]{1,0:T(8,128)S(1)} %add_add_fusion.1), channel_id=1, source_target_pairs={{0,3},{1,0},{2,1},{3,2},{4,7},{5,4},{6,5},{7,6},{8,11},{9,8},{10,9... | collective-permute-start | bytes 12296 | tf_op jit(solution)/shard_map/ppermute | solution.py:701
  66.1 5.1 %collective-permute-start.15 = (f32[8,128]{1,0:T(8,128)S(1)}, f32[8,128]{1,0:T(8,128)S(1)}, u32[]{:S(2)}, u32[]{:S(2)}) collective-permute-start(f32[8,128]{1,0:T(8,128)S(1)} %add_add_fusion.1), channel_id=1, source_target_pairs={{0,2},{1,3},{2,0},{3,1},{4,6},{5,7},{6,4},{7,5},{8,10},{9,11},{10,... | collective-permute-start | bytes 12296 | tf_op jit(solution)/shard_map/ppermute | solution.py:701
  69.6 4.8 %collective-permute-start.14 = (f32[8,128]{1,0:T(8,128)S(1)}, f32[8,128]{1,0:T(8,128)S(1)}, u32[]{:S(2)}, u32[]{:S(2)}) collective-permute-start(f32[8,128]{1,0:T(8,128)S(1)} %add_add_fusion.1), channel_id=1, source_target_pairs={{0,1},{1,2},{2,3},{3,0},{4,5},{5,6},{6,7},{7,4},{8,9},{9,10},{10,1... | collective-permute-start | bytes 12296 | tf_op jit(solution)/shard_map/ppermute | solution.py:701

commit v3 on v2

--- a/solution.py
+++ b/solution.py
@@ -15,6 +15,7 @@
 PATCH = 64
 MOST = 5
 WIDE = MOST * PATCH
+SIDE = 384
 ROWS = 32
 EXTRA = 40
 LANES = 128
@@ -188,168 +189,188 @@
     out[24:25, :] = offsets
 
 
-def south_kernel(*refs):
-    first, seconds = refs[0], refs[1 : 1 + GROUP]
-    nxt, info, anchor_t, depth, forward, ends, back, final, pick, rows, out, r0, r1 = refs[1 + GROUP :]
-    step = pl.program_id(0)
-    last = pl.num_programs(0) - 1
-
-    @pl.when(step == 0)
-    def _():
-        r0[...] = jnp.zeros_like(r0)
-        r1[...] = jnp.zeros_like(r1)
-
-    seconds = [ref[0, 0, :, :WIDE] for ref in seconds]
-    seconds[-1] = jnp.where(step == last, nxt[0, :, :WIDE], seconds[-1])
-    firsts = [first[j, 0, :, :WIDE] for j in range(GROUP)]
-    correlate_group(
-        block_pairs(firsts) + block_pairs(seconds),
-        depth[...], forward[...], ends[...], back[0], final[...], rows[...], r0, r1, GROUP * step,
-    )
-
-    @pl.when(step == last)
-    def _():
-        finish_terms(pick[...], r0, r1, info[2:3, :], info[3:4, :], out)
-        out[25:26, :] = info[4:5, :]
-        out[32:, :] = anchor_t[...]
-
-
-def side_kernel(own, from_east, from_west, own_extra, extra, info, depth, forward, ends, back, final, pick, rows, out, r0, r1):
-    step = pl.program_id(0)
-    steps = pl.num_programs(0)
-
-    @pl.when(step == 0)
-    def _():
-        r0[...] = jnp.zeros_like(r0)
-        r1[...] = jnp.zeros_like(r1)
-
-    east_part = step < steps // 2
-    others = []
-    for slot in range(GROUP // 2):
-        packed = jnp.where(east_part, from_east[slot], from_west[slot])
-        others += [packed[:, LANES * i : LANES * (i + 1)] for i in range(5)]
-    owns = block_pairs([own[j, 0, :, :WIDE] for j in range(GROUP)])
-    correlate_group(
-        owns + [own_extra[0, 0]] + others + [extra[0, :, :LANES]],
-        depth[...], forward[...], ends[...], back[0], final[...], rows[...], r0, r1, GROUP * step,
-    )
-
-    @pl.when(step == steps - 1)
-    def _():
-        lane = lax.broadcasted_iota(jnp.int32, (8, LANES), 1)
-        info_west = extra[0, 0:16, 2 * LANES : 3 * LANES].astype(F32)[0:8]
-        table = jnp.where(lane < GROUP * (steps // 2), info[...], info_west)
-        table = jnp.where(lane == EXTRA, pltpu.roll(info_west, EXTRA, axis=1), table)
-        finish_terms(pick[...], r0, r1, table[0:1], table[1:2], out)
-
-
-def const_spec(shape):
-    return pl.BlockSpec(shape, lambda i: (0,) * len(shape))
+def south_kernel(strips, nxt, info, anchor_t, depth, forward, ends, backs, final, pick, rows, out, first, second, r0, r1, sems, last_sem):
+    tiles = first.shape[0]
+    steps = tiles // GROUP
+    side = pl.ds(0, SIDE)
+
+    def first_copy(c):
+        at = pl.ds(GROUP * c, GROUP)
+        return pltpu.make_async_copy(strips.at[at, 2, :, side], first.at[at], sems.at[0, c])
+
+    def second_copy(c, count=GROUP):
+        below = strips.at[pl.ds(GROUP * c + 1, count), 1, :, side]
+        return pltpu.make_async_copy(below, second.at[pl.ds(GROUP * c, count)], sems.at[1, c])
+
+    last_copies = (
+        second_copy(steps - 1, GROUP - 1),
+        pltpu.make_async_copy(nxt.at[0], second.at[tiles - 1], last_sem),
+    )
+    for c in range(steps):
+        first_copy(c).start()
+        if c < steps - 1:
+            second_copy(c).start()
+        else:
+            for copy in last_copies:
+                copy.start()
+    r0[...] = jnp.zeros_like(r0)
+    r1[...] = jnp.zeros_like(r1)
+
+    def step(c, carry):
+        first_copy(c).wait()
+
+        @pl.when(c < steps - 1)
+        def _():
+            second_copy(c).wait()
+
+        @pl.when(c == steps - 1)
+        def _():
+            for copy in last_copies:
+                copy.wait()
+
+        columns = [
+            block_pairs([ref[GROUP * c + j, :, :WIDE] for j in range(GROUP)]) for ref in (first, second)
+        ]
+        correlate_group(
+            columns[0] + columns[1],
+            depth[...], forward[...], ends[...], backs[0], final[...], rows[...], r0, r1, GROUP * c,
+        )
+        return carry
+
+    lax.fori_loop(0, steps, step, 0)
+    finish_terms(pick[...], r0, r1, info[2:3, :], info[3:4, :], out)
+    out[25:26, :] = info[4:5, :]
+    out[32:, :] = anchor_t[NODES - MESH_X : NODES, :]
+
+
+def side_kernel(strips, from_east, from_west, info, depth, forward, ends, backs, final, pick, rows, out, own, other, own_extra, r0, r1, sems, extra_sems):
+    steps = own.shape[0] // GROUP
+    slots = GROUP // 2
+    count = from_east.shape[0]
+    side = pl.ds(0, SIDE)
+
+    def own_copy(c, which):
+        at = pl.ds(GROUP * c, GROUP)
+        return pltpu.make_async_copy(strips.at[at, which, :, side], own.at[at], sems.at[0, c])
+
+    def other_copy(c, source, start):
+        return pltpu.make_async_copy(
+            source.at[pl.ds(start, slots)], other.at[pl.ds(slots * c, slots)], sems.at[1, c]
+        )
+
+    extra_copies = (
+        pltpu.make_async_copy(strips.at[0, 0, :, pl.ds(0, LANES)], own_extra, extra_sems.at[0]),
+        pltpu.make_async_copy(from_west.at[count], other.at[2 * count], extra_sems.at[1]),
+    )
+    for c in range(steps):
+        east = c < steps // 2
+        own_copy(c, 3 if east else 0).start()
+        other_copy(c, from_east if east else from_west, slots * (c % (steps // 2))).start()
+        if c == 0:
+            for copy in extra_copies:
+                copy.start()
+    r0[...] = jnp.zeros_like(r0)
+    r1[...] = jnp.zeros_like(r1)
+    for copy in extra_copies:
+        copy.wait()
+
+    def step(c, carry):
+        own_copy(c, 0).wait()
+        other_copy(c, from_east, 0).wait()
+        owns = block_pairs([own[GROUP * c + j, :, :WIDE] for j in range(GROUP)])
+        others = [
+            other[slots * c + slot, :, LANES * i : LANES * (i + 1)] for slot in range(slots) for i in range(5)
+        ]
+        correlate_group(
+            owns + [own_extra[...]] + others + [other[2 * count, :, :LANES]],
+            depth[...], forward[...], ends[...], backs[c // (steps // 2)], final[...], rows[...], r0, r1, GROUP * c,
+        )
+        return carry
+
+    lax.fori_loop(0, steps, step, 0)
+    lane = lax.broadcasted_iota(jnp.int32, (8, LANES), 1)
+    info_west = other[2 * count, 0:16, 2 * LANES : 3 * LANES].astype(F32)[0:8]
+    table = jnp.where(lane < GROUP * (steps // 2), info[...], info_west)
+    table = jnp.where(lane == EXTRA, pltpu.roll(info_west, EXTRA, axis=1), table)
+    finish_terms(pick[...], r0, r1, table[0:1], table[1:2], out)
 
 
 SUMS = [pltpu.VMEM((3, LANES, LANES), F32), pltpu.VMEM((3, LANES, LANES), F32)]
 VMEM_BYTES = 48 * 1024 * 1024
-
-
-def table_specs(tabs, back_map):
-    depth, forward, ends, backs, final, pick, rows = tabs
-    return [
-        const_spec(depth.shape),
-        const_spec(forward.shape),
-        const_spec(ends.shape),
-        pl.BlockSpec((1, 2 * LANES, 2 * LANES), back_map),
-        const_spec(final.shape),
-        const_spec(pick.shape),
-        const_spec(rows.shape),
-    ]
-
-
-def correlation_cost(pairs):
-    return pl.CostEstimate(
-        flops=pairs * MOST * 12_000_000, bytes_accessed=pairs * 2 * 64 * 384 * 2, transcendentals=0
+ANY = pl.BlockSpec(memory_space=pl.ANY)
+VMEM = pl.BlockSpec(memory_space=pltpu.VMEM)
+
+
+def pair_call(kernel, name, tiles, rows, specs, buffers, semaphores):
+    steps = tiles // GROUP
+    return pl.pallas_call(
+        kernel,
+        name=name,
+        in_specs=specs + [VMEM] * 7,
+        out_specs=VMEM,
+        out_shape=jax.ShapeDtypeStruct((rows, LANES), F32),
+        scratch_shapes=buffers + SUMS + [pltpu.SemaphoreType.DMA((2, steps))] + semaphores,
+        compiler_params=pltpu.CompilerParams(vmem_limit_bytes=VMEM_BYTES),
+        cost_estimate=pl.CostEstimate(
+            flops=tiles * MOST * 12_000_000,
+            bytes_accessed=tiles * 2 * PATCH * SIDE * 2,
+            transcendentals=0,
+        ),
     )
 
 
 def south_terms(strips, nxt, info, anchor_t, tabs):
     tiles = strips.shape[0]
-    steps = tiles // GROUP
-    side = 384
-
-    def second_spec(j):
-        return pl.BlockSpec(
-            (1, 1, PATCH, side), lambda i: (jnp.minimum(GROUP * i + 1 + j, tiles - 1), 1, 0, 0)
-        )
-
-    return pl.pallas_call(
-        south_kernel,
-        name="south_pairs",
-        grid=(steps,),
-        in_specs=[pl.BlockSpec((GROUP, 1, PATCH, side), lambda i: (i, 2, 0, 0))]
-        + [second_spec(j) for j in range(GROUP)]
-        + [const_spec(nxt.shape), const_spec(info.shape)]
-        + [pl.BlockSpec((MESH_X, LANES), lambda i: (MESH_Y - 1, 0))]
-        + table_specs(tabs, lambda i: (0, 0, 0)),
-        out_specs=const_spec((64, LANES)),
-        out_shape=jax.ShapeDtypeStruct((64, LANES), F32),
-        scratch_shapes=SUMS,
-        compiler_params=pltpu.CompilerParams(vmem_limit_bytes=VMEM_BYTES),
-        cost_estimate=correlation_cost(tiles),
-    )(*[strips] * (1 + GROUP), nxt, info, anchor_t, *tabs)
+    buffers = [pltpu.VMEM((tiles, PATCH, SIDE), BF16)] * 2
+    return pair_call(
+        south_kernel, "south_pairs", tiles, 64, [ANY, ANY, VMEM, VMEM], buffers, [pltpu.SemaphoreType.DMA]
+    )(strips, nxt, info, anchor_t, *tabs)
 
 
 def side_terms(strips, from_east, from_west, info, tabs):
     tiles = strips.shape[0]
-    steps = tiles // GROUP
-    mid = steps // 2
-    packed = (GROUP // 2, PATCH, 2 * WIDE)
-    return pl.pallas_call(
-        side_kernel,
-        name="side_pairs",
-        grid=(steps,),
-        in_specs=[
-            pl.BlockSpec((GROUP, 1, PATCH, 384), lambda i: (i, jnp.where(i < mid, 3, 0), 0, 0)),
-            pl.BlockSpec(packed, lambda i: (jnp.minimum(i, mid - 1), 0, 0)),
-            pl.BlockSpec(packed, lambda i: (jnp.maximum(i - mid, 0), 0, 0)),
-            pl.BlockSpec((1, 1, PATCH, LANES), lambda i: (0, 0, 0, 0)),
-            pl.BlockSpec((1, PATCH, 2 * WIDE), lambda i: (tiles // 4, 0, 0)),
-            const_spec(info.shape),
-        ]
-        + table_specs(tabs, lambda i: (jnp.where(i < mid, 0, 1), 0, 0)),
-        out_specs=const_spec((32, LANES)),
-        out_shape=jax.ShapeDtypeStruct((32, LANES), F32),
-        scratch_shapes=SUMS,
-        compiler_params=pltpu.CompilerParams(vmem_limit_bytes=VMEM_BYTES),
-        cost_estimate=correlation_cost(tiles),
-    )(strips, from_east, from_west, strips, from_west, info, *tabs)
-
-
-def prepare_kernel(strips, counts, offsets, stiffness, anchor, west, east, north, info, anchor_t, left, right, small, wide, sems):
+    buffers = [
+        pltpu.VMEM((tiles, PATCH, SIDE), BF16),
+        pltpu.VMEM((tiles // 2 + 1, PATCH, 2 * WIDE), BF16),
+        pltpu.VMEM((PATCH, LANES), BF16),
+    ]
+    return pair_call(
+        side_kernel, "side_pairs", tiles, 32, [ANY, ANY, ANY, VMEM], buffers, [pltpu.SemaphoreType.DMA((2,))]
+    )(strips, from_east, from_west, info, *tabs)
+
+
+def edge_kernel(strips, north, sem):
+    copy = pltpu.make_async_copy(strips.at[0, 1, :, pl.ds(0, SIDE)], north.at[0], sem)
+    copy.start()
+    copy.wait()
+
+
+def prepare_kernel(strips, counts, offsets, stiffness, anchor, west, east, info, anchor_t, left, right, small, wide, sems):
     tiles = anchor.shape[0]
     half = tiles // 2
     moves = [
-        (strips.at[pl.ds(half, half), 3, :, pl.ds(0, 384)], right),
-        (strips.at[pl.ds(0, half), 0, :, pl.ds(0, 384)], left),
+        (strips.at[pl.ds(half, half), 3, :, pl.ds(0, SIDE)], right),
+        (strips.at[pl.ds(0, half), 0, :, pl.ds(0, SIDE)], left),
         (strips.at[0, 3, :, pl.ds(0, LANES)], east.at[half // 2, :, pl.ds(0, LANES)]),
-        (strips.at[0, 1, :, pl.ds(0, 384)], north.at[0]),
     ]
     moves = [pltpu.make_async_copy(a, b, sems.at[k]) for k, (a, b) in enumerate(moves)]
     for move in moves:
         move.start()
     small[...] = jnp.zeros_like(small)
-    small[0:tiles, 0:1] = counts[:, 0:1].astype(F32)
-    small[0:tiles, 1:2] = offsets[:, 0:1].astype(F32)
-    small[0:tiles, 2:3] = counts[:, 1:2].astype(F32)
-    small[0:tiles, 3:4] = offsets[:, 1:2].astype(F32)
-    small[0:tiles, 4:5] = stiffness[...]
-    flat = small[...].T
-    info[...] = flat[0:8, :]
+    here = pl.ds(0, tiles)
+    small[0:1, here] = counts[0:1, :].astype(F32)
+    small[1:2, here] = offsets[0:1, :].astype(F32)
+    small[2:3, here] = counts[1:2, :].astype(F32)
+    small[3:4, here] = offsets[1:2, :].astype(F32)
+    small[4:5, here] = stiffness[...]
+    info[...] = small[0:8, :]
     wide[...] = jnp.zeros_like(wide)
-    wide[0:tiles, :] = anchor[...]
-    wide[COMP : COMP + tiles, :] = anchor[...]
+    for first in (0, COMP):
+        wide[first : first + tiles, :] = anchor[:, 0, :]
     for i in range(NODES // LANES):
         anchor_t[LANES * i : LANES * (i + 1), :] = wide[:, LANES * i : LANES * (i + 1)].T
     east[half // 2, :, LANES:] = jnp.zeros((PATCH, 2 * WIDE - LANES), BF16)
-    east[half // 2, 0:16, 2 * LANES : 3 * LANES] = flat[0:16, :].astype(BF16)
+    east[half // 2, 0:16, 2 * LANES : 3 * LANES] = small[...].astype(BF16)
     for move, source, packed in ((moves[0], right, east), (moves[1], left, west)):
         move.wait()
         for slot in range(half // 2):
@@ -357,7 +378,6 @@
             for i, x in enumerate(columns):
                 packed[slot, :, LANES * i : LANES * (i + 1)] = x
     moves[2].wait()
-    moves[3].wait()
 
 
 def prepare(strips, counts, offsets, stiffness, anchor):
@@ -368,20 +388,19 @@
         prepare_kernel,
         name="prepare",
         in_specs=[pl.BlockSpec(memory_space=pl.ANY)] + [vmem] * 4,
-        out_specs=[vmem] * 5,
+        out_specs=[vmem] * 4,
         out_shape=[
             jax.ShapeDtypeStruct((slots, PATCH, 2 * WIDE), BF16),
             jax.ShapeDtypeStruct((slots + 1, PATCH, 2 * WIDE), BF16),
-            jax.ShapeDtypeStruct((1, PATCH, 384), BF16),
             jax.ShapeDtypeStruct((8, LANES), F32),
             jax.ShapeDtypeStruct((NODES, LANES), F32),
         ],
         scratch_shapes=[
-            pltpu.VMEM((tiles // 2, PATCH, 384), BF16),
-            pltpu.VMEM((tiles // 2, PATCH, 384), BF16),
-            pltpu.VMEM((LANES, LANES), F32),
+            pltpu.VMEM((tiles // 2, PATCH, SIDE), BF16),
+            pltpu.VMEM((tiles // 2, PATCH, SIDE), BF16),
+            pltpu.VMEM((16, LANES), F32),
             pltpu.VMEM((LANES, NODES), F32),
-            pltpu.SemaphoreType.DMA((4,)),
+            pltpu.SemaphoreType.DMA((3,)),
         ],
         compiler_params=pltpu.CompilerParams(vmem_limit_bytes=VMEM_BYTES),
     )(strips, counts, offsets, stiffness, anchor)
@@ -721,12 +740,21 @@
     tiles = strips.shape[0]
     own = strips[:, 0]
     field = (TALL, LANES)
-    to_west, to_east, to_north, info, anchor_t = prepare(
-        own, pair_counts[:, 0], pair_offsets[:, 0], tile_stiffness, anchor[:, 0]
-    )
+    to_north = pl.pallas_call(
+        edge_kernel,
+        name="edge",
+        in_specs=[ANY],
+        out_specs=VMEM,
+        out_shape=jax.ShapeDtypeStruct((1, PATCH, SIDE), BF16),
+        scratch_shapes=[pltpu.SemaphoreType.DMA],
+    )(own)
+    next_top = shifted(to_north, "col", -1)
+    to_west, to_east, info, anchor_t = prepare(
+        own, pair_counts[:, 0].T, pair_offsets[:, 0].T, tile_stiffness.T, anchor
+    )
+    to_west, to_east, next_top = lax.optimization_barrier((to_west, to_east, next_top))
     strips_west = shifted(to_east, "row", 1)
     strips_east = shifted(to_west, "row", -1)
-    next_top = shifted(to_north, "col", -1)
     tabs = tables()
     terms_south = south_terms(own, next_top, info, anchor_t, tabs)
     from_north = shifted(terms_south, "col", 1)

time: 76.2 us -> 75.9 us (level)
  starting transfers between devices: 29.5 us -> 34.2 us
  local copies, waits for them, and re-layouts: 3.98 us -> 0.75 us
  waiting for transfers between devices: 22.7 us -> 20.1 us
  Pallas kernels: 18.7 us -> 19.7 us
    ppermute x7, starting transfers between devices: 14.4 us -> 17.3 us  [shifted(): lax.ppermute(x, axis, [(i, i + by) for i in range(peers) if 0 <= i + by <...]
    ppermute x7, waiting for transfers between devices: 9.29 us -> 7.6 us  [shifted(): lax.ppermute(x, axis, [(i, i + by) for i in range(peers) if 0 <= i + by <...]
    ppermute x10, starting transfers between devices: 15.2 us -> 16.8 us  [add_over(): got.append(lax.ppermute(x, axis, pairs))]
    unnamed x16 -> x22, local copies, waits for them, and re-layouts: 1.7 us -> 0.06 us
    squeeze x2 -> x0, local copies, waits for them, and re-layouts: 1.59 us -> none  [the longest x1 0.82 us: per_device(): pair_counts[:, 0]]
    ppermute x10, waiting for transfers between devices: 13.4 us -> 12.5 us  [add_over(): got.append(lax.ppermute(x, axis, pairs))]
    pallas_call x2 -> x3, Pallas kernels: 14 us -> 14.9 us  [the longest x1 6.78 us: side_terms(): pair_call(side_kernel, 'side_pairs', tiles, 32, [ANY, ANY, ANY, VMEM], bu...]
  transfers between devices with their start and end apart: 17 -> 17, of which waited for: 9 -> 9; matrix products, arithmetic and copies ran while one was open for 1% -> 1% of each run, Pallas kernels for 18% -> 20%
where the time goes in v3:
time: 75.9 us; the launch traced here: 75.6 us
  starting transfers between devices  34.2 us (45%)
  waiting for transfers between devices  20.1 us (26%)
  Pallas kernels  19.7 us (26%)
  between operations  0.94 us (1%)
    ppermute x7, starting transfers between devices, shifted(): lax.ppermute(x, axis, [(i, i + by) for i in range(peers) if 0 <= i + by <...  17.3 us
    ppermute x10, starting transfers between devices, add_over(): got.append(lax.ppermute(x, axis, pairs))  16.8 us
    ppermute x10, waiting for transfers between devices, add_over(): got.append(lax.ppermute(x, axis, pairs))  12.5 us
    ppermute x7, waiting for transfers between devices, shifted(): lax.ppermute(x, axis, [(i, i + by) for i in range(peers) if 0 <= i + by <...  7.6 us
    pallas_call x1, Pallas kernels, side_terms(): pair_call(side_kernel, 'side_pairs', tiles, 32, [ANY, ANY, ANY, VMEM], bu...  6.78 us
    pallas_call x1, Pallas kernels, south_terms(): pair_call(south_kernel, 'south_pairs', tiles, 64, [ANY, ANY, VMEM, VMEM],...  6.6 us
    pallas_call x3, Pallas kernels, call(): pl.pallas_call(kernel, name=name, in_specs=[vmem] * len(args), out_specs=...  3 us
    pallas_call x1, Pallas kernels, prepare(): pl.pallas_call(prepare_kernel, name='prepare', in_specs=[pl.BlockSpec(mem...  1.76 us
  transfers between devices with their start and end apart: 17, of which 9 were waited for; matrix products, arithmetic and copies ran while one was open for 1% of the time, Pallas kernels for 20%

profile of v3, /device:TPU:0, one launch (start us, length us, event | category | flops | bytes accessed | tf_op | source)
XLA Modules:
  0.0 75.6 jit_solution(17830093256322435266)
XLA Ops:
  0.8 1.5 %edge.1 = bf16[1,64,384]{2,1,0:T(8,128)(2,1)} custom-call(bf16[40,4,64,512]{3,2,1,0:T(8,128)(2,1)} %bitcast.18), custom_call_target="tpu_custom_call" | custom-call | tf_op jit(solution)/shard_map/edge/pallas_call | solution.py:743
  2.3 1.3 %collective-permute-start = (bf16[1,64,384]{2,1,0:T(8,128)(2,1)}, bf16[1,64,384]{2,1,0:T(8,128)(2,1)S(1)}, u32[]{:S(2)}, u32[]{:S(2)}) collective-permute-start(bf16[1,64,384]{2,1,0:T(8,128)(2,1)} %edge.1), channel_id=1, source_target_pairs={{1,0},{2,1},{3,2},{5,4},{6,5},{7,6},{9,8},{10,9},{11,10},{13,12},{... | collective-permute-start | bytes 147464 | tf_op jit(solution)/shard_map/ppermute | solution.py:709
  3.6 1.8 %prepare.1 = (bf16[10,64,640]{2,1,0:T(8,128)(2,1)S(1)}, bf16[11,64,640]{2,1,0:T(8,128)(2,1)S(1)}, f32[8,128]{1,0:T(8,128)S(1)}, f32[896,128]{1,0:T(8,128)S(1)}) custom-call(bf16[40,4,64,512]{3,2,1,0:T(8,128)(2,1)} %bitcast.19, s32[2,40]{1,0:T(2,128)S(1)} %bitcast.15, s32[2,40]{1,0:T(2,128)S(1)} %bitcast.16, f32[1,40]{1,0:T(1,128)S(1)} %bitcast.17, ...), custom_call_target="tpu_custom_call" | custom-call | tf_op jit(solution)/shard_map/prepare/pallas_call | solution.py:387
  5.4 3.1 %collective-permute-done.nxt = bf16[1,64,384]{2,1,0:T(8,128)(2,1)S(1)} collective-permute-done((bf16[1,64,384]{2,1,0:T(8,128)(2,1)}, bf16[1,64,384]{2,1,0:T(8,128)(2,1)S(1)}, u32[]{:S(2)}, u32[]{:S(2)}) %collective-permute-start) | collective-permute-done | bytes 49184 | tf_op jit(solution)/shard_map/ppermute | solution.py:709
  8.5 1.3 %collective-permute-start.2 = (bf16[11,64,640]{2,1,0:T(8,128)(2,1)S(1)}, bf16[11,64,640]{2,1,0:T(8,128)(2,1)S(1)}, u32[]{:S(2)}, u32[]{:S(2)}) collective-permute-start(bf16[11,64,640]{2,1,0:T(8,128)(2,1)S(1)} %get-tuple-element.27), channel_id=1, source_target_pairs={{0,4},{4,8},{8,12},{12,16},{16,20},{20,24},{24,28},{28,32},{32,36}... | collective-permute-start | bytes 2703368 | tf_op jit(solution)/shard_map/ppermute | solution.py:709
  9.8 1.3 %collective-permute-start.1 = (bf16[10,64,640]{2,1,0:T(8,128)(2,1)S(1)}, bf16[10,64,640]{2,1,0:T(8,128)(2,1)S(1)}, u32[]{:S(2)}, u32[]{:S(2)}) collective-permute-start(bf16[10,64,640]{2,1,0:T(8,128)(2,1)S(1)} %get-tuple-element.26), channel_id=1, source_target_pairs={{4,0},{8,4},{12,8},{16,12},{20,16},{24,20},{28,24},{32,28},{36,32}... | collective-permute-start | bytes 2457608 | tf_op jit(solution)/shard_map/ppermute | solution.py:709
  11.2 6.6 %south_pairs.1.terms_south.refs_0_ = f32[64,128]{1,0:T(8,128)S(1)} custom-call(bf16[40,4,64,512]{3,2,1,0:T(8,128)(2,1)} %bitcast.20, bf16[1,64,384]{2,1,0:T(8,128)(2,1)S(1)} %collective-permute-done.nxt, f32[8,128]{1,0:T(8,128)S(1)} %get-tuple-element.24.info.refs_6_, f32[896,128]{1,0:T(8,128)S(1)} %get-tuple-element.25.anchor_t.refs_7_, ...), custom_call_target="tpu_custom_call" | custom-call | flops 2400000000 | bytes 3932160 | tf_op jit(solution)/shard_map/south_pairs/pallas_call | solution.py:325
  17.8 3.6 %collective-permute-start.3 = (f32[64,128]{1,0:T(8,128)S(1)}, f32[64,128]{1,0:T(8,128)S(1)}, u32[]{:S(2)}, u32[]{:S(2)}) collective-permute-start(f32[64,128]{1,0:T(8,128)S(1)} %south_pairs.1.terms_south.refs_0_), channel_id=1, source_target_pairs={{0,1},{1,2},{2,3},{4,5},{5,6},{6,7},{8,9},{9,10},{10,11},{12,13},{... | collective-permute-start | bytes 98312 | tf_op jit(solution)/shard_map/ppermute | solution.py:709
  21.4 6.8 %side_pairs.1.terms_side.refs_1_ = f32[32,128]{1,0:T(8,128)S(1)} custom-call(bf16[40,4,64,512]{3,2,1,0:T(8,128)(2,1)} %bitcast.21, bf16[10,64,640]{2,1,0:T(8,128)(2,1)S(1)} %collective-permute-done.1.from_east, bf16[11,64,640]{2,1,0:T(8,128)(2,1)S(1)} %collective-permute-done.2.from_west, f32[8,128]{1,0:T(8,128)S(1)} %get-tuple-element.24.info.refs_6_, ...), custom_call_target="tpu_custom_call" | custom-call | flops 2400000000 | bytes 3932160 | tf_op jit(solution)/shard_map/side_pairs/pallas_call | solution.py:337
  28.3 1.3 %collective-permute-start.4 = (f32[72,128]{1,0:T(8,128)S(1)}, f32[72,128]{1,0:T(8,128)S(1)}, u32[]{:S(2)}, u32[]{:S(2)}) collective-permute-start(f32[72,128]{1,0:T(8,128)S(1)} %get-tuple-element.28), channel_id=1, source_target_pairs={{4,0},{8,4},{12,8},{16,12},{20,16},{24,20},{28,24},{32,28},{36,32}... | collective-permute-start | bytes 110600 | tf_op jit(solution)/shard_map/ppermute | solution.py:709
  29.6 7.3 %collective-permute-start.5 = (f32[64,128]{1,0:T(8,128)S(1)}, f32[64,128]{1,0:T(8,128)S(1)}, u32[]{:S(2)}, u32[]{:S(2)}) collective-permute-start(f32[64,128]{1,0:T(8,128)S(1)} %get-tuple-element.29), channel_id=1, source_target_pairs={{0,4},{4,8},{8,12},{12,16},{16,20},{20,24},{24,28},{28,32},{32,36}... | collective-permute-start | bytes 98312 | tf_op jit(solution)/shard_map/ppermute | solution.py:709
  36.9 1.3 %collective-permute-start.6 = (f32[64,128]{1,0:T(8,128)S(1)}, f32[64,128]{1,0:T(8,128)S(1)}, u32[]{:S(2)}, u32[]{:S(2)}) collective-permute-start(f32[64,128]{1,0:T(8,128)S(1)} %get-tuple-element.30), channel_id=1, source_target_pairs={{1,0},{2,1},{3,2},{5,4},{6,5},{7,6},{9,8},{10,9},{11,10},{13,12},{... | collective-permute-start | bytes 98312 | tf_op jit(solution)/shard_map/ppermute | solution.py:709
  38.2 4.5 %collective-permute-done.6.refs_4_ = f32[64,128]{1,0:T(8,128)S(1)} collective-permute-done((f32[64,128]{1,0:T(8,128)S(1)}, f32[64,128]{1,0:T(8,128)S(1)}, u32[]{:S(2)}, u32[]{:S(2)}) %collective-permute-start.6) | collective-permute-done | bytes 32800 | tf_op jit(solution)/shard_map/ppermute | solution.py:709
  42.7 1.5 %powers.1 = (f32[1024,128]{1,0:T(8,128)S(1)}, f32[1024,128]{1,0:T(8,128)S(1)}, f32[1024,128]{1,0:T(8,128)S(1)}, f32[1024,128]{1,0:T(8,128)S(1)}, f32[40,48]{1,0:T(8,128)S(1)}, /*index=5*/f32[8,128]{1,0:T(8,128)S(1)}) custom-call(f32[64,128]{1,0:T(8,128)S(1)} %south_pairs.1.terms_south.refs_0_, f32[32,128]{1,0:T(8,128)S(1)} %side_pairs.1.terms_side.refs_1_, ...), custom_call_target="tpu_custom_call" | custom-call | flops 4000000 | bytes 2000000 | tf_op jit(solution)/shard_map/powers/pallas_call | solution.py:414
  44.2 0.7 collective-permute-start.7
  44.9 0.8 %collective-permute-done.7 = f32[8,128]{1,0:T(8,128)S(1)} collective-permute-done((f32[8,128]{1,0:T(8,128)S(1)}, f32[8,128]{1,0:T(8,128)S(1)}, u32[]{:S(2)}, u32[]{:S(2)}) %collective-permute-start.7) | collective-permute-done | bytes 4128 | tf_op jit(solution)/shard_map/ppermute | solution.py:720
  45.7 6.5 %collective-permute-start.10 = (f32[8,128]{1,0:T(8,128)S(1)}, f32[8,128]{1,0:T(8,128)S(1)}, u32[]{:S(2)}, u32[]{:S(2)}) collective-permute-start(f32[8,128]{1,0:T(8,128)S(1)} %add.30), channel_id=1, source_target_pairs={{0,24},{4,28},{8,0},{12,4},{16,8},{20,12},{24,16},{28,20},{32,56},... | collective-permute-start | bytes 12296 | tf_op jit(solution)/shard_map/ppermute | solution.py:720
  52.2 0.9 %collective-permute-start.8 = (f32[8,128]{1,0:T(8,128)S(1)}, f32[8,128]{1,0:T(8,128)S(1)}, u32[]{:S(2)}, u32[]{:S(2)}) collective-permute-start(f32[8,128]{1,0:T(8,128)S(1)} %add.30), channel_id=1, source_target_pairs={{0,8},{4,12},{8,16},{12,20},{16,24},{20,28},{24,0},{28,4},{32,40},... | collective-permute-start | bytes 12296 | tf_op jit(solution)/shard_map/ppermute | solution.py:720
  53.0 0.5 collective-permute-done.10
  53.5 3.8 %collective-permute-done.9 = f32[8,128]{1,0:T(8,128)S(1)} collective-permute-done((f32[8,128]{1,0:T(8,128)S(1)}, f32[8,128]{1,0:T(8,128)S(1)}, u32[]{:S(2)}, u32[]{:S(2)}) %collective-permute-start.9) | collective-permute-done | bytes 4128 | tf_op jit(solution)/shard_map/ppermute | solution.py:720
  57.3 1.1 %collective-permute-start.13 = (f32[8,128]{1,0:T(8,128)S(1)}, f32[8,128]{1,0:T(8,128)S(1)}, u32[]{:S(2)}, u32[]{:S(2)}) collective-permute-start(f32[8,128]{1,0:T(8,128)S(1)} %add_add_fusion.2), channel_id=1, source_target_pairs={{0,96},{4,100},{8,104},{12,108},{16,112},{20,116},{24,120},{28,124... | collective-permute-start | bytes 12296 | tf_op jit(solution)/shard_map/ppermute | solution.py:720
  58.4 2.5 %collective-permute-start.12 = (f32[8,128]{1,0:T(8,128)S(1)}, f32[8,128]{1,0:T(8,128)S(1)}, u32[]{:S(2)}, u32[]{:S(2)}) collective-permute-start(f32[8,128]{1,0:T(8,128)S(1)} %add_add_fusion.2), channel_id=1, source_target_pairs={{0,64},{4,68},{8,72},{12,76},{16,80},{20,84},{24,88},{28,92},{32,9... | collective-permute-start | bytes 12296 | tf_op jit(solution)/shard_map/ppermute | solution.py:720
  60.9 0.6 collective-permute-start.11
  61.5 2.0 %collective-permute-done.12 = f32[8,128]{1,0:T(8,128)S(1)} collective-permute-done((f32[8,128]{1,0:T(8,128)S(1)}, f32[8,128]{1,0:T(8,128)S(1)}, u32[]{:S(2)}, u32[]{:S(2)}) %collective-permute-start.12) | collective-permute-done | bytes 4128 | tf_op jit(solution)/shard_map/ppermute | solution.py:720
  63.5 2.2 %collective-permute-done.11 = f32[8,128]{1,0:T(8,128)S(1)} collective-permute-done((f32[8,128]{1,0:T(8,128)S(1)}, f32[8,128]{1,0:T(8,128)S(1)}, u32[]{:S(2)}, u32[]{:S(2)}) %collective-permute-start.11) | collective-permute-done | bytes 4128 | tf_op jit(solution)/shard_map/ppermute | solution.py:720
  65.7 1.7 %collective-permute-start.16 = (f32[8,128]{1,0:T(8,128)S(1)}, f32[8,128]{1,0:T(8,128)S(1)}, u32[]{:S(2)}, u32[]{:S(2)}) collective-permute-start(f32[8,128]{1,0:T(8,128)S(1)} %add_add_fusion.1), channel_id=1, source_target_pairs={{0,3},{1,0},{2,1},{3,2},{4,7},{5,4},{6,5},{7,6},{8,11},{9,8},{10,9... | collective-permute-start | bytes 12296 | tf_op jit(solution)/shard_map/ppermute | solution.py:720
  67.5 1.9 %collective-permute-start.15 = (f32[8,128]{1,0:T(8,128)S(1)}, f32[8,128]{1,0:T(8,128)S(1)}, u32[]{:S(2)}, u32[]{:S(2)}) collective-permute-start(f32[8,128]{1,0:T(8,128)S(1)} %add_add_fusion.1), channel_id=1, source_target_pairs={{0,2},{1,3},{2,0},{3,1},{4,6},{5,7},{6,4},{7,5},{8,10},{9,11},{10,... | collective-permute-start | bytes 12296 | tf_op jit(solution)/shard_map/ppermute | solution.py:720
  69.4 1.0 %collective-permute-start.14 = (f32[8,128]{1,0:T(8,128)S(1)}, f32[8,128]{1,0:T(8,128)S(1)}, u32[]{:S(2)}, u32[]{:S(2)}) collective-permute-start(f32[8,128]{1,0:T(8,128)S(1)} %add_add_fusion.1), channel_id=1, source_target_pairs={{0,1},{1,2},{2,3},{3,0},{4,5},{5,6},{6,7},{7,4},{8,9},{9,10},{10,1... | collective-permute-start | bytes 12296 | tf_op jit(solution)/shard_map/ppermute | solution.py:720
  70.4 0.7 copy.18
  71.0 1.5 %collective-permute-done.15 = f32[8,128]{1,0:T(8,128)S(1)} collective-permute-done((f32[8,128]{1,0:T(8,128)S(1)}, f32[8,128]{1,0:T(8,128)S(1)}, u32[]{:S(2)}, u32[]{:S(2)}) %collective-permute-start.15) | collective-permute-done | bytes 4128 | tf_op jit(solution)/shard_map/ppermute | solution.py:720
  72.6 1.6 %collective-permute-done.14 = f32[8,128]{1,0:T(8,128)S(1)} collective-permute-done((f32[8,128]{1,0:T(8,128)S(1)}, f32[8,128]{1,0:T(8,128)S(1)}, u32[]{:S(2)}, u32[]{:S(2)}) %collective-permute-start.14) | collective-permute-done | bytes 4128 | tf_op jit(solution)/shard_map/ppermute | solution.py:720
  74.2 1.4 %combine.1 = (f32[40,2,896]{2,1,0:T(2,128)}, f32[40,2,896]{2,1,0:T(2,128)}) custom-call(f32[8,128]{1,0:T(8,128)S(1)} %add_add_fusion.gram, f32[1024,128]{1,0:T(8,128)S(1)} %get-tuple-element.33.v0, f32[1024,128]{1,0:T(8,128)S(1)} %get-tuple-element.34.v1, f32[1024,128]{1,0:T(8,128)S(1)} %get-tuple-element.35.v2, f32[1024,128]{1,0:T(8,128)S(1)} %get-tuple-element.36.v3), custom_call_target="tpu_custom_call" | custom-call | flops 4000000 | bytes 2000000 | tf_op jit(solution)/shard_map/combine/pallas_call | solution.py:414
  (36 shorter events, 0.2 us)
Async XLA Ops:
  0.6 3.0 %copy-start.8 = (s32[40,1,2]{0,2,1:T(2,128)S(1)}, s32[40,1,2]{0,2,1:T(2,128)}, u32[]{:S(2)}) copy-start(s32[40,1,2]{0,2,1:T(2,128)} %param.13) | copy-start | bytes 964
  0.6 3.0 %copy-start.9 = (s32[40,1,2]{0,2,1:T(2,128)S(1)}, s32[40,1,2]{0,2,1:T(2,128)}, u32[]{:S(2)}) copy-start(s32[40,1,2]{0,2,1:T(2,128)} %param.14) | copy-start | bytes 964
  0.7 3.0 %copy-start.10 = (f32[40,1]{0,1:T(1,128)S(1)}, f32[40,1]{0,1:T(1,128)}, u32[]{:S(2)}) copy-start(f32[40,1]{0,1:T(1,128)} %param.15) | copy-start | bytes 484
  0.7 3.0 %copy-start.3 = (f32[40,1,896]{2,1,0:T(1,128)S(1)}, f32[40,1,896]{2,1,0:T(1,128)}, u32[]{:S(2)}) copy-start(f32[40,1,896]{2,1,0:T(1,128)} %anchor.1) | copy-start | bytes 430084
  0.7 10.5 %copy-start = (bf16[256,512]{1,0:T(8,128)(2,1)S(1)}, bf16[256,512]{1,0:T(8,128)(2,1)}, u32[]{:S(2)}) copy-start(bf16[256,512]{1,0:T(8,128)(2,1)} %constant.16.clone.ends) | copy-start | bytes 786436
  0.7 10.5 %copy-start.1 = (bf16[2,256,256]{2,1,0:T(8,128)(2,1)S(1)}, bf16[2,256,256]{2,1,0:T(8,128)(2,1)}, u32[]{:S(2)}) copy-start(bf16[2,256,256]{2,1,0:T(8,128)(2,1)} %constant.17.clone.backs) | copy-start | bytes 786436
  0.7 10.5 %copy-start.2 = (bf16[256,256]{1,0:T(8,128)(2,1)S(1)}, bf16[256,256]{1,0:T(8,128)(2,1)}, u32[]{:S(2)}) copy-start(bf16[256,256]{1,0:T(8,128)(2,1)} %constant.15.clone.forward) | copy-start | bytes 393220
  0.7 10.4 %copy-start.4 = (f32[64,128]{1,0:T(8,128)S(1)}, f32[64,128]{1,0:T(8,128)}, u32[]{:S(2)}) copy-start(f32[64,128]{1,0:T(8,128)} %constant.20.clone.rows) | copy-start | bytes 98308
  0.7 10.4 %copy-start.5 = (bf16[64,64]{1,0:T(8,128)(2,1)S(1)}, bf16[64,64]{1,0:T(8,128)(2,1)}, u32[]{:S(2)}) copy-start(bf16[64,64]{1,0:T(8,128)(2,1)} %constant.14.clone.depth) | copy-start | bytes 24580
  0.7 10.4 %copy-start.6 = (bf16[64,64]{1,0:T(8,128)(2,1)S(1)}, bf16[64,64]{1,0:T(8,128)(2,1)}, u32[]{:S(2)}) copy-start(bf16[64,64]{1,0:T(8,128)(2,1)} %constant.18.clone.final) | copy-start | bytes 24580
  0.7 10.4 %copy-start.7 = (f32[8,128]{1,0:T(8,128)S(1)}, f32[8,128]{1,0:T(8,128)}, u32[]{:S(2)}) copy-start(f32[8,128]{1,0:T(8,128)} %constant.19.clone.pick) | copy-start | bytes 12292
  2.3 6.2 %collective-permute-start = (bf16[1,64,384]{2,1,0:T(8,128)(2,1)}, bf16[1,64,384]{2,1,0:T(8,128)(2,1)S(1)}, u32[]{:S(2)}, u32[]{:S(2)}) collective-permute-start(bf16[1,64,384]{2,1,0:T(8,128)(2,1)} %edge.1), channel_id=1, source_target_pairs={{1,0},{2,1},{3,2},{5,4},{6,5},{7,6},{9,8},{10,9},{11,10},{13,12},{... | collective-permute-start | bytes 147464 | tf_op jit(solution)/shard_map/ppermute | solution.py:709
  8.5 12.9 %collective-permute-start.2 = (bf16[11,64,640]{2,1,0:T(8,128)(2,1)S(1)}, bf16[11,64,640]{2,1,0:T(8,128)(2,1)S(1)}, u32[]{:S(2)}, u32[]{:S(2)}) collective-permute-start(bf16[11,64,640]{2,1,0:T(8,128)(2,1)S(1)} %get-tuple-element.27), channel_id=1, source_target_pairs={{0,4},{4,8},{8,12},{12,16},{16,20},{20,24},{24,28},{28,32},{32,36}... | collective-permute-start | bytes 2703368 | tf_op jit(solution)/shard_map/ppermute | solution.py:709
  9.8 11.5 %collective-permute-start.1 = (bf16[10,64,640]{2,1,0:T(8,128)(2,1)S(1)}, bf16[10,64,640]{2,1,0:T(8,128)(2,1)S(1)}, u32[]{:S(2)}, u32[]{:S(2)}) collective-permute-start(bf16[10,64,640]{2,1,0:T(8,128)(2,1)S(1)} %get-tuple-element.26), channel_id=1, source_target_pairs={{4,0},{8,4},{12,8},{16,12},{20,16},{24,20},{28,24},{32,28},{36,32}... | collective-permute-start | bytes 2457608 | tf_op jit(solution)/shard_map/ppermute | solution.py:709
  17.8 10.4 %collective-permute-start.3 = (f32[64,128]{1,0:T(8,128)S(1)}, f32[64,128]{1,0:T(8,128)S(1)}, u32[]{:S(2)}, u32[]{:S(2)}) collective-permute-start(f32[64,128]{1,0:T(8,128)S(1)} %south_pairs.1.terms_south.refs_0_), channel_id=1, source_target_pairs={{0,1},{1,2},{2,3},{4,5},{5,6},{6,7},{8,9},{9,10},{10,11},{12,13},{... | collective-permute-start | bytes 98312 | tf_op jit(solution)/shard_map/ppermute | solution.py:709
  28.3 14.4 %collective-permute-start.4 = (f32[72,128]{1,0:T(8,128)S(1)}, f32[72,128]{1,0:T(8,128)S(1)}, u32[]{:S(2)}, u32[]{:S(2)}) collective-permute-start(f32[72,128]{1,0:T(8,128)S(1)} %get-tuple-element.28), channel_id=1, source_target_pairs={{4,0},{8,4},{12,8},{16,12},{20,16},{24,20},{28,24},{32,28},{36,32}... | collective-permute-start | bytes 110600 | tf_op jit(solution)/shard_map/ppermute | solution.py:709
  29.6 8.6 %collective-permute-start.5 = (f32[64,128]{1,0:T(8,128)S(1)}, f32[64,128]{1,0:T(8,128)S(1)}, u32[]{:S(2)}, u32[]{:S(2)}) collective-permute-start(f32[64,128]{1,0:T(8,128)S(1)} %get-tuple-element.29), channel_id=1, source_target_pairs={{0,4},{4,8},{8,12},{12,16},{16,20},{20,24},{24,28},{28,32},{32,36}... | collective-permute-start | bytes 98312 | tf_op jit(solution)/shard_map/ppermute | solution.py:709
  36.9 5.8 %collective-permute-start.6 = (f32[64,128]{1,0:T(8,128)S(1)}, f32[64,128]{1,0:T(8,128)S(1)}, u32[]{:S(2)}, u32[]{:S(2)}) collective-permute-start(f32[64,128]{1,0:T(8,128)S(1)} %get-tuple-element.30), channel_id=1, source_target_pairs={{1,0},{2,1},{3,2},{5,4},{6,5},{7,6},{9,8},{10,9},{11,10},{13,12},{... | collective-permute-start | bytes 98312 | tf_op jit(solution)/shard_map/ppermute | solution.py:709
  44.2 1.5 %collective-permute-start.7 = (f32[8,128]{1,0:T(8,128)S(1)}, f32[8,128]{1,0:T(8,128)S(1)}, u32[]{:S(2)}, u32[]{:S(2)}) collective-permute-start(f32[8,128]{1,0:T(8,128)S(1)} %get-tuple-element.32), channel_id=1, source_target_pairs={{0,4},{4,0},{8,12},{12,8},{16,20},{20,16},{24,28},{28,24},{32,36},... | collective-permute-start | bytes 12296 | tf_op jit(solution)/shard_map/ppermute | solution.py:720
  45.7 7.8 %collective-permute-start.10 = (f32[8,128]{1,0:T(8,128)S(1)}, f32[8,128]{1,0:T(8,128)S(1)}, u32[]{:S(2)}, u32[]{:S(2)}) collective-permute-start(f32[8,128]{1,0:T(8,128)S(1)} %add.30), channel_id=1, source_target_pairs={{0,24},{4,28},{8,0},{12,4},{16,8},{20,12},{24,16},{28,20},{32,56},... | collective-permute-start | bytes 12296 | tf_op jit(solution)/shard_map/ppermute | solution.py:720
  52.2 5.1 %collective-permute-start.9 = (f32[8,128]{1,0:T(8,128)S(1)}, f32[8,128]{1,0:T(8,128)S(1)}, u32[]{:S(2)}, u32[]{:S(2)}) collective-permute-start(f32[8,128]{1,0:T(8,128)S(1)} %add.30), channel_id=1, source_target_pairs={{0,16},{4,20},{8,24},{12,28},{16,0},{20,4},{24,8},{28,12},{32,48},... | collective-permute-start | bytes 12296 | tf_op jit(solution)/shard_map/ppermute | solution.py:720
  52.2 5.1 %collective-permute-start.8 = (f32[8,128]{1,0:T(8,128)S(1)}, f32[8,128]{1,0:T(8,128)S(1)}, u32[]{:S(2)}, u32[]{:S(2)}) collective-permute-start(f32[8,128]{1,0:T(8,128)S(1)} %add.30), channel_id=1, source_target_pairs={{0,8},{4,12},{8,16},{12,20},{16,24},{20,28},{24,0},{28,4},{32,40},... | collective-permute-start | bytes 12296 | tf_op jit(solution)/shard_map/ppermute | solution.py:720
  57.3 4.2 %collective-permute-start.13 = (f32[8,128]{1,0:T(8,128)S(1)}, f32[8,128]{1,0:T(8,128)S(1)}, u32[]{:S(2)}, u32[]{:S(2)}) collective-permute-start(f32[8,128]{1,0:T(8,128)S(1)} %add_add_fusion.2), channel_id=1, source_target_pairs={{0,96},{4,100},{8,104},{12,108},{16,112},{20,116},{24,120},{28,124... | collective-permute-start | bytes 12296 | tf_op jit(solution)/shard_map/ppermute | solution.py:720
  58.4 5.1 %collective-permute-start.12 = (f32[8,128]{1,0:T(8,128)S(1)}, f32[8,128]{1,0:T(8,128)S(1)}, u32[]{:S(2)}, u32[]{:S(2)}) collective-permute-start(f32[8,128]{1,0:T(8,128)S(1)} %add_add_fusion.2), channel_id=1, source_target_pairs={{0,64},{4,68},{8,72},{12,76},{16,80},{20,84},{24,88},{28,92},{32,9... | collective-permute-start | bytes 12296 | tf_op jit(solution)/shard_map/ppermute | solution.py:720
  60.9 4.8 %collective-permute-start.11 = (f32[8,128]{1,0:T(8,128)S(1)}, f32[8,128]{1,0:T(8,128)S(1)}, u32[]{:S(2)}, u32[]{:S(2)}) collective-permute-start(f32[8,128]{1,0:T(8,128)S(1)} %add_add_fusion.2), channel_id=1, source_target_pairs={{0,32},{4,36},{8,40},{12,44},{16,48},{20,52},{24,56},{28,60},{32,6... | collective-permute-start | bytes 12296 | tf_op jit(solution)/shard_map/ppermute | solution.py:720
  65.7 5.3 %collective-permute-start.16 = (f32[8,128]{1,0:T(8,128)S(1)}, f32[8,128]{1,0:T(8,128)S(1)}, u32[]{:S(2)}, u32[]{:S(2)}) collective-permute-start(f32[8,128]{1,0:T(8,128)S(1)} %add_add_fusion.1), channel_id=1, source_target_pairs={{0,3},{1,0},{2,1},{3,2},{4,7},{5,4},{6,5},{7,6},{8,11},{9,8},{10,9... | collective-permute-start | bytes 12296 | tf_op jit(solution)/shard_map/ppermute | solution.py:720
  67.5 5.1 %collective-permute-start.15 = (f32[8,128]{1,0:T(8,128)S(1)}, f32[8,128]{1,0:T(8,128)S(1)}, u32[]{:S(2)}, u32[]{:S(2)}) collective-permute-start(f32[8,128]{1,0:T(8,128)S(1)} %add_add_fusion.1), channel_id=1, source_target_pairs={{0,2},{1,3},{2,0},{3,1},{4,6},{5,7},{6,4},{7,5},{8,10},{9,11},{10,... | collective-permute-start | bytes 12296 | tf_op jit(solution)/shard_map/ppermute | solution.py:720
  69.4 4.8 %collective-permute-start.14 = (f32[8,128]{1,0:T(8,128)S(1)}, f32[8,128]{1,0:T(8,128)S(1)}, u32[]{:S(2)}, u32[]{:S(2)}) collective-permute-start(f32[8,128]{1,0:T(8,128)S(1)} %add_add_fusion.1), channel_id=1, source_target_pairs={{0,1},{1,2},{2,3},{3,0},{4,5},{5,6},{6,7},{7,4},{8,9},{9,10},{10,1... | collective-permute-start | bytes 12296 | tf_op jit(solution)/shard_map/ppermute | solution.py:720

commit v4 on v3

--- a/solution.py
+++ b/solution.py
@@ -243,29 +243,29 @@
     out[32:, :] = anchor_t[NODES - MESH_X : NODES, :]
 
 
-def side_kernel(strips, from_east, from_west, info, depth, forward, ends, backs, final, pick, rows, out, own, other, own_extra, r0, r1, sems, extra_sems):
-    steps = own.shape[0] // GROUP
+def side_kernel(role, strips, received, info, depth, forward, ends, backs, final, pick, rows, out, own, other, own_extra, r0, r1, sems, extra_sems):
+    half = own.shape[0]
+    steps = half // GROUP
     slots = GROUP // 2
-    count = from_east.shape[0]
-    side = pl.ds(0, SIDE)
-
-    def own_copy(c, which):
-        at = pl.ds(GROUP * c, GROUP)
-        return pltpu.make_async_copy(strips.at[at, which, :, side], own.at[at], sems.at[0, c])
-
-    def other_copy(c, source, start):
-        return pltpu.make_async_copy(
-            source.at[pl.ds(start, slots)], other.at[pl.ds(slots * c, slots)], sems.at[1, c]
-        )
+    spare = half // 2
+    west = role[0]
+    base = west * half
+
+    def own_copy(c):
+        source = strips.at[pl.ds(base + GROUP * c, GROUP), 3 - 3 * west, :, pl.ds(0, SIDE)]
+        return pltpu.make_async_copy(source, own.at[pl.ds(GROUP * c, GROUP)], sems.at[0, c])
+
+    def other_copy(c):
+        at = pl.ds(slots * c, slots)
+        return pltpu.make_async_copy(received.at[at], other.at[at], sems.at[1, c])
 
     extra_copies = (
         pltpu.make_async_copy(strips.at[0, 0, :, pl.ds(0, LANES)], own_extra, extra_sems.at[0]),
-        pltpu.make_async_copy(from_west.at[count], other.at[2 * count], extra_sems.at[1]),
+        pltpu.make_async_copy(received.at[spare], other.at[spare], extra_sems.at[1]),
     )
     for c in range(steps):
-        east = c < steps // 2
-        own_copy(c, 3 if east else 0).start()
-        other_copy(c, from_east if east else from_west, slots * (c % (steps // 2))).start()
+        own_copy(c).start()
+        other_copy(c).start()
         if c == 0:
             for copy in extra_copies:
                 copy.start()
@@ -275,23 +275,25 @@
         copy.wait()
 
     def step(c, carry):
-        own_copy(c, 0).wait()
-        other_copy(c, from_east, 0).wait()
+        own_copy(c).wait()
+        other_copy(c).wait()
         owns = block_pairs([own[GROUP * c + j, :, :WIDE] for j in range(GROUP)])
         others = [
             other[slots * c + slot, :, LANES * i : LANES * (i + 1)] for slot in range(slots) for i in range(5)
         ]
         correlate_group(
-            owns + [own_extra[...]] + others + [other[2 * count, :, :LANES]],
-            depth[...], forward[...], ends[...], backs[c // (steps // 2)], final[...], rows[...], r0, r1, GROUP * c,
+            owns + [own_extra[...]] + others + [other[spare, :, :LANES]],
+            depth[...], forward[...], ends[...], backs[west], final[...], rows[...], r0, r1, base + GROUP * c,
         )
         return carry
 
     lax.fori_loop(0, steps, step, 0)
     lane = lax.broadcasted_iota(jnp.int32, (8, LANES), 1)
-    info_west = other[2 * count, 0:16, 2 * LANES : 3 * LANES].astype(F32)[0:8]
-    table = jnp.where(lane < GROUP * (steps // 2), info[...], info_west)
-    table = jnp.where(lane == EXTRA, pltpu.roll(info_west, EXTRA, axis=1), table)
+    info_west = other[spare, 0:16, 2 * LANES : 3 * LANES].astype(F32)[0:8]
+    table = jnp.where(west == 1, info_west, info[0:8, :])
+    mine = (lane >= base) & (lane < base + half)
+    table = jnp.where(mine, table, 0.0)
+    table = jnp.where((lane == EXTRA) & (west == 1), pltpu.roll(info_west, EXTRA, axis=1), table)
     finish_terms(pick[...], r0, r1, table[0:1], table[1:2], out)
 
 
@@ -299,6 +301,7 @@
 VMEM_BYTES = 48 * 1024 * 1024
 ANY = pl.BlockSpec(memory_space=pl.ANY)
 VMEM = pl.BlockSpec(memory_space=pltpu.VMEM)
+SMEM = pl.BlockSpec(memory_space=pltpu.SMEM)
 
 
 def pair_call(kernel, name, tiles, rows, specs, buffers, semaphores):
@@ -327,95 +330,118 @@
     )(strips, nxt, info, anchor_t, *tabs)
 
 
-def side_terms(strips, from_east, from_west, info, tabs):
-    tiles = strips.shape[0]
+def side_terms(name, role, strips, received, info, tabs):
+    half = strips.shape[0] // 2
     buffers = [
-        pltpu.VMEM((tiles, PATCH, SIDE), BF16),
-        pltpu.VMEM((tiles // 2 + 1, PATCH, 2 * WIDE), BF16),
+        pltpu.VMEM((half, PATCH, SIDE), BF16),
+        pltpu.VMEM((half // 2 + 1, PATCH, 2 * WIDE), BF16),
         pltpu.VMEM((PATCH, LANES), BF16),
     ]
     return pair_call(
-        side_kernel, "side_pairs", tiles, 32, [ANY, ANY, ANY, VMEM], buffers, [pltpu.SemaphoreType.DMA((2,))]
-    )(strips, from_east, from_west, info, *tabs)
-
-
-def edge_kernel(strips, north, sem):
-    copy = pltpu.make_async_copy(strips.at[0, 1, :, pl.ds(0, SIDE)], north.at[0], sem)
-    copy.start()
-    copy.wait()
-
-
-def prepare_kernel(strips, counts, offsets, stiffness, anchor, west, east, info, anchor_t, left, right, small, wide, sems):
-    tiles = anchor.shape[0]
-    half = tiles // 2
+        side_kernel, name, half, 32, [SMEM, ANY, ANY, VMEM], buffers, [pltpu.SemaphoreType.DMA((2,))]
+    )(role, strips, received, info, *tabs)
+
+
+def pack(role, strips, info, packed, buffer, sems):
+    half = buffer.shape[0]
+    east = 1 - role[0]
     moves = [
-        (strips.at[pl.ds(half, half), 3, :, pl.ds(0, SIDE)], right),
-        (strips.at[pl.ds(0, half), 0, :, pl.ds(0, SIDE)], left),
-        (strips.at[0, 3, :, pl.ds(0, LANES)], east.at[half // 2, :, pl.ds(0, LANES)]),
+        pltpu.make_async_copy(
+            strips.at[pl.ds(east * half, half), 3 * east, :, pl.ds(0, SIDE)], buffer, sems.at[0]
+        ),
+        pltpu.make_async_copy(
+            strips.at[0, 3, :, pl.ds(0, LANES)], packed.at[half // 2, :, pl.ds(0, LANES)], sems.at[1]
+        ),
     ]
-    moves = [pltpu.make_async_copy(a, b, sems.at[k]) for k, (a, b) in enumerate(moves)]
     for move in moves:
         move.start()
-    small[...] = jnp.zeros_like(small)
+    packed[half // 2, :, LANES:] = jnp.zeros((PATCH, 2 * WIDE - LANES), BF16)
+    packed[half // 2, 0:16, 2 * LANES : 3 * LANES] = info.astype(BF16)
+    yield
+    moves[0].wait()
+    for slot in range(half // 2):
+        columns = block_pairs([buffer[2 * slot + j, :, :WIDE] for j in range(2)])
+        for i, x in enumerate(columns):
+            packed[slot, :, LANES * i : LANES * (i + 1)] = x
+    moves[1].wait()
+
+
+def pack_across_kernel(role, strips, counts, offsets, stiffness, packed, north, info, buffer, sems, edge_sem):
+    tiles = counts.shape[1]
+    edge = pltpu.make_async_copy(strips.at[0, 1, :, pl.ds(0, SIDE)], north.at[0], edge_sem)
+    edge.start()
     here = pl.ds(0, tiles)
-    small[0:1, here] = counts[0:1, :].astype(F32)
-    small[1:2, here] = offsets[0:1, :].astype(F32)
-    small[2:3, here] = counts[1:2, :].astype(F32)
-    small[3:4, here] = offsets[1:2, :].astype(F32)
-    small[4:5, here] = stiffness[...]
-    info[...] = small[0:8, :]
-    wide[...] = jnp.zeros_like(wide)
-    for first in (0, COMP):
-        wide[first : first + tiles, :] = anchor[:, 0, :]
-    for i in range(NODES // LANES):
-        anchor_t[LANES * i : LANES * (i + 1), :] = wide[:, LANES * i : LANES * (i + 1)].T
-    east[half // 2, :, LANES:] = jnp.zeros((PATCH, 2 * WIDE - LANES), BF16)
-    east[half // 2, 0:16, 2 * LANES : 3 * LANES] = small[...].astype(BF16)
-    for move, source, packed in ((moves[0], right, east), (moves[1], left, west)):
-        move.wait()
-        for slot in range(half // 2):
-            columns = block_pairs([source[2 * slot + j, :, :WIDE] for j in range(2)])
-            for i, x in enumerate(columns):
-                packed[slot, :, LANES * i : LANES * (i + 1)] = x
-    moves[2].wait()
-
-
-def prepare(strips, counts, offsets, stiffness, anchor):
+    info[...] = jnp.zeros_like(info)
+    info[0:1, here] = counts[0:1, :].astype(F32)
+    info[1:2, here] = offsets[0:1, :].astype(F32)
+    info[2:3, here] = counts[1:2, :].astype(F32)
+    info[3:4, here] = offsets[1:2, :].astype(F32)
+    info[4:5, here] = stiffness[...]
+    for _ in pack(role, strips, info[...], packed, buffer, sems):
+        pass
+    edge.wait()
+
+
+def pack_within_kernel(role, strips, info, anchor, packed, anchor_t, buffer, sems, wide):
     tiles = anchor.shape[0]
-    vmem = pl.BlockSpec(memory_space=pltpu.VMEM)
-    slots = tiles // 4
+    for _ in pack(role, strips, info[...], packed, buffer, sems):
+        wide[...] = jnp.zeros_like(wide)
+        for first in (0, COMP):
+            wide[first : first + tiles, :] = anchor[:, 0, :]
+        for i in range(NODES // LANES):
+            anchor_t[LANES * i : LANES * (i + 1), :] = wide[:, LANES * i : LANES * (i + 1)].T
+
+
+def pack_across(role, strips, counts, offsets, stiffness):
+    tiles = strips.shape[0]
     return pl.pallas_call(
-        prepare_kernel,
-        name="prepare",
-        in_specs=[pl.BlockSpec(memory_space=pl.ANY)] + [vmem] * 4,
-        out_specs=[vmem] * 4,
+        pack_across_kernel,
+        name="pack_across",
+        in_specs=[SMEM, ANY] + [VMEM] * 3,
+        out_specs=[VMEM] * 3,
         out_shape=[
-            jax.ShapeDtypeStruct((slots, PATCH, 2 * WIDE), BF16),
-            jax.ShapeDtypeStruct((slots + 1, PATCH, 2 * WIDE), BF16),
-            jax.ShapeDtypeStruct((8, LANES), F32),
+            jax.ShapeDtypeStruct((tiles // 4 + 1, PATCH, 2 * WIDE), BF16),
+            jax.ShapeDtypeStruct((1, PATCH, SIDE), BF16),
+            jax.ShapeDtypeStruct((16, LANES), F32),
+        ],
+        scratch_shapes=[
+            pltpu.VMEM((tiles // 2, PATCH, SIDE), BF16),
+            pltpu.SemaphoreType.DMA((2,)),
+            pltpu.SemaphoreType.DMA,
+        ],
+        compiler_params=pltpu.CompilerParams(vmem_limit_bytes=VMEM_BYTES),
+    )(role, strips, counts, offsets, stiffness)
+
+
+def pack_within(role, strips, info, anchor):
+    tiles = strips.shape[0]
+    return pl.pallas_call(
+        pack_within_kernel,
+        name="pack_within",
+        in_specs=[SMEM, ANY, VMEM, VMEM],
+        out_specs=[VMEM] * 2,
+        out_shape=[
+            jax.ShapeDtypeStruct((tiles // 4 + 1, PATCH, 2 * WIDE), BF16),
             jax.ShapeDtypeStruct((NODES, LANES), F32),
         ],
         scratch_shapes=[
             pltpu.VMEM((tiles // 2, PATCH, SIDE), BF16),
-            pltpu.VMEM((tiles // 2, PATCH, SIDE), BF16),
-            pltpu.VMEM((16, LANES), F32),
+            pltpu.SemaphoreType.DMA((2,)),
             pltpu.VMEM((LANES, NODES), F32),
-            pltpu.SemaphoreType.DMA((3,)),
         ],
         compiler_params=pltpu.CompilerParams(vmem_limit_bytes=VMEM_BYTES),
-    )(strips, counts, offsets, stiffness, anchor)
-
-
-def whole(kernel, outs, name, scratch=()):
-    vmem = pl.BlockSpec(memory_space=pltpu.VMEM)
+    )(role, strips, info, anchor)
+
+
+def whole(kernel, outs, name, scratch=(), with_role=True):
     shapes = [jax.ShapeDtypeStruct(s, F32) for s in outs]
 
     def call(*args):
         return pl.pallas_call(
             kernel,
             name=name,
-            in_specs=[vmem] * len(args),
-            out_specs=[vmem] * len(outs),
+            in_specs=[SMEM] + [VMEM] * (len(args) - 1) if with_role else [VMEM] * len(args),
+            out_specs=[VMEM] * len(outs),
             out_shape=shapes,
             scratch_shapes=list(scratch),
             compiler_params=pltpu.CompilerParams(vmem_limit_bytes=VMEM_BYTES),
@@ -503,23 +529,32 @@
     return jnp.sum(a[0:NODES, :] * b[0:NODES, :], axis=0, keepdims=True)
 
 
-def message_kernel(tiles, terms_south, terms_side, from_north, info, anchor_t, to_west, to_east, to_north):
+def write_message(role, terms, terms_south, from_north, info, anchor_t, tiles, out):
     lane = lax.broadcasted_iota(jnp.int32, (1, LANES), 1)
-    side = terms_side[...]
-    for out in (to_west, to_east, to_north):
-        out[0:32, :] = side
-        out[25:26, :] = info[4:5, :]
+    out[0:32, :] = terms[...]
+    out[25:26, :] = info[4:5, :]
     south = terms_south[0:32, :]
     north = roll_tiles(south, 1, from_north[0:32, :], tiles)
-    for q, terms in enumerate((south, north)):
+    for q, table in enumerate((south, north)):
         for k, row in enumerate((0, 8, 16, 24)):
-            to_west[32 + 4 * q + k : 33 + 4 * q + k, :] = terms[row : row + 1]
-    first = anchor_t[pl.ds(0, MESH_Y, stride=MESH_X), :]
-    second = anchor_t[pl.ds(1, MESH_Y, stride=MESH_X), :]
-    to_west[40 : 40 + MESH_Y, :] = jnp.where(lane < COMP, first, second)
-    to_west[40 + MESH_Y :, :] = jnp.zeros((4, LANES), F32)
-    to_east[32 : 32 + MESH_Y, :] = anchor_t[pl.ds(MESH_X - 1, MESH_Y, stride=MESH_X), :]
-    to_east[32 + MESH_Y :, :] = jnp.zeros((4, LANES), F32)
+            out[32 + 4 * q + k : 33 + 4 * q + k, :] = table[row : row + 1]
+    first, second, edge = [
+        anchor_t[pl.ds(j, MESH_Y, stride=MESH_X), :] for j in (0, 1, MESH_X - 1)
+    ]
+    to_west = jnp.where(lane < COMP, first, second)
+    out[40 : 40 + MESH_Y, :] = jnp.where(role[0] == 1, to_west, edge)
+    out[40 + MESH_Y :, :] = jnp.zeros((MESH_X - MESH_Y, LANES), F32)
+
+
+def message_kernel(tiles, role, terms, terms_south, from_north, info, anchor_t, out):
+    write_message(role, terms, terms_south, from_north, info, anchor_t, tiles, out)
+
+
+def last_message_kernel(tiles, role, terms, other_terms, terms_south, from_north, info, anchor_t, out, to_north):
+    lane = lax.broadcasted_iota(jnp.int32, (1, LANES), 1)
+    write_message(role, terms, terms_south, from_north, info, anchor_t, tiles, out)
+    to_north[0:32, :] = terms[...] + other_terms[...]
+    to_north[25:26, :] = info[4:5, :]
     to_north[32:, :] = jnp.where(
         lane == 0, anchor_t[0:MESH_X, :], pltpu.roll(anchor_t[MESH_X : 2 * MESH_X, :], 1, axis=1)
     )
@@ -554,12 +589,15 @@
 
 
 def mesh_kernel(tiles, *refs):
-    terms_south, terms_side, from_east, from_west, from_south, from_north, info, anchor_t = refs[:8]
-    v0, v1, v2, v3, match, gram, flip = refs[8:]
+    role, terms_south, terms_within, terms_across, within, across, from_south, from_north, info, anchor_t = refs[:10]
+    v0, v1, v2, v3, match, gram, flip = refs[10:]
+    within_is_east = role[0] == 0
+    from_east = jnp.where(within_is_east, within[...], across[...])
+    from_west = jnp.where(within_is_east, across[...], within[...])
     lane = lax.broadcasted_iota(jnp.int32, (1, LANES), 1)
     node = lax.broadcasted_iota(jnp.int32, (MESH_X, LANES), 0)
     low, inside = lane < tiles // 2, lane < tiles
-    side = terms_side[...]
+    side = terms_within[...] + terms_across[...]
     south_terms = terms_south[0:32, :]
     terms = [
         jnp.where(low, side, from_east[0:32, :]),
@@ -591,7 +629,7 @@
     turned = pltpu.roll(packed, COMP, axis=1)
     anchor_e0 = jnp.where(lane < COMP, packed, turned)
     anchor_e1 = jnp.where(lane < COMP, turned, packed)
-    anchor_w0 = from_west[32:64, :]
+    anchor_w0 = from_west[40:72, :]
     last = tiles - 1
     outside_south = pick_lane(from_south[25:26, :], 0, last)
     anchor_s0 = pick_lane(from_south[32:64, :], 0, last)
@@ -709,6 +747,12 @@
     return lax.ppermute(x, axis, [(i, i + by) for i in range(peers) if 0 <= i + by < peers])
 
 
+def swapped(x, axis, first):
+    peers = lax.axis_size(axis)
+    pairs = [(i, i + 1) for i in range(first, peers - 1, 2)]
+    return lax.ppermute(x, axis, pairs + [(b, a) for a, b in pairs])
+
+
 def add_over(x, axis, stride, radix):
     peers = lax.axis_size(axis)
     got = []
@@ -740,44 +784,44 @@
     tiles = strips.shape[0]
     own = strips[:, 0]
     field = (TALL, LANES)
-    to_north = pl.pallas_call(
-        edge_kernel,
-        name="edge",
-        in_specs=[ANY],
-        out_specs=VMEM,
-        out_shape=jax.ShapeDtypeStruct((1, PATCH, SIDE), BF16),
-        scratch_shapes=[pltpu.SemaphoreType.DMA],
-    )(own)
+    within_role = (lax.axis_index("row") % 2).astype(jnp.int32).reshape(1)
+    across_role = 1 - within_role
+    packed_across, to_north, info = pack_across(
+        across_role, own, pair_counts[:, 0].T, pair_offsets[:, 0].T, tile_stiffness.T
+    )
+    strips_across = swapped(packed_across, "row", 1)
     next_top = shifted(to_north, "col", -1)
-    to_west, to_east, info, anchor_t = prepare(
-        own, pair_counts[:, 0].T, pair_offsets[:, 0].T, tile_stiffness.T, anchor
-    )
-    to_west, to_east, next_top = lax.optimization_barrier((to_west, to_east, next_top))
-    strips_west = shifted(to_east, "row", 1)
-    strips_east = shifted(to_west, "row", -1)
+    packed_within, anchor_t = pack_within(within_role, own, info, anchor)
+    packed_within, next_top = lax.optimization_barrier((packed_within, next_top))
+    strips_within = swapped(packed_within, "row", 0)
     tabs = tables()
     terms_south = south_terms(own, next_top, info, anchor_t, tabs)
     from_north = shifted(terms_south, "col", 1)
-    terms_side = side_terms(own, strips_east, strips_west, info, tabs)
-    to_west, to_east, to_north = whole(
-        functools.partial(message_kernel, tiles),
-        [(72, LANES), (64, LANES), (64, LANES)],
-        "messages",
-    )(terms_south, terms_side, from_north, info, anchor_t)
-    from_east = shifted(to_west, "row", -1)
-    from_west = shifted(to_east, "row", 1)
+    terms_within = side_terms("within_pairs", within_role, own, strips_within, info, tabs)
+    message = (72, LANES)
+    (to_within,) = whole(functools.partial(message_kernel, tiles), [message], "message")(
+        within_role, terms_within, terms_south, from_north, info, anchor_t
+    )
+    to_within, strips_across = lax.optimization_barrier((to_within, strips_across))
+    within = swapped(to_within, "row", 0)
+    terms_across = side_terms("across_pairs", across_role, own, strips_across, info, tabs)
+    to_across, to_north = whole(
+        functools.partial(last_message_kernel, tiles), [message, (64, LANES)], "last_message"
+    )(across_role, terms_across, terms_within, terms_south, from_north, info, anchor_t)
+    across = swapped(to_across, "row", 1)
     from_south = shifted(to_north, "col", -1)
     v0, v1, v2, v3, match, gram = whole(
         functools.partial(mesh_kernel, tiles),
         [field, field, field, field, (tiles, 48), (8, LANES)],
         "powers",
         [pltpu.VMEM((LANES, LANES), F32)],
-    )(terms_south, terms_side, from_east, from_west, from_south, from_north, info, anchor_t)
+    )(within_role, terms_south, terms_within, terms_across, within, across, from_south, from_north, info, anchor_t)
     gram = sum_everywhere(gram)
     positions, residual = whole(
         functools.partial(final_kernel, tiles),
         [(tiles, 2, NODES), (tiles, 2, NODES)],
         "combine",
+        with_role=False,
     )(gram, v0, v1, v2, v3)
     return match.reshape(tiles, 1, 2, 3, 8), positions[:, None], residual[:, None]
 

time: 75.9 us -> 73.5 us (0.968)
  starting transfers between devices: 34.2 us -> 27.4 us
  local copies, waits for them, and re-layouts: 0.75 us -> 2.77 us
  Pallas kernels: 19.7 us -> 21.2 us
  waiting for transfers between devices: 20.1 us -> 20.9 us
    ppermute x7 -> x3, starting transfers between devices: 17.3 us -> 6.15 us  [shifted(): lax.ppermute(x, axis, [(i, i + by) for i in range(peers) if 0 <= i + by <...]
    ppermute x0 -> x4, starting transfers between devices: none -> 4.39 us  [swapped(): return lax.ppermute(x, axis, pairs + [(b, a) for a, b in pairs])]
    unnamed x22, local copies, waits for them, and re-layouts: 0.06 us -> 2.08 us
    pallas_call x6 -> x8, Pallas kernels: 13.1 us -> 14.6 us  [the longest x2 8.55 us: side_terms(): pair_call(side_kernel, name, half, 32, [SMEM, ANY, ANY, VMEM], buffers, [...]
    ppermute x7 -> x3, waiting for transfers between devices: 7.6 us -> 7.73 us  [shifted(): lax.ppermute(x, axis, [(i, i + by) for i in range(peers) if 0 <= i + by <...]
  transfers between devices with their start and end apart: 17 -> 17, of which waited for: 9 -> 9; matrix products, arithmetic and copies ran while one was open for 1% -> 1% of each run, Pallas kernels for 20% -> 17%
where the time goes in v4:
time: 73.5 us; the launch traced here: 73.1 us
  starting transfers between devices  27.4 us (37%)
  Pallas kernels  21.2 us (29%)
  waiting for transfers between devices  20.9 us (28%)
  local copies, waits for them, and re-layouts  2.77 us (4%)
  between operations  0.87 us (1%)
    ppermute x10, starting transfers between devices, add_over(): got.append(lax.ppermute(x, axis, pairs))  16.9 us
    ppermute x10, waiting for transfers between devices, add_over(): got.append(lax.ppermute(x, axis, pairs))  13.1 us
    pallas_call x2, Pallas kernels, side_terms(): pair_call(side_kernel, name, half, 32, [SMEM, ANY, ANY, VMEM], buffers, [...  8.55 us
    ppermute x3, waiting for transfers between devices, shifted(): lax.ppermute(x, axis, [(i, i + by) for i in range(peers) if 0 <= i + by <...  7.73 us
    pallas_call x1, Pallas kernels, south_terms(): pair_call(south_kernel, 'south_pairs', tiles, 64, [ANY, ANY, VMEM, VMEM],...  6.59 us
    ppermute x3, starting transfers between devices, shifted(): lax.ppermute(x, axis, [(i, i + by) for i in range(peers) if 0 <= i + by <...  6.15 us
    ppermute x4, starting transfers between devices, swapped(): return lax.ppermute(x, axis, pairs + [(b, a) for a, b in pairs])  4.39 us
    pallas_call x4, Pallas kernels, call(): pl.pallas_call(kernel, name=name, in_specs=[SMEM] + [VMEM] * (len(args) -...  3.06 us
  transfers between devices with their start and end apart: 17, of which 9 were waited for; matrix products, arithmetic and copies ran while one was open for 1% of the time, Pallas kernels for 17%

profile of v4, /device:TPU:0, one launch (start us, length us, event | category | flops | bytes accessed | tf_op | source)
XLA Modules:
  0.0 73.1 jit_solution(11095554011210458477)
XLA Ops:
  0.7 0.7 copy-done.8
  1.4 0.7 copy-done.9
  2.0 0.7 copy-done.10
  2.8 1.5 %pack_across.1 = (bf16[11,64,640]{2,1,0:T(8,128)(2,1)S(1)}, bf16[1,64,384]{2,1,0:T(8,128)(2,1)S(1)}, f32[16,128]{1,0:T(8,128)S(1)}) custom-call(s32[1]{0:T(128)S(6)} %sub.3.role, bf16[40,4,64,512]{3,2,1,0:T(8,128)(2,1)} %bitcast.19, s32[2,40]{1,0:T(2,128)S(1)} %bitcast.16, s32[2,40]{1,0:T(2,128)S(1)} %bitcast.17, f32[1,40]{1,0:T(1,128)S(1)} %bitcast.18), custom_call_target="tpu_custom_call" | custom-call | tf_op jit(solution)/shard_map/pack_across/pallas_call | solution.py:397
  4.3 1.3 %collective-permute-start = (bf16[1,64,384]{2,1,0:T(8,128)(2,1)S(1)}, bf16[1,64,384]{2,1,0:T(8,128)(2,1)S(1)}, u32[]{:S(2)}, u32[]{:S(2)}) collective-permute-start(bf16[1,64,384]{2,1,0:T(8,128)(2,1)S(1)} %get-tuple-element.24), channel_id=1, source_target_pairs={{1,0},{2,1},{3,2},{5,4},{6,5},{7,6},{9,8},{10,9},{11,10},{13,12},{... | collective-permute-start | bytes 147464 | tf_op jit(solution)/shard_map/ppermute | solution.py:747
  5.6 1.4 %pack_within.1 = (bf16[11,64,640]{2,1,0:T(8,128)(2,1)S(1)}, f32[896,128]{1,0:T(8,128)S(1)}) custom-call(s32[1]{0:T(128)} %bitcast.role.refs_0_, bf16[40,4,64,512]{3,2,1,0:T(8,128)(2,1)} %bitcast.20, f32[16,128]{1,0:T(8,128)S(1)} %get-tuple-element.22.info.refs_8_, f32[40,1,896]{2,1,0:T(1,128)S(1)} %copy-done.6), custom_call_target="tpu_custom_call" | custom-call | tf_op jit(solution)/shard_map/pack_within/pallas_call | solution.py:418
  7.1 3.2 %collective-permute-done.nxt = bf16[1,64,384]{2,1,0:T(8,128)(2,1)S(1)} collective-permute-done((bf16[1,64,384]{2,1,0:T(8,128)(2,1)S(1)}, bf16[1,64,384]{2,1,0:T(8,128)(2,1)S(1)}, u32[]{:S(2)}, u32[]{:S(2)}) %collective-permute-start) | collective-permute-done | bytes 49184 | tf_op jit(solution)/shard_map/ppermute | solution.py:747
  10.3 0.7 collective-permute-start.3
  11.1 6.6 %south_pairs.1.terms_south.refs_1_ = f32[64,128]{1,0:T(8,128)S(1)} custom-call(bf16[40,4,64,512]{3,2,1,0:T(8,128)(2,1)} %bitcast.21, bf16[1,64,384]{2,1,0:T(8,128)(2,1)S(1)} %collective-permute-done.nxt, f32[16,128]{1,0:T(8,128)S(1)} %get-tuple-element.22.info.refs_8_, f32[896,128]{1,0:T(8,128)S(1)} %get-tuple-element.26.anchor_t.refs_9_, ...), custom_call_target="tpu_custom_call" | custom-call | flops 2400000000 | bytes 3932160 | tf_op jit(solution)/shard_map/south_pairs/pallas_call | solution.py:328
  17.7 3.6 %collective-permute-start.2 = (f32[64,128]{1,0:T(8,128)S(1)}, f32[64,128]{1,0:T(8,128)S(1)}, u32[]{:S(2)}, u32[]{:S(2)}) collective-permute-start(f32[64,128]{1,0:T(8,128)S(1)} %south_pairs.1.terms_south.refs_1_), channel_id=1, source_target_pairs={{0,1},{1,2},{2,3},{4,5},{5,6},{6,7},{8,9},{9,10},{10,11},{12,13},{... | collective-permute-start | bytes 98312 | tf_op jit(solution)/shard_map/ppermute | solution.py:747
  21.3 4.3 %within_pairs.1.terms.other_terms.refs_2_ = f32[32,128]{1,0:T(8,128)S(1)} custom-call(s32[1]{0:T(128)} %bitcast.role.refs_0_, bf16[40,4,64,512]{3,2,1,0:T(8,128)(2,1)} %bitcast.22, bf16[11,64,640]{2,1,0:T(8,128)(2,1)S(1)} %collective-permute-done.1.received, f32[16,128]{1,0:T(8,128)S(1)} %get-tuple-element.22.info.refs_8_, bf16[64,64]{1,0:T(8,128)(2,1)S(1)} %copy-done.4, ...), custom_call_target="tpu_custom_call" | custom-call | flops 1200000000 | bytes 1966080 | tf_op jit(solution)/shard_map/within_pairs/pallas_call | solution.py:340
  25.6 4.3 %across_pairs.1.terms.refs_3_ = f32[32,128]{1,0:T(8,128)S(1)} custom-call(s32[1]{0:T(128)S(6)} %sub.3.role, bf16[40,4,64,512]{3,2,1,0:T(8,128)(2,1)} %bitcast.23, bf16[11,64,640]{2,1,0:T(8,128)(2,1)S(1)} %collective-permute-done.3.received, f32[16,128]{1,0:T(8,128)S(1)} %get-tuple-element.22.info.refs_8_, bf16[64,64]{1,0:T(8,128)(2,1)S(1)} %copy-done.4, ...), custom_call_target="tpu_custom_call" | custom-call | flops 1200000000 | bytes 1966080 | tf_op jit(solution)/shard_map/across_pairs/pallas_call | solution.py:340
  29.9 3.0 %collective-permute-start.4 = (f32[72,128]{1,0:T(8,128)S(1)}, f32[72,128]{1,0:T(8,128)S(1)}, u32[]{:S(2)}, u32[]{:S(2)}) collective-permute-start(f32[72,128]{1,0:T(8,128)S(1)} %message.1), channel_id=1, source_target_pairs={{0,4},{8,12},{16,20},{24,28},{32,36},{40,44},{48,52},{56,60},{64,6... | collective-permute-start | bytes 110600 | tf_op jit(solution)/shard_map/ppermute | solution.py:753
  33.0 0.7 collective-permute-start.5
  33.7 1.3 %collective-permute-start.6 = (f32[64,128]{1,0:T(8,128)S(1)}, f32[64,128]{1,0:T(8,128)S(1)}, u32[]{:S(2)}, u32[]{:S(2)}) collective-permute-start(f32[64,128]{1,0:T(8,128)S(1)} %get-tuple-element.32), channel_id=1, source_target_pairs={{1,0},{2,1},{3,2},{5,4},{6,5},{7,6},{9,8},{10,9},{11,10},{13,12},{... | collective-permute-start | bytes 98312 | tf_op jit(solution)/shard_map/ppermute | solution.py:747
  35.0 4.5 %collective-permute-done.6.refs_6_ = f32[64,128]{1,0:T(8,128)S(1)} collective-permute-done((f32[64,128]{1,0:T(8,128)S(1)}, f32[64,128]{1,0:T(8,128)S(1)}, u32[]{:S(2)}, u32[]{:S(2)}) %collective-permute-start.6) | collective-permute-done | bytes 32800 | tf_op jit(solution)/shard_map/ppermute | solution.py:747
  39.5 1.5 %powers.1 = (f32[1024,128]{1,0:T(8,128)S(1)}, f32[1024,128]{1,0:T(8,128)S(1)}, f32[1024,128]{1,0:T(8,128)S(1)}, f32[1024,128]{1,0:T(8,128)S(1)}, f32[40,48]{1,0:T(8,128)S(1)}, /*index=5*/f32[8,128]{1,0:T(8,128)S(1)}) custom-call(s32[1]{0:T(128)} %bitcast.role.refs_0_, f32[64,128]{1,0:T(8,128)S(1)} %south_pairs.1.terms_south.refs_1_, ...), custom_call_target="tpu_custom_call" | custom-call | flops 4000000 | bytes 2000000 | tf_op jit(solution)/shard_map/powers/pallas_call | solution.py:440
  41.0 2.2 %collective-permute-start.7 = (f32[8,128]{1,0:T(8,128)S(1)}, f32[8,128]{1,0:T(8,128)S(1)}, u32[]{:S(2)}, u32[]{:S(2)}) collective-permute-start(f32[8,128]{1,0:T(8,128)S(1)} %get-tuple-element.34), channel_id=1, source_target_pairs={{0,4},{4,0},{8,12},{12,8},{16,20},{20,16},{24,28},{28,24},{32,36},... | collective-permute-start | bytes 12296 | tf_op jit(solution)/shard_map/ppermute | solution.py:764
  43.2 0.8 %collective-permute-done.7 = f32[8,128]{1,0:T(8,128)S(1)} collective-permute-done((f32[8,128]{1,0:T(8,128)S(1)}, f32[8,128]{1,0:T(8,128)S(1)}, u32[]{:S(2)}, u32[]{:S(2)}) %collective-permute-start.7) | collective-permute-done | bytes 4128 | tf_op jit(solution)/shard_map/ppermute | solution.py:764
  44.1 4.6 %collective-permute-start.10 = (f32[8,128]{1,0:T(8,128)S(1)}, f32[8,128]{1,0:T(8,128)S(1)}, u32[]{:S(2)}, u32[]{:S(2)}) collective-permute-start(f32[8,128]{1,0:T(8,128)S(1)} %add.35), channel_id=1, source_target_pairs={{0,24},{4,28},{8,0},{12,4},{16,8},{20,12},{24,16},{28,20},{32,56},... | collective-permute-start | bytes 12296 | tf_op jit(solution)/shard_map/ppermute | solution.py:764
  48.7 0.9 %collective-permute-start.8 = (f32[8,128]{1,0:T(8,128)S(1)}, f32[8,128]{1,0:T(8,128)S(1)}, u32[]{:S(2)}, u32[]{:S(2)}) collective-permute-start(f32[8,128]{1,0:T(8,128)S(1)} %add.35), channel_id=1, source_target_pairs={{0,8},{4,12},{8,16},{12,20},{16,24},{20,28},{24,0},{28,4},{32,40},... | collective-permute-start | bytes 12296 | tf_op jit(solution)/shard_map/ppermute | solution.py:764
  49.5 0.5 collective-permute-done.10
  50.0 3.8 %collective-permute-done.9 = f32[8,128]{1,0:T(8,128)S(1)} collective-permute-done((f32[8,128]{1,0:T(8,128)S(1)}, f32[8,128]{1,0:T(8,128)S(1)}, u32[]{:S(2)}, u32[]{:S(2)}) %collective-permute-start.9) | collective-permute-done | bytes 4128 | tf_op jit(solution)/shard_map/ppermute | solution.py:764
  53.8 4.2 %collective-permute-start.13 = (f32[8,128]{1,0:T(8,128)S(1)}, f32[8,128]{1,0:T(8,128)S(1)}, u32[]{:S(2)}, u32[]{:S(2)}) collective-permute-start(f32[8,128]{1,0:T(8,128)S(1)} %add_add_fusion.2), channel_id=1, source_target_pairs={{0,96},{4,100},{8,104},{12,108},{16,112},{20,116},{24,120},{28,124... | collective-permute-start | bytes 12296 | tf_op jit(solution)/shard_map/ppermute | solution.py:764
  58.0 0.5 collective-permute-start.12
  58.5 0.9 %collective-permute-start.11 = (f32[8,128]{1,0:T(8,128)S(1)}, f32[8,128]{1,0:T(8,128)S(1)}, u32[]{:S(2)}, u32[]{:S(2)}) collective-permute-start(f32[8,128]{1,0:T(8,128)S(1)} %add_add_fusion.2), channel_id=1, source_target_pairs={{0,32},{4,36},{8,40},{12,44},{16,48},{20,52},{24,56},{28,60},{32,6... | collective-permute-start | bytes 12296 | tf_op jit(solution)/shard_map/ppermute | solution.py:764
  59.4 3.7 %collective-permute-done.12 = f32[8,128]{1,0:T(8,128)S(1)} collective-permute-done((f32[8,128]{1,0:T(8,128)S(1)}, f32[8,128]{1,0:T(8,128)S(1)}, u32[]{:S(2)}, u32[]{:S(2)}) %collective-permute-start.12) | collective-permute-done | bytes 4128 | tf_op jit(solution)/shard_map/ppermute | solution.py:764
  63.3 3.6 %collective-permute-start.15 = (f32[8,128]{1,0:T(8,128)S(1)}, f32[8,128]{1,0:T(8,128)S(1)}, u32[]{:S(2)}, u32[]{:S(2)}) collective-permute-start(f32[8,128]{1,0:T(8,128)S(1)} %add_add_fusion.1), channel_id=1, source_target_pairs={{0,2},{1,3},{2,0},{3,1},{4,6},{5,7},{6,4},{7,5},{8,10},{9,11},{10,... | collective-permute-start | bytes 12296 | tf_op jit(solution)/shard_map/ppermute | solution.py:764
  66.9 0.7 copy.18
  67.6 0.9 %collective-permute-done.15 = f32[8,128]{1,0:T(8,128)S(1)} collective-permute-done((f32[8,128]{1,0:T(8,128)S(1)}, f32[8,128]{1,0:T(8,128)S(1)}, u32[]{:S(2)}, u32[]{:S(2)}) %collective-permute-start.15) | collective-permute-done | bytes 4128 | tf_op jit(solution)/shard_map/ppermute | solution.py:764
  68.5 3.2 %collective-permute-done.14 = f32[8,128]{1,0:T(8,128)S(1)} collective-permute-done((f32[8,128]{1,0:T(8,128)S(1)}, f32[8,128]{1,0:T(8,128)S(1)}, u32[]{:S(2)}, u32[]{:S(2)}) %collective-permute-start.14) | collective-permute-done | bytes 4128 | tf_op jit(solution)/shard_map/ppermute | solution.py:764
  71.8 1.4 %combine.1 = (f32[40,2,896]{2,1,0:T(2,128)}, f32[40,2,896]{2,1,0:T(2,128)}) custom-call(f32[8,128]{1,0:T(8,128)S(1)} %add_add_fusion.gram, f32[1024,128]{1,0:T(8,128)S(1)} %get-tuple-element.35.v0, f32[1024,128]{1,0:T(8,128)S(1)} %get-tuple-element.36.v1, f32[1024,128]{1,0:T(8,128)S(1)} %get-tuple-element.37.v2, f32[1024,128]{1,0:T(8,128)S(1)} %get-tuple-element.38.v3), custom_call_target="tpu_custom_call" | custom-call | flops 4000000 | bytes 2000000 | tf_op jit(solution)/shard_map/combine/pallas_call | solution.py:440
  (38 shorter events, 0.5 us)
Async XLA Ops:
  0.6 5.0 %copy-start.6 = (f32[40,1,896]{2,1,0:T(1,128)S(1)}, f32[40,1,896]{2,1,0:T(1,128)}, u32[]{:S(2)}) copy-start(f32[40,1,896]{2,1,0:T(1,128)} %anchor.1) | copy-start | bytes 430084
  0.7 0.7 copy-start.8
  1.4 0.7 copy-start.9
  2.0 0.7 copy-start.10
  2.7 8.3 %copy-start = (bf16[256,512]{1,0:T(8,128)(2,1)S(1)}, bf16[256,512]{1,0:T(8,128)(2,1)}, u32[]{:S(2)}) copy-start(bf16[256,512]{1,0:T(8,128)(2,1)} %constant.37.clone.ends) | copy-start | bytes 786436
  2.7 8.3 %copy-start.1 = (bf16[2,256,256]{2,1,0:T(8,128)(2,1)S(1)}, bf16[2,256,256]{2,1,0:T(8,128)(2,1)}, u32[]{:S(2)}) copy-start(bf16[2,256,256]{2,1,0:T(8,128)(2,1)} %constant.38.clone.backs) | copy-start | bytes 786436
  2.7 8.3 %copy-start.2 = (bf16[256,256]{1,0:T(8,128)(2,1)S(1)}, bf16[256,256]{1,0:T(8,128)(2,1)}, u32[]{:S(2)}) copy-start(bf16[256,256]{1,0:T(8,128)(2,1)} %constant.36.clone.forward) | copy-start | bytes 393220
  2.7 8.3 %copy-start.3 = (f32[64,128]{1,0:T(8,128)S(1)}, f32[64,128]{1,0:T(8,128)}, u32[]{:S(2)}) copy-start(f32[64,128]{1,0:T(8,128)} %constant.41.clone.rows) | copy-start | bytes 98308
  2.7 8.3 %copy-start.4 = (bf16[64,64]{1,0:T(8,128)(2,1)S(1)}, bf16[64,64]{1,0:T(8,128)(2,1)}, u32[]{:S(2)}) copy-start(bf16[64,64]{1,0:T(8,128)(2,1)} %constant.35.clone.depth) | copy-start | bytes 24580
  2.7 8.3 %copy-start.5 = (bf16[64,64]{1,0:T(8,128)(2,1)S(1)}, bf16[64,64]{1,0:T(8,128)(2,1)}, u32[]{:S(2)}) copy-start(bf16[64,64]{1,0:T(8,128)(2,1)} %constant.39.clone.final) | copy-start | bytes 24580
  2.7 8.3 %copy-start.7 = (f32[8,128]{1,0:T(8,128)S(1)}, f32[8,128]{1,0:T(8,128)}, u32[]{:S(2)}) copy-start(f32[8,128]{1,0:T(8,128)} %constant.40.clone.pick) | copy-start | bytes 12292
  4.3 6.0 %collective-permute-start = (bf16[1,64,384]{2,1,0:T(8,128)(2,1)S(1)}, bf16[1,64,384]{2,1,0:T(8,128)(2,1)S(1)}, u32[]{:S(2)}, u32[]{:S(2)}) collective-permute-start(bf16[1,64,384]{2,1,0:T(8,128)(2,1)S(1)} %get-tuple-element.24), channel_id=1, source_target_pairs={{1,0},{2,1},{3,2},{5,4},{6,5},{7,6},{9,8},{10,9},{11,10},{13,12},{... | collective-permute-start | bytes 147464 | tf_op jit(solution)/shard_map/ppermute | solution.py:747
  10.3 11.0 %collective-permute-start.1 = (bf16[11,64,640]{2,1,0:T(8,128)(2,1)S(1)}, bf16[11,64,640]{2,1,0:T(8,128)(2,1)S(1)}, u32[]{:S(2)}, u32[]{:S(2)}) collective-permute-start(bf16[11,64,640]{2,1,0:T(8,128)(2,1)S(1)} %get-tuple-element.27), channel_id=1, source_target_pairs={{0,4},{8,12},{16,20},{24,28},{32,36},{40,44},{48,52},{56,60},{64,6... | collective-permute-start | bytes 2703368 | tf_op jit(solution)/shard_map/ppermute | solution.py:753
  10.3 15.3 %collective-permute-start.3 = (bf16[11,64,640]{2,1,0:T(8,128)(2,1)S(1)}, bf16[11,64,640]{2,1,0:T(8,128)(2,1)S(1)}, u32[]{:S(2)}, u32[]{:S(2)}) collective-permute-start(bf16[11,64,640]{2,1,0:T(8,128)(2,1)S(1)} %get-tuple-element.28), channel_id=1, source_target_pairs={{4,8},{12,16},{20,24},{28,32},{36,40},{44,48},{52,56},{60,64},{68,... | collective-permute-start | bytes 2703368 | tf_op jit(solution)/shard_map/ppermute | solution.py:753
  17.7 7.9 %collective-permute-start.2 = (f32[64,128]{1,0:T(8,128)S(1)}, f32[64,128]{1,0:T(8,128)S(1)}, u32[]{:S(2)}, u32[]{:S(2)}) collective-permute-start(f32[64,128]{1,0:T(8,128)S(1)} %south_pairs.1.terms_south.refs_1_), channel_id=1, source_target_pairs={{0,1},{1,2},{2,3},{4,5},{5,6},{6,7},{8,9},{9,10},{10,11},{12,13},{... | collective-permute-start | bytes 98312 | tf_op jit(solution)/shard_map/ppermute | solution.py:747
  29.9 9.6 %collective-permute-start.4 = (f32[72,128]{1,0:T(8,128)S(1)}, f32[72,128]{1,0:T(8,128)S(1)}, u32[]{:S(2)}, u32[]{:S(2)}) collective-permute-start(f32[72,128]{1,0:T(8,128)S(1)} %message.1), channel_id=1, source_target_pairs={{0,4},{8,12},{16,20},{24,28},{32,36},{40,44},{48,52},{56,60},{64,6... | collective-permute-start | bytes 110600 | tf_op jit(solution)/shard_map/ppermute | solution.py:753
  33.0 6.5 %collective-permute-start.5 = (f32[72,128]{1,0:T(8,128)S(1)}, f32[72,128]{1,0:T(8,128)S(1)}, u32[]{:S(2)}, u32[]{:S(2)}) collective-permute-start(f32[72,128]{1,0:T(8,128)S(1)} %get-tuple-element.31), channel_id=1, source_target_pairs={{4,8},{12,16},{20,24},{28,32},{36,40},{44,48},{52,56},{60,64},{68,... | collective-permute-start | bytes 110600 | tf_op jit(solution)/shard_map/ppermute | solution.py:753
  33.7 5.8 %collective-permute-start.6 = (f32[64,128]{1,0:T(8,128)S(1)}, f32[64,128]{1,0:T(8,128)S(1)}, u32[]{:S(2)}, u32[]{:S(2)}) collective-permute-start(f32[64,128]{1,0:T(8,128)S(1)} %get-tuple-element.32), channel_id=1, source_target_pairs={{1,0},{2,1},{3,2},{5,4},{6,5},{7,6},{9,8},{10,9},{11,10},{13,12},{... | collective-permute-start | bytes 98312 | tf_op jit(solution)/shard_map/ppermute | solution.py:747
  41.0 3.0 %collective-permute-start.7 = (f32[8,128]{1,0:T(8,128)S(1)}, f32[8,128]{1,0:T(8,128)S(1)}, u32[]{:S(2)}, u32[]{:S(2)}) collective-permute-start(f32[8,128]{1,0:T(8,128)S(1)} %get-tuple-element.34), channel_id=1, source_target_pairs={{0,4},{4,0},{8,12},{12,8},{16,20},{20,16},{24,28},{28,24},{32,36},... | collective-permute-start | bytes 12296 | tf_op jit(solution)/shard_map/ppermute | solution.py:764
  44.1 6.0 %collective-permute-start.10 = (f32[8,128]{1,0:T(8,128)S(1)}, f32[8,128]{1,0:T(8,128)S(1)}, u32[]{:S(2)}, u32[]{:S(2)}) collective-permute-start(f32[8,128]{1,0:T(8,128)S(1)} %add.35), channel_id=1, source_target_pairs={{0,24},{4,28},{8,0},{12,4},{16,8},{20,12},{24,16},{28,20},{32,56},... | collective-permute-start | bytes 12296 | tf_op jit(solution)/shard_map/ppermute | solution.py:764
  48.7 5.1 %collective-permute-start.9 = (f32[8,128]{1,0:T(8,128)S(1)}, f32[8,128]{1,0:T(8,128)S(1)}, u32[]{:S(2)}, u32[]{:S(2)}) collective-permute-start(f32[8,128]{1,0:T(8,128)S(1)} %add.35), channel_id=1, source_target_pairs={{0,16},{4,20},{8,24},{12,28},{16,0},{20,4},{24,8},{28,12},{32,48},... | collective-permute-start | bytes 12296 | tf_op jit(solution)/shard_map/ppermute | solution.py:764
  48.7 5.1 %collective-permute-start.8 = (f32[8,128]{1,0:T(8,128)S(1)}, f32[8,128]{1,0:T(8,128)S(1)}, u32[]{:S(2)}, u32[]{:S(2)}) collective-permute-start(f32[8,128]{1,0:T(8,128)S(1)} %add.35), channel_id=1, source_target_pairs={{0,8},{4,12},{8,16},{12,20},{16,24},{20,28},{24,0},{28,4},{32,40},... | collective-permute-start | bytes 12296 | tf_op jit(solution)/shard_map/ppermute | solution.py:764
  53.8 5.6 %collective-permute-start.13 = (f32[8,128]{1,0:T(8,128)S(1)}, f32[8,128]{1,0:T(8,128)S(1)}, u32[]{:S(2)}, u32[]{:S(2)}) collective-permute-start(f32[8,128]{1,0:T(8,128)S(1)} %add_add_fusion.2), channel_id=1, source_target_pairs={{0,96},{4,100},{8,104},{12,108},{16,112},{20,116},{24,120},{28,124... | collective-permute-start | bytes 12296 | tf_op jit(solution)/shard_map/ppermute | solution.py:764
  58.0 5.1 %collective-permute-start.12 = (f32[8,128]{1,0:T(8,128)S(1)}, f32[8,128]{1,0:T(8,128)S(1)}, u32[]{:S(2)}, u32[]{:S(2)}) collective-permute-start(f32[8,128]{1,0:T(8,128)S(1)} %add_add_fusion.2), channel_id=1, source_target_pairs={{0,64},{4,68},{8,72},{12,76},{16,80},{20,84},{24,88},{28,92},{32,9... | collective-permute-start | bytes 12296 | tf_op jit(solution)/shard_map/ppermute | solution.py:764
  58.5 4.8 %collective-permute-start.11 = (f32[8,128]{1,0:T(8,128)S(1)}, f32[8,128]{1,0:T(8,128)S(1)}, u32[]{:S(2)}, u32[]{:S(2)}) collective-permute-start(f32[8,128]{1,0:T(8,128)S(1)} %add_add_fusion.2), channel_id=1, source_target_pairs={{0,32},{4,36},{8,40},{12,44},{16,48},{20,52},{24,56},{28,60},{32,6... | collective-permute-start | bytes 12296 | tf_op jit(solution)/shard_map/ppermute | solution.py:764
  63.3 4.3 %collective-permute-start.16 = (f32[8,128]{1,0:T(8,128)S(1)}, f32[8,128]{1,0:T(8,128)S(1)}, u32[]{:S(2)}, u32[]{:S(2)}) collective-permute-start(f32[8,128]{1,0:T(8,128)S(1)} %add_add_fusion.1), channel_id=1, source_target_pairs={{0,3},{1,0},{2,1},{3,2},{4,7},{5,4},{6,5},{7,6},{8,11},{9,8},{10,9... | collective-permute-start | bytes 12296 | tf_op jit(solution)/shard_map/ppermute | solution.py:764
  63.3 5.2 %collective-permute-start.15 = (f32[8,128]{1,0:T(8,128)S(1)}, f32[8,128]{1,0:T(8,128)S(1)}, u32[]{:S(2)}, u32[]{:S(2)}) collective-permute-start(f32[8,128]{1,0:T(8,128)S(1)} %add_add_fusion.1), channel_id=1, source_target_pairs={{0,2},{1,3},{2,0},{3,1},{4,6},{5,7},{6,4},{7,5},{8,10},{9,11},{10,... | collective-permute-start | bytes 12296 | tf_op jit(solution)/shard_map/ppermute | solution.py:764
  66.9 4.8 %collective-permute-start.14 = (f32[8,128]{1,0:T(8,128)S(1)}, f32[8,128]{1,0:T(8,128)S(1)}, u32[]{:S(2)}, u32[]{:S(2)}) collective-permute-start(f32[8,128]{1,0:T(8,128)S(1)} %add_add_fusion.1), channel_id=1, source_target_pairs={{0,1},{1,2},{2,3},{3,0},{4,5},{5,6},{6,7},{7,4},{8,9},{9,10},{10,1... | collective-permute-start | bytes 12296 | tf_op jit(solution)/shard_map/ppermute | solution.py:764

commit v5 on v4

--- a/solution.py
+++ b/solution.py
@@ -204,7 +204,7 @@
 
     last_copies = (
         second_copy(steps - 1, GROUP - 1),
-        pltpu.make_async_copy(nxt.at[0], second.at[tiles - 1], last_sem),
+        pltpu.make_async_copy(nxt.at[0, :, side], second.at[tiles - 1], last_sem),
     )
     for c in range(steps):
         first_copy(c).start()
@@ -243,7 +243,7 @@
     out[32:, :] = anchor_t[NODES - MESH_X : NODES, :]
 
 
-def side_kernel(role, strips, received, info, depth, forward, ends, backs, final, pick, rows, out, own, other, own_extra, r0, r1, sems, extra_sems):
+def side_kernel(role, strips, received, next_top, info, depth, forward, ends, backs, final, pick, rows, out, own, other, r0, r1, sems, extra_sem):
     half = own.shape[0]
     steps = half // GROUP
     slots = GROUP // 2
@@ -259,20 +259,15 @@
         at = pl.ds(slots * c, slots)
         return pltpu.make_async_copy(received.at[at], other.at[at], sems.at[1, c])
 
-    extra_copies = (
-        pltpu.make_async_copy(strips.at[0, 0, :, pl.ds(0, LANES)], own_extra, extra_sems.at[0]),
-        pltpu.make_async_copy(received.at[spare], other.at[spare], extra_sems.at[1]),
-    )
+    extra_copy = pltpu.make_async_copy(received.at[spare], other.at[spare], extra_sem)
     for c in range(steps):
         own_copy(c).start()
         other_copy(c).start()
         if c == 0:
-            for copy in extra_copies:
-                copy.start()
+            extra_copy.start()
     r0[...] = jnp.zeros_like(r0)
     r1[...] = jnp.zeros_like(r1)
-    for copy in extra_copies:
-        copy.wait()
+    extra_copy.wait()
 
     def step(c, carry):
         own_copy(c).wait()
@@ -282,7 +277,7 @@
             other[slots * c + slot, :, LANES * i : LANES * (i + 1)] for slot in range(slots) for i in range(5)
         ]
         correlate_group(
-            owns + [own_extra[...]] + others + [other[spare, :, :LANES]],
+            owns + [next_top[0, :, SIDE : SIDE + LANES]] + others + [other[spare, :, :LANES]],
             depth[...], forward[...], ends[...], backs[west], final[...], rows[...], r0, r1, base + GROUP * c,
         )
         return carry
@@ -291,9 +286,8 @@
     lane = lax.broadcasted_iota(jnp.int32, (8, LANES), 1)
     info_west = other[spare, 0:16, 2 * LANES : 3 * LANES].astype(F32)[0:8]
     table = jnp.where(west == 1, info_west, info[0:8, :])
-    mine = (lane >= base) & (lane < base + half)
+    mine = (lane >= base) & (lane < base + half) | (lane == EXTRA) & (west == 1)
     table = jnp.where(mine, table, 0.0)
-    table = jnp.where((lane == EXTRA) & (west == 1), pltpu.roll(info_west, EXTRA, axis=1), table)
     finish_terms(pick[...], r0, r1, table[0:1], table[1:2], out)
 
 
@@ -330,107 +324,158 @@
     )(strips, nxt, info, anchor_t, *tabs)
 
 
-def side_terms(name, role, strips, received, info, tabs):
+def side_terms(name, role, strips, received, next_top, info, tabs):
     half = strips.shape[0] // 2
     buffers = [
         pltpu.VMEM((half, PATCH, SIDE), BF16),
         pltpu.VMEM((half // 2 + 1, PATCH, 2 * WIDE), BF16),
-        pltpu.VMEM((PATCH, LANES), BF16),
     ]
     return pair_call(
-        side_kernel, name, half, 32, [SMEM, ANY, ANY, VMEM], buffers, [pltpu.SemaphoreType.DMA((2,))]
-    )(role, strips, received, info, *tabs)
-
-
-def pack(role, strips, info, packed, buffer, sems):
-    half = buffer.shape[0]
-    east = 1 - role[0]
-    moves = [
-        pltpu.make_async_copy(
-            strips.at[pl.ds(east * half, half), 3 * east, :, pl.ds(0, SIDE)], buffer, sems.at[0]
-        ),
-        pltpu.make_async_copy(
-            strips.at[0, 3, :, pl.ds(0, LANES)], packed.at[half // 2, :, pl.ds(0, LANES)], sems.at[1]
-        ),
+        side_kernel, name, half, 32, [SMEM, ANY, ANY, VMEM, VMEM], buffers, [pltpu.SemaphoreType.DMA]
+    )(role, strips, received, next_top, info, *tabs)
+
+
+STATICS = COMP
+
+
+def pieces(x):
+    high = x.astype(BF16).astype(F32)
+    middle = (x - high).astype(BF16).astype(F32)
+    return high, middle, x - high - middle
+
+
+def edge_kernel(strips, counts, offsets, stiffness, anchor, north, info, left, count_s, offset_s, stiff_s, anchor_s, turn, sems):
+    tiles = counts.shape[1]
+    lanes = pl.ds(0, LANES)
+    copies = [
+        (strips.at[0, 1, :, pl.ds(0, SIDE)], north.at[0, :, pl.ds(0, SIDE)]),
+        (strips.at[0, 3, :, lanes], north.at[0, :, pl.ds(4 * LANES, LANES)]),
+        (strips.at[0, 0, :, lanes], left),
+        (counts, count_s),
+        (offsets, offset_s),
+        (stiffness, stiff_s),
+        (anchor.at[0], anchor_s),
     ]
-    for move in moves:
-        move.start()
-    packed[half // 2, :, LANES:] = jnp.zeros((PATCH, 2 * WIDE - LANES), BF16)
-    packed[half // 2, 0:16, 2 * LANES : 3 * LANES] = info.astype(BF16)
-    yield
-    moves[0].wait()
-    for slot in range(half // 2):
-        columns = block_pairs([buffer[2 * slot + j, :, :WIDE] for j in range(2)])
-        for i, x in enumerate(columns):
-            packed[slot, :, LANES * i : LANES * (i + 1)] = x
-    moves[1].wait()
-
-
-def pack_across_kernel(role, strips, counts, offsets, stiffness, packed, north, info, buffer, sems, edge_sem):
-    tiles = counts.shape[1]
-    edge = pltpu.make_async_copy(strips.at[0, 1, :, pl.ds(0, SIDE)], north.at[0], edge_sem)
-    edge.start()
+    copies = [pltpu.make_async_copy(a, b, sems.at[k]) for k, (a, b) in enumerate(copies)]
+    for copy in copies:
+        copy.start()
+    turn[...] = jnp.zeros_like(turn)
+    info[...] = jnp.zeros_like(info)
+    for copy in copies:
+        copy.wait()
     here = pl.ds(0, tiles)
-    info[...] = jnp.zeros_like(info)
-    info[0:1, here] = counts[0:1, :].astype(F32)
-    info[1:2, here] = offsets[0:1, :].astype(F32)
-    info[2:3, here] = counts[1:2, :].astype(F32)
-    info[3:4, here] = offsets[1:2, :].astype(F32)
-    info[4:5, here] = stiffness[...]
-    for _ in pack(role, strips, info[...], packed, buffer, sems):
-        pass
-    edge.wait()
-
-
-def pack_within_kernel(role, strips, info, anchor, packed, anchor_t, buffer, sems, wide):
+    info[0:1, here] = count_s[0:1, :].astype(F32)
+    info[1:2, here] = offset_s[0:1, :].astype(F32)
+    info[2:3, here] = count_s[1:2, :].astype(F32)
+    info[3:4, here] = offset_s[1:2, :].astype(F32)
+    info[4:5, here] = stiff_s[...]
+    turn[0:1, :] = anchor_s[0:1, lanes]
+    columns = list(pieces(turn[...].T[0:PATCH, 0:1])) + list(pieces(info[4:5, 0:1]))
+    columns += [info[0:1, 0:1], info[1:2, 0:1]]
+    lane = lax.broadcasted_iota(jnp.int32, (PATCH, LANES), 1)
+    block = jnp.where(lane < COMP, left[...].astype(F32), 0.0)
+    for k, x in enumerate(columns):
+        block = jnp.where(lane == STATICS + k, x, block)
+    north[0, :, SIDE : SIDE + LANES] = block.astype(BF16)
+
+
+def pack_kernel(role, strips, anchor, across, within, anchor_t, buffers, wide, sems):
     tiles = anchor.shape[0]
-    for _ in pack(role, strips, info[...], packed, buffer, sems):
-        wide[...] = jnp.zeros_like(wide)
-        for first in (0, COMP):
-            wide[first : first + tiles, :] = anchor[:, 0, :]
-        for i in range(NODES // LANES):
-            anchor_t[LANES * i : LANES * (i + 1), :] = wide[:, LANES * i : LANES * (i + 1)].T
-
-
-def pack_across(role, strips, counts, offsets, stiffness):
+    half = tiles // 2
+    moves = []
+    for k, east in enumerate((role[0], 1 - role[0])):
+        source = strips.at[pl.ds(east * half, half), 3 * east, :, pl.ds(0, SIDE)]
+        moves.append(pltpu.make_async_copy(source, buffers.at[k], sems.at[k]))
+        moves[k].start()
+    wide[...] = jnp.zeros_like(wide)
+    for first in (0, COMP):
+        wide[first : first + tiles, :] = anchor[:, 0, :]
+    for i in range(NODES // LANES):
+        anchor_t[LANES * i : LANES * (i + 1), :] = wide[:, LANES * i : LANES * (i + 1)].T
+    for k, packed in enumerate((across, within)):
+        moves[k].wait()
+        for slot in range(half // 2):
+            columns = block_pairs([buffers[k, 2 * slot + j, :, :WIDE] for j in range(2)])
+            for i, x in enumerate(columns):
+                packed[slot, :, LANES * i : LANES * (i + 1)] = x
+        packed[half // 2] = jnp.zeros((PATCH, 2 * WIDE), BF16)
+
+
+def fill_kernel(next_top, info, across_in, within_in, across, within, slot, sems):
+    spare = across.shape[0] - 1
+    lane = lax.broadcasted_iota(jnp.int32, (16, LANES), 1)
+    row = lax.broadcasted_iota(jnp.int32, (16, LANES), 0)
+    statics = next_top[0, 0:16, SIDE : SIDE + LANES].astype(F32)
+    count = pltpu.roll(statics, (EXTRA - STATICS - 6) % LANES, axis=1)
+    offset = pltpu.roll(statics, (EXTRA - STATICS - 7) % LANES, axis=1)
+    facts = jnp.where(lane == EXTRA, jnp.where(row == 0, count, offset), info[...])
+    slot[...] = jnp.zeros_like(slot)
+    slot[:, 0:LANES] = next_top[0, :, 4 * LANES :]
+    slot[0:16, 2 * LANES : 3 * LANES] = facts.astype(BF16)
+    copies = [
+        pltpu.make_async_copy(slot, packed.at[spare, :, pl.ds(0, SIDE)], sems.at[k])
+        for k, packed in enumerate((across, within))
+    ]
+    for copy in copies:
+        copy.start()
+    for copy in copies:
+        copy.wait()
+
+
+def edge(strips, counts, offsets, stiffness, anchor):
     tiles = strips.shape[0]
+    dma = pltpu.SemaphoreType.DMA
     return pl.pallas_call(
-        pack_across_kernel,
-        name="pack_across",
-        in_specs=[SMEM, ANY] + [VMEM] * 3,
-        out_specs=[VMEM] * 3,
+        edge_kernel,
+        name="edge",
+        in_specs=[ANY] * 5,
+        out_specs=[VMEM] * 2,
         out_shape=[
-            jax.ShapeDtypeStruct((tiles // 4 + 1, PATCH, 2 * WIDE), BF16),
-            jax.ShapeDtypeStruct((1, PATCH, SIDE), BF16),
+            jax.ShapeDtypeStruct((1, PATCH, 2 * WIDE), BF16),
             jax.ShapeDtypeStruct((16, LANES), F32),
         ],
         scratch_shapes=[
-            pltpu.VMEM((tiles // 2, PATCH, SIDE), BF16),
+            pltpu.VMEM((PATCH, LANES), BF16),
+            pltpu.VMEM((2, tiles), jnp.int32),
+            pltpu.VMEM((2, tiles), jnp.int32),
+            pltpu.VMEM((1, tiles), F32),
+            pltpu.VMEM((1, NODES), F32),
+            pltpu.VMEM((LANES, LANES), F32),
+            dma((7,)),
+        ],
+    )(strips, counts, offsets, stiffness, anchor)
+
+
+def pack(role, strips, anchor):
+    tiles = strips.shape[0]
+    packed = jax.ShapeDtypeStruct((tiles // 4 + 1, PATCH, 2 * WIDE), BF16)
+    return pl.pallas_call(
+        pack_kernel,
+        name="pack",
+        in_specs=[SMEM, ANY, VMEM],
+        out_specs=[VMEM] * 3,
+        out_shape=[packed, packed, jax.ShapeDtypeStruct((NODES, LANES), F32)],
+        scratch_shapes=[
+            pltpu.VMEM((2, tiles // 2, PATCH, SIDE), BF16),
+            pltpu.VMEM((LANES, NODES), F32),
             pltpu.SemaphoreType.DMA((2,)),
-            pltpu.SemaphoreType.DMA,
         ],
         compiler_params=pltpu.CompilerParams(vmem_limit_bytes=VMEM_BYTES),
-    )(role, strips, counts, offsets, stiffness)
-
-
-def pack_within(role, strips, info, anchor):
-    tiles = strips.shape[0]
+        cost_estimate=pl.CostEstimate(flops=0, bytes_accessed=6_000_000, transcendentals=0),
+    )(role, strips, anchor)
+
+
+def fill(next_top, info, across, within):
+    packed = jax.ShapeDtypeStruct(across.shape, BF16)
     return pl.pallas_call(
-        pack_within_kernel,
-        name="pack_within",
-        in_specs=[SMEM, ANY, VMEM, VMEM],
-        out_specs=[VMEM] * 2,
-        out_shape=[
-            jax.ShapeDtypeStruct((tiles // 4 + 1, PATCH, 2 * WIDE), BF16),
-            jax.ShapeDtypeStruct((NODES, LANES), F32),
-        ],
-        scratch_shapes=[
-            pltpu.VMEM((tiles // 2, PATCH, SIDE), BF16),
-            pltpu.SemaphoreType.DMA((2,)),
-            pltpu.VMEM((LANES, NODES), F32),
-        ],
-        compiler_params=pltpu.CompilerParams(vmem_limit_bytes=VMEM_BYTES),
-    )(role, strips, info, anchor)
+        fill_kernel,
+        name="fill",
+        in_specs=[VMEM, VMEM, ANY, ANY],
+        out_specs=[ANY, ANY],
+        out_shape=[packed, packed],
+        input_output_aliases={2: 0, 3: 1},
+        scratch_shapes=[pltpu.VMEM((PATCH, SIDE), BF16), pltpu.SemaphoreType.DMA((2,))],
+    )(next_top, info, across, within)
 
 
 def whole(kernel, outs, name, scratch=(), with_role=True):
@@ -529,35 +574,18 @@
     return jnp.sum(a[0:NODES, :] * b[0:NODES, :], axis=0, keepdims=True)
 
 
-def write_message(role, terms, terms_south, from_north, info, anchor_t, tiles, out):
+def message_kernel(tiles, role, terms, terms_south, from_north, info, anchor_t, out):
     lane = lax.broadcasted_iota(jnp.int32, (1, LANES), 1)
     out[0:32, :] = terms[...]
     out[25:26, :] = info[4:5, :]
-    south = terms_south[0:32, :]
-    north = roll_tiles(south, 1, from_north[0:32, :], tiles)
-    for q, table in enumerate((south, north)):
-        for k, row in enumerate((0, 8, 16, 24)):
-            out[32 + 4 * q + k : 33 + 4 * q + k, :] = table[row : row + 1]
-    first, second, edge = [
-        anchor_t[pl.ds(j, MESH_Y, stride=MESH_X), :] for j in (0, 1, MESH_X - 1)
-    ]
+    north = roll_tiles(terms_south[0:32, :], 1, from_north[0:32, :], tiles)
+    out[32:40, :] = jnp.zeros((8, LANES), F32)
+    for k, row in enumerate((0, 8, 16, 24)):
+        out[32 + k : 33 + k, :] = north[row : row + 1]
+    first, second, last = [anchor_t[pl.ds(j, MESH_Y, stride=MESH_X), :] for j in (0, 1, MESH_X - 1)]
     to_west = jnp.where(lane < COMP, first, second)
-    out[40 : 40 + MESH_Y, :] = jnp.where(role[0] == 1, to_west, edge)
+    out[40 : 40 + MESH_Y, :] = jnp.where(role[0] == 1, to_west, last)
     out[40 + MESH_Y :, :] = jnp.zeros((MESH_X - MESH_Y, LANES), F32)
-
-
-def message_kernel(tiles, role, terms, terms_south, from_north, info, anchor_t, out):
-    write_message(role, terms, terms_south, from_north, info, anchor_t, tiles, out)
-
-
-def last_message_kernel(tiles, role, terms, other_terms, terms_south, from_north, info, anchor_t, out, to_north):
-    lane = lax.broadcasted_iota(jnp.int32, (1, LANES), 1)
-    write_message(role, terms, terms_south, from_north, info, anchor_t, tiles, out)
-    to_north[0:32, :] = terms[...] + other_terms[...]
-    to_north[25:26, :] = info[4:5, :]
-    to_north[32:, :] = jnp.where(
-        lane == 0, anchor_t[0:MESH_X, :], pltpu.roll(anchor_t[MESH_X : 2 * MESH_X, :], 1, axis=1)
-    )
 
 
 def roll_tiles(x, by, outside, tiles):
@@ -589,7 +617,7 @@
 
 
 def mesh_kernel(tiles, *refs):
-    role, terms_south, terms_within, terms_across, within, across, from_south, from_north, info, anchor_t = refs[:10]
+    role, terms_south, terms_within, terms_across, within, across, next_top, from_north, info, anchor_t = refs[:10]
     v0, v1, v2, v3, match, gram, flip = refs[10:]
     within_is_east = role[0] == 0
     from_east = jnp.where(within_is_east, within[...], across[...])
@@ -631,29 +659,23 @@
     anchor_e1 = jnp.where(lane < COMP, turned, packed)
     anchor_w0 = from_west[40:72, :]
     last = tiles - 1
-    outside_south = pick_lane(from_south[25:26, :], 0, last)
-    anchor_s0 = pick_lane(from_south[32:64, :], 0, last)
-    anchor_s1 = pick_lane(from_south[32:64, :], 1, last)
+    statics = next_top[0, :, SIDE : SIDE + LANES].astype(F32)
+    outside_south = sum(pick_lane(statics[0:1], STATICS + k, last) for k in (3, 4, 5))
+    anchor_south = sum(pick_lane(statics, STATICS + k, last) for k in (0, 1, 2))
+    anchor_s0, anchor_s1 = anchor_south[:MESH_X], anchor_south[MESH_X:]
     outside_north = pick_lane(from_north[25:26, :], last, 0)
     anchor_n0 = pick_lane(from_north[32:64, :], last, 0)
 
     degree_c = jnp.where((node == 0) | (node == MESH_Y - 1), 2.0, 3.0)
     degree_r = jnp.where((node == 0) | (node == MESH_X - 1), 2.0, 3.0)
 
-    near_s = near_pair(*[both(from_east[32 + k : 33 + k, :]) for k in (0, 2, 1, 3)])
-    near_n = near_pair(*[both(from_east[36 + k : 37 + k, :]) for k in (0, 2, 1, 3)])
-    at_ends = lambda a, b, x, y: jnp.where(node == a, x, 0.0) - jnp.where(node == b, y, 0.0)
+    near_n = near_pair(*[both(from_east[32 + k : 33 + k, :]) for k in (0, 2, 1, 3)])
     e0 = -force_e
-    e1 = at_ends(MESH_Y - 1, 0, near_s[0], near_n[0])
-    e2 = at_ends(MESH_Y - 1, 0, near_s[1], near_n[1])
-    e1_pairs = at_ends(MESH_Y - 1, 0, near_s[2], near_n[2])
+    e1, e2, e1_pairs = [-jnp.where(node == 0, x, 0.0) for x in near_n]
     w0 = force_w
-    near_e = near_pair(*[pick_lane(from_south[k : k + 1, :], 0, last) for k in (0, 8, 16, 24)])
-    near_w = near_pair(*[pick_lane(from_south[k : k + 1, :], EXTRA, last) for k in (0, 8, 16, 24)])
+    near_w = near_pair(*[pick_lane(side[k : k + 1, :], EXTRA, last) for k in (0, 8, 16, 24)])
     s0 = -force_s
-    s1 = at_ends(MESH_X - 1, 0, near_e[0], near_w[0])
-    s2 = at_ends(MESH_X - 1, 0, near_e[1], near_w[1])
-    s1_pairs = at_ends(MESH_X - 1, 0, near_e[2], near_w[2])
+    s1, s2, s1_pairs = [-jnp.where(node == 0, x, 0.0) for x in near_w]
     n0 = force_n
 
     apply_inside(v0, v1, stiffness, anchor_t)
@@ -755,13 +777,9 @@
 
 def add_over(x, axis, stride, radix):
     peers = lax.axis_size(axis)
-    got = []
-    for k in range(1, radix):
-        pairs = []
-        for i in range(peers):
-            digit = i // stride % radix
-            pairs.append((i, i + ((digit + k) % radix - digit) * stride))
-        got.append(lax.ppermute(x, axis, pairs))
+    got = [
+        lax.ppermute(x, axis, [(i, i ^ (k * stride)) for i in range(peers)]) for k in range(1, radix)
+    ]
     for other in got:
         x = x + other
     return x
@@ -786,36 +804,32 @@
     field = (TALL, LANES)
     within_role = (lax.axis_index("row") % 2).astype(jnp.int32).reshape(1)
     across_role = 1 - within_role
-    packed_across, to_north, info = pack_across(
-        across_role, own, pair_counts[:, 0].T, pair_offsets[:, 0].T, tile_stiffness.T
-    )
+    to_north, info = edge(
+        own, pair_counts[:, 0].T, pair_offsets[:, 0].T, tile_stiffness.T, anchor
+    )
+    next_top = shifted(to_north, "col", -1)
+    packed_across, packed_within, anchor_t = pack(within_role, own, anchor)
+    packed_across, packed_within = fill(next_top, info, packed_across, packed_within)
     strips_across = swapped(packed_across, "row", 1)
-    next_top = shifted(to_north, "col", -1)
-    packed_within, anchor_t = pack_within(within_role, own, info, anchor)
-    packed_within, next_top = lax.optimization_barrier((packed_within, next_top))
     strips_within = swapped(packed_within, "row", 0)
     tabs = tables()
     terms_south = south_terms(own, next_top, info, anchor_t, tabs)
     from_north = shifted(terms_south, "col", 1)
-    terms_within = side_terms("within_pairs", within_role, own, strips_within, info, tabs)
-    message = (72, LANES)
-    (to_within,) = whole(functools.partial(message_kernel, tiles), [message], "message")(
-        within_role, terms_within, terms_south, from_north, info, anchor_t
-    )
+    message = whole(functools.partial(message_kernel, tiles), [(72, LANES)], "message")
+    terms_within = side_terms("within_pairs", within_role, own, strips_within, next_top, info, tabs)
+    (to_within,) = message(within_role, terms_within, terms_south, from_north, info, anchor_t)
     to_within, strips_across = lax.optimization_barrier((to_within, strips_across))
     within = swapped(to_within, "row", 0)
-    terms_across = side_terms("across_pairs", across_role, own, strips_across, info, tabs)
-    to_across, to_north = whole(
-        functools.partial(last_message_kernel, tiles), [message, (64, LANES)], "last_message"
-    )(across_role, terms_across, terms_within, terms_south, from_north, info, anchor_t)
+    terms_across = side_terms("across_pairs", across_role, own, strips_across, next_top, info, tabs)
+    terms_across, within = lax.optimization_barrier((terms_across, within))
+    (to_across,) = message(across_role, terms_across, terms_south, from_north, info, anchor_t)
     across = swapped(to_across, "row", 1)
-    from_south = shifted(to_north, "col", -1)
     v0, v1, v2, v3, match, gram = whole(
         functools.partial(mesh_kernel, tiles),
         [field, field, field, field, (tiles, 48), (8, LANES)],
         "powers",
         [pltpu.VMEM((LANES, LANES), F32)],
-    )(within_role, terms_south, terms_within, terms_across, within, across, from_south, from_north, info, anchor_t)
+    )(within_role, terms_south, terms_within, terms_across, within, across, next_top, from_north, info, anchor_t)
     gram = sum_everywhere(gram)
     positions, residual = whole(
         functools.partial(final_kernel, tiles),

time: 73.5 us -> 72.6 us (0.988)
  waiting for transfers between devices: 20.9 us -> 13.5 us
  starting transfers between devices: 27.4 us -> 30.2 us
  Pallas kernels: 21.2 us -> 23.4 us
  local copies, waits for them, and re-layouts: 2.77 us -> 4.12 us
    ppermute x3 -> x2, waiting for transfers between devices: 7.73 us -> 1.61 us  [shifted(): lax.ppermute(x, axis, [(i, i + by) for i in range(peers) if 0 <= i + by <...]
    ppermute x10, starting transfers between devices: 16.9 us -> 20.9 us  [add_over(): lax.ppermute(x, axis, [(i, i ^ k * stride) for i in range(peers)])]
    pallas_call x4 -> x5, Pallas kernels: 11.5 us -> 13.7 us  [the longest x2 8.54 us: side_terms(): pair_call(side_kernel, name, half, 32, [SMEM, ANY, ANY, VMEM, VMEM], buff...]
    unnamed x22 -> x28, local copies, waits for them, and re-layouts: 2.08 us -> 3.43 us
    ppermute x3 -> x2, starting transfers between devices: 6.15 us -> 4.86 us  [shifted(): lax.ppermute(x, axis, [(i, i + by) for i in range(peers) if 0 <= i + by <...]
    ppermute x10, waiting for transfers between devices: 13.1 us -> 11.9 us  [add_over(): lax.ppermute(x, axis, [(i, i ^ k * stride) for i in range(peers)])]
  transfers between devices with their start and end apart: 17 -> 16, of which waited for: 9 -> 8; matrix products, arithmetic and copies ran while one was open for 1% -> 1% of each run, Pallas kernels for 17% -> 24%
where the time goes in v5:
time: 72.6 us; the launch traced here: 72.2 us
  starting transfers between devices  30.2 us (42%)
  Pallas kernels  23.4 us (32%)
  waiting for transfers between devices  13.5 us (19%)
  local copies, waits for them, and re-layouts  4.12 us (6%)
  between operations  0.95 us (1%)
    ppermute x10, starting transfers between devices, add_over(): lax.ppermute(x, axis, [(i, i ^ k * stride) for i in range(peers)])  20.9 us
    ppermute x10, waiting for transfers between devices, add_over(): lax.ppermute(x, axis, [(i, i ^ k * stride) for i in range(peers)])  11.9 us
    pallas_call x2, Pallas kernels, side_terms(): pair_call(side_kernel, name, half, 32, [SMEM, ANY, ANY, VMEM, VMEM], buff...  8.54 us
    pallas_call x1, Pallas kernels, south_terms(): pair_call(south_kernel, 'south_pairs', tiles, 64, [ANY, ANY, VMEM, VMEM],...  6.63 us
    ppermute x2, starting transfers between devices, shifted(): lax.ppermute(x, axis, [(i, i + by) for i in range(peers) if 0 <= i + by <...  4.86 us
    ppermute x4, starting transfers between devices, swapped(): return lax.ppermute(x, axis, pairs + [(b, a) for a, b in pairs])  4.45 us
    unnamed x28, local copies, waits for them, and re-layouts  3.43 us
    pallas_call x4, Pallas kernels, call(): pl.pallas_call(kernel, name=name, in_specs=[SMEM] + [VMEM] * (len(args) -...  3.06 us
  transfers between devices with their start and end apart: 16, of which 8 were waited for; matrix products, arithmetic and copies ran while one was open for 1% of the time, Pallas kernels for 24%

profile of v5, /device:TPU:0, one launch (start us, length us, event | category | flops | bytes accessed | tf_op | source)
XLA Modules:
  0.0 72.2 jit_solution(1033963248687740463)
XLA Ops:
  0.7 1.8 %edge.1 = (bf16[1,64,640]{2,1,0:T(8,128)(2,1)}, f32[16,128]{1,0:T(8,128)}) custom-call(bf16[40,4,64,512]{3,2,1,0:T(8,128)(2,1)} %bitcast.16, s32[2,40]{1,0:T(2,128)} %bitcast.22, s32[2,40]{1,0:T(2,128)} %bitcast.23, f32[1,40]{1,0:T(1,128)} %bitcast.24, f32[40,1,896]{2,1,0:T(1,128)} %anchor.3), custom_call_target="tpu_custom_call" | custom-call | tf_op jit(solution)/shard_map/edge/pallas_call | solution.py:428
  2.5 1.3 %collective-permute-start = (bf16[1,64,640]{2,1,0:T(8,128)(2,1)}, bf16[1,64,640]{2,1,0:T(8,128)(2,1)S(1)}, u32[]{:S(2)}, u32[]{:S(2)}) collective-permute-start(bf16[1,64,640]{2,1,0:T(8,128)(2,1)} %get-tuple-element.22), channel_id=1, source_target_pairs={{1,0},{2,1},{3,2},{5,4},{6,5},{7,6},{9,8},{10,9},{11,10},{13,12},{... | collective-permute-start | bytes 245768 | tf_op jit(solution)/shard_map/ppermute | solution.py:769
  3.8 1.7 %pack.1 = (bf16[11,64,640]{2,1,0:T(8,128)(2,1)S(1)}, bf16[11,64,640]{2,1,0:T(8,128)(2,1)S(1)}, f32[896,128]{1,0:T(8,128)S(1)}) custom-call(s32[1]{0:T(128)} %bitcast.role.refs_0_, bf16[40,4,64,512]{3,2,1,0:T(8,128)(2,1)} %bitcast.17, f32[40,1,896]{2,1,0:T(1,128)S(1)} %copy-done.8), custom_call_target="tpu_custom_call" | custom-call | bytes 6000000 | tf_op jit(solution)/shard_map/pack/pallas_call | solution.py:452
  5.6 0.9 %copy-done.6 = bf16[11,64,640]{2,1,0:T(8,128)(2,1)} copy-done((bf16[11,64,640]{2,1,0:T(8,128)(2,1)}, bf16[11,64,640]{2,1,0:T(8,128)(2,1)S(1)}, u32[]{:S(2)}) %copy-start.6) | copy-done | bytes 901144
  6.5 0.9 %copy-done.7 = bf16[11,64,640]{2,1,0:T(8,128)(2,1)} copy-done((bf16[11,64,640]{2,1,0:T(8,128)(2,1)}, bf16[11,64,640]{2,1,0:T(8,128)(2,1)S(1)}, u32[]{:S(2)}) %copy-start.7) | copy-done | bytes 901144
  7.5 1.6 %collective-permute-done.nxt.next_top.refs_6_ = bf16[1,64,640]{2,1,0:T(8,128)(2,1)S(1)} collective-permute-done((bf16[1,64,640]{2,1,0:T(8,128)(2,1)}, bf16[1,64,640]{2,1,0:T(8,128)(2,1)S(1)}, u32[]{:S(2)}, u32[]{:S(2)}) %collective-permute-start) | collective-permute-done | bytes 81952 | tf_op jit(solution)/shard_map/ppermute | solution.py:769
  9.7 1.6 %fill.1 = (bf16[11,64,640]{2,1,0:T(8,128)(2,1)}, bf16[11,64,640]{2,1,0:T(8,128)(2,1)}) custom-call(bf16[1,64,640]{2,1,0:T(8,128)(2,1)} %copy-done.2, f32[16,128]{1,0:T(8,128)} %get-tuple-element.23.info.refs_8_, bf16[11,64,640]{2,1,0:T(8,128)(2,1)} %copy-done.6, bf16[11,64,640]{2,1,0:T(8,128)(2,1)} %copy-done.7), custom_call_target="tpu_custom_call", output_to_operand_aliasing={{0}: (2, {}), {1}: (3, {})} | custom-call | tf_op jit(solution)/shard_map/fill/pallas_call | solution.py:470
  11.4 0.7 collective-permute-start.3
  12.3 0.9 %copy-done.3 = bf16[1,64,640]{2,1,0:T(8,128)(2,1)S(1)} copy-done((bf16[1,64,640]{2,1,0:T(8,128)(2,1)S(1)}, bf16[1,64,640]{2,1,0:T(8,128)(2,1)}, u32[]{:S(2)}) %copy-start.3) | copy-done | bytes 81944
  13.1 6.6 %south_pairs.1.terms_south.refs_1_ = f32[64,128]{1,0:T(8,128)S(1)} custom-call(bf16[40,4,64,512]{3,2,1,0:T(8,128)(2,1)} %bitcast.18, bf16[1,64,640]{2,1,0:T(8,128)(2,1)S(1)} %copy-done.3, f32[16,128]{1,0:T(8,128)S(1)} %copy-done.9, f32[896,128]{1,0:T(8,128)S(1)} %get-tuple-element.24.anchor_t.refs_9_, bf16[64,64]{1,0:T(8,128)(2,1)S(1)} %copy-done.11, ...), custom_call_target="tpu_custom_call" | custom-call | flops 2400000000 | bytes 3932160 | tf_op jit(solution)/shard_map/south_pairs/pallas_call | solution.py:322
  19.8 3.6 %collective-permute-start.2 = (f32[64,128]{1,0:T(8,128)S(1)}, f32[64,128]{1,0:T(8,128)S(1)}, u32[]{:S(2)}, u32[]{:S(2)}) collective-permute-start(f32[64,128]{1,0:T(8,128)S(1)} %south_pairs.1.terms_south.refs_1_), channel_id=1, source_target_pairs={{0,1},{1,2},{2,3},{4,5},{5,6},{6,7},{8,9},{9,10},{10,11},{12,13},{... | collective-permute-start | bytes 98312 | tf_op jit(solution)/shard_map/ppermute | solution.py:769
  23.4 4.3 %within_pairs.1.terms.refs_2_ = f32[32,128]{1,0:T(8,128)S(1)} custom-call(s32[1]{0:T(128)} %bitcast.role.refs_0_, bf16[40,4,64,512]{3,2,1,0:T(8,128)(2,1)} %bitcast.19, bf16[11,64,640]{2,1,0:T(8,128)(2,1)S(1)} %collective-permute-done.1.received, bf16[1,64,640]{2,1,0:T(8,128)(2,1)S(1)} %copy-done.4, f32[16,128]{1,0:T(8,128)S(1)} %copy-done.9, ...), custom_call_target="tpu_custom_call" | custom-call | flops 1200000000 | bytes 1966080 | tf_op jit(solution)/shard_map/within_pairs/pallas_call | solution.py:333
  27.7 3.0 %collective-permute-start.4 = (f32[72,128]{1,0:T(8,128)S(1)}, f32[72,128]{1,0:T(8,128)S(1)}, u32[]{:S(2)}, u32[]{:S(2)}) collective-permute-start(f32[72,128]{1,0:T(8,128)S(1)} %message.2), channel_id=1, source_target_pairs={{0,4},{8,12},{16,20},{24,28},{32,36},{40,44},{48,52},{56,60},{64,6... | collective-permute-start | bytes 110600 | tf_op jit(solution)/shard_map/ppermute | solution.py:775
  30.7 4.3 %across_pairs.1.terms.refs_3_ = f32[32,128]{1,0:T(8,128)S(1)} custom-call(s32[1]{0:T(128)S(6)} %sub.3.role, bf16[40,4,64,512]{3,2,1,0:T(8,128)(2,1)} %bitcast.20, bf16[11,64,640]{2,1,0:T(8,128)(2,1)S(1)} %collective-permute-done.3.received, bf16[1,64,640]{2,1,0:T(8,128)(2,1)S(1)} %copy-done.4, f32[16,128]{1,0:T(8,128)S(1)} %copy-done.9, ...), custom_call_target="tpu_custom_call" | custom-call | flops 1200000000 | bytes 1966080 | tf_op jit(solution)/shard_map/across_pairs/pallas_call | solution.py:333
  35.8 1.5 %powers.1 = (f32[1024,128]{1,0:T(8,128)S(1)}, f32[1024,128]{1,0:T(8,128)S(1)}, f32[1024,128]{1,0:T(8,128)S(1)}, f32[1024,128]{1,0:T(8,128)S(1)}, f32[40,48]{1,0:T(8,128)S(1)}, /*index=5*/f32[8,128]{1,0:T(8,128)S(1)}) custom-call(s32[1]{0:T(128)} %bitcast.role.refs_0_, f32[64,128]{1,0:T(8,128)S(1)} %south_pairs.1.terms_south.refs_1_, ...), custom_call_target="tpu_custom_call" | custom-call | flops 4000000 | bytes 2000000 | tf_op jit(solution)/shard_map/powers/pallas_call | solution.py:485
  37.3 5.0 %collective-permute-start.6 = (f32[8,128]{1,0:T(8,128)S(1)}, f32[8,128]{1,0:T(8,128)S(1)}, u32[]{:S(2)}, u32[]{:S(2)}) collective-permute-start(f32[8,128]{1,0:T(8,128)S(1)} %get-tuple-element.34), channel_id=1, source_target_pairs={{0,4},{4,0},{8,12},{12,8},{16,20},{20,16},{24,28},{28,24},{32,36},... | collective-permute-start | bytes 12296 | tf_op jit(solution)/shard_map/ppermute | solution.py:781
  42.3 0.8 %collective-permute-done.6 = f32[8,128]{1,0:T(8,128)S(1)} collective-permute-done((f32[8,128]{1,0:T(8,128)S(1)}, f32[8,128]{1,0:T(8,128)S(1)}, u32[]{:S(2)}, u32[]{:S(2)}) %collective-permute-start.6) | collective-permute-done | bytes 4128 | tf_op jit(solution)/shard_map/ppermute | solution.py:781
  43.1 2.0 %collective-permute-start.7 = (f32[8,128]{1,0:T(8,128)S(1)}, f32[8,128]{1,0:T(8,128)S(1)}, u32[]{:S(2)}, u32[]{:S(2)}) collective-permute-start(f32[8,128]{1,0:T(8,128)S(1)} %add.35), channel_id=1, source_target_pairs={{0,8},{4,12},{8,0},{12,4},{16,24},{20,28},{24,16},{28,20},{32,40},... | collective-permute-start | bytes 12296 | tf_op jit(solution)/shard_map/ppermute | solution.py:781
  45.1 4.6 %collective-permute-start.8 = (f32[8,128]{1,0:T(8,128)S(1)}, f32[8,128]{1,0:T(8,128)S(1)}, u32[]{:S(2)}, u32[]{:S(2)}) collective-permute-start(f32[8,128]{1,0:T(8,128)S(1)} %add.35), channel_id=1, source_target_pairs={{0,16},{4,20},{8,24},{12,28},{16,0},{20,4},{24,8},{28,12},{32,48},... | collective-permute-start | bytes 12296 | tf_op jit(solution)/shard_map/ppermute | solution.py:781
  49.7 1.6 %collective-permute-done.8 = f32[8,128]{1,0:T(8,128)S(1)} collective-permute-done((f32[8,128]{1,0:T(8,128)S(1)}, f32[8,128]{1,0:T(8,128)S(1)}, u32[]{:S(2)}, u32[]{:S(2)}) %collective-permute-start.8) | collective-permute-done | bytes 4128 | tf_op jit(solution)/shard_map/ppermute | solution.py:781
  51.3 3.2 %collective-permute-done.9 = f32[8,128]{1,0:T(8,128)S(1)} collective-permute-done((f32[8,128]{1,0:T(8,128)S(1)}, f32[8,128]{1,0:T(8,128)S(1)}, u32[]{:S(2)}, u32[]{:S(2)}) %collective-permute-start.9) | collective-permute-done | bytes 4128 | tf_op jit(solution)/shard_map/ppermute | solution.py:781
  54.5 1.5 %collective-permute-start.10 = (f32[8,128]{1,0:T(8,128)S(1)}, f32[8,128]{1,0:T(8,128)S(1)}, u32[]{:S(2)}, u32[]{:S(2)}) collective-permute-start(f32[8,128]{1,0:T(8,128)S(1)} %add_add_fusion.2), channel_id=1, source_target_pairs={{0,32},{4,36},{8,40},{12,44},{16,48},{20,52},{24,56},{28,60},{32,0... | collective-permute-start | bytes 12296 | tf_op jit(solution)/shard_map/ppermute | solution.py:781
  56.0 2.5 %collective-permute-start.11 = (f32[8,128]{1,0:T(8,128)S(1)}, f32[8,128]{1,0:T(8,128)S(1)}, u32[]{:S(2)}, u32[]{:S(2)}) collective-permute-start(f32[8,128]{1,0:T(8,128)S(1)} %add_add_fusion.2), channel_id=1, source_target_pairs={{0,64},{4,68},{8,72},{12,76},{16,80},{20,84},{24,88},{28,92},{32,9... | collective-permute-start | bytes 12296 | tf_op jit(solution)/shard_map/ppermute | solution.py:781
  58.4 0.7 %collective-permute-start.12 = (f32[8,128]{1,0:T(8,128)S(1)}, f32[8,128]{1,0:T(8,128)S(1)}, u32[]{:S(2)}, u32[]{:S(2)}) collective-permute-start(f32[8,128]{1,0:T(8,128)S(1)} %add_add_fusion.2), channel_id=1, source_target_pairs={{0,96},{4,100},{8,104},{12,108},{16,112},{20,116},{24,120},{28,124... | collective-permute-start | bytes 12296 | tf_op jit(solution)/shard_map/ppermute | solution.py:781
  59.2 1.9 %collective-permute-done.11 = f32[8,128]{1,0:T(8,128)S(1)} collective-permute-done((f32[8,128]{1,0:T(8,128)S(1)}, f32[8,128]{1,0:T(8,128)S(1)}, u32[]{:S(2)}, u32[]{:S(2)}) %collective-permute-start.11) | collective-permute-done | bytes 4128 | tf_op jit(solution)/shard_map/ppermute | solution.py:781
  61.1 2.2 %collective-permute-done.12 = f32[8,128]{1,0:T(8,128)S(1)} collective-permute-done((f32[8,128]{1,0:T(8,128)S(1)}, f32[8,128]{1,0:T(8,128)S(1)}, u32[]{:S(2)}, u32[]{:S(2)}) %collective-permute-start.12) | collective-permute-done | bytes 4128 | tf_op jit(solution)/shard_map/ppermute | solution.py:781
  63.3 1.6 %collective-permute-start.13 = (f32[8,128]{1,0:T(8,128)S(1)}, f32[8,128]{1,0:T(8,128)S(1)}, u32[]{:S(2)}, u32[]{:S(2)}) collective-permute-start(f32[8,128]{1,0:T(8,128)S(1)} %add_add_fusion.1), channel_id=1, source_target_pairs={{0,1},{1,0},{2,3},{3,2},{4,5},{5,4},{6,7},{7,6},{8,9},{9,8},{10,11... | collective-permute-start | bytes 12296 | tf_op jit(solution)/shard_map/ppermute | solution.py:781
  64.8 1.1 %collective-permute-start.14 = (f32[8,128]{1,0:T(8,128)S(1)}, f32[8,128]{1,0:T(8,128)S(1)}, u32[]{:S(2)}, u32[]{:S(2)}) collective-permute-start(f32[8,128]{1,0:T(8,128)S(1)} %add_add_fusion.1), channel_id=1, source_target_pairs={{0,2},{1,3},{2,0},{3,1},{4,6},{5,7},{6,4},{7,5},{8,10},{9,11},{10,... | collective-permute-start | bytes 12296 | tf_op jit(solution)/shard_map/ppermute | solution.py:781
  66.0 2.0 %collective-permute-start.15 = (f32[8,128]{1,0:T(8,128)S(1)}, f32[8,128]{1,0:T(8,128)S(1)}, u32[]{:S(2)}, u32[]{:S(2)}) collective-permute-start(f32[8,128]{1,0:T(8,128)S(1)} %add_add_fusion.1), channel_id=1, source_target_pairs={{0,3},{1,2},{2,1},{3,0},{4,7},{5,6},{6,5},{7,4},{8,11},{9,10},{10,... | collective-permute-start | bytes 12296 | tf_op jit(solution)/shard_map/ppermute | solution.py:781
  68.7 1.3 %collective-permute-done.14 = f32[8,128]{1,0:T(8,128)S(1)} collective-permute-done((f32[8,128]{1,0:T(8,128)S(1)}, f32[8,128]{1,0:T(8,128)S(1)}, u32[]{:S(2)}, u32[]{:S(2)}) %collective-permute-start.14) | collective-permute-done | bytes 4128 | tf_op jit(solution)/shard_map/ppermute | solution.py:781
  70.0 0.9 %collective-permute-done.15 = f32[8,128]{1,0:T(8,128)S(1)} collective-permute-done((f32[8,128]{1,0:T(8,128)S(1)}, f32[8,128]{1,0:T(8,128)S(1)}, u32[]{:S(2)}, u32[]{:S(2)}) %collective-permute-start.15) | collective-permute-done | bytes 4128 | tf_op jit(solution)/shard_map/ppermute | solution.py:781
  70.8 1.4 %combine.1 = (f32[40,2,896]{2,1,0:T(2,128)}, f32[40,2,896]{2,1,0:T(2,128)}) custom-call(f32[8,128]{1,0:T(8,128)S(1)} %add_add_fusion.gram, f32[1024,128]{1,0:T(8,128)S(1)} %get-tuple-element.35.v0, f32[1024,128]{1,0:T(8,128)S(1)} %get-tuple-element.36.v1, f32[1024,128]{1,0:T(8,128)S(1)} %get-tuple-element.37.v2, f32[1024,128]{1,0:T(8,128)S(1)} %get-tuple-element.38.v3), custom_call_target="tpu_custom_call" | custom-call | flops 4000000 | bytes 2000000 | tf_op jit(solution)/shard_map/combine/pallas_call | solution.py:485
  (43 shorter events, 2.3 us)
Async XLA Ops:
  0.6 3.2 %copy-start.8 = (f32[40,1,896]{2,1,0:T(1,128)S(1)}, f32[40,1,896]{2,1,0:T(1,128)}, u32[]{:S(2)}) copy-start(f32[40,1,896]{2,1,0:T(1,128)} %anchor.3) | copy-start | bytes 430084
  0.6 11.5 %copy-start = (bf16[256,512]{1,0:T(8,128)(2,1)S(1)}, bf16[256,512]{1,0:T(8,128)(2,1)}, u32[]{:S(2)}) copy-start(bf16[256,512]{1,0:T(8,128)(2,1)} %constant.37.clone.ends) | copy-start | bytes 786436
  0.7 11.5 %copy-start.1 = (bf16[2,256,256]{2,1,0:T(8,128)(2,1)S(1)}, bf16[2,256,256]{2,1,0:T(8,128)(2,1)}, u32[]{:S(2)}) copy-start(bf16[2,256,256]{2,1,0:T(8,128)(2,1)} %constant.38.clone.backs) | copy-start | bytes 786436
  0.7 11.5 %copy-start.5 = (bf16[256,256]{1,0:T(8,128)(2,1)S(1)}, bf16[256,256]{1,0:T(8,128)(2,1)}, u32[]{:S(2)}) copy-start(bf16[256,256]{1,0:T(8,128)(2,1)} %constant.36.clone.forward) | copy-start | bytes 393220
  0.7 11.5 %copy-start.10 = (f32[64,128]{1,0:T(8,128)S(1)}, f32[64,128]{1,0:T(8,128)}, u32[]{:S(2)}) copy-start(f32[64,128]{1,0:T(8,128)} %constant.41.clone.rows) | copy-start | bytes 98308
  0.7 11.5 %copy-start.11 = (bf16[64,64]{1,0:T(8,128)(2,1)S(1)}, bf16[64,64]{1,0:T(8,128)(2,1)}, u32[]{:S(2)}) copy-start(bf16[64,64]{1,0:T(8,128)(2,1)} %constant.35.clone.depth) | copy-start | bytes 24580
  0.7 11.5 %copy-start.12 = (bf16[64,64]{1,0:T(8,128)(2,1)S(1)}, bf16[64,64]{1,0:T(8,128)(2,1)}, u32[]{:S(2)}) copy-start(bf16[64,64]{1,0:T(8,128)(2,1)} %constant.39.clone.final) | copy-start | bytes 24580
  0.7 11.5 %copy-start.13 = (f32[8,128]{1,0:T(8,128)S(1)}, f32[8,128]{1,0:T(8,128)}, u32[]{:S(2)}) copy-start(f32[8,128]{1,0:T(8,128)} %constant.40.clone.pick) | copy-start | bytes 12292
  2.5 9.7 %copy-start.9 = (f32[16,128]{1,0:T(8,128)S(1)}, f32[16,128]{1,0:T(8,128)}, u32[]{:S(2)}) copy-start(f32[16,128]{1,0:T(8,128)} %get-tuple-element.23.info.refs_8_) | copy-start | bytes 24580
  2.5 6.5 %collective-permute-start = (bf16[1,64,640]{2,1,0:T(8,128)(2,1)}, bf16[1,64,640]{2,1,0:T(8,128)(2,1)S(1)}, u32[]{:S(2)}, u32[]{:S(2)}) collective-permute-start(bf16[1,64,640]{2,1,0:T(8,128)(2,1)} %get-tuple-element.22), channel_id=1, source_target_pairs={{1,0},{2,1},{3,2},{5,4},{6,5},{7,6},{9,8},{10,9},{11,10},{13,12},{... | collective-permute-start | bytes 245768 | tf_op jit(solution)/shard_map/ppermute | solution.py:769
  5.6 0.9 %copy-start.6 = (bf16[11,64,640]{2,1,0:T(8,128)(2,1)}, bf16[11,64,640]{2,1,0:T(8,128)(2,1)S(1)}, u32[]{:S(2)}) copy-start(bf16[11,64,640]{2,1,0:T(8,128)(2,1)S(1)} %get-tuple-element.25.across_in) | copy-start | bytes 2703364
  6.5 0.9 %copy-start.7 = (bf16[11,64,640]{2,1,0:T(8,128)(2,1)}, bf16[11,64,640]{2,1,0:T(8,128)(2,1)S(1)}, u32[]{:S(2)}) copy-start(bf16[11,64,640]{2,1,0:T(8,128)(2,1)S(1)} %get-tuple-element.26.within_in) | copy-start | bytes 2703364
  9.1 0.6 copy-start.2
  11.3 12.0 %collective-permute-start.1 = (bf16[11,64,640]{2,1,0:T(8,128)(2,1)}, bf16[11,64,640]{2,1,0:T(8,128)(2,1)S(1)}, u32[]{:S(2)}, u32[]{:S(2)}) collective-permute-start(bf16[11,64,640]{2,1,0:T(8,128)(2,1)} %get-tuple-element.27), channel_id=1, source_target_pairs={{0,4},{8,12},{16,20},{24,28},{32,36},{40,44},{48,52},{56,60},{64,6... | collective-permute-start | bytes 2703368 | tf_op jit(solution)/shard_map/ppermute | solution.py:775
  11.4 16.3 %collective-permute-start.3 = (bf16[11,64,640]{2,1,0:T(8,128)(2,1)}, bf16[11,64,640]{2,1,0:T(8,128)(2,1)S(1)}, u32[]{:S(2)}, u32[]{:S(2)}) collective-permute-start(bf16[11,64,640]{2,1,0:T(8,128)(2,1)} %get-tuple-element.28), channel_id=1, source_target_pairs={{4,8},{12,16},{20,24},{28,32},{36,40},{44,48},{52,56},{60,64},{68,... | collective-permute-start | bytes 2703368 | tf_op jit(solution)/shard_map/ppermute | solution.py:775
  12.2 0.9 %copy-start.3 = (bf16[1,64,640]{2,1,0:T(8,128)(2,1)S(1)}, bf16[1,64,640]{2,1,0:T(8,128)(2,1)}, u32[]{:S(2)}) copy-start(bf16[1,64,640]{2,1,0:T(8,128)(2,1)} %copy-done.2) | copy-start | bytes 245764
  13.1 10.2 %copy-start.4 = (bf16[1,64,640]{2,1,0:T(8,128)(2,1)S(1)}, bf16[1,64,640]{2,1,0:T(8,128)(2,1)}, u32[]{:S(2)}) copy-start(bf16[1,64,640]{2,1,0:T(8,128)(2,1)} %copy-done.2) | copy-start | bytes 245764
  19.8 7.9 %collective-permute-start.2 = (f32[64,128]{1,0:T(8,128)S(1)}, f32[64,128]{1,0:T(8,128)S(1)}, u32[]{:S(2)}, u32[]{:S(2)}) collective-permute-start(f32[64,128]{1,0:T(8,128)S(1)} %south_pairs.1.terms_south.refs_1_), channel_id=1, source_target_pairs={{0,1},{1,2},{2,3},{4,5},{5,6},{6,7},{8,9},{9,10},{10,11},{12,13},{... | collective-permute-start | bytes 98312 | tf_op jit(solution)/shard_map/ppermute | solution.py:769
  27.7 7.3 %collective-permute-start.4 = (f32[72,128]{1,0:T(8,128)S(1)}, f32[72,128]{1,0:T(8,128)S(1)}, u32[]{:S(2)}, u32[]{:S(2)}) collective-permute-start(f32[72,128]{1,0:T(8,128)S(1)} %message.2), channel_id=1, source_target_pairs={{0,4},{8,12},{16,20},{24,28},{32,36},{40,44},{48,52},{56,60},{64,6... | collective-permute-start | bytes 110600 | tf_op jit(solution)/shard_map/ppermute | solution.py:775
  35.1 0.7 collective-permute-start.5
  37.3 5.8 %collective-permute-start.6 = (f32[8,128]{1,0:T(8,128)S(1)}, f32[8,128]{1,0:T(8,128)S(1)}, u32[]{:S(2)}, u32[]{:S(2)}) collective-permute-start(f32[8,128]{1,0:T(8,128)S(1)} %get-tuple-element.34), channel_id=1, source_target_pairs={{0,4},{4,0},{8,12},{12,8},{16,20},{20,16},{24,28},{28,24},{32,36},... | collective-permute-start | bytes 12296 | tf_op jit(solution)/shard_map/ppermute | solution.py:781
  43.1 6.6 %collective-permute-start.7 = (f32[8,128]{1,0:T(8,128)S(1)}, f32[8,128]{1,0:T(8,128)S(1)}, u32[]{:S(2)}, u32[]{:S(2)}) collective-permute-start(f32[8,128]{1,0:T(8,128)S(1)} %add.35), channel_id=1, source_target_pairs={{0,8},{4,12},{8,0},{12,4},{16,24},{20,28},{24,16},{28,20},{32,40},... | collective-permute-start | bytes 12296 | tf_op jit(solution)/shard_map/ppermute | solution.py:781
  45.1 6.2 %collective-permute-start.8 = (f32[8,128]{1,0:T(8,128)S(1)}, f32[8,128]{1,0:T(8,128)S(1)}, u32[]{:S(2)}, u32[]{:S(2)}) collective-permute-start(f32[8,128]{1,0:T(8,128)S(1)} %add.35), channel_id=1, source_target_pairs={{0,16},{4,20},{8,24},{12,28},{16,0},{20,4},{24,8},{28,12},{32,48},... | collective-permute-start | bytes 12296 | tf_op jit(solution)/shard_map/ppermute | solution.py:781
  49.7 4.8 %collective-permute-start.9 = (f32[8,128]{1,0:T(8,128)S(1)}, f32[8,128]{1,0:T(8,128)S(1)}, u32[]{:S(2)}, u32[]{:S(2)}) collective-permute-start(f32[8,128]{1,0:T(8,128)S(1)} %add.35), channel_id=1, source_target_pairs={{0,24},{4,28},{8,16},{12,20},{16,8},{20,12},{24,0},{28,4},{32,56},... | collective-permute-start | bytes 12296 | tf_op jit(solution)/shard_map/ppermute | solution.py:781
  54.5 4.7 %collective-permute-start.10 = (f32[8,128]{1,0:T(8,128)S(1)}, f32[8,128]{1,0:T(8,128)S(1)}, u32[]{:S(2)}, u32[]{:S(2)}) collective-permute-start(f32[8,128]{1,0:T(8,128)S(1)} %add_add_fusion.2), channel_id=1, source_target_pairs={{0,32},{4,36},{8,40},{12,44},{16,48},{20,52},{24,56},{28,60},{32,0... | collective-permute-start | bytes 12296 | tf_op jit(solution)/shard_map/ppermute | solution.py:781
  56.0 5.1 %collective-permute-start.11 = (f32[8,128]{1,0:T(8,128)S(1)}, f32[8,128]{1,0:T(8,128)S(1)}, u32[]{:S(2)}, u32[]{:S(2)}) collective-permute-start(f32[8,128]{1,0:T(8,128)S(1)} %add_add_fusion.2), channel_id=1, source_target_pairs={{0,64},{4,68},{8,72},{12,76},{16,80},{20,84},{24,88},{28,92},{32,9... | collective-permute-start | bytes 12296 | tf_op jit(solution)/shard_map/ppermute | solution.py:781
  58.4 4.8 %collective-permute-start.12 = (f32[8,128]{1,0:T(8,128)S(1)}, f32[8,128]{1,0:T(8,128)S(1)}, u32[]{:S(2)}, u32[]{:S(2)}) collective-permute-start(f32[8,128]{1,0:T(8,128)S(1)} %add_add_fusion.2), channel_id=1, source_target_pairs={{0,96},{4,100},{8,104},{12,108},{16,112},{20,116},{24,120},{28,124... | collective-permute-start | bytes 12296 | tf_op jit(solution)/shard_map/ppermute | solution.py:781
  63.3 5.4 %collective-permute-start.13 = (f32[8,128]{1,0:T(8,128)S(1)}, f32[8,128]{1,0:T(8,128)S(1)}, u32[]{:S(2)}, u32[]{:S(2)}) collective-permute-start(f32[8,128]{1,0:T(8,128)S(1)} %add_add_fusion.1), channel_id=1, source_target_pairs={{0,1},{1,0},{2,3},{3,2},{4,5},{5,4},{6,7},{7,6},{8,9},{9,8},{10,11... | collective-permute-start | bytes 12296 | tf_op jit(solution)/shard_map/ppermute | solution.py:781
  64.8 5.1 %collective-permute-start.14 = (f32[8,128]{1,0:T(8,128)S(1)}, f32[8,128]{1,0:T(8,128)S(1)}, u32[]{:S(2)}, u32[]{:S(2)}) collective-permute-start(f32[8,128]{1,0:T(8,128)S(1)} %add_add_fusion.1), channel_id=1, source_target_pairs={{0,2},{1,3},{2,0},{3,1},{4,6},{5,7},{6,4},{7,5},{8,10},{9,11},{10,... | collective-permute-start | bytes 12296 | tf_op jit(solution)/shard_map/ppermute | solution.py:781
  66.0 4.8 %collective-permute-start.15 = (f32[8,128]{1,0:T(8,128)S(1)}, f32[8,128]{1,0:T(8,128)S(1)}, u32[]{:S(2)}, u32[]{:S(2)}) collective-permute-start(f32[8,128]{1,0:T(8,128)S(1)} %add_add_fusion.1), channel_id=1, source_target_pairs={{0,3},{1,2},{2,1},{3,0},{4,7},{5,6},{6,5},{7,4},{8,11},{9,10},{10,... | collective-permute-start | bytes 12296 | tf_op jit(solution)/shard_map/ppermute | solution.py:781

commit v6 on v5

--- a/solution.py
+++ b/solution.py
@@ -243,7 +243,7 @@
     out[32:, :] = anchor_t[NODES - MESH_X : NODES, :]
 
 
-def side_kernel(role, strips, received, next_top, info, depth, forward, ends, backs, final, pick, rows, out, own, other, r0, r1, sems, extra_sem):
+def side_kernel(role, strips, received, next_top, corner, info, depth, forward, ends, backs, final, pick, rows, out, own, other, r0, r1, sems, extra_sem):
     half = own.shape[0]
     steps = half // GROUP
     slots = GROUP // 2
@@ -277,14 +277,16 @@
             other[slots * c + slot, :, LANES * i : LANES * (i + 1)] for slot in range(slots) for i in range(5)
         ]
         correlate_group(
-            owns + [next_top[0, :, SIDE : SIDE + LANES]] + others + [other[spare, :, :LANES]],
+            owns + [next_top[0, :, SIDE:]] + others + [corner[0, :, :LANES]],
             depth[...], forward[...], ends[...], backs[west], final[...], rows[...], r0, r1, base + GROUP * c,
         )
         return carry
 
     lax.fori_loop(0, steps, step, 0)
     lane = lax.broadcasted_iota(jnp.int32, (8, LANES), 1)
-    info_west = other[spare, 0:16, 2 * LANES : 3 * LANES].astype(F32)[0:8]
+    info_west = other[spare, 0:16, 0:LANES].astype(F32)[0:8]
+    corner_facts = corner[0, 0:16, LANES:].astype(F32)[0:8]
+    info_west = jnp.where(lane == EXTRA, corner_facts, info_west)
     table = jnp.where(west == 1, info_west, info[0:8, :])
     mine = (lane >= base) & (lane < base + half) | (lane == EXTRA) & (west == 1)
     table = jnp.where(mine, table, 0.0)
@@ -324,15 +326,15 @@
     )(strips, nxt, info, anchor_t, *tabs)
 
 
-def side_terms(name, role, strips, received, next_top, info, tabs):
+def side_terms(name, role, strips, received, next_top, corner, info, tabs):
     half = strips.shape[0] // 2
     buffers = [
         pltpu.VMEM((half, PATCH, SIDE), BF16),
         pltpu.VMEM((half // 2 + 1, PATCH, 2 * WIDE), BF16),
     ]
     return pair_call(
-        side_kernel, name, half, 32, [SMEM, ANY, ANY, VMEM, VMEM], buffers, [pltpu.SemaphoreType.DMA]
-    )(role, strips, received, next_top, info, *tabs)
+        side_kernel, name, half, 32, [SMEM, ANY, ANY, VMEM, VMEM, VMEM], buffers, [pltpu.SemaphoreType.DMA]
+    )(role, strips, received, next_top, corner, info, *tabs)
 
 
 STATICS = COMP
@@ -344,12 +346,12 @@
     return high, middle, x - high - middle
 
 
-def edge_kernel(strips, counts, offsets, stiffness, anchor, north, info, left, count_s, offset_s, stiff_s, anchor_s, turn, sems):
+def edge_kernel(strips, counts, offsets, stiffness, anchor, north, corner, info, left, count_s, offset_s, stiff_s, anchor_s, turn, sems):
     tiles = counts.shape[1]
     lanes = pl.ds(0, LANES)
     copies = [
         (strips.at[0, 1, :, pl.ds(0, SIDE)], north.at[0, :, pl.ds(0, SIDE)]),
-        (strips.at[0, 3, :, lanes], north.at[0, :, pl.ds(4 * LANES, LANES)]),
+        (strips.at[0, 3, :, lanes], corner.at[0, :, lanes]),
         (strips.at[0, 0, :, lanes], left),
         (counts, count_s),
         (offsets, offset_s),
@@ -376,10 +378,13 @@
     block = jnp.where(lane < COMP, left[...].astype(F32), 0.0)
     for k, x in enumerate(columns):
         block = jnp.where(lane == STATICS + k, x, block)
-    north[0, :, SIDE : SIDE + LANES] = block.astype(BF16)
-
-
-def pack_kernel(role, strips, anchor, across, within, anchor_t, buffers, wide, sems):
+    north[0, :, SIDE:] = block.astype(BF16)
+    row = lax.broadcasted_iota(jnp.int32, (PATCH, LANES), 0)
+    facts = jnp.where(row == 0, columns[-2], jnp.where(row == 1, columns[-1], 0.0))
+    corner[0, :, LANES:] = jnp.where(lane == EXTRA, facts, 0.0).astype(BF16)
+
+
+def pack_kernel(role, strips, info, anchor, across, within, anchor_t, buffers, wide, sems):
     tiles = anchor.shape[0]
     half = tiles // 2
     moves = []
@@ -399,27 +404,7 @@
             for i, x in enumerate(columns):
                 packed[slot, :, LANES * i : LANES * (i + 1)] = x
         packed[half // 2] = jnp.zeros((PATCH, 2 * WIDE), BF16)
-
-
-def fill_kernel(next_top, info, across_in, within_in, across, within, slot, sems):
-    spare = across.shape[0] - 1
-    lane = lax.broadcasted_iota(jnp.int32, (16, LANES), 1)
-    row = lax.broadcasted_iota(jnp.int32, (16, LANES), 0)
-    statics = next_top[0, 0:16, SIDE : SIDE + LANES].astype(F32)
-    count = pltpu.roll(statics, (EXTRA - STATICS - 6) % LANES, axis=1)
-    offset = pltpu.roll(statics, (EXTRA - STATICS - 7) % LANES, axis=1)
-    facts = jnp.where(lane == EXTRA, jnp.where(row == 0, count, offset), info[...])
-    slot[...] = jnp.zeros_like(slot)
-    slot[:, 0:LANES] = next_top[0, :, 4 * LANES :]
-    slot[0:16, 2 * LANES : 3 * LANES] = facts.astype(BF16)
-    copies = [
-        pltpu.make_async_copy(slot, packed.at[spare, :, pl.ds(0, SIDE)], sems.at[k])
-        for k, packed in enumerate((across, within))
-    ]
-    for copy in copies:
-        copy.start()
-    for copy in copies:
-        copy.wait()
+        packed[half // 2, 0:16, 0:LANES] = info[...].astype(BF16)
 
 
 def edge(strips, counts, offsets, stiffness, anchor):
@@ -429,9 +414,10 @@
         edge_kernel,
         name="edge",
         in_specs=[ANY] * 5,
-        out_specs=[VMEM] * 2,
+        out_specs=[VMEM] * 3,
         out_shape=[
-            jax.ShapeDtypeStruct((1, PATCH, 2 * WIDE), BF16),
+            jax.ShapeDtypeStruct((1, PATCH, SIDE + LANES), BF16),
+            jax.ShapeDtypeStruct((1, PATCH, 2 * LANES), BF16),
             jax.ShapeDtypeStruct((16, LANES), F32),
         ],
         scratch_shapes=[
@@ -446,13 +432,13 @@
     )(strips, counts, offsets, stiffness, anchor)
 
 
-def pack(role, strips, anchor):
+def pack(role, strips, info, anchor):
     tiles = strips.shape[0]
     packed = jax.ShapeDtypeStruct((tiles // 4 + 1, PATCH, 2 * WIDE), BF16)
     return pl.pallas_call(
         pack_kernel,
         name="pack",
-        in_specs=[SMEM, ANY, VMEM],
+        in_specs=[SMEM, ANY, VMEM, VMEM],
         out_specs=[VMEM] * 3,
         out_shape=[packed, packed, jax.ShapeDtypeStruct((NODES, LANES), F32)],
         scratch_shapes=[
@@ -462,20 +448,7 @@
         ],
         compiler_params=pltpu.CompilerParams(vmem_limit_bytes=VMEM_BYTES),
         cost_estimate=pl.CostEstimate(flops=0, bytes_accessed=6_000_000, transcendentals=0),
-    )(role, strips, anchor)
-
-
-def fill(next_top, info, across, within):
-    packed = jax.ShapeDtypeStruct(across.shape, BF16)
-    return pl.pallas_call(
-        fill_kernel,
-        name="fill",
-        in_specs=[VMEM, VMEM, ANY, ANY],
-        out_specs=[ANY, ANY],
-        out_shape=[packed, packed],
-        input_output_aliases={2: 0, 3: 1},
-        scratch_shapes=[pltpu.VMEM((PATCH, SIDE), BF16), pltpu.SemaphoreType.DMA((2,))],
-    )(next_top, info, across, within)
+    )(role, strips, info, anchor)
 
 
 def whole(kernel, outs, name, scratch=(), with_role=True):
@@ -659,7 +632,7 @@
     anchor_e1 = jnp.where(lane < COMP, turned, packed)
     anchor_w0 = from_west[40:72, :]
     last = tiles - 1
-    statics = next_top[0, :, SIDE : SIDE + LANES].astype(F32)
+    statics = next_top[0, :, SIDE:].astype(F32)
     outside_south = sum(pick_lane(statics[0:1], STATICS + k, last) for k in (3, 4, 5))
     anchor_south = sum(pick_lane(statics, STATICS + k, last) for k in (0, 1, 2))
     anchor_s0, anchor_s1 = anchor_south[:MESH_X], anchor_south[MESH_X:]
@@ -769,6 +742,14 @@
     return lax.ppermute(x, axis, [(i, i + by) for i in range(peers) if 0 <= i + by < peers])
 
 
+def diagonal(x):
+    rows, cols = lax.axis_size("row"), lax.axis_size("col")
+    pairs = [
+        ((r - 1) * cols + c + 1, r * cols + c) for r in range(1, rows) for c in range(cols - 1)
+    ]
+    return lax.ppermute(x, ("row", "col"), pairs)
+
+
 def swapped(x, axis, first):
     peers = lax.axis_size(axis)
     pairs = [(i, i + 1) for i in range(first, peers - 1, 2)]
@@ -804,23 +785,24 @@
     field = (TALL, LANES)
     within_role = (lax.axis_index("row") % 2).astype(jnp.int32).reshape(1)
     across_role = 1 - within_role
-    to_north, info = edge(
+    to_north, to_corner, info = edge(
         own, pair_counts[:, 0].T, pair_offsets[:, 0].T, tile_stiffness.T, anchor
     )
     next_top = shifted(to_north, "col", -1)
-    packed_across, packed_within, anchor_t = pack(within_role, own, anchor)
-    packed_across, packed_within = fill(next_top, info, packed_across, packed_within)
+    corner = diagonal(to_corner)
+    packed_across, packed_within, anchor_t = pack(within_role, own, info, anchor)
     strips_across = swapped(packed_across, "row", 1)
+    packed_within, next_top = lax.optimization_barrier((packed_within, next_top))
     strips_within = swapped(packed_within, "row", 0)
     tabs = tables()
     terms_south = south_terms(own, next_top, info, anchor_t, tabs)
     from_north = shifted(terms_south, "col", 1)
     message = whole(functools.partial(message_kernel, tiles), [(72, LANES)], "message")
-    terms_within = side_terms("within_pairs", within_role, own, strips_within, next_top, info, tabs)
+    terms_within = side_terms("within_pairs", within_role, own, strips_within, next_top, corner, info, tabs)
     (to_within,) = message(within_role, terms_within, terms_south, from_north, info, anchor_t)
     to_within, strips_across = lax.optimization_barrier((to_within, strips_across))
     within = swapped(to_within, "row", 0)
-    terms_across = side_terms("across_pairs", across_role, own, strips_across, next_top, info, tabs)
+    terms_across = side_terms("across_pairs", across_role, own, strips_across, next_top, corner, info, tabs)
     terms_across, within = lax.optimization_barrier((terms_across, within))
     (to_across,) = message(across_role, terms_across, terms_south, from_north, info, anchor_t)
     across = swapped(to_across, "row", 1)

time: 72.6 us -> 72.6 us (level)
  starting transfers between devices: 30.2 us -> 35 us
  local copies, waits for them, and re-layouts: 4.12 us -> 1.44 us
  Pallas kernels: 23.4 us -> 21.7 us
    ppermute x2, starting transfers between devices: 4.86 us -> 9.38 us  [shifted(): lax.ppermute(x, axis, [(i, i + by) for i in range(peers) if 0 <= i + by <...]
    ppermute x4, starting transfers between devices: 4.45 us -> 1.43 us  [swapped(): return lax.ppermute(x, axis, pairs + [(b, a) for a, b in pairs])]
    unnamed x28 -> x20, local copies, waits for them, and re-layouts: 3.43 us -> 0.75 us
    ppermute x10, starting transfers between devices: 20.9 us -> 23.6 us  [add_over(): lax.ppermute(x, axis, [(i, i ^ k * stride) for i in range(peers)])]
    pallas_call x4 -> x3, Pallas kernels: 11.9 us -> 10.3 us  [the longest x2 8.56 us: side_terms(): pair_call(side_kernel, name, half, 32, [SMEM, ANY, ANY, VMEM, VMEM, VMEM]...]
    ppermute x10, waiting for transfers between devices: 11.9 us -> 10.4 us  [add_over(): lax.ppermute(x, axis, [(i, i ^ k * stride) for i in range(peers)])]
    ppermute x2, waiting for transfers between devices: 1.61 us -> 2.6 us  [shifted(): lax.ppermute(x, axis, [(i, i + by) for i in range(peers) if 0 <= i + by <...]
  transfers between devices with their start and end apart: 16 -> 17, of which waited for: 8 -> 9; matrix products, arithmetic and copies ran while one was open for 1% -> 1% of each run, Pallas kernels for 24% -> 23%
where the time goes in v6:
time: 72.6 us; the launch traced here: 72.2 us
  starting transfers between devices  35 us (48%)
  Pallas kernels  21.7 us (30%)
  waiting for transfers between devices  13 us (18%)
  local copies, waits for them, and re-layouts  1.44 us (2%)
  between operations  0.94 us (1%)
    ppermute x10, starting transfers between devices, add_over(): lax.ppermute(x, axis, [(i, i ^ k * stride) for i in range(peers)])  23.6 us
    ppermute x10, waiting for transfers between devices, add_over(): lax.ppermute(x, axis, [(i, i ^ k * stride) for i in range(peers)])  10.4 us
    ppermute x2, starting transfers between devices, shifted(): lax.ppermute(x, axis, [(i, i + by) for i in range(peers) if 0 <= i + by <...  9.38 us
    pallas_call x2, Pallas kernels, side_terms(): pair_call(side_kernel, name, half, 32, [SMEM, ANY, ANY, VMEM, VMEM, VMEM]...  8.56 us
    pallas_call x1, Pallas kernels, south_terms(): pair_call(south_kernel, 'south_pairs', tiles, 64, [ANY, ANY, VMEM, VMEM],...  6.59 us
    pallas_call x4, Pallas kernels, call(): pl.pallas_call(kernel, name=name, in_specs=[SMEM] + [VMEM] * (len(args) -...  3.09 us
    ppermute x2, waiting for transfers between devices, shifted(): lax.ppermute(x, axis, [(i, i + by) for i in range(peers) if 0 <= i + by <...  2.6 us
    pallas_call x1, Pallas kernels, edge(): pl.pallas_call(edge_kernel, name='edge', in_specs=[ANY] * 5, out_specs=[V...  1.76 us
  transfers between devices with their start and end apart: 17, of which 9 were waited for; matrix products, arithmetic and copies ran while one was open for 1% of the time, Pallas kernels for 23%

profile of v6, /device:TPU:0, one launch (start us, length us, event | category | flops | bytes accessed | tf_op | source)
XLA Modules:
  0.0 72.2 jit_solution(577201661410318943)
XLA Ops:
  0.7 1.8 %edge.1 = (bf16[1,64,512]{2,1,0:T(8,128)(2,1)}, bf16[1,64,256]{2,1,0:T(8,128)(2,1)}, f32[16,128]{1,0:T(8,128)}) custom-call(bf16[40,4,64,512]{3,2,1,0:T(8,128)(2,1)} %bitcast.16, s32[2,40]{1,0:T(2,128)} %bitcast.22, s32[2,40]{1,0:T(2,128)} %bitcast.23, f32[1,40]{1,0:T(1,128)} %bitcast.24, f32[40,1,896]{2,1,0:T(1,128)} %anchor.3), custom_call_target="tpu_custom_call" | custom-call | tf_op jit(solution)/shard_map/edge/pallas_call | solution.py:413
  2.5 1.3 %collective-permute-start = (bf16[1,64,512]{2,1,0:T(8,128)(2,1)}, bf16[1,64,512]{2,1,0:T(8,128)(2,1)S(1)}, u32[]{:S(2)}, u32[]{:S(2)}) collective-permute-start(bf16[1,64,512]{2,1,0:T(8,128)(2,1)} %get-tuple-element.25), channel_id=1, source_target_pairs={{1,0},{2,1},{3,2},{5,4},{6,5},{7,6},{9,8},{10,9},{11,10},{13,12},{... | collective-permute-start | bytes 196616 | tf_op jit(solution)/shard_map/ppermute | solution.py:742
  3.8 0.7 copy-done.4
  4.5 1.7 %pack.1 = (bf16[11,64,640]{2,1,0:T(8,128)(2,1)S(1)}, bf16[11,64,640]{2,1,0:T(8,128)(2,1)S(1)}, f32[896,128]{1,0:T(8,128)S(1)}) custom-call(s32[1]{0:T(128)} %bitcast.role.refs_0_, bf16[40,4,64,512]{3,2,1,0:T(8,128)(2,1)} %bitcast.17, f32[16,128]{1,0:T(8,128)S(1)} %copy-done.4, f32[40,1,896]{2,1,0:T(1,128)S(1)} %copy-done.3), custom_call_target="tpu_custom_call" | custom-call | bytes 6000000 | tf_op jit(solution)/shard_map/pack/pallas_call | solution.py:438
  6.3 2.6 %collective-permute-done.nxt.next_top.refs_6_ = bf16[1,64,512]{2,1,0:T(8,128)(2,1)S(1)} collective-permute-done((bf16[1,64,512]{2,1,0:T(8,128)(2,1)}, bf16[1,64,512]{2,1,0:T(8,128)(2,1)S(1)}, u32[]{:S(2)}, u32[]{:S(2)}) %collective-permute-start) | collective-permute-done | bytes 65568 | tf_op jit(solution)/shard_map/ppermute | solution.py:742
  8.9 0.7 collective-permute-start.4
  9.6 0.7 collective-permute-start.2
  10.4 6.6 %south_pairs.1.terms_south.refs_1_ = f32[64,128]{1,0:T(8,128)S(1)} custom-call(bf16[40,4,64,512]{3,2,1,0:T(8,128)(2,1)} %bitcast.18, bf16[1,64,512]{2,1,0:T(8,128)(2,1)S(1)} %collective-permute-done.nxt.next_top.refs_6_, f32[16,128]{1,0:T(8,128)S(1)} %copy-done.4, f32[896,128]{1,0:T(8,128)S(1)} %get-tuple-element.27.anchor_t.refs_9_, ...), custom_call_target="tpu_custom_call" | custom-call | flops 2400000000 | bytes 3932160 | tf_op jit(solution)/shard_map/south_pairs/pallas_call | solution.py:324
  16.9 8.1 %collective-permute-start.3 = (f32[64,128]{1,0:T(8,128)S(1)}, f32[64,128]{1,0:T(8,128)S(1)}, u32[]{:S(2)}, u32[]{:S(2)}) collective-permute-start(f32[64,128]{1,0:T(8,128)S(1)} %south_pairs.1.terms_south.refs_1_), channel_id=1, source_target_pairs={{0,1},{1,2},{2,3},{4,5},{5,6},{6,7},{8,9},{9,10},{10,11},{12,13},{... | collective-permute-start | bytes 98312 | tf_op jit(solution)/shard_map/ppermute | solution.py:742
  25.1 4.3 %within_pairs.1.terms.refs_2_ = f32[32,128]{1,0:T(8,128)S(1)} custom-call(s32[1]{0:T(128)} %bitcast.role.refs_0_, bf16[40,4,64,512]{3,2,1,0:T(8,128)(2,1)} %bitcast.19, bf16[11,64,640]{2,1,0:T(8,128)(2,1)S(1)} %collective-permute-done.1.received, bf16[1,64,512]{2,1,0:T(8,128)(2,1)S(1)} %collective-permute-done.nxt.next_top.refs_6_, ...), custom_call_target="tpu_custom_call" | custom-call | flops 1200000000 | bytes 1966080 | tf_op jit(solution)/shard_map/within_pairs/pallas_call | solution.py:335
  29.5 4.3 %across_pairs.1.terms.refs_3_ = f32[32,128]{1,0:T(8,128)S(1)} custom-call(s32[1]{0:T(128)S(6)} %sub.3.role, bf16[40,4,64,512]{3,2,1,0:T(8,128)(2,1)} %bitcast.20, bf16[11,64,640]{2,1,0:T(8,128)(2,1)S(1)} %collective-permute-done.4.received, bf16[1,64,512]{2,1,0:T(8,128)(2,1)S(1)} %collective-permute-done.nxt.next_top.refs_6_, ...), custom_call_target="tpu_custom_call" | custom-call | flops 1200000000 | bytes 1966080 | tf_op jit(solution)/shard_map/across_pairs/pallas_call | solution.py:335
  33.9 0.7 collective-permute-start.6
  34.6 1.6 %powers.1 = (f32[1024,128]{1,0:T(8,128)S(1)}, f32[1024,128]{1,0:T(8,128)S(1)}, f32[1024,128]{1,0:T(8,128)S(1)}, f32[1024,128]{1,0:T(8,128)S(1)}, f32[40,48]{1,0:T(8,128)S(1)}, /*index=5*/f32[8,128]{1,0:T(8,128)S(1)}) custom-call(s32[1]{0:T(128)} %bitcast.role.refs_0_, f32[64,128]{1,0:T(8,128)S(1)} %south_pairs.1.terms_south.refs_1_, ...), custom_call_target="tpu_custom_call" | custom-call | flops 4000000 | bytes 2000000 | tf_op jit(solution)/shard_map/powers/pallas_call | solution.py:458
  36.1 5.1 %collective-permute-start.7 = (f32[8,128]{1,0:T(8,128)S(1)}, f32[8,128]{1,0:T(8,128)S(1)}, u32[]{:S(2)}, u32[]{:S(2)}) collective-permute-start(f32[8,128]{1,0:T(8,128)S(1)} %get-tuple-element.36), channel_id=1, source_target_pairs={{0,4},{4,0},{8,12},{12,8},{16,20},{20,16},{24,28},{28,24},{32,36},... | collective-permute-start | bytes 12296 | tf_op jit(solution)/shard_map/ppermute | solution.py:762
  41.3 0.8 %collective-permute-done.7 = f32[8,128]{1,0:T(8,128)S(1)} collective-permute-done((f32[8,128]{1,0:T(8,128)S(1)}, f32[8,128]{1,0:T(8,128)S(1)}, u32[]{:S(2)}, u32[]{:S(2)}) %collective-permute-start.7) | collective-permute-done | bytes 4128 | tf_op jit(solution)/shard_map/ppermute | solution.py:762
  42.1 7.6 %collective-permute-start.10 = (f32[8,128]{1,0:T(8,128)S(1)}, f32[8,128]{1,0:T(8,128)S(1)}, u32[]{:S(2)}, u32[]{:S(2)}) collective-permute-start(f32[8,128]{1,0:T(8,128)S(1)} %add.35), channel_id=1, source_target_pairs={{0,24},{4,28},{8,16},{12,20},{16,8},{20,12},{24,0},{28,4},{32,56},... | collective-permute-start | bytes 12296 | tf_op jit(solution)/shard_map/ppermute | solution.py:762
  49.7 1.5 %collective-permute-start.9 = (f32[8,128]{1,0:T(8,128)S(1)}, f32[8,128]{1,0:T(8,128)S(1)}, u32[]{:S(2)}, u32[]{:S(2)}) collective-permute-start(f32[8,128]{1,0:T(8,128)S(1)} %add.35), channel_id=1, source_target_pairs={{0,16},{4,20},{8,24},{12,28},{16,0},{20,4},{24,8},{28,12},{32,48},... | collective-permute-start | bytes 12296 | tf_op jit(solution)/shard_map/ppermute | solution.py:762
  51.1 0.1 collective-permute-done.10
  51.2 2.0 %collective-permute-done.8 = f32[8,128]{1,0:T(8,128)S(1)} collective-permute-done((f32[8,128]{1,0:T(8,128)S(1)}, f32[8,128]{1,0:T(8,128)S(1)}, u32[]{:S(2)}, u32[]{:S(2)}) %collective-permute-start.8) | collective-permute-done | bytes 4128 | tf_op jit(solution)/shard_map/ppermute | solution.py:762
  53.3 1.5 %collective-permute-done.9 = f32[8,128]{1,0:T(8,128)S(1)} collective-permute-done((f32[8,128]{1,0:T(8,128)S(1)}, f32[8,128]{1,0:T(8,128)S(1)}, u32[]{:S(2)}, u32[]{:S(2)}) %collective-permute-start.9) | collective-permute-done | bytes 4128 | tf_op jit(solution)/shard_map/ppermute | solution.py:762
  54.8 1.5 %collective-permute-start.11 = (f32[8,128]{1,0:T(8,128)S(1)}, f32[8,128]{1,0:T(8,128)S(1)}, u32[]{:S(2)}, u32[]{:S(2)}) collective-permute-start(f32[8,128]{1,0:T(8,128)S(1)} %add_add_fusion.2), channel_id=1, source_target_pairs={{0,32},{4,36},{8,40},{12,44},{16,48},{20,52},{24,56},{28,60},{32,0... | collective-permute-start | bytes 12296 | tf_op jit(solution)/shard_map/ppermute | solution.py:762
  56.3 1.6 %collective-permute-start.12 = (f32[8,128]{1,0:T(8,128)S(1)}, f32[8,128]{1,0:T(8,128)S(1)}, u32[]{:S(2)}, u32[]{:S(2)}) collective-permute-start(f32[8,128]{1,0:T(8,128)S(1)} %add_add_fusion.2), channel_id=1, source_target_pairs={{0,64},{4,68},{8,72},{12,76},{16,80},{20,84},{24,88},{28,92},{32,9... | collective-permute-start | bytes 12296 | tf_op jit(solution)/shard_map/ppermute | solution.py:762
  57.9 1.6 %collective-permute-start.13 = (f32[8,128]{1,0:T(8,128)S(1)}, f32[8,128]{1,0:T(8,128)S(1)}, u32[]{:S(2)}, u32[]{:S(2)}) collective-permute-start(f32[8,128]{1,0:T(8,128)S(1)} %add_add_fusion.2), channel_id=1, source_target_pairs={{0,96},{4,100},{8,104},{12,108},{16,112},{20,116},{24,120},{28,124... | collective-permute-start | bytes 12296 | tf_op jit(solution)/shard_map/ppermute | solution.py:762
  59.5 1.9 %collective-permute-done.12 = f32[8,128]{1,0:T(8,128)S(1)} collective-permute-done((f32[8,128]{1,0:T(8,128)S(1)}, f32[8,128]{1,0:T(8,128)S(1)}, u32[]{:S(2)}, u32[]{:S(2)}) %collective-permute-start.12) | collective-permute-done | bytes 4128 | tf_op jit(solution)/shard_map/ppermute | solution.py:762
  61.4 1.3 %collective-permute-done.13 = f32[8,128]{1,0:T(8,128)S(1)} collective-permute-done((f32[8,128]{1,0:T(8,128)S(1)}, f32[8,128]{1,0:T(8,128)S(1)}, u32[]{:S(2)}, u32[]{:S(2)}) %collective-permute-start.13) | collective-permute-done | bytes 4128 | tf_op jit(solution)/shard_map/ppermute | solution.py:762
  62.7 1.6 %collective-permute-start.14 = (f32[8,128]{1,0:T(8,128)S(1)}, f32[8,128]{1,0:T(8,128)S(1)}, u32[]{:S(2)}, u32[]{:S(2)}) collective-permute-start(f32[8,128]{1,0:T(8,128)S(1)} %add_add_fusion.1), channel_id=1, source_target_pairs={{0,1},{1,0},{2,3},{3,2},{4,5},{5,4},{6,7},{7,6},{8,9},{9,8},{10,11... | collective-permute-start | bytes 12296 | tf_op jit(solution)/shard_map/ppermute | solution.py:762
  64.3 1.7 %collective-permute-start.15 = (f32[8,128]{1,0:T(8,128)S(1)}, f32[8,128]{1,0:T(8,128)S(1)}, u32[]{:S(2)}, u32[]{:S(2)}) collective-permute-start(f32[8,128]{1,0:T(8,128)S(1)} %add_add_fusion.1), channel_id=1, source_target_pairs={{0,2},{1,3},{2,0},{3,1},{4,6},{5,7},{6,4},{7,5},{8,10},{9,11},{10,... | collective-permute-start | bytes 12296 | tf_op jit(solution)/shard_map/ppermute | solution.py:762
  66.0 1.4 %collective-permute-start.16 = (f32[8,128]{1,0:T(8,128)S(1)}, f32[8,128]{1,0:T(8,128)S(1)}, u32[]{:S(2)}, u32[]{:S(2)}) collective-permute-start(f32[8,128]{1,0:T(8,128)S(1)} %add_add_fusion.1), channel_id=1, source_target_pairs={{0,3},{1,2},{2,1},{3,0},{4,7},{5,6},{6,5},{7,4},{8,11},{9,10},{10,... | collective-permute-start | bytes 12296 | tf_op jit(solution)/shard_map/ppermute | solution.py:762
  67.4 0.7 copy.18
  68.1 1.3 %collective-permute-done.15 = f32[8,128]{1,0:T(8,128)S(1)} collective-permute-done((f32[8,128]{1,0:T(8,128)S(1)}, f32[8,128]{1,0:T(8,128)S(1)}, u32[]{:S(2)}, u32[]{:S(2)}) %collective-permute-start.15) | collective-permute-done | bytes 4128 | tf_op jit(solution)/shard_map/ppermute | solution.py:762
  69.4 1.4 %collective-permute-done.16 = f32[8,128]{1,0:T(8,128)S(1)} collective-permute-done((f32[8,128]{1,0:T(8,128)S(1)}, f32[8,128]{1,0:T(8,128)S(1)}, u32[]{:S(2)}, u32[]{:S(2)}) %collective-permute-start.16) | collective-permute-done | bytes 4128 | tf_op jit(solution)/shard_map/ppermute | solution.py:762
  70.8 1.4 %combine.1 = (f32[40,2,896]{2,1,0:T(2,128)}, f32[40,2,896]{2,1,0:T(2,128)}) custom-call(f32[8,128]{1,0:T(8,128)S(1)} %add_add_fusion.gram, f32[1024,128]{1,0:T(8,128)S(1)} %get-tuple-element.37.v0, f32[1024,128]{1,0:T(8,128)S(1)} %get-tuple-element.38.v1, f32[1024,128]{1,0:T(8,128)S(1)} %get-tuple-element.39.v2, f32[1024,128]{1,0:T(8,128)S(1)} %get-tuple-element.40.v3), custom_call_target="tpu_custom_call" | custom-call | flops 4000000 | bytes 2000000 | tf_op jit(solution)/shard_map/combine/pallas_call | solution.py:458
  (36 shorter events, 0.3 us)
Async XLA Ops:
  0.6 3.2 %copy-start.3 = (f32[40,1,896]{2,1,0:T(1,128)S(1)}, f32[40,1,896]{2,1,0:T(1,128)}, u32[]{:S(2)}) copy-start(f32[40,1,896]{2,1,0:T(1,128)} %anchor.3) | copy-start | bytes 430084
  0.6 9.6 %copy-start = (bf16[256,512]{1,0:T(8,128)(2,1)S(1)}, bf16[256,512]{1,0:T(8,128)(2,1)}, u32[]{:S(2)}) copy-start(bf16[256,512]{1,0:T(8,128)(2,1)} %constant.37.clone.ends) | copy-start | bytes 786436
  0.7 9.6 %copy-start.1 = (bf16[2,256,256]{2,1,0:T(8,128)(2,1)S(1)}, bf16[2,256,256]{2,1,0:T(8,128)(2,1)}, u32[]{:S(2)}) copy-start(bf16[2,256,256]{2,1,0:T(8,128)(2,1)} %constant.38.clone.backs) | copy-start | bytes 786436
  0.7 9.6 %copy-start.2 = (bf16[256,256]{1,0:T(8,128)(2,1)S(1)}, bf16[256,256]{1,0:T(8,128)(2,1)}, u32[]{:S(2)}) copy-start(bf16[256,256]{1,0:T(8,128)(2,1)} %constant.36.clone.forward) | copy-start | bytes 393220
  0.7 9.6 %copy-start.5 = (f32[64,128]{1,0:T(8,128)S(1)}, f32[64,128]{1,0:T(8,128)}, u32[]{:S(2)}) copy-start(f32[64,128]{1,0:T(8,128)} %constant.41.clone.rows) | copy-start | bytes 98308
  0.7 9.6 %copy-start.6 = (bf16[64,64]{1,0:T(8,128)(2,1)S(1)}, bf16[64,64]{1,0:T(8,128)(2,1)}, u32[]{:S(2)}) copy-start(bf16[64,64]{1,0:T(8,128)(2,1)} %constant.35.clone.depth) | copy-start | bytes 24580
  0.7 9.6 %copy-start.7 = (bf16[64,64]{1,0:T(8,128)(2,1)S(1)}, bf16[64,64]{1,0:T(8,128)(2,1)}, u32[]{:S(2)}) copy-start(bf16[64,64]{1,0:T(8,128)(2,1)} %constant.39.clone.final) | copy-start | bytes 24580
  0.7 9.6 %copy-start.8 = (f32[8,128]{1,0:T(8,128)S(1)}, f32[8,128]{1,0:T(8,128)}, u32[]{:S(2)}) copy-start(f32[8,128]{1,0:T(8,128)} %constant.40.clone.pick) | copy-start | bytes 12292
  2.5 7.1 %copy-start.9 = (bf16[1,64,256]{2,1,0:T(8,128)(2,1)S(1)}, bf16[1,64,256]{2,1,0:T(8,128)(2,1)}, u32[]{:S(2)}) copy-start(bf16[1,64,256]{2,1,0:T(8,128)(2,1)} %get-tuple-element.29) | copy-start | bytes 98308
  2.5 6.4 %collective-permute-start = (bf16[1,64,512]{2,1,0:T(8,128)(2,1)}, bf16[1,64,512]{2,1,0:T(8,128)(2,1)S(1)}, u32[]{:S(2)}, u32[]{:S(2)}) collective-permute-start(bf16[1,64,512]{2,1,0:T(8,128)(2,1)} %get-tuple-element.25), channel_id=1, source_target_pairs={{1,0},{2,1},{3,2},{5,4},{6,5},{7,6},{9,8},{10,9},{11,10},{13,12},{... | collective-permute-start | bytes 196616 | tf_op jit(solution)/shard_map/ppermute | solution.py:742
  3.8 0.7 copy-start.4
  8.9 16.2 %collective-permute-start.1 = (bf16[11,64,640]{2,1,0:T(8,128)(2,1)S(1)}, bf16[11,64,640]{2,1,0:T(8,128)(2,1)S(1)}, u32[]{:S(2)}, u32[]{:S(2)}) collective-permute-start(bf16[11,64,640]{2,1,0:T(8,128)(2,1)S(1)} %get-tuple-element.28), channel_id=1, source_target_pairs={{0,4},{8,12},{16,20},{24,28},{32,36},{40,44},{48,52},{56,60},{64,6... | collective-permute-start | bytes 2703368 | tf_op jit(solution)/shard_map/ppermute | solution.py:756
  8.9 20.5 %collective-permute-start.4 = (bf16[11,64,640]{2,1,0:T(8,128)(2,1)S(1)}, bf16[11,64,640]{2,1,0:T(8,128)(2,1)S(1)}, u32[]{:S(2)}, u32[]{:S(2)}) collective-permute-start(bf16[11,64,640]{2,1,0:T(8,128)(2,1)S(1)} %get-tuple-element.30), channel_id=1, source_target_pairs={{4,8},{12,16},{20,24},{28,32},{36,40},{44,48},{52,56},{60,64},{68,... | collective-permute-start | bytes 2703368 | tf_op jit(solution)/shard_map/ppermute | solution.py:756
  9.6 15.4 %collective-permute-start.2 = (bf16[1,64,256]{2,1,0:T(8,128)(2,1)S(1)}, bf16[1,64,256]{2,1,0:T(8,128)(2,1)S(1)}, u32[]{:S(2)}, u32[]{:S(2)}) collective-permute-start(bf16[1,64,256]{2,1,0:T(8,128)(2,1)S(1)} %copy-done.9), channel_id=1, source_target_pairs={{1,4},{2,5},{3,6},{5,8},{6,9},{7,10},{9,12},{10,13},{11,14},{13,16... | collective-permute-start | bytes 98312 | tf_op jit(solution)/shard_map/ppermute | solution.py:750
  16.9 12.4 %collective-permute-start.3 = (f32[64,128]{1,0:T(8,128)S(1)}, f32[64,128]{1,0:T(8,128)S(1)}, u32[]{:S(2)}, u32[]{:S(2)}) collective-permute-start(f32[64,128]{1,0:T(8,128)S(1)} %south_pairs.1.terms_south.refs_1_), channel_id=1, source_target_pairs={{0,1},{1,2},{2,3},{4,5},{5,6},{6,7},{8,9},{9,10},{10,11},{12,13},{... | collective-permute-start | bytes 98312 | tf_op jit(solution)/shard_map/ppermute | solution.py:742
  29.4 4.4 %collective-permute-start.5 = (f32[72,128]{1,0:T(8,128)S(1)}, f32[72,128]{1,0:T(8,128)S(1)}, u32[]{:S(2)}, u32[]{:S(2)}) collective-permute-start(f32[72,128]{1,0:T(8,128)S(1)} %message.2), channel_id=1, source_target_pairs={{0,4},{8,12},{16,20},{24,28},{32,36},{40,44},{48,52},{56,60},{64,6... | collective-permute-start | bytes 110600 | tf_op jit(solution)/shard_map/ppermute | solution.py:756
  33.9 0.7 collective-permute-start.6
  36.1 6.0 %collective-permute-start.7 = (f32[8,128]{1,0:T(8,128)S(1)}, f32[8,128]{1,0:T(8,128)S(1)}, u32[]{:S(2)}, u32[]{:S(2)}) collective-permute-start(f32[8,128]{1,0:T(8,128)S(1)} %get-tuple-element.36), channel_id=1, source_target_pairs={{0,4},{4,0},{8,12},{12,8},{16,20},{20,16},{24,28},{28,24},{32,36},... | collective-permute-start | bytes 12296 | tf_op jit(solution)/shard_map/ppermute | solution.py:762
  42.1 9.1 %collective-permute-start.10 = (f32[8,128]{1,0:T(8,128)S(1)}, f32[8,128]{1,0:T(8,128)S(1)}, u32[]{:S(2)}, u32[]{:S(2)}) collective-permute-start(f32[8,128]{1,0:T(8,128)S(1)} %add.35), channel_id=1, source_target_pairs={{0,24},{4,28},{8,16},{12,20},{16,8},{20,12},{24,0},{28,4},{32,56},... | collective-permute-start | bytes 12296 | tf_op jit(solution)/shard_map/ppermute | solution.py:762
  49.6 3.6 %collective-permute-start.8 = (f32[8,128]{1,0:T(8,128)S(1)}, f32[8,128]{1,0:T(8,128)S(1)}, u32[]{:S(2)}, u32[]{:S(2)}) collective-permute-start(f32[8,128]{1,0:T(8,128)S(1)} %add.35), channel_id=1, source_target_pairs={{0,8},{4,12},{8,0},{12,4},{16,24},{20,28},{24,16},{28,20},{32,40},... | collective-permute-start | bytes 12296 | tf_op jit(solution)/shard_map/ppermute | solution.py:762
  49.7 5.1 %collective-permute-start.9 = (f32[8,128]{1,0:T(8,128)S(1)}, f32[8,128]{1,0:T(8,128)S(1)}, u32[]{:S(2)}, u32[]{:S(2)}) collective-permute-start(f32[8,128]{1,0:T(8,128)S(1)} %add.35), channel_id=1, source_target_pairs={{0,16},{4,20},{8,24},{12,28},{16,0},{20,4},{24,8},{28,12},{32,48},... | collective-permute-start | bytes 12296 | tf_op jit(solution)/shard_map/ppermute | solution.py:762
  54.8 4.7 %collective-permute-start.11 = (f32[8,128]{1,0:T(8,128)S(1)}, f32[8,128]{1,0:T(8,128)S(1)}, u32[]{:S(2)}, u32[]{:S(2)}) collective-permute-start(f32[8,128]{1,0:T(8,128)S(1)} %add_add_fusion.2), channel_id=1, source_target_pairs={{0,32},{4,36},{8,40},{12,44},{16,48},{20,52},{24,56},{28,60},{32,0... | collective-permute-start | bytes 12296 | tf_op jit(solution)/shard_map/ppermute | solution.py:762
  56.3 5.1 %collective-permute-start.12 = (f32[8,128]{1,0:T(8,128)S(1)}, f32[8,128]{1,0:T(8,128)S(1)}, u32[]{:S(2)}, u32[]{:S(2)}) collective-permute-start(f32[8,128]{1,0:T(8,128)S(1)} %add_add_fusion.2), channel_id=1, source_target_pairs={{0,64},{4,68},{8,72},{12,76},{16,80},{20,84},{24,88},{28,92},{32,9... | collective-permute-start | bytes 12296 | tf_op jit(solution)/shard_map/ppermute | solution.py:762
  57.9 4.8 %collective-permute-start.13 = (f32[8,128]{1,0:T(8,128)S(1)}, f32[8,128]{1,0:T(8,128)S(1)}, u32[]{:S(2)}, u32[]{:S(2)}) collective-permute-start(f32[8,128]{1,0:T(8,128)S(1)} %add_add_fusion.2), channel_id=1, source_target_pairs={{0,96},{4,100},{8,104},{12,108},{16,112},{20,116},{24,120},{28,124... | collective-permute-start | bytes 12296 | tf_op jit(solution)/shard_map/ppermute | solution.py:762
  62.7 5.4 %collective-permute-start.14 = (f32[8,128]{1,0:T(8,128)S(1)}, f32[8,128]{1,0:T(8,128)S(1)}, u32[]{:S(2)}, u32[]{:S(2)}) collective-permute-start(f32[8,128]{1,0:T(8,128)S(1)} %add_add_fusion.1), channel_id=1, source_target_pairs={{0,1},{1,0},{2,3},{3,2},{4,5},{5,4},{6,7},{7,6},{8,9},{9,8},{10,11... | collective-permute-start | bytes 12296 | tf_op jit(solution)/shard_map/ppermute | solution.py:762
  64.3 5.1 %collective-permute-start.15 = (f32[8,128]{1,0:T(8,128)S(1)}, f32[8,128]{1,0:T(8,128)S(1)}, u32[]{:S(2)}, u32[]{:S(2)}) collective-permute-start(f32[8,128]{1,0:T(8,128)S(1)} %add_add_fusion.1), channel_id=1, source_target_pairs={{0,2},{1,3},{2,0},{3,1},{4,6},{5,7},{6,4},{7,5},{8,10},{9,11},{10,... | collective-permute-start | bytes 12296 | tf_op jit(solution)/shard_map/ppermute | solution.py:762
  66.0 4.8 %collective-permute-start.16 = (f32[8,128]{1,0:T(8,128)S(1)}, f32[8,128]{1,0:T(8,128)S(1)}, u32[]{:S(2)}, u32[]{:S(2)}) collective-permute-start(f32[8,128]{1,0:T(8,128)S(1)} %add_add_fusion.1), channel_id=1, source_target_pairs={{0,3},{1,2},{2,1},{3,0},{4,7},{5,6},{6,5},{7,4},{8,11},{9,10},{10,... | collective-permute-start | bytes 12296 | tf_op jit(solution)/shard_map/ppermute | solution.py:762

commit v7 on v5

--- a/solution.py
+++ b/solution.py
@@ -88,7 +88,7 @@
     return real, imag
 
 
-def correlate_group(cols, depth, forward, ends, back, final, rows, r0, r1, at):
+def correlate_group(cols, depth, forward, ends, back, final, rows, r0, r1, at, extra=None):
     count = len(cols)
     half = count // 2
     lanes = [slice(LANES * i, LANES * (i + 1)) for i in range(count)]
@@ -146,8 +146,8 @@
         moment = jnp.sum(power * rows, axis=0, keepdims=True)
         place = i % 5
         if i == 5 * (half // 5):
-            r0[0, EXTRA : EXTRA + 1, :] = total
-            r1[0, EXTRA : EXTRA + 1, :] = moment
+            r0[0, pl.ds(extra, 1), :] = total
+            r1[0, pl.ds(extra, 1), :] = moment
         elif place < 4:
             row = at + 2 * (i // 5) + place // 2
             r0[place % 2, pl.ds(row, 1), :] = total
@@ -166,7 +166,8 @@
 
 def finish_terms(pick, r0, r1, counts, offsets, out):
     scale = 1.0 / float(PATCH * PATCH) ** 2
-    even = lax.broadcasted_iota(jnp.int32, (1, LANES), 1) % 2 == 0
+    lane = lax.broadcasted_iota(jnp.int32, (1, LANES), 1)
+    even = lane % 2 == 0
     plain = [lane_sums(pick, r0[s]) for s in range(3)]
     tilted = [lane_sums(pick, r1[s]) for s in range(3)]
     out[...] = jnp.zeros_like(out)
@@ -181,6 +182,10 @@
             along = jnp.where(even, plain[2][2:3], plain[2][3:4])
             deep = jnp.where(even, tilted[2][0:1], tilted[2][1:2])
         valid = counts > float(k) + 0.5
+        if k < 2:
+            valid = valid | (lane == EXTRA + 1)
+        if k == 1:
+            valid = valid | (lane == EXTRA)
         weight = weight * scale
         inverse = scale / (weight + SMALL_WEIGHT)
         out[k : k + 1, :] = jnp.where(valid, weight, 0.0)
@@ -189,7 +194,7 @@
     out[24:25, :] = offsets
 
 
-def south_kernel(strips, nxt, info, anchor_t, depth, forward, ends, backs, final, pick, rows, out, first, second, r0, r1, sems, last_sem):
+def south_kernel(strips, nxt, info, depth, forward, ends, backs, final, pick, rows, out, first, second, r0, r1, sems, last_sem):
     tiles = first.shape[0]
     steps = tiles // GROUP
     side = pl.ds(0, SIDE)
@@ -239,11 +244,9 @@
 
     lax.fori_loop(0, steps, step, 0)
     finish_terms(pick[...], r0, r1, info[2:3, :], info[3:4, :], out)
-    out[25:26, :] = info[4:5, :]
-    out[32:, :] = anchor_t[NODES - MESH_X : NODES, :]
-
-
-def side_kernel(role, strips, received, next_top, info, depth, forward, ends, backs, final, pick, rows, out, own, other, r0, r1, sems, extra_sem):
+
+
+def side_kernel(part, role, strips, received, next_top, last_bottom, info, depth, forward, ends, backs, final, pick, rows, out, own, other, top, columns, r0, r1, sems, extra_sems):
     half = own.shape[0]
     steps = half // GROUP
     slots = GROUP // 2
@@ -259,15 +262,28 @@
         at = pl.ds(slots * c, slots)
         return pltpu.make_async_copy(received.at[at], other.at[at], sems.at[1, c])
 
-    extra_copy = pltpu.make_async_copy(received.at[spare], other.at[spare], extra_sem)
+    extra_copies = (
+        pltpu.make_async_copy(received.at[spare], other.at[spare], extra_sems.at[0]),
+        pltpu.make_async_copy(strips.at[0, 1, :, pl.ds(0, SIDE)], top, extra_sems.at[1]),
+    )
     for c in range(steps):
         own_copy(c).start()
         other_copy(c).start()
         if c == 0:
-            extra_copy.start()
+            for copy in extra_copies:
+                copy.start()
     r0[...] = jnp.zeros_like(r0)
     r1[...] = jnp.zeros_like(r1)
-    extra_copy.wait()
+    for copy in extra_copies:
+        copy.wait()
+    swapped_order = west == 1
+    here, above = top[:, :WIDE], last_bottom[0, :, :WIDE]
+    mine, theirs = jnp.where(swapped_order, here, above), jnp.where(swapped_order, above, here)
+    two = slice(part * LANES, (part + 1) * LANES)
+    columns[0, 0] = jnp.concatenate([next_top[0, :, SIDE : SIDE + COMP], mine[:, 4 * PATCH :]], axis=1)
+    columns[0, 1] = jnp.concatenate([other[spare, :, :COMP], theirs[:, 4 * PATCH :]], axis=1)
+    columns[1, 0] = mine[:, two]
+    columns[1, 1] = theirs[:, two]
 
     def step(c, carry):
         own_copy(c).wait()
@@ -277,8 +293,8 @@
             other[slots * c + slot, :, LANES * i : LANES * (i + 1)] for slot in range(slots) for i in range(5)
         ]
         correlate_group(
-            owns + [next_top[0, :, SIDE : SIDE + LANES]] + others + [other[spare, :, :LANES]],
-            depth[...], forward[...], ends[...], backs[west], final[...], rows[...], r0, r1, base + GROUP * c,
+            owns + [columns[c, 0]] + others + [columns[c, 1]],
+            depth[...], forward[...], ends[...], backs[west], final[...], rows[...], r0, r1, base + GROUP * c, EXTRA + c,
         )
         return carry
 
@@ -316,45 +332,59 @@
     )
 
 
-def south_terms(strips, nxt, info, anchor_t, tabs):
+def south_terms(strips, nxt, info, tabs):
     tiles = strips.shape[0]
     buffers = [pltpu.VMEM((tiles, PATCH, SIDE), BF16)] * 2
     return pair_call(
-        south_kernel, "south_pairs", tiles, 64, [ANY, ANY, VMEM, VMEM], buffers, [pltpu.SemaphoreType.DMA]
-    )(strips, nxt, info, anchor_t, *tabs)
-
-
-def side_terms(name, role, strips, received, next_top, info, tabs):
+        south_kernel, "south_pairs", tiles, 32, [ANY, VMEM, VMEM], buffers, [pltpu.SemaphoreType.DMA]
+    )(strips, nxt, info, *tabs)
+
+
+def side_terms(name, part, role, strips, received, next_top, last_bottom, info, tabs):
     half = strips.shape[0] // 2
     buffers = [
         pltpu.VMEM((half, PATCH, SIDE), BF16),
         pltpu.VMEM((half // 2 + 1, PATCH, 2 * WIDE), BF16),
+        pltpu.VMEM((PATCH, SIDE), BF16),
+        pltpu.VMEM((2, 2, PATCH, LANES), BF16),
     ]
     return pair_call(
-        side_kernel, name, half, 32, [SMEM, ANY, ANY, VMEM, VMEM], buffers, [pltpu.SemaphoreType.DMA]
-    )(role, strips, received, next_top, info, *tabs)
+        functools.partial(side_kernel, part),
+        name,
+        half,
+        32,
+        [SMEM, ANY, ANY, VMEM, VMEM, VMEM],
+        buffers,
+        [pltpu.SemaphoreType.DMA((2,))],
+    )(role, strips, received, next_top, last_bottom, info, *tabs)
 
 
 STATICS = COMP
+MESSAGE = (1, PATCH, 2 * WIDE)
 
 
 def pieces(x):
     high = x.astype(BF16).astype(F32)
     middle = (x - high).astype(BF16).astype(F32)
-    return high, middle, x - high - middle
-
-
-def edge_kernel(strips, counts, offsets, stiffness, anchor, north, info, left, count_s, offset_s, stiff_s, anchor_s, turn, sems):
+    return [high, middle, x - high - middle]
+
+
+def edge_kernel(col_role, strips, counts, offsets, stiffness, anchor, one, two, info, left, count_s, offset_s, stiff_s, anchor_s, turn, sems):
     tiles = counts.shape[1]
     lanes = pl.ds(0, LANES)
-    copies = [
-        (strips.at[0, 1, :, pl.ds(0, SIDE)], north.at[0, :, pl.ds(0, SIDE)]),
-        (strips.at[0, 3, :, lanes], north.at[0, :, pl.ds(4 * LANES, LANES)]),
+    even = 1 - col_role[0]
+    right = strips.at[0, 3, :, lanes]
+    copies = [(right, out.at[0, :, pl.ds(4 * LANES, LANES)]) for out in (one, two)]
+    for out, south in ((one, even), (two, 1 - even)):
+        strip = strips.at[(tiles - 1) * south, 1 + south, :, pl.ds(0, SIDE)]
+        copies.append((strip, out.at[0, :, pl.ds(0, SIDE)]))
+    copies += [
         (strips.at[0, 0, :, lanes], left),
         (counts, count_s),
         (offsets, offset_s),
         (stiffness, stiff_s),
-        (anchor.at[0], anchor_s),
+        (anchor.at[0], anchor_s.at[0]),
+        (anchor.at[tiles - 1], anchor_s.at[1]),
     ]
     copies = [pltpu.make_async_copy(a, b, sems.at[k]) for k, (a, b) in enumerate(copies)]
     for copy in copies:
@@ -369,14 +399,24 @@
     info[2:3, here] = count_s[1:2, :].astype(F32)
     info[3:4, here] = offset_s[1:2, :].astype(F32)
     info[4:5, here] = stiff_s[...]
-    turn[0:1, :] = anchor_s[0:1, lanes]
-    columns = list(pieces(turn[...].T[0:PATCH, 0:1])) + list(pieces(info[4:5, 0:1]))
-    columns += [info[0:1, 0:1], info[1:2, 0:1]]
+    turn[0:1, :] = anchor_s[0, 0:1, lanes]
+    turn[1:2, :] = anchor_s[1, 0:1, pl.ds(NODES - LANES, LANES)]
+    turned = turn[...].T
+    first, last = slice(0, 1), slice(tiles - 1, tiles)
+    bottom_row = jnp.concatenate([turned[LANES - MESH_X :, 1:2], turned[: PATCH - MESH_X, 2:3]], axis=0)
+    north = pieces(turned[:PATCH, 0:1]) + pieces(info[4:5, first]) + [info[0:1, first], info[1:2, first]]
+    south = pieces(bottom_row) + pieces(info[4:5, last]) + [info[2:3, last], info[3:4, last]]
     lane = lax.broadcasted_iota(jnp.int32, (PATCH, LANES), 1)
     block = jnp.where(lane < COMP, left[...].astype(F32), 0.0)
-    for k, x in enumerate(columns):
-        block = jnp.where(lane == STATICS + k, x, block)
-    north[0, :, SIDE : SIDE + LANES] = block.astype(BF16)
+    blocks = []
+    for columns in (south, north):
+        filled = block
+        for k, x in enumerate(columns):
+            filled = jnp.where(lane == STATICS + k, x, filled)
+        blocks.append(filled)
+    own = pl.ds(SIDE, LANES)
+    one[0, :, own] = jnp.where(even == 1, blocks[0], blocks[1]).astype(BF16)
+    two[0, :, own] = jnp.where(even == 1, blocks[1], blocks[0]).astype(BF16)
 
 
 def pack_kernel(role, strips, anchor, across, within, anchor_t, buffers, wide, sems):
@@ -398,10 +438,12 @@
             columns = block_pairs([buffers[k, 2 * slot + j, :, :WIDE] for j in range(2)])
             for i, x in enumerate(columns):
                 packed[slot, :, LANES * i : LANES * (i + 1)] = x
-        packed[half // 2] = jnp.zeros((PATCH, 2 * WIDE), BF16)
-
-
-def fill_kernel(next_top, info, across_in, within_in, across, within, slot, sems):
+
+
+def fill_kernel(col_role, one, two, info, across_in, within_in, next_top, last_bottom, across, within):
+    even = col_role[0] == 0
+    next_top[...] = jnp.where(even, one[...], two[...])
+    last_bottom[...] = jnp.where(even, two[...], one[...])
     spare = across.shape[0] - 1
     lane = lax.broadcasted_iota(jnp.int32, (16, LANES), 1)
     row = lax.broadcasted_iota(jnp.int32, (16, LANES), 0)
@@ -409,41 +451,31 @@
     count = pltpu.roll(statics, (EXTRA - STATICS - 6) % LANES, axis=1)
     offset = pltpu.roll(statics, (EXTRA - STATICS - 7) % LANES, axis=1)
     facts = jnp.where(lane == EXTRA, jnp.where(row == 0, count, offset), info[...])
-    slot[...] = jnp.zeros_like(slot)
-    slot[:, 0:LANES] = next_top[0, :, 4 * LANES :]
-    slot[0:16, 2 * LANES : 3 * LANES] = facts.astype(BF16)
-    copies = [
-        pltpu.make_async_copy(slot, packed.at[spare, :, pl.ds(0, SIDE)], sems.at[k])
-        for k, packed in enumerate((across, within))
-    ]
-    for copy in copies:
-        copy.start()
-    for copy in copies:
-        copy.wait()
-
-
-def edge(strips, counts, offsets, stiffness, anchor):
+    for packed in (across, within):
+        packed[spare] = jnp.zeros((PATCH, 2 * WIDE), BF16)
+        packed[spare, :, 0:LANES] = next_top[0, :, 4 * LANES :]
+        packed[spare, 0:16, 2 * LANES : 3 * LANES] = facts.astype(BF16)
+
+
+def edge(col_role, strips, counts, offsets, stiffness, anchor):
     tiles = strips.shape[0]
-    dma = pltpu.SemaphoreType.DMA
+    message = jax.ShapeDtypeStruct(MESSAGE, BF16)
     return pl.pallas_call(
         edge_kernel,
         name="edge",
-        in_specs=[ANY] * 5,
-        out_specs=[VMEM] * 2,
-        out_shape=[
-            jax.ShapeDtypeStruct((1, PATCH, 2 * WIDE), BF16),
-            jax.ShapeDtypeStruct((16, LANES), F32),
-        ],
+        in_specs=[SMEM] + [ANY] * 5,
+        out_specs=[VMEM] * 3,
+        out_shape=[message, message, jax.ShapeDtypeStruct((16, LANES), F32)],
         scratch_shapes=[
             pltpu.VMEM((PATCH, LANES), BF16),
             pltpu.VMEM((2, tiles), jnp.int32),
             pltpu.VMEM((2, tiles), jnp.int32),
             pltpu.VMEM((1, tiles), F32),
-            pltpu.VMEM((1, NODES), F32),
+            pltpu.VMEM((2, 1, NODES), F32),
             pltpu.VMEM((LANES, LANES), F32),
-            dma((7,)),
+            pltpu.SemaphoreType.DMA((10,)),
         ],
-    )(strips, counts, offsets, stiffness, anchor)
+    )(col_role, strips, counts, offsets, stiffness, anchor)
 
 
 def pack(role, strips, anchor):
@@ -465,17 +497,18 @@
     )(role, strips, anchor)
 
 
-def fill(next_top, info, across, within):
+def fill(col_role, one, two, info, across, within):
     packed = jax.ShapeDtypeStruct(across.shape, BF16)
+    message = jax.ShapeDtypeStruct(MESSAGE, BF16)
     return pl.pallas_call(
         fill_kernel,
         name="fill",
-        in_specs=[VMEM, VMEM, ANY, ANY],
-        out_specs=[ANY, ANY],
-        out_shape=[packed, packed],
-        input_output_aliases={2: 0, 3: 1},
-        scratch_shapes=[pltpu.VMEM((PATCH, SIDE), BF16), pltpu.SemaphoreType.DMA((2,))],
-    )(next_top, info, across, within)
+        in_specs=[SMEM] + [VMEM] * 5,
+        out_specs=[VMEM] * 4,
+        out_shape=[message, message, packed, packed],
+        input_output_aliases={4: 2, 5: 3},
+        compiler_params=pltpu.CompilerParams(vmem_limit_bytes=VMEM_BYTES),
+    )(col_role, one, two, info, across, within)
 
 
 def whole(kernel, outs, name, scratch=(), with_role=True):
@@ -574,11 +607,11 @@
     return jnp.sum(a[0:NODES, :] * b[0:NODES, :], axis=0, keepdims=True)
 
 
-def message_kernel(tiles, role, terms, terms_south, from_north, info, anchor_t, out):
+def message_kernel(tiles, role, terms, terms_within, terms_south, last_bottom, info, anchor_t, out):
     lane = lax.broadcasted_iota(jnp.int32, (1, LANES), 1)
     out[0:32, :] = terms[...]
     out[25:26, :] = info[4:5, :]
-    north = roll_tiles(terms_south[0:32, :], 1, from_north[0:32, :], tiles)
+    north = north_terms(terms_south[...], terms_within[...], terms_within[...], bottom_statics(last_bottom))
     out[32:40, :] = jnp.zeros((8, LANES), F32)
     for k, row in enumerate((0, 8, 16, 24)):
         out[32 + k : 33 + k, :] = north[row : row + 1]
@@ -588,13 +621,29 @@
     out[40 + MESH_Y :, :] = jnp.zeros((MESH_X - MESH_Y, LANES), F32)
 
 
-def roll_tiles(x, by, outside, tiles):
-    lane = lax.broadcasted_iota(jnp.int32, (1, LANES), 1) % COMP
-    if by == 1:
-        edge, beyond = lane == 0, pltpu.roll(outside, LANES - (tiles - 1), axis=1)
-    else:
-        edge, beyond = lane == tiles - 1, pltpu.roll(outside, tiles - 1, axis=1)
-    return jnp.where(edge, beyond, pltpu.roll(x, by % LANES, axis=1))
+def bottom_statics(last_bottom):
+    return last_bottom[0, :, SIDE : SIDE + LANES].astype(F32)
+
+
+def north_terms(south, within, across, statics):
+    lane = lax.broadcasted_iota(jnp.int32, (32, LANES), 1)
+    row = lax.broadcasted_iota(jnp.int32, (32, LANES), 0)
+    block = row % 8
+    to_front = lambda x, source: pltpu.roll(x, LANES - source, axis=1)
+    first = jnp.where(
+        block < 2,
+        to_front(within, EXTRA + 1),
+        jnp.where(
+            block < 4,
+            pltpu.roll(to_front(across, EXTRA + 1), 2, axis=0),
+            pltpu.roll(to_front(within, EXTRA), 3, axis=0),
+        ),
+    )
+    count = to_front(statics[0:1], STATICS + 6)
+    offset = to_front(statics[0:1], STATICS + 7)
+    first = jnp.where((row < 24) & (block < MOST) & (block.astype(F32) < count), first, 0.0)
+    first = jnp.where(row == 24, offset, first)
+    return jnp.where(lane == 0, first, pltpu.roll(south, 1, axis=1))
 
 
 def pick_lane(x, source, target):
@@ -617,7 +666,7 @@
 
 
 def mesh_kernel(tiles, *refs):
-    role, terms_south, terms_within, terms_across, within, across, next_top, from_north, info, anchor_t = refs[:10]
+    role, terms_south, terms_within, terms_across, within, across, next_top, last_bottom, info, anchor_t = refs[:10]
     v0, v1, v2, v3, match, gram, flip = refs[10:]
     within_is_east = role[0] == 0
     from_east = jnp.where(within_is_east, within[...], across[...])
@@ -631,7 +680,7 @@
         jnp.where(low, side, from_east[0:32, :]),
         jnp.where(low, from_west[0:32, :], side),
         south_terms,
-        roll_tiles(south_terms, 1, from_north[0:32, :], tiles),
+        north_terms(south_terms, terms_within[...], terms_across[...], bottom_statics(last_bottom)),
     ]
     tables_here = []
     for q, table in enumerate(terms):
@@ -663,8 +712,9 @@
     outside_south = sum(pick_lane(statics[0:1], STATICS + k, last) for k in (3, 4, 5))
     anchor_south = sum(pick_lane(statics, STATICS + k, last) for k in (0, 1, 2))
     anchor_s0, anchor_s1 = anchor_south[:MESH_X], anchor_south[MESH_X:]
-    outside_north = pick_lane(from_north[25:26, :], last, 0)
-    anchor_n0 = pick_lane(from_north[32:64, :], last, 0)
+    statics = bottom_statics(last_bottom)
+    outside_north = sum(pick_lane(statics[0:1], STATICS + k, 0) for k in (3, 4, 5))
+    anchor_n0 = sum(pick_lane(statics[:MESH_X], STATICS + k, 0) for k in (0, 1, 2))
 
     degree_c = jnp.where((node == 0) | (node == MESH_Y - 1), 2.0, 3.0)
     degree_r = jnp.where((node == 0) | (node == MESH_X - 1), 2.0, 3.0)
@@ -804,32 +854,42 @@
     field = (TALL, LANES)
     within_role = (lax.axis_index("row") % 2).astype(jnp.int32).reshape(1)
     across_role = 1 - within_role
-    to_north, info = edge(
-        own, pair_counts[:, 0].T, pair_offsets[:, 0].T, tile_stiffness.T, anchor
-    )
-    next_top = shifted(to_north, "col", -1)
+    col_role = (lax.axis_index("col") % 2).astype(jnp.int32).reshape(1)
+    one, two, info = edge(
+        col_role, own, pair_counts[:, 0].T, pair_offsets[:, 0].T, tile_stiffness.T, anchor
+    )
+    one, two = swapped(one, "col", 0), swapped(two, "col", 1)
     packed_across, packed_within, anchor_t = pack(within_role, own, anchor)
-    packed_across, packed_within = fill(next_top, info, packed_across, packed_within)
+    next_top, last_bottom, packed_across, packed_within = fill(
+        col_role, one, two, info, packed_across, packed_within
+    )
     strips_across = swapped(packed_across, "row", 1)
     strips_within = swapped(packed_within, "row", 0)
     tabs = tables()
-    terms_south = south_terms(own, next_top, info, anchor_t, tabs)
-    from_north = shifted(terms_south, "col", 1)
+    terms_south = south_terms(own, next_top, info, tabs)
     message = whole(functools.partial(message_kernel, tiles), [(72, LANES)], "message")
-    terms_within = side_terms("within_pairs", within_role, own, strips_within, next_top, info, tabs)
-    (to_within,) = message(within_role, terms_within, terms_south, from_north, info, anchor_t)
+    terms_within = side_terms(
+        "within_pairs", 0, within_role, own, strips_within, next_top, last_bottom, info, tabs
+    )
+    (to_within,) = message(
+        within_role, terms_within, terms_within, terms_south, last_bottom, info, anchor_t
+    )
     to_within, strips_across = lax.optimization_barrier((to_within, strips_across))
     within = swapped(to_within, "row", 0)
-    terms_across = side_terms("across_pairs", across_role, own, strips_across, next_top, info, tabs)
+    terms_across = side_terms(
+        "across_pairs", 1, across_role, own, strips_across, next_top, last_bottom, info, tabs
+    )
     terms_across, within = lax.optimization_barrier((terms_across, within))
-    (to_across,) = message(across_role, terms_across, terms_south, from_north, info, anchor_t)
+    (to_across,) = message(
+        across_role, terms_across, terms_within, terms_south, last_bottom, info, anchor_t
+    )
     across = swapped(to_across, "row", 1)
     v0, v1, v2, v3, match, gram = whole(
         functools.partial(mesh_kernel, tiles),
         [field, field, field, field, (tiles, 48), (8, LANES)],
         "powers",
         [pltpu.VMEM((LANES, LANES), F32)],
-    )(within_role, terms_south, terms_within, terms_across, within, across, next_top, from_north, info, anchor_t)
+    )(within_role, terms_south, terms_within, terms_across, within, across, next_top, last_bottom, info, anchor_t)
     gram = sum_everywhere(gram)
     positions, residual = whole(
         functools.partial(final_kernel, tiles),

time: 72.6 us -> 70.4 us (0.970)
  local copies, waits for them, and re-layouts: 4.12 us -> 0.74 us
  starting transfers between devices: 30.2 us -> 33.1 us
  Pallas kernels: 23.4 us -> 22.4 us
    ppermute x10, starting transfers between devices: 20.9 us -> 25.9 us  [add_over(): lax.ppermute(x, axis, [(i, i ^ k * stride) for i in range(peers)])]
    ppermute x2 -> x0, starting transfers between devices: 4.86 us -> none  [shifted(): lax.ppermute(x, axis, [(i, i + by) for i in range(peers) if 0 <= i + by <...]
    unnamed x28 -> x18, local copies, waits for them, and re-layouts: 3.43 us -> 0.06 us
    ppermute x4 -> x6, starting transfers between devices: 4.45 us -> 7.21 us  [swapped(): return lax.ppermute(x, axis, pairs + [(b, a) for a, b in pairs])]
    ppermute x2 -> x0, waiting for transfers between devices: 1.61 us -> none  [shifted(): lax.ppermute(x, axis, [(i, i + by) for i in range(peers) if 0 <= i + by <...]
    pallas_call x5, Pallas kernels: 18.6 us -> 17.6 us  [the longest x2 8.95 us: side_terms(): pair_call(functools.partial(side_kernel, part), name, half, 32, [SMEM, AN...]
  transfers between devices with their start and end apart: 16 -> 16, of which waited for: 8 -> 8; matrix products, arithmetic and copies ran while one was open for 1% -> 1% of each run, Pallas kernels for 24% -> 25%
where the time goes in v7:
time: 70.4 us; the launch traced here: 70.1 us
  starting transfers between devices  33.1 us (47%)
  Pallas kernels  22.4 us (32%)
  waiting for transfers between devices  12.9 us (18%)
  between operations  0.91 us (1%)
  local copies, waits for them, and re-layouts  0.74 us (1%)
    ppermute x10, starting transfers between devices, add_over(): lax.ppermute(x, axis, [(i, i ^ k * stride) for i in range(peers)])  25.9 us
    ppermute x10, waiting for transfers between devices, add_over(): lax.ppermute(x, axis, [(i, i ^ k * stride) for i in range(peers)])  12.4 us
    pallas_call x2, Pallas kernels, side_terms(): pair_call(functools.partial(side_kernel, part), name, half, 32, [SMEM, AN...  8.95 us
    ppermute x6, starting transfers between devices, swapped(): return lax.ppermute(x, axis, pairs + [(b, a) for a, b in pairs])  7.21 us
    pallas_call x1, Pallas kernels, south_terms(): pair_call(south_kernel, 'south_pairs', tiles, 32, [ANY, VMEM, VMEM], buff...  6.6 us
    pallas_call x4, Pallas kernels, call(): pl.pallas_call(kernel, name=name, in_specs=[SMEM] + [VMEM] * (len(args) -...  3.12 us
    pallas_call x1, Pallas kernels, edge(): pl.pallas_call(edge_kernel, name='edge', in_specs=[SMEM] + [ANY] * 5, out...  1.93 us
    pallas_call x1, Pallas kernels, pack(): pl.pallas_call(pack_kernel, name='pack', in_specs=[SMEM, ANY, VMEM], out_...  1.75 us
  transfers between devices with their start and end apart: 16, of which 8 were waited for; matrix products, arithmetic and copies ran while one was open for 1% of the time, Pallas kernels for 25%

profile of v7, /device:TPU:0, one launch (start us, length us, event | category | flops | bytes accessed | tf_op | source)
XLA Modules:
  0.0 70.1 jit_solution(9670087719762111410)
XLA Ops:
  0.7 1.9 %edge.1 = (bf16[1,64,640]{2,1,0:T(8,128)(2,1)}, bf16[1,64,640]{2,1,0:T(8,128)(2,1)}, f32[16,128]{1,0:T(8,128)}) custom-call(s32[1]{0:T(128)} %bitcast.2.col_role, bf16[40,4,64,512]{3,2,1,0:T(8,128)(2,1)} %bitcast.17, s32[2,40]{1,0:T(2,128)} %bitcast.23, s32[2,40]{1,0:T(2,128)} %bitcast.24, f32[1,40]{1,0:T(1,128)} %bitcast.25, f32[40,1,896]{2,1,0:T(1,128)} %anchor.3), custom_call_target="tpu_custom_call" | custom-call | tf_op jit(solution)/shard_map/edge/pallas_call | solution.py:463
  2.7 1.7 %collective-permute-start = (bf16[1,64,640]{2,1,0:T(8,128)(2,1)}, bf16[1,64,640]{2,1,0:T(8,128)(2,1)S(1)}, u32[]{:S(2)}, u32[]{:S(2)}) collective-permute-start(bf16[1,64,640]{2,1,0:T(8,128)(2,1)} %get-tuple-element.25), channel_id=1, source_target_pairs={{0,1},{2,3},{1,0},{3,2},{4,5},{6,7},{5,4},{7,6},{8,9},{10,11},{9,8... | collective-permute-start | bytes 245768 | tf_op jit(solution)/shard_map/ppermute | solution.py:825
  4.4 0.7 collective-permute-start.1
  5.1 1.7 %pack.1 = (bf16[11,64,640]{2,1,0:T(8,128)(2,1)S(1)}, bf16[11,64,640]{2,1,0:T(8,128)(2,1)S(1)}, f32[896,128]{1,0:T(8,128)S(1)}) custom-call(s32[1]{0:T(128)} %bitcast.role.refs_0_, bf16[40,4,64,512]{3,2,1,0:T(8,128)(2,1)} %bitcast.18, f32[40,1,896]{2,1,0:T(1,128)S(1)} %copy-done.3), custom_call_target="tpu_custom_call" | custom-call | bytes 6000000 | tf_op jit(solution)/shard_map/pack/pallas_call | solution.py:484
  6.9 0.6 collective-permute-done.one
  7.6 0.7 %collective-permute-start.3 = (bf16[11,64,640]{2,1,0:T(8,128)(2,1)S(1)}, bf16[11,64,640]{2,1,0:T(8,128)(2,1)S(1)}, u32[]{:S(2)}, u32[]{:S(2)}) collective-permute-start(bf16[11,64,640]{2,1,0:T(8,128)(2,1)S(1)} %get-tuple-element.34), channel_id=1, source_target_pairs={{4,8},{12,16},{20,24},{28,32},{36,40},{44,48},{52,56},{60,64},{68,... | collective-permute-start | bytes 2703368 | tf_op jit(solution)/shard_map/ppermute | solution.py:825
  8.4 6.6 %south_pairs.1.terms_south.refs_1_ = f32[32,128]{1,0:T(8,128)S(1)} custom-call(bf16[40,4,64,512]{3,2,1,0:T(8,128)(2,1)} %bitcast.19, bf16[1,64,640]{2,1,0:T(8,128)(2,1)S(1)} %get-tuple-element.30.nxt.next_top.refs_6_, f32[16,128]{1,0:T(8,128)S(1)} %copy-done.4, bf16[64,64]{1,0:T(8,128)(2,1)S(1)} %copy-done.6, bf16[256,256]{1,0:T(8,128)(2,1)S(1)} %copy-done.2, ...), custom_call_target="tpu_custom_call" | custom-call | flops 2400000000 | bytes 3932160 | tf_op jit(solution)/shard_map/south_pairs/pallas_call | solution.py:338
  15.0 4.5 %within_pairs.1.terms.terms_within.refs_2_ = f32[32,128]{1,0:T(8,128)S(1)} custom-call(s32[1]{0:T(128)} %bitcast.role.refs_0_, bf16[40,4,64,512]{3,2,1,0:T(8,128)(2,1)} %bitcast.20, bf16[11,64,640]{2,1,0:T(8,128)(2,1)S(1)} %collective-permute-done.2.received, bf16[1,64,640]{2,1,0:T(8,128)(2,1)S(1)} %get-tuple-element.30.nxt.next_top.refs_6_, ...), custom_call_target="tpu_custom_call" | custom-call | flops 1200000000 | bytes 1966080 | tf_op jit(solution)/shard_map/within_pairs/pallas_call | solution.py:351
  19.5 0.1 message.2
  19.6 3.4 %collective-permute-start.4 = (f32[72,128]{1,0:T(8,128)S(1)}, f32[72,128]{1,0:T(8,128)S(1)}, u32[]{:S(2)}, u32[]{:S(2)}) collective-permute-start(f32[72,128]{1,0:T(8,128)S(1)} %message.2), channel_id=1, source_target_pairs={{0,4},{8,12},{16,20},{24,28},{32,36},{40,44},{48,52},{56,60},{64,6... | collective-permute-start | bytes 110600 | tf_op jit(solution)/shard_map/ppermute | solution.py:825
  23.0 4.5 %across_pairs.1.terms.refs_3_ = f32[32,128]{1,0:T(8,128)S(1)} custom-call(s32[1]{0:T(128)S(6)} %sub.3.role, bf16[40,4,64,512]{3,2,1,0:T(8,128)(2,1)} %bitcast.21, bf16[11,64,640]{2,1,0:T(8,128)(2,1)S(1)} %collective-permute-done.3.received, bf16[1,64,640]{2,1,0:T(8,128)(2,1)S(1)} %get-tuple-element.30.nxt.next_top.refs_6_, ...), custom_call_target="tpu_custom_call" | custom-call | flops 1200000000 | bytes 1966080 | tf_op jit(solution)/shard_map/across_pairs/pallas_call | solution.py:351
  27.5 0.1 message.3
  27.5 0.7 collective-permute-start.5
  28.2 1.6 %powers.1 = (f32[1024,128]{1,0:T(8,128)S(1)}, f32[1024,128]{1,0:T(8,128)S(1)}, f32[1024,128]{1,0:T(8,128)S(1)}, f32[1024,128]{1,0:T(8,128)S(1)}, f32[40,48]{1,0:T(8,128)S(1)}, /*index=5*/f32[8,128]{1,0:T(8,128)S(1)}) custom-call(s32[1]{0:T(128)} %bitcast.role.refs_0_, f32[32,128]{1,0:T(8,128)S(1)} %south_pairs.1.terms_south.refs_1_, ...), custom_call_target="tpu_custom_call" | custom-call | flops 4000000 | bytes 2000000 | tf_op jit(solution)/shard_map/powers/pallas_call | solution.py:518
  29.8 5.0 %collective-permute-start.6 = (f32[8,128]{1,0:T(8,128)S(1)}, f32[8,128]{1,0:T(8,128)S(1)}, u32[]{:S(2)}, u32[]{:S(2)}) collective-permute-start(f32[8,128]{1,0:T(8,128)S(1)} %get-tuple-element.40), channel_id=1, source_target_pairs={{0,4},{4,0},{8,12},{12,8},{16,20},{20,16},{24,28},{28,24},{32,36},... | collective-permute-start | bytes 12296 | tf_op jit(solution)/shard_map/ppermute | solution.py:831
  34.7 0.8 %collective-permute-done.6 = f32[8,128]{1,0:T(8,128)S(1)} collective-permute-done((f32[8,128]{1,0:T(8,128)S(1)}, f32[8,128]{1,0:T(8,128)S(1)}, u32[]{:S(2)}, u32[]{:S(2)}) %collective-permute-start.6) | collective-permute-done | bytes 4128 | tf_op jit(solution)/shard_map/ppermute | solution.py:831
  35.6 2.0 %collective-permute-start.7 = (f32[8,128]{1,0:T(8,128)S(1)}, f32[8,128]{1,0:T(8,128)S(1)}, u32[]{:S(2)}, u32[]{:S(2)}) collective-permute-start(f32[8,128]{1,0:T(8,128)S(1)} %add.39), channel_id=1, source_target_pairs={{0,8},{4,12},{8,0},{12,4},{16,24},{20,28},{24,16},{28,20},{32,40},... | collective-permute-start | bytes 12296 | tf_op jit(solution)/shard_map/ppermute | solution.py:831
  37.5 7.2 %collective-permute-start.8 = (f32[8,128]{1,0:T(8,128)S(1)}, f32[8,128]{1,0:T(8,128)S(1)}, u32[]{:S(2)}, u32[]{:S(2)}) collective-permute-start(f32[8,128]{1,0:T(8,128)S(1)} %add.39), channel_id=1, source_target_pairs={{0,16},{4,20},{8,24},{12,28},{16,0},{20,4},{24,8},{28,12},{32,48},... | collective-permute-start | bytes 12296 | tf_op jit(solution)/shard_map/ppermute | solution.py:831
  44.7 1.6 %collective-permute-done.8 = f32[8,128]{1,0:T(8,128)S(1)} collective-permute-done((f32[8,128]{1,0:T(8,128)S(1)}, f32[8,128]{1,0:T(8,128)S(1)}, u32[]{:S(2)}, u32[]{:S(2)}) %collective-permute-start.8) | collective-permute-done | bytes 4128 | tf_op jit(solution)/shard_map/ppermute | solution.py:831
  46.3 3.2 %collective-permute-done.9 = f32[8,128]{1,0:T(8,128)S(1)} collective-permute-done((f32[8,128]{1,0:T(8,128)S(1)}, f32[8,128]{1,0:T(8,128)S(1)}, u32[]{:S(2)}, u32[]{:S(2)}) %collective-permute-start.9) | collective-permute-done | bytes 4128 | tf_op jit(solution)/shard_map/ppermute | solution.py:831
  49.5 1.5 %collective-permute-start.10 = (f32[8,128]{1,0:T(8,128)S(1)}, f32[8,128]{1,0:T(8,128)S(1)}, u32[]{:S(2)}, u32[]{:S(2)}) collective-permute-start(f32[8,128]{1,0:T(8,128)S(1)} %add_add_fusion.2), channel_id=1, source_target_pairs={{0,32},{4,36},{8,40},{12,44},{16,48},{20,52},{24,56},{28,60},{32,0... | collective-permute-start | bytes 12296 | tf_op jit(solution)/shard_map/ppermute | solution.py:831
  51.0 1.6 %collective-permute-start.11 = (f32[8,128]{1,0:T(8,128)S(1)}, f32[8,128]{1,0:T(8,128)S(1)}, u32[]{:S(2)}, u32[]{:S(2)}) collective-permute-start(f32[8,128]{1,0:T(8,128)S(1)} %add_add_fusion.2), channel_id=1, source_target_pairs={{0,64},{4,68},{8,72},{12,76},{16,80},{20,84},{24,88},{28,92},{32,9... | collective-permute-start | bytes 12296 | tf_op jit(solution)/shard_map/ppermute | solution.py:831
  52.6 1.6 %collective-permute-start.12 = (f32[8,128]{1,0:T(8,128)S(1)}, f32[8,128]{1,0:T(8,128)S(1)}, u32[]{:S(2)}, u32[]{:S(2)}) collective-permute-start(f32[8,128]{1,0:T(8,128)S(1)} %add_add_fusion.2), channel_id=1, source_target_pairs={{0,96},{4,100},{8,104},{12,108},{16,112},{20,116},{24,120},{28,124... | collective-permute-start | bytes 12296 | tf_op jit(solution)/shard_map/ppermute | solution.py:831
  54.2 1.9 %collective-permute-done.11 = f32[8,128]{1,0:T(8,128)S(1)} collective-permute-done((f32[8,128]{1,0:T(8,128)S(1)}, f32[8,128]{1,0:T(8,128)S(1)}, u32[]{:S(2)}, u32[]{:S(2)}) %collective-permute-start.11) | collective-permute-done | bytes 4128 | tf_op jit(solution)/shard_map/ppermute | solution.py:831
  56.1 1.3 %collective-permute-done.12 = f32[8,128]{1,0:T(8,128)S(1)} collective-permute-done((f32[8,128]{1,0:T(8,128)S(1)}, f32[8,128]{1,0:T(8,128)S(1)}, u32[]{:S(2)}, u32[]{:S(2)}) %collective-permute-start.12) | collective-permute-done | bytes 4128 | tf_op jit(solution)/shard_map/ppermute | solution.py:831
  57.5 4.3 %collective-permute-start.13 = (f32[8,128]{1,0:T(8,128)S(1)}, f32[8,128]{1,0:T(8,128)S(1)}, u32[]{:S(2)}, u32[]{:S(2)}) collective-permute-start(f32[8,128]{1,0:T(8,128)S(1)} %add_add_fusion.1), channel_id=1, source_target_pairs={{0,1},{1,0},{2,3},{3,2},{4,5},{5,4},{6,7},{7,6},{8,9},{9,8},{10,11... | collective-permute-start | bytes 12296 | tf_op jit(solution)/shard_map/ppermute | solution.py:831
  61.8 2.1 %collective-permute-start.14 = (f32[8,128]{1,0:T(8,128)S(1)}, f32[8,128]{1,0:T(8,128)S(1)}, u32[]{:S(2)}, u32[]{:S(2)}) collective-permute-start(f32[8,128]{1,0:T(8,128)S(1)} %add_add_fusion.1), channel_id=1, source_target_pairs={{0,2},{1,3},{2,0},{3,1},{4,6},{5,7},{6,4},{7,5},{8,10},{9,11},{10,... | collective-permute-start | bytes 12296 | tf_op jit(solution)/shard_map/ppermute | solution.py:831
  63.9 0.6 collective-permute-start.15
  64.5 0.7 copy.20
  65.2 1.7 %collective-permute-done.14 = f32[8,128]{1,0:T(8,128)S(1)} collective-permute-done((f32[8,128]{1,0:T(8,128)S(1)}, f32[8,128]{1,0:T(8,128)S(1)}, u32[]{:S(2)}, u32[]{:S(2)}) %collective-permute-start.14) | collective-permute-done | bytes 4128 | tf_op jit(solution)/shard_map/ppermute | solution.py:831
  66.9 1.8 %collective-permute-done.15 = f32[8,128]{1,0:T(8,128)S(1)} collective-permute-done((f32[8,128]{1,0:T(8,128)S(1)}, f32[8,128]{1,0:T(8,128)S(1)}, u32[]{:S(2)}, u32[]{:S(2)}) %collective-permute-start.15) | collective-permute-done | bytes 4128 | tf_op jit(solution)/shard_map/ppermute | solution.py:831
  68.7 1.4 %combine.1 = (f32[40,2,896]{2,1,0:T(2,128)}, f32[40,2,896]{2,1,0:T(2,128)}) custom-call(f32[8,128]{1,0:T(8,128)S(1)} %add_add_fusion.gram, f32[1024,128]{1,0:T(8,128)S(1)} %get-tuple-element.41.v0, f32[1024,128]{1,0:T(8,128)S(1)} %get-tuple-element.42.v1, f32[1024,128]{1,0:T(8,128)S(1)} %get-tuple-element.43.v2, f32[1024,128]{1,0:T(8,128)S(1)} %get-tuple-element.44.v3), custom_call_target="tpu_custom_call" | custom-call | flops 4000000 | bytes 2000000 | tf_op jit(solution)/shard_map/combine/pallas_call | solution.py:518
  (33 shorter events, 0.2 us)
Async XLA Ops:
  0.6 4.5 %copy-start.3 = (f32[40,1,896]{2,1,0:T(1,128)S(1)}, f32[40,1,896]{2,1,0:T(1,128)}, u32[]{:S(2)}) copy-start(f32[40,1,896]{2,1,0:T(1,128)} %anchor.3) | copy-start | bytes 430084
  0.7 7.6 %copy-start = (bf16[256,512]{1,0:T(8,128)(2,1)S(1)}, bf16[256,512]{1,0:T(8,128)(2,1)}, u32[]{:S(2)}) copy-start(bf16[256,512]{1,0:T(8,128)(2,1)} %constant.44.clone.ends) | copy-start | bytes 786436
  0.7 7.6 %copy-start.1 = (bf16[2,256,256]{2,1,0:T(8,128)(2,1)S(1)}, bf16[2,256,256]{2,1,0:T(8,128)(2,1)}, u32[]{:S(2)}) copy-start(bf16[2,256,256]{2,1,0:T(8,128)(2,1)} %constant.45.clone.backs) | copy-start | bytes 786436
  0.7 7.6 %copy-start.2 = (bf16[256,256]{1,0:T(8,128)(2,1)S(1)}, bf16[256,256]{1,0:T(8,128)(2,1)}, u32[]{:S(2)}) copy-start(bf16[256,256]{1,0:T(8,128)(2,1)} %constant.43.clone.forward) | copy-start | bytes 393220
  0.7 7.6 %copy-start.5 = (f32[64,128]{1,0:T(8,128)S(1)}, f32[64,128]{1,0:T(8,128)}, u32[]{:S(2)}) copy-start(f32[64,128]{1,0:T(8,128)} %constant.48.clone.rows) | copy-start | bytes 98308
  0.7 7.6 %copy-start.6 = (bf16[64,64]{1,0:T(8,128)(2,1)S(1)}, bf16[64,64]{1,0:T(8,128)(2,1)}, u32[]{:S(2)}) copy-start(bf16[64,64]{1,0:T(8,128)(2,1)} %constant.42.clone.depth) | copy-start | bytes 24580
  0.7 7.6 %copy-start.7 = (bf16[64,64]{1,0:T(8,128)(2,1)S(1)}, bf16[64,64]{1,0:T(8,128)(2,1)}, u32[]{:S(2)}) copy-start(bf16[64,64]{1,0:T(8,128)(2,1)} %constant.46.clone.final) | copy-start | bytes 24580
  0.7 7.6 %copy-start.8 = (f32[8,128]{1,0:T(8,128)S(1)}, f32[8,128]{1,0:T(8,128)}, u32[]{:S(2)}) copy-start(f32[8,128]{1,0:T(8,128)} %constant.47.clone.pick) | copy-start | bytes 12292
  2.7 4.7 %copy-start.4 = (f32[16,128]{1,0:T(8,128)S(1)}, f32[16,128]{1,0:T(8,128)}, u32[]{:S(2)}) copy-start(f32[16,128]{1,0:T(8,128)} %get-tuple-element.27.info.refs_8_) | copy-start | bytes 24580
  2.7 4.7 %collective-permute-start = (bf16[1,64,640]{2,1,0:T(8,128)(2,1)}, bf16[1,64,640]{2,1,0:T(8,128)(2,1)S(1)}, u32[]{:S(2)}, u32[]{:S(2)}) collective-permute-start(bf16[1,64,640]{2,1,0:T(8,128)(2,1)} %get-tuple-element.25), channel_id=1, source_target_pairs={{0,1},{2,3},{1,0},{3,2},{4,5},{6,7},{5,4},{7,6},{8,9},{10,11},{9,8... | collective-permute-start | bytes 245768 | tf_op jit(solution)/shard_map/ppermute | solution.py:825
  4.4 3.0 %collective-permute-start.1 = (bf16[1,64,640]{2,1,0:T(8,128)(2,1)}, bf16[1,64,640]{2,1,0:T(8,128)(2,1)S(1)}, u32[]{:S(2)}, u32[]{:S(2)}) collective-permute-start(bf16[1,64,640]{2,1,0:T(8,128)(2,1)} %get-tuple-element.26), channel_id=1, source_target_pairs={{1,2},{2,1},{5,6},{6,5},{9,10},{10,9},{13,14},{14,13},{17,18},{18,... | collective-permute-start | bytes 245768 | tf_op jit(solution)/shard_map/ppermute | solution.py:825
  7.5 7.5 %collective-permute-start.2 = (bf16[11,64,640]{2,1,0:T(8,128)(2,1)S(1)}, bf16[11,64,640]{2,1,0:T(8,128)(2,1)S(1)}, u32[]{:S(2)}, u32[]{:S(2)}) collective-permute-start(bf16[11,64,640]{2,1,0:T(8,128)(2,1)S(1)} %get-tuple-element.31), channel_id=1, source_target_pairs={{0,4},{8,12},{16,20},{24,28},{32,36},{40,44},{48,52},{56,60},{64,6... | collective-permute-start | bytes 2703368 | tf_op jit(solution)/shard_map/ppermute | solution.py:825
  7.6 12.0 %collective-permute-start.3 = (bf16[11,64,640]{2,1,0:T(8,128)(2,1)S(1)}, bf16[11,64,640]{2,1,0:T(8,128)(2,1)S(1)}, u32[]{:S(2)}, u32[]{:S(2)}) collective-permute-start(bf16[11,64,640]{2,1,0:T(8,128)(2,1)S(1)} %get-tuple-element.34), channel_id=1, source_target_pairs={{4,8},{12,16},{20,24},{28,32},{36,40},{44,48},{52,56},{60,64},{68,... | collective-permute-start | bytes 2703368 | tf_op jit(solution)/shard_map/ppermute | solution.py:825
  19.6 7.9 %collective-permute-start.4 = (f32[72,128]{1,0:T(8,128)S(1)}, f32[72,128]{1,0:T(8,128)S(1)}, u32[]{:S(2)}, u32[]{:S(2)}) collective-permute-start(f32[72,128]{1,0:T(8,128)S(1)} %message.2), channel_id=1, source_target_pairs={{0,4},{8,12},{16,20},{24,28},{32,36},{40,44},{48,52},{56,60},{64,6... | collective-permute-start | bytes 110600 | tf_op jit(solution)/shard_map/ppermute | solution.py:825
  27.5 0.7 collective-permute-start.5
  29.8 5.8 %collective-permute-start.6 = (f32[8,128]{1,0:T(8,128)S(1)}, f32[8,128]{1,0:T(8,128)S(1)}, u32[]{:S(2)}, u32[]{:S(2)}) collective-permute-start(f32[8,128]{1,0:T(8,128)S(1)} %get-tuple-element.40), channel_id=1, source_target_pairs={{0,4},{4,0},{8,12},{12,8},{16,20},{20,16},{24,28},{28,24},{32,36},... | collective-permute-start | bytes 12296 | tf_op jit(solution)/shard_map/ppermute | solution.py:831
  35.6 9.1 %collective-permute-start.7 = (f32[8,128]{1,0:T(8,128)S(1)}, f32[8,128]{1,0:T(8,128)S(1)}, u32[]{:S(2)}, u32[]{:S(2)}) collective-permute-start(f32[8,128]{1,0:T(8,128)S(1)} %add.39), channel_id=1, source_target_pairs={{0,8},{4,12},{8,0},{12,4},{16,24},{20,28},{24,16},{28,20},{32,40},... | collective-permute-start | bytes 12296 | tf_op jit(solution)/shard_map/ppermute | solution.py:831
  37.5 8.8 %collective-permute-start.8 = (f32[8,128]{1,0:T(8,128)S(1)}, f32[8,128]{1,0:T(8,128)S(1)}, u32[]{:S(2)}, u32[]{:S(2)}) collective-permute-start(f32[8,128]{1,0:T(8,128)S(1)} %add.39), channel_id=1, source_target_pairs={{0,16},{4,20},{8,24},{12,28},{16,0},{20,4},{24,8},{28,12},{32,48},... | collective-permute-start | bytes 12296 | tf_op jit(solution)/shard_map/ppermute | solution.py:831
  44.7 4.8 %collective-permute-start.9 = (f32[8,128]{1,0:T(8,128)S(1)}, f32[8,128]{1,0:T(8,128)S(1)}, u32[]{:S(2)}, u32[]{:S(2)}) collective-permute-start(f32[8,128]{1,0:T(8,128)S(1)} %add.39), channel_id=1, source_target_pairs={{0,24},{4,28},{8,16},{12,20},{16,8},{20,12},{24,0},{28,4},{32,56},... | collective-permute-start | bytes 12296 | tf_op jit(solution)/shard_map/ppermute | solution.py:831
  49.5 4.7 %collective-permute-start.10 = (f32[8,128]{1,0:T(8,128)S(1)}, f32[8,128]{1,0:T(8,128)S(1)}, u32[]{:S(2)}, u32[]{:S(2)}) collective-permute-start(f32[8,128]{1,0:T(8,128)S(1)} %add_add_fusion.2), channel_id=1, source_target_pairs={{0,32},{4,36},{8,40},{12,44},{16,48},{20,52},{24,56},{28,60},{32,0... | collective-permute-start | bytes 12296 | tf_op jit(solution)/shard_map/ppermute | solution.py:831
  51.0 5.1 %collective-permute-start.11 = (f32[8,128]{1,0:T(8,128)S(1)}, f32[8,128]{1,0:T(8,128)S(1)}, u32[]{:S(2)}, u32[]{:S(2)}) collective-permute-start(f32[8,128]{1,0:T(8,128)S(1)} %add_add_fusion.2), channel_id=1, source_target_pairs={{0,64},{4,68},{8,72},{12,76},{16,80},{20,84},{24,88},{28,92},{32,9... | collective-permute-start | bytes 12296 | tf_op jit(solution)/shard_map/ppermute | solution.py:831
  52.6 4.8 %collective-permute-start.12 = (f32[8,128]{1,0:T(8,128)S(1)}, f32[8,128]{1,0:T(8,128)S(1)}, u32[]{:S(2)}, u32[]{:S(2)}) collective-permute-start(f32[8,128]{1,0:T(8,128)S(1)} %add_add_fusion.2), channel_id=1, source_target_pairs={{0,96},{4,100},{8,104},{12,108},{16,112},{20,116},{24,120},{28,124... | collective-permute-start | bytes 12296 | tf_op jit(solution)/shard_map/ppermute | solution.py:831
  57.5 7.7 %collective-permute-start.13 = (f32[8,128]{1,0:T(8,128)S(1)}, f32[8,128]{1,0:T(8,128)S(1)}, u32[]{:S(2)}, u32[]{:S(2)}) collective-permute-start(f32[8,128]{1,0:T(8,128)S(1)} %add_add_fusion.1), channel_id=1, source_target_pairs={{0,1},{1,0},{2,3},{3,2},{4,5},{5,4},{6,7},{7,6},{8,9},{9,8},{10,11... | collective-permute-start | bytes 12296 | tf_op jit(solution)/shard_map/ppermute | solution.py:831
  61.8 5.1 %collective-permute-start.14 = (f32[8,128]{1,0:T(8,128)S(1)}, f32[8,128]{1,0:T(8,128)S(1)}, u32[]{:S(2)}, u32[]{:S(2)}) collective-permute-start(f32[8,128]{1,0:T(8,128)S(1)} %add_add_fusion.1), channel_id=1, source_target_pairs={{0,2},{1,3},{2,0},{3,1},{4,6},{5,7},{6,4},{7,5},{8,10},{9,11},{10,... | collective-permute-start | bytes 12296 | tf_op jit(solution)/shard_map/ppermute | solution.py:831
  63.9 4.8 %collective-permute-start.15 = (f32[8,128]{1,0:T(8,128)S(1)}, f32[8,128]{1,0:T(8,128)S(1)}, u32[]{:S(2)}, u32[]{:S(2)}) collective-permute-start(f32[8,128]{1,0:T(8,128)S(1)} %add_add_fusion.1), channel_id=1, source_target_pairs={{0,3},{1,2},{2,1},{3,0},{4,7},{5,6},{6,5},{7,4},{8,11},{9,10},{10,... | collective-permute-start | bytes 12296 | tf_op jit(solution)/shard_map/ppermute | solution.py:831
